TPU v7x, 128 devices: a whole 4x4x4 slice. The times are simulated.
128 devices in a mesh: dp: 16 (over z, x), mp: 8 (over y, core).
Axes of the slice: x: 4, y: 4, z: 4, core: 2. Of those that a mesh axis runs over, the one named last changes fastest.
Arguments:
- tokens: bfloat16 [32768, 2048], P('dp'), may hold values from -0.75 to 0.75
- out_grad: bfloat16 [32768, 2048], P('dp'), may hold values from -3 to 3
- down_rows: bfloat16 [8192, 2048], P(('dp', 'mp')), may hold values from -1 to 1
- up_rows: bfloat16 [8192, 2048], P(('dp', 'mp')), may hold values from -1 to 1
- requests: int32 [128, 128, 2], P(('dp', 'mp')), may hold values from 0 to 64, as said below
- places: int32 [8, 32768, 16], P('mp', 'dp'), may hold values from 0 to 255, as said below
- gate_weights: float32 [8, 32768, 16], P('mp', 'dp'), may hold values from 0.05 to 0.5
Outputs:
- input_grad: bfloat16 [32768, 2048], P(('dp', 'mp'))
- down_grad: float32 [8192, 2048], P(('dp', 'mp'))
- up_grad: float32 [8192, 2048], P(('dp', 'mp'))
Inputs may be any that keep to these rules, and one draw needn't show every extreme that they name: requests[d, o] lists distinct rows, numbered within owner o's block of 64, that device d uses; the used ones come first and the rest of the 2 places hold 64. Every device uses at least one row of every owner, and all 2 places of some owner. The 16 entries of one head and token are distinct places, each of which names an expert in the request list of the device holding that head and token.
All inputs are finite; a program needn't handle non-finite values.
Results may differ from a plain program's by a relative error of at most 0.013.
Values may be sent and summed in bfloat16 or wider, within the bound.
No kernel may reach another device: no remote copies, remote signals or barrier semaphores. Data moves between devices by JAX's collectives and lax.ppermute only.
A program may use at most 128 MiB of HBM per device.

v0:
```python
import jax
import jax.numpy as jnp
from jax import lax
from jax.sharding import PartitionSpec as P

SQRT_HALF = 0.7071067811865476
INV_ROOT_TAU = 0.3989422804014327


def gelu_parts(pre):
    normal_cdf = 0.5 * (1.0 + lax.erf(pre * SQRT_HALF))
    density = INV_ROOT_TAU * jnp.exp(-0.5 * pre * pre)
    return (pre * normal_cdf, normal_cdf + pre * density)


def local_terms(block_tokens, block_grad, fetched_down, fetched_up, block_places, block_gates):
    token_count = block_tokens.shape[0]
    place_count = fetched_down.shape[0]
    chosen = jnp.transpose(block_places, (1, 0, 2)).reshape(token_count, -1)
    weights_in = jnp.transpose(block_gates, (1, 0, 2)).reshape(token_count, -1)
    columns = jnp.arange(place_count, dtype=jnp.int32)
    weight = jnp.sum(
        jnp.where(
            chosen[:, :, None] == columns[None, None, :],
            weights_in[:, :, None],
            jnp.zeros((), weights_in.dtype),
        ),
        axis=1,
    )
    pre = lax.dot_general(
        block_tokens, fetched_down, (((1,), (1,)), ((), ())), preferred_element_type=jnp.float32
    )
    back = lax.dot_general(
        block_grad, fetched_up, (((1,), (1,)), ((), ())), preferred_element_type=jnp.float32
    )
    active, slope = gelu_parts(pre)
    coef = (weight * slope * back).astype(jnp.bfloat16)
    gated = (weight * active).astype(jnp.bfloat16)
    part_down = lax.dot_general(
        coef, block_tokens, (((0,), (0,)), ((), ())), preferred_element_type=jnp.float32
    )
    part_up = lax.dot_general(
        gated, block_grad, (((0,), (0,)), ((), ())), preferred_element_type=jnp.float32
    )
    return (coef, part_down, part_up)


def shards(tokens, out_grad, down_rows, up_rows, requests, places, gate_weights):
    n_data = lax.axis_size("dp")
    n_model = lax.axis_size("mp")
    devices = n_data * n_model
    row_count = down_rows.shape[0]
    width = tokens.shape[1]
    wanted = requests[0]
    capacity = wanted.shape[1]
    asked = lax.all_to_all(wanted, ("dp", "mp"), split_axis=0, concat_axis=0, tiled=True)
    live = (wanted < row_count).reshape(-1)
    table = jnp.concatenate([down_rows, up_rows], axis=1)
    outgoing = jnp.take(table, jnp.minimum(asked, row_count - 1).reshape(-1), axis=0).reshape(
        devices, capacity, 2 * width
    )
    arrived = lax.all_to_all(outgoing, ("dp", "mp"), split_axis=0, concat_axis=0, tiled=True)
    arrived = arrived.reshape(devices * capacity, 2 * width)
    arrived = jnp.where(live[:, None], arrived, jnp.zeros((), arrived.dtype))
    fetched_down = arrived[:, :width]
    fetched_up = arrived[:, width:]
    coef, part_down, part_up = local_terms(
        tokens, out_grad, fetched_down, fetched_up, places, gate_weights
    )
    pushed = jnp.concatenate([part_down, part_up], axis=1).reshape(devices, capacity, 2 * width)
    returned = lax.all_to_all(
        pushed.astype(jnp.bfloat16), ("dp", "mp"), split_axis=0, concat_axis=0, tiled=True
    ).astype(pushed.dtype)
    returned = returned.reshape(devices * capacity, 2 * width)
    selector = (asked.reshape(1, -1) == jnp.arange(row_count, dtype=jnp.int32)[:, None]).astype(
        jnp.float32
    )
    summed = jnp.dot(
        selector, returned, precision=lax.Precision.HIGHEST, preferred_element_type=jnp.float32
    )
    down_grad = summed[:, :width]
    up_grad = summed[:, width:]
    input_grad = lax.psum_scatter(
        jnp.dot(coef, fetched_down, preferred_element_type=jnp.float32).astype(jnp.bfloat16),
        "mp",
        scatter_dimension=0,
        tiled=True,
    )
    return (input_grad, down_grad, up_grad)


def solution(mesh):
    in_specs = (
        P("dp", None),
        P("dp", None),
        P(("dp", "mp"), None),
        P(("dp", "mp"), None),
        P(("dp", "mp"), None, None),
        P("mp", "dp", None),
        P("mp", "dp", None),
    )
    out_specs = (P(("dp", "mp"), None), P(("dp", "mp"), None), P(("dp", "mp"), None))
    return jax.shard_map(shards, mesh=mesh, in_specs=in_specs, out_specs=out_specs, check_vma=False)
```

profile of v0, /device:TPU:1, one launch (start us, length us, event | category | flops | bytes accessed | tf_op | source)
XLA Modules:
  0.0 171.5 jit_solution(10159898412558711153)
XLA Ops:
  7.2 1.4 copy.26
  8.6 11.5 %all-to-all-start = ((s32[128,1,2]{2,1,0:T(1,128)}), s32[128,1,2]{2,1,0:T(1,128)S(1)}, u32[]{:S(2)}, u32[]{:S(2)}) async-start(s32[128,1,2]{2,1,0:T(1,128)} %bitcast.2), calls=%async_computation | async-start | bytes 131072 | tf_op jit(solution)/shard_map/all_to_all | solution.py:56
  20.1 1.1 pad_maximum_fusion.1
  21.1 8.5 %all-to-all-done = s32[128,1,2]{2,1,0:T(1,128)S(1)} async-done(((s32[128,1,2]{2,1,0:T(1,128)}), s32[128,1,2]{2,1,0:T(1,128)S(1)}, u32[]{:S(2)}, u32[]{:S(2)}) %all-to-all-start) | async-done | bytes 1056 | tf_op jit(solution)/shard_map/all_to_all | solution.py:56
  29.6 0.5 broadcast.62
  30.1 1.0 fusion.13
  31.1 0.1 min.29
  31.3 1.8 %gather_fusion = bf16[256,4096]{1,0:T(8,128)(2,1)S(1)} fusion(bf16[64,4096]{1,0:T(8,128)(2,1)S(1)} %pad_maximum_fusion.1, s32[1024]{0:T(1024)S(1)} %pad_clamp_fusion), kind=kCustom, calls=%fused_computation | custom fusion | bytes 4195328 | tf_op jit(solution)/shard_map/jit(_take)/gather | solution.py:59
  33.2 2.6 %gather.7 = bf16[128,2,4096]{2,1,0:T(2,128)(2,1)} reshape(bf16[256,4096]{1,0:T(8,128)(2,1)S(1)} %gather_fusion) | data formatting | bytes 4194304 | tf_op jit(solution)/shard_map/jit(_take)/gather | solution.py:59
  35.8 5.0 %broadcast_select_fusion = bf16[128,2,4096]{2,1,0:T(2,128)(2,1)} fusion(bf16[128,2,4096]{2,1,0:T(2,128)(2,1)} %gather.7, pred[128,2]{1,0:T(8,128)(4,1)S(1)} %compare_and_fusion), kind=kLoop, calls=%fused_computation.4 | loop fusion | flops 1048576 | bytes 4194560 | tf_op jit(solution)/shard_map/jit(_take)/select_n | solution.py:59
  40.8 4.4 %all-to-all-start.1 = ((bf16[128,2,4096]{2,1,0:T(2,128)(2,1)}), bf16[128,2,4096]{2,1,0:T(2,128)(2,1)S(1)}, u32[]{:S(2)}, u32[]{:S(2)}) async-start(bf16[128,2,4096]{2,1,0:T(2,128)(2,1)} %broadcast_select_fusion), calls=%async_computation.1 | async-start | bytes 4194304 | tf_op jit(solution)/shard_map/all_to_all | solution.py:62
  45.2 0.2 reduce-scatter.2.cloned.1.call-start
  45.5 0.0 copy-done.3
  45.5 0.1 copy.25
  45.6 0.1 lt.39
  45.8 0.0 copy-done.1
  45.8 0.3 copy.23
  46.1 0.0 copy-done.2
  46.1 1.3 copy.24
  47.5 15.2 %select_reduce_fusion = f32[2048,256]{1,0:T(8,128)} fusion(f32[2048,16]{1,0:T(8,128)} %copy.24, s32[2048,16]{1,0:T(8,128)S(1)} %copy.23), kind=kLoop, calls=%fused_computation.1 | loop fusion | flops 24641536 | bytes 2359296 | tf_op jit(solution)/shard_map/reduce_sum | solution.py:22
  62.7 2.9 %copy.27 = f32[2048,256]{0,1:T(8,128)} copy(f32[2048,256]{1,0:T(8,128)} %select_reduce_fusion) | data formatting | bytes 4194304 | tf_op jit(solution)/shard_map/reduce_sum | solution.py:22
  65.6 9.8 %all-to-all-done.1 = bf16[128,2,4096]{2,1,0:T(2,128)(2,1)S(1)} async-done(((bf16[128,2,4096]{2,1,0:T(2,128)(2,1)}), bf16[128,2,4096]{2,1,0:T(2,128)(2,1)S(1)}, u32[]{:S(2)}, u32[]{:S(2)}) %all-to-all-start.1) | async-done | bytes 2097184 | tf_op jit(solution)/shard_map/all_to_all | solution.py:62
  75.4 2.2 %reshape.67 = bf16[256,4096]{1,0:T(8,128)(2,1)} reshape(bf16[128,2,4096]{2,1,0:T(2,128)(2,1)S(1)} %all-to-all-done.1) | data formatting | bytes 4194304 | tf_op jit(solution)/shard_map/reshape | solution.py:63
  77.6 1.9 %broadcast_select_fusion.1 = bf16[256,4096]{1,0:T(8,128)(2,1)S(1)} fusion(bf16[256,4096]{1,0:T(8,128)(2,1)} %reshape.67, pred[256]{0:T(512)(128)(4,1)S(1)} %lt.39), kind=kLoop, calls=%fused_computation.20 | loop fusion | flops 1048576 | bytes 4194560 | tf_op jit(solution)/shard_map/jit(_where)/select_n | solution.py:64
  79.6 0.0 copy-start
  79.6 0.0 slice-start.1
  79.6 5.9 %convolution_bitcast_fusion.1 = f32[2048,256]{0,1:T(8,128)S(1)} fusion(bf16[2048,2048]{1,0:T(8,128)(2,1)} %param.7, bf16[256,4096]{1,0:T(8,128)(2,1)S(1)} %broadcast_select_fusion.1), kind=kOutput, calls=%fused_computation.8 | convolution fusion | flops 2147483648 | bytes 11534336 | tf_op jit(solution)/shard_map/dot_general | solution.py:30
  85.5 0.0 slice-done
  85.5 0.0 copy-done
  85.5 0.0 slice-done.1
  85.5 0.0 copy-start.4
  85.6 3.2 %fusion.1 = bf16[2048,256]{0,1:T(8,128)(2,1)S(1)} fusion(bf16[2048,2048]{1,0:T(8,128)(2,1)S(1)} %bitcast.25, f32[2048,256]{0,1:T(8,128)S(1)} %copy-done, f32[2048,256]{0,1:T(8,128)S(1)} %convolution_bitcast_fusion.1, bf16[256,4096]{1,0:T(8,128)(2,1)S(1)} %broadcast_select_fusion.1), kind=kOutput, calls=%fused_computation.9 | convolution fusion | flops 2153250816 | bytes 14680064 | tf_op jit(solution)/shard_map/dot_general | solution.py:33
  88.7 0.0 copy-done.4
  88.7 5.6 %convolution_convert_fusion = bf16[2048,2048]{1,0:T(8,128)(2,1)} fusion(bf16[2048,256]{0,1:T(8,128)(2,1)S(1)} %fusion.1, bf16[256,4096]{1,0:T(8,128)(2,1)S(1)} %broadcast_select_fusion.1), kind=kOutput, calls=%fused_computation.3 | convolution fusion | flops 2151677952 | bytes 10485760 | tf_op jit(solution)/shard_map/dot_general | solution.py:84
  94.4 0.0 reduce-scatter.2.cloned.1.call-update
  94.4 0.0 copy-start.5
  94.4 5.9 %convolution_convert_fusion.2 = bf16[256,2048]{1,0:T(8,128)(2,1)S(1)} fusion(bf16[2048,256]{0,1:T(8,128)(2,1)S(1)} %fusion.1, bf16[2048,2048]{1,0:T(8,128)(2,1)} %param.7), kind=kOutput, calls=%fused_computation.11 | convolution fusion | flops 2148007936 | bytes 10485760 | tf_op jit(solution)/shard_map/dot_general | solution.py:39
  100.3 0.0 copy-done.5
  100.3 5.7 %convolution_convert_fusion.1 = bf16[256,2048]{1,0:T(8,128)(2,1)S(1)} fusion(bf16[2048,2048]{1,0:T(8,128)(2,1)} %param.8, f32[2048,256]{0,1:T(8,128)S(1)} %copy-done, f32[2048,256]{0,1:T(8,128)S(1)} %copy-done.5), kind=kOutput, calls=%fused_computation.10 | convolution fusion | flops 2151153664 | bytes 13631488 | tf_op jit(solution)/shard_map/dot_general | solution.py:42
  106.0 0.1 pad_maximum_fusion
  106.2 2.7 %convert_element_type.18 = bf16[128,2,4096]{2,1,0:T(2,128)(2,1)} reshape(bf16[256,4096]{1,0:T(8,128)(2,1)S(1)} %pad_maximum_fusion) | data formatting | bytes 4194304 | tf_op jit(solution)/shard_map/convert_element_type | solution.py:72
  108.8 4.8 %all-to-all-start.2 = ((bf16[128,2,4096]{2,1,0:T(2,128)(2,1)}), bf16[128,2,4096]{2,1,0:T(2,128)(2,1)S(1)}, u32[]{:S(2)}, u32[]{:S(2)}) async-start(bf16[128,2,4096]{2,1,0:T(2,128)(2,1)} %convert_element_type.18), calls=%async_computation.3 | async-start | bytes 4194304 | tf_op jit(solution)/shard_map/all_to_all | solution.py:71
  113.6 0.1 all_to_all.17
  113.7 31.7 %all-to-all-done.2 = bf16[128,2,4096]{2,1,0:T(2,128)(2,1)S(1)} async-done(((bf16[128,2,4096]{2,1,0:T(2,128)(2,1)}), bf16[128,2,4096]{2,1,0:T(2,128)(2,1)S(1)}, u32[]{:S(2)}, u32[]{:S(2)}) %all-to-all-start.2) | async-done | bytes 2097184 | tf_op jit(solution)/shard_map/all_to_all | solution.py:71
  145.5 2.2 %reshape.68 = bf16[256,4096]{1,0:T(8,128)(2,1)} reshape(bf16[128,2,4096]{2,1,0:T(2,128)(2,1)S(1)} %all-to-all-done.2) | data formatting | bytes 4194304 | tf_op jit(solution)/shard_map/reshape | solution.py:74
  147.7 2.1 %fusion.10 = f32[64,4096]{1,0:T(8,128)S(1)} fusion(bf16[256,4096]{1,0:T(8,128)(2,1)} %reshape.68, s32[256]{0:T(256)S(1)} %all_to_all.17), kind=kOutput, calls=%fused_computation.27 | convolution fusion | flops 134234112 | bytes 3146752 | tf_op jit(solution)/shard_map/dot_general | solution.py:78
  149.8 1.1 fusion.14
  150.9 13.7 %reduce-scatter.2.cloned.1.call-done = bf16[256,2048]{1,0:T(8,128)(2,1)} async-done(((bf16[2048,2048]{1,0:T(8,128)(2,1)}), bf16[256,2048]{1,0:T(8,128)(2,1)}) %reduce-scatter.2.cloned.1.call-update) | async-done | bytes 1048592 | tf_op jit(solution)/shard_map/reduce_scatter | solution.py:83
  (9 shorter events, 0.0 us)
Async XLA Ops:
  8.6 21.1 %all-to-all-start = ((s32[128,1,2]{2,1,0:T(1,128)}), s32[128,1,2]{2,1,0:T(1,128)S(1)}, u32[]{:S(2)}, u32[]{:S(2)}) async-start(s32[128,1,2]{2,1,0:T(1,128)} %bitcast.2), calls=%async_computation | async-start | bytes 131072 | tf_op jit(solution)/shard_map/all_to_all | solution.py:56
  40.8 4.6 %copy-start.3 = (s32[1,128,2]{1,2,0:T(2,128)S(1)}, s32[1,128,2]{1,2,0:T(2,128)}, u32[]{:S(2)}) copy-start(s32[1,128,2]{1,2,0:T(2,128)} %param.11) | copy-start | bytes 3076
  40.8 5.0 %copy-start.1 = (s32[1,2048,16]{1,2,0:T(8,128)S(1)}, s32[1,2048,16]{1,2,0:T(8,128)}, u32[]{:S(2)}) copy-start(s32[1,2048,16]{1,2,0:T(8,128)} %param.12) | copy-start | bytes 393220
  40.8 5.3 %copy-start.2 = (f32[1,2048,16]{1,2,0:T(8,128)S(1)}, f32[1,2048,16]{1,2,0:T(8,128)}, u32[]{:S(2)}) copy-start(f32[1,2048,16]{1,2,0:T(8,128)} %param.13) | copy-start | bytes 393220
  40.8 34.6 %all-to-all-start.1 = ((bf16[128,2,4096]{2,1,0:T(2,128)(2,1)}), bf16[128,2,4096]{2,1,0:T(2,128)(2,1)S(1)}, u32[]{:S(2)}, u32[]{:S(2)}) async-start(bf16[128,2,4096]{2,1,0:T(2,128)(2,1)} %broadcast_select_fusion), calls=%async_computation.1 | async-start | bytes 4194304 | tf_op jit(solution)/shard_map/all_to_all | solution.py:62
  45.2 119.4 %reduce-scatter.2.cloned.1.call-start = ((), (), s32[]{:S(2)}) async-start(), calls=%async_computation.4 | async-start | bytes 9437184 | tf_op jit(solution)/shard_map/reduce_scatter | solution.py:83
  77.6 7.9 %slice-start = ((s8[8388608]{0:T(1024)(128)(4,1)}), s8[4194304]{0:T(1024)(128)(4,1)S(1)}, s32[]{:S(2)}) async-start(s8[8388608]{0:T(1024)(128)(4,1)} %bitcast.24), calls=%async_computation.5 | async-start | bytes 8388608
  79.6 5.9 %copy-start = (f32[2048,256]{0,1:T(8,128)S(1)}, f32[2048,256]{0,1:T(8,128)}, u32[]{:S(2)}) copy-start(f32[2048,256]{0,1:T(8,128)} %copy.27) | copy-start | bytes 6291460
  79.6 5.9 %slice-start.1 = ((s8[8388608]{0:T(1024)(128)(4,1)}), s8[4194304]{0:T(1024)(128)(4,1)S(1)}, s32[]{:S(2)}) async-start(s8[8388608]{0:T(1024)(128)(4,1)} %bitcast.24), calls=%async_computation.6 | async-start | bytes 8388608
  85.5 3.2 %copy-start.4 = (f32[2048,256]{0,1:T(8,128)}, f32[2048,256]{0,1:T(8,128)S(1)}, u32[]{:S(2)}) copy-start(f32[2048,256]{0,1:T(8,128)S(1)} %convolution_bitcast_fusion.1) | copy-start | bytes 6291460
  94.4 5.9 %copy-start.5 = (f32[2048,256]{0,1:T(8,128)S(1)}, f32[2048,256]{0,1:T(8,128)}, u32[]{:S(2)}) copy-start(f32[2048,256]{0,1:T(8,128)} %copy-done.4) | copy-start | bytes 6291460
  108.8 36.6 %all-to-all-start.2 = ((bf16[128,2,4096]{2,1,0:T(2,128)(2,1)}), bf16[128,2,4096]{2,1,0:T(2,128)(2,1)S(1)}, u32[]{:S(2)}, u32[]{:S(2)}) async-start(bf16[128,2,4096]{2,1,0:T(2,128)(2,1)} %convert_element_type.18), calls=%async_computation.3 | async-start | bytes 4194304 | tf_op jit(solution)/shard_map/all_to_all | solution.py:71
Sparse Core Ops, SparseCore 0:
  94.5 70.0 reduce-scatter.1
where the time goes:
time: 172 us; the launch traced here: 171 us
  waiting for transfers between devices  63.8 us (37%)
  matrix products  28.4 us (17%)
  other arithmetic  24.4 us (14%)
  starting transfers between devices  20.9 us (12%)
  local copies, waits for them, and re-layouts  19.7 us (11%)
  between operations  14.3 us (8%)
    all_to_all x1, waiting for transfers between devices, shards(): lax.all_to_all(pushed.astype(jnp.bfloat16), ('dp', 'mp'), split_axis=0, c...  31.7 us
    reduce_sum x1, other arithmetic, local_terms(): jnp.sum(jnp.where(chosen[:, :, None] == columns[None, None, :], weights_i...  15.2 us
    reduce_scatter x1, waiting for transfers between devices, shards(): lax.psum_scatter(jnp.dot(coef, fetched_down, preferred_element_type=jnp.f...  13.7 us
    all_to_all x1, starting transfers between devices, shards(): lax.all_to_all(wanted, ('dp', 'mp'), split_axis=0, concat_axis=0, tiled=T...  11.5 us
    all_to_all x1, waiting for transfers between devices, shards(): lax.all_to_all(outgoing, ('dp', 'mp'), split_axis=0, concat_axis=0, tiled...  9.82 us
    all_to_all x1, waiting for transfers between devices, shards(): lax.all_to_all(wanted, ('dp', 'mp'), split_axis=0, concat_axis=0, tiled=T...  8.49 us
    dot_general x1, matrix products, local_terms(): lax.dot_general(block_tokens, fetched_down, (((1,), (1,)), ((), ())), pre...  5.89 us
    dot_general x1, matrix products, local_terms(): lax.dot_general(coef, block_tokens, (((0,), (0,)), ((), ())), preferred_e...  5.86 us
  transfers between devices with their start and end apart: 4, of which 4 were waited for; matrix products, arithmetic and copies ran while one was open for 24% of the time, Pallas kernels for 0%

commit v1 on v0

v1 whole, which is shorter than its diff:
```python
import functools
import jax
import jax.numpy as jnp
from jax import lax
from jax.experimental import pallas as pl
from jax.experimental.pallas import tpu as pltpu
from jax.sharding import Mesh, PartitionSpec as P

SQRT_HALF = 0.7071067811865476
INV_ROOT_TAU = 0.3989422804014327
N_Y = 4
N_CORE = 2
F32 = jnp.float32
BF16 = jnp.bfloat16
NT = (((1,), (1,)), ((), ()))
NN = (((1,), (0,)), ((), ()))
TN = (((0,), (0,)), ((), ()))
VMEM = pl.BlockSpec(memory_space=pltpu.VMEM)
SMEM = pl.BlockSpec(memory_space=pltpu.SMEM)


def dot(a, b, dims):
    return lax.dot_general(a, b, dims, preferred_element_type=F32)


def iota(shape, axis):
    return lax.broadcasted_iota(jnp.int32, shape, axis)


def cost(flops, bytes_accessed, transcendentals=0):
    return pl.CostEstimate(flops=flops, bytes_accessed=bytes_accessed, transcendentals=transcendentals)


def ids_kernel(req_ref, out_ref):
    capacity, owners = req_ref.shape
    slots = out_ref.shape[0]
    row = iota((slots, owners), 0)
    lane = iota((slots, owners), 1)
    per_peer = N_Y * capacity
    peer = row // per_peer
    owner = (peer // N_CORE) * (N_Y * N_CORE) + ((row % per_peer) // capacity) * N_CORE + peer % N_CORE
    total = jnp.zeros((slots, 1), jnp.int32)
    for r in range(capacity):
        hit = (lane == owner) & (row % capacity == r)
        picked = jnp.where(hit, req_ref[r : r + 1, :], 0)
        total = total + jnp.sum(picked, axis=1, keepdims=True)
    out_ref[...] = jnp.broadcast_to(total, out_ref.shape)


def expand_ids(wanted):
    owners, capacity = wanted.shape
    slots = owners * capacity
    return pl.pallas_call(
        ids_kernel,
        out_shape=jax.ShapeDtypeStruct((slots, 128), jnp.int32),
        in_specs=[VMEM],
        out_specs=VMEM,
        cost_estimate=cost(10**5, 10**5),
        name="ids",
    )(jnp.transpose(wanted))


def gather_kernel(y_ref, asked_ref, t0, t1, t2, t3, out_ref):
    y = y_ref[0]
    slots = asked_ref.shape[0]
    rows = t0.shape[0]
    col = iota((slots, rows), 1)
    owner_y = (iota((slots, rows), 0) % (N_Y * 2)) // 2
    same = asked_ref[:, :rows] == col
    total = jnp.zeros(out_ref.shape, F32)
    for r, table in enumerate((t0, t1, t2, t3)):
        hit = same & (owner_y == (y + r) % N_Y)
        total = total + dot(hit.astype(F32).astype(BF16), table[...], NN)
    out_ref[...] = total.astype(BF16)


def gather_rows(y, asked, tables, name):
    slots = asked.shape[0]
    width = tables[0].shape[1]
    return pl.pallas_call(
        gather_kernel,
        out_shape=jax.ShapeDtypeStruct((slots, width), BF16),
        in_specs=[SMEM] + [VMEM] * 5,
        out_specs=VMEM,
        cost_estimate=cost(2 * 256 * 256 * 2048, 3 * 10**6),
        name=name,
    )(y, asked, *tables)


def weight_kernel(places_ref, gates_ref, out_ref):
    topk, block = places_ref.shape
    slots = out_ref.shape[0]
    slot = places_ref[...]
    slot = (slot & ~15) | (((slot >> 1) & 1) << 3) | (((slot >> 2) & 3) << 1) | (slot & 1)
    gates = gates_ref[...]
    for s in range(0, slots, 32):
        row = iota((32, block), 0) + s
        total = jnp.zeros((32, block), F32)
        for k in range(topk):
            total = jnp.where(row == slot[k : k + 1, :], gates[k : k + 1, :], total)
        out_ref[s : s + 32, :] = total


def build_weight(places, gates, slots):
    topk, tokens = places.shape
    block = 512
    return pl.pallas_call(
        weight_kernel,
        grid=(tokens // block,),
        out_shape=jax.ShapeDtypeStruct((slots, tokens), F32),
        in_specs=[pl.BlockSpec((topk, block), lambda i: (0, i))] * 2,
        out_specs=pl.BlockSpec((slots, block), lambda i: (0, i)),
        cost_estimate=cost(3 * topk * slots * tokens, 4 * slots * tokens),
        name="weight",
    )(places, gates)


def first_kernel(tok_ref, grad_ref, down_ref, weight_ref, slope_ref, part_ref, acc):
    i = pl.program_id(0)

    @pl.when(i == 0)
    def _():
        acc[...] = jnp.zeros_like(acc)

    pre = dot(down_ref[...], tok_ref[...], NT)
    weight = weight_ref[...]
    cdf = 0.5 * (1.0 + lax.erf(pre * SQRT_HALF))
    density = INV_ROOT_TAU * jnp.exp(-0.5 * pre * pre)
    gated = (weight * (pre * cdf)).astype(BF16)
    slope_ref[...] = weight * (cdf + pre * density)
    acc[...] += dot(gated, grad_ref[...], NN)

    @pl.when(i == pl.num_programs(0) - 1)
    def _():
        part_ref[...] = acc[...].astype(BF16)


def first_terms(tokens, grads, down, weight):
    count, width = tokens.shape
    slots = down.shape[0]
    block = 256
    return pl.pallas_call(
        first_kernel,
        grid=(count // block,),
        out_shape=(
            jax.ShapeDtypeStruct((slots, count), F32),
            jax.ShapeDtypeStruct((slots, width), BF16),
        ),
        in_specs=[
            pl.BlockSpec((block, width), lambda i: (i, 0)),
            pl.BlockSpec((block, width), lambda i: (i, 0)),
            pl.BlockSpec((slots, width), lambda i: (0, 0)),
            pl.BlockSpec((slots, block), lambda i: (0, i)),
        ],
        out_specs=(
            pl.BlockSpec((slots, block), lambda i: (0, i)),
            pl.BlockSpec((slots, width), lambda i: (0, 0)),
        ),
        scratch_shapes=[pltpu.VMEM((slots, width), F32)],
        compiler_params=pltpu.CompilerParams(vmem_limit_bytes=32 << 20),
        cost_estimate=cost(4 * count * width * slots, 20 << 20),
        name="first",
    )(tokens, grads, down, weight)


def second_kernel(tok_ref, grad_ref, up_ref, slope_ref, coef_ref, part_ref, acc):
    i = pl.program_id(0)

    @pl.when(i == 0)
    def _():
        acc[...] = jnp.zeros_like(acc)

    back = dot(up_ref[...], grad_ref[...], NT)
    coef = (slope_ref[...] * back).astype(BF16)
    coef_ref[0] = coef
    acc[...] += dot(coef, tok_ref[...], NN)

    @pl.when(i == pl.num_programs(0) - 1)
    def _():
        part_ref[...] = acc[...].astype(BF16)


def second_terms(tokens, grads, up, slope):
    count, width = tokens.shape
    slots = up.shape[0]
    block = 256
    per_chip = count // N_Y // block
    return pl.pallas_call(
        second_kernel,
        grid=(count // block,),
        out_shape=(
            jax.ShapeDtypeStruct((N_Y, slots, count // N_Y), BF16),
            jax.ShapeDtypeStruct((slots, width), BF16),
        ),
        in_specs=[
            pl.BlockSpec((block, width), lambda i: (i, 0)),
            pl.BlockSpec((block, width), lambda i: (i, 0)),
            pl.BlockSpec((slots, width), lambda i: (0, 0)),
            pl.BlockSpec((slots, block), lambda i: (0, i)),
        ],
        out_specs=(
            pl.BlockSpec((1, slots, block), lambda i: (i // per_chip, 0, i % per_chip)),
            pl.BlockSpec((slots, width), lambda i: (0, 0)),
        ),
        scratch_shapes=[pltpu.VMEM((slots, width), F32)],
        compiler_params=pltpu.CompilerParams(vmem_limit_bytes=32 << 20),
        cost_estimate=cost(4 * count * width * slots, 20 << 20),
        name="second",
    )(tokens, grads, up, slope)


def scatter_kernel(asked_ref, got_ref, out_ref):
    slots = asked_ref.shape[0]
    rows = out_ref.shape[1]
    col = iota((slots, rows), 1)
    owner_y = (iota((slots, rows), 0) % (N_Y * 2)) // 2
    same = asked_ref[:, :rows] == col
    for y in range(N_Y):
        hit = (same & (owner_y == y)).astype(F32).astype(BF16)
        out_ref[y] = dot(hit, got_ref[...], TN).astype(BF16)


def scatter_rows(asked, got, rows, name):
    width = got.shape[1]
    return pl.pallas_call(
        scatter_kernel,
        out_shape=jax.ShapeDtypeStruct((N_Y, rows, width), BF16),
        in_specs=[VMEM] * 2,
        out_specs=VMEM,
        cost_estimate=cost(2 * 256 * 256 * 2048, 2 * 10**6),
        name=name,
    )(asked, got)


def final_kernel(pos_ref, coef_ref, d0, d1, d2, d3, keep_ref, give_ref):
    y = pos_ref[0]
    core = pos_ref[1]
    half = keep_ref.shape[0]

    def product(which):
        total = jnp.zeros(keep_ref.shape, F32)
        for r, rows in enumerate((d0, d1, d2, d3)):
            block = coef_ref[(y + r) % N_Y, :, pl.ds(pl.multiple_of(which * half, half), half)]
            total = total + dot(block, rows[...], TN)
        return total

    give_ref[...] = product(1 - core).astype(BF16)
    keep_ref[...] = product(core)


def final_product(pos, coef, rows):
    slots, width = rows[0].shape
    half = coef.shape[2] // N_CORE
    block = 512
    return pl.pallas_call(
        final_kernel,
        grid=(width // block,),
        out_shape=(
            jax.ShapeDtypeStruct((half, width), F32),
            jax.ShapeDtypeStruct((half, width), BF16),
        ),
        in_specs=[SMEM, pl.BlockSpec(coef.shape, lambda j: (0, 0, 0))]
        + [pl.BlockSpec((slots, block), lambda j: (0, j))] * 4,
        out_specs=(
            pl.BlockSpec((half, block), lambda j: (0, j)),
            pl.BlockSpec((half, block), lambda j: (0, j)),
        ),
        cost_estimate=cost(2 * 512 * 1024 * 2048, 8 << 20),
        name="final",
    )(pos, coef, *rows)


def around(x):
    return (x,) + tuple(
        lax.ppermute(x, "y", [(i, (i - r) % N_Y) for i in range(N_Y)]) for r in range(1, N_Y)
    )


def exchange(x):
    return lax.all_to_all(x, ("dp", "core"), split_axis=0, concat_axis=0, tiled=True)


def shards(tokens, out_grad, down_rows, up_rows, requests, places, gate_weights):
    peers = lax.axis_size("dp") * N_CORE
    row_count, width = down_rows.shape
    y = lax.axis_index("y").astype(jnp.int32)
    core = lax.axis_index("core").astype(jnp.int32)
    y_at = jnp.stack([y])
    pos = jnp.stack([y, core])

    down_tables = around(down_rows)
    up_tables = around(up_rows)
    ids = expand_ids(requests[0])
    slots = ids.shape[0]
    per_peer = slots // peers
    asked = exchange(ids.reshape(peers, per_peer, 128)).reshape(slots, 128)

    def fetch(tables, name):
        rows = gather_rows(y_at, asked, tables, name)
        return exchange(rows.reshape(peers, per_peer, width)).reshape(slots, width)

    down = fetch(down_tables, "gather_down")
    up = fetch(up_tables, "gather_up")
    weight = build_weight(jnp.transpose(places[0]), jnp.transpose(gate_weights[0]), slots)
    down_all = around(down)
    slope, part_up = first_terms(tokens, out_grad, down, weight)
    coef, part_down = second_terms(tokens, out_grad, up, slope)

    def give_back(part, name):
        got = exchange(part.reshape(peers, per_peer, width)).reshape(slots, width)
        sums = scatter_rows(asked, got, row_count, name)
        shared = lax.all_to_all(sums, "y", split_axis=0, concat_axis=0, tiled=True)
        return jnp.sum(shared.astype(F32), axis=0)

    up_grad = give_back(part_up, "scatter_up")
    down_grad = give_back(part_down, "scatter_down")
    coef_all = lax.all_to_all(coef, "y", split_axis=0, concat_axis=0, tiled=True)
    keep, give = final_product(pos, coef_all, down_all)
    other = lax.ppermute(give, "core", [(0, 1), (1, 0)])
    input_grad = (keep + other.astype(F32)).astype(BF16)
    return (input_grad, down_grad, up_grad)


def solution(mesh):
    axes = ("dp", "y", "core")
    fine = Mesh(mesh.devices.reshape(mesh.devices.shape[0], N_Y, N_CORE), axes)
    in_specs = (
        P("dp", None),
        P("dp", None),
        P(axes, None),
        P(axes, None),
        P(axes, None, None),
        P(("y", "core"), "dp", None),
        P(("y", "core"), "dp", None),
    )
    out_specs = (P(axes, None), P(axes, None), P(axes, None))
    return jax.shard_map(shards, mesh=fine, in_specs=in_specs, out_specs=out_specs, check_vma=False)
```

time: 172 us -> 237 us (1.38)
  Pallas kernels: 0 us -> 51.1 us
  blocking collectives: 0 us -> 43.5 us
  matrix products: 28.4 us -> 0 us
  starting transfers between devices: 20.9 us -> 45.9 us
  other arithmetic: 24.4 us -> 5.33 us
  between operations: 14.3 us -> 0.78 us
  waiting for transfers between devices: 63.8 us -> 71.9 us
  local copies, waits for them, and re-layouts: 19.7 us -> 16.3 us
    pallas_call x0 -> x9, Pallas kernels: none -> 51.1 us  [the longest x1 13 us: first_terms(): pl.pallas_call(first_kernel, grid=(count // block,), out_shape=(jax.Shape...]
    all_to_all x0 -> x2, blocking collectives: none -> 43.5 us  [the longest x1 25.3 us: exchange(): lax.all_to_all(x, ('dp', 'core'), split_axis=0, concat_axis=0, tiled=True)]
    ppermute x0 -> x10, waiting for transfers between devices: none -> 39.9 us  [the longest x9 39.9 us: around(): lax.ppermute(x, 'y', [(i, (i - r) % N_Y) for i in range(N_Y)])]
    dot_general x6 -> x0, matrix products: 28.4 us -> none  [the longest x1 5.89 us: local_terms(): lax.dot_general(block_tokens, fetched_down, (((1,), (1,)), ((), ())), pre...]
    all_to_all x3 -> x6, waiting for transfers between devices: 50 us -> 32 us  [the longest x4 18.7 us: exchange(): lax.all_to_all(x, ('dp', 'core'), split_axis=0, concat_axis=0, tiled=True)]
    unnamed x17 -> x32, local copies, waits for them, and re-layouts: 1.45 us -> 16.3 us
    reduce_scatter x1 -> x0, waiting for transfers between devices: 13.7 us -> none  [shards(): lax.psum_scatter(jnp.dot(coef, fetched_down, preferred_element_type=jnp.f...]
    ppermute x0 -> x10, starting transfers between devices: none -> 13.6 us  [the longest x9 11 us: around(): lax.ppermute(x, 'y', [(i, (i - r) % N_Y) for i in range(N_Y)])]
  transfers between devices with their start and end apart: 4 -> 16, of which waited for: 4 -> 9; matrix products, arithmetic and copies ran while one was open for 24% -> 1% of each run, Pallas kernels for 0% -> 15%
where the time goes in v1:
time: 237 us; the launch traced here: 235 us
  waiting for transfers between devices  71.9 us (30%)
  Pallas kernels  51.1 us (22%)
  starting transfers between devices  45.9 us (19%)
  blocking collectives  43.5 us (18%)
  local copies, waits for them, and re-layouts  16.3 us (7%)
  other arithmetic  5.33 us (2%)
    ppermute x9, waiting for transfers between devices, around(): lax.ppermute(x, 'y', [(i, (i - r) % N_Y) for i in range(N_Y)])  39.9 us
    all_to_all x4, starting transfers between devices, exchange(): lax.all_to_all(x, ('dp', 'core'), split_axis=0, concat_axis=0, tiled=True)  25.3 us
    all_to_all x1, blocking collectives, exchange(): lax.all_to_all(x, ('dp', 'core'), split_axis=0, concat_axis=0, tiled=True)  25.3 us
    all_to_all x4, waiting for transfers between devices, exchange(): lax.all_to_all(x, ('dp', 'core'), split_axis=0, concat_axis=0, tiled=True)  18.7 us
    all_to_all x1, blocking collectives, shards(): lax.all_to_all(coef, 'y', split_axis=0, concat_axis=0, tiled=True)  18.2 us
    unnamed x32, local copies, waits for them, and re-layouts  16.3 us
    all_to_all x2, waiting for transfers between devices, give_back(): shared = lax.all_to_all(sums, 'y', split_axis=0, concat_axis=0, tiled=True)  13.3 us
    pallas_call x1, Pallas kernels, first_terms(): pl.pallas_call(first_kernel, grid=(count // block,), out_shape=(jax.Shape...  13 us
  transfers between devices with their start and end apart: 16, of which 9 were waited for; matrix products, arithmetic and copies ran while one was open for 1% of the time, Pallas kernels for 15%

profile of v1, /device:TPU:1, one launch (start us, length us, event | category | flops | bytes accessed | tf_op | source)
XLA Modules:
  0.0 234.9 jit_solution(2989114949019059527)
XLA Ops:
  0.6 3.8 %collective-permute-start.4 = (bf16[64,2048]{1,0:T(8,128)(2,1)}, bf16[64,2048]{1,0:T(8,128)(2,1)S(1)}, u32[]{:S(2)}, u32[]{:S(2)}) collective-permute-start(bf16[64,2048]{1,0:T(8,128)(2,1)} %t0.3), channel_id=1, source_target_pairs={{0,4},{2,6},{4,0},{6,2},{1,5},{3,7},{5,1},{7,3},{8,12},{10,14},{12... | collective-permute-start | bytes 786440 | tf_op jit(solution)/shard_map/ppermute | solution.py:275
  4.4 0.8 collective-permute-start.3
  5.2 0.7 collective-permute-start.5
  5.9 1.6 ids.1
  7.5 9.4 %all-to-all-start = ((s32[32,8,128]{2,1,0:T(8,128)}), s32[32,8,128]{2,1,0:T(8,128)S(1)}, u32[]{:S(2)}, u32[]{:S(2)}) async-start(s32[32,8,128]{2,1,0:T(8,128)} %bitcast.36), calls=%async_computation | async-start | bytes 262144 | tf_op jit(solution)/shard_map/all_to_all | solution.py:280
  17.0 7.6 %all-to-all-done = s32[32,8,128]{2,1,0:T(8,128)S(1)} async-done(((s32[32,8,128]{2,1,0:T(8,128)}), s32[32,8,128]{2,1,0:T(8,128)S(1)}, u32[]{:S(2)}, u32[]{:S(2)}) %all-to-all-start) | async-done | bytes 131104 | tf_op jit(solution)/shard_map/all_to_all | solution.py:280
  24.6 0.6 copy-done.8
  25.2 0.1 copy-done.10
  25.5 3.5 %gather_down.1 = bf16[256,2048]{1,0:T(8,128)(2,1)} custom-call(s32[1]{0:T(128)} %bitcast.y_ref, s32[256,128]{1,0:T(8,128)} %bitcast.32, bf16[64,2048]{1,0:T(8,128)(2,1)} %t0.3, bf16[64,2048]{1,0:T(8,128)(2,1)} %copy-done.11, bf16[64,2048]{1,0:T(8,128)(2,1)} %copy-done.10, bf16[64,2048]{1,0:T(8,128)(2,1)} %copy-done.12), custom_call_target="tpu_custom_call" | custom-call | flops 268435456 | bytes 3000000 | tf_op jit(solution)/shard_map/gather_down/pallas_call | solution.py:80
  29.0 4.0 %all-to-all-start.2 = ((bf16[32,8,2048]{2,1,0:T(8,128)(2,1)}), bf16[32,8,2048]{2,1,0:T(8,128)(2,1)S(1)}, u32[]{:S(2)}, u32[]{:S(2)}) async-start(bf16[32,8,2048]{2,1,0:T(8,128)(2,1)} %bitcast.28), calls=%async_computation.2 | async-start | bytes 2097152 | tf_op jit(solution)/shard_map/all_to_all | solution.py:280
  33.0 0.5 collective-permute-start.1
  33.5 2.3 %collective-permute-start = (bf16[64,2048]{1,0:T(8,128)(2,1)S(1)}, bf16[64,2048]{1,0:T(8,128)(2,1)S(1)}, u32[]{:S(2)}, u32[]{:S(2)}) collective-permute-start(bf16[64,2048]{1,0:T(8,128)(2,1)S(1)} %copy-done.9), channel_id=1, source_target_pairs={{0,6},{2,0},{4,2},{6,4},{1,7},{3,1},{5,3},{7,5},{8,14},{10,8},{12,... | collective-permute-start | bytes 786440 | tf_op jit(solution)/shard_map/ppermute | solution.py:275
  35.8 6.3 %collective-permute-done.1.t2 = bf16[64,2048]{1,0:T(8,128)(2,1)S(1)} collective-permute-done((bf16[64,2048]{1,0:T(8,128)(2,1)S(1)}, bf16[64,2048]{1,0:T(8,128)(2,1)S(1)}, u32[]{:S(2)}, u32[]{:S(2)}) %collective-permute-start.1) | collective-permute-done | bytes 262176 | tf_op jit(solution)/shard_map/ppermute | solution.py:275
  42.1 5.2 %collective-permute-done.t1 = bf16[64,2048]{1,0:T(8,128)(2,1)S(1)} collective-permute-done((bf16[64,2048]{1,0:T(8,128)(2,1)S(1)}, bf16[64,2048]{1,0:T(8,128)(2,1)S(1)}, u32[]{:S(2)}, u32[]{:S(2)}) %collective-permute-start) | collective-permute-done | bytes 262176 | tf_op jit(solution)/shard_map/ppermute | solution.py:275
  47.3 1.1 collective-permute-done.2.t3
  48.4 0.7 copy-done.15
  49.1 3.4 %gather_up.1 = bf16[256,2048]{1,0:T(8,128)(2,1)} custom-call(s32[1]{0:T(128)} %bitcast.y_ref, s32[256,128]{1,0:T(8,128)} %bitcast.33, bf16[64,2048]{1,0:T(8,128)(2,1)} %t0.2, bf16[64,2048]{1,0:T(8,128)(2,1)} %copy-done.14, bf16[64,2048]{1,0:T(8,128)(2,1)} %copy-done.13, bf16[64,2048]{1,0:T(8,128)(2,1)} %copy-done.15), custom_call_target="tpu_custom_call" | custom-call | flops 268435456 | bytes 3000000 | tf_op jit(solution)/shard_map/gather_up/pallas_call | solution.py:80
  52.5 7.9 %all-to-all-start.1 = ((bf16[32,8,2048]{2,1,0:T(8,128)(2,1)}), bf16[32,8,2048]{2,1,0:T(8,128)(2,1)S(1)}, u32[]{:S(2)}, u32[]{:S(2)}) async-start(bf16[32,8,2048]{2,1,0:T(8,128)(2,1)} %bitcast.29), calls=%async_computation.1 | async-start | bytes 2097152 | tf_op jit(solution)/shard_map/all_to_all | solution.py:280
  60.5 4.6 %weight.1.weight_ref = f32[256,2048]{1,0:T(8,128)} custom-call(s32[16,2048]{1,0:T(8,128)} %bitcast.37, f32[16,2048]{1,0:T(8,128)} %bitcast.38), custom_call_target="tpu_custom_call" | custom-call | flops 25165824 | bytes 2097152 | tf_op jit(solution)/shard_map/weight/pallas_call | solution.py:107
  65.1 3.4 %copy-done = bf16[2048,2048]{1,0:T(8,128)(2,1)S(1)} copy-done((bf16[2048,2048]{1,0:T(8,128)(2,1)S(1)}, bf16[2048,2048]{1,0:T(8,128)(2,1)}, u32[]{:S(2)}) %copy-start) | copy-done | bytes 8388632
  68.5 1.6 copy-done.3
  70.1 13.0 %first.1 = (f32[256,2048]{1,0:T(8,128)S(1)}, bf16[256,2048]{1,0:T(8,128)(2,1)S(1)}) custom-call(bf16[2048,2048]{1,0:T(8,128)(2,1)S(1)} %copy-done, bf16[2048,2048]{1,0:T(8,128)(2,1)} %grad_ref.3, bf16[256,2048]{1,0:T(8,128)(2,1)S(1)} %bitcast.21, f32[256,2048]{1,0:T(8,128)S(1)} %copy-done.3), custom_call_target="tpu_custom_call" | custom-call | flops 4294967296 | bytes 20971520 | tf_op jit(solution)/shard_map/first/pallas_call | solution.py:142
  83.1 1.3 copy-done.5
  84.4 3.4 %copy-done.1 = bf16[2048,2048]{1,0:T(8,128)(2,1)S(1)} copy-done((bf16[2048,2048]{1,0:T(8,128)(2,1)S(1)}, bf16[2048,2048]{1,0:T(8,128)(2,1)}, u32[]{:S(2)}) %copy-start.1) | copy-done | bytes 8388632
  87.8 3.4 %copy-done.2 = bf16[2048,2048]{1,0:T(8,128)(2,1)S(1)} copy-done((bf16[2048,2048]{1,0:T(8,128)(2,1)S(1)}, bf16[2048,2048]{1,0:T(8,128)(2,1)}, u32[]{:S(2)}) %copy-start.2) | copy-done | bytes 8388632
  91.2 1.6 copy-done.6
  92.8 12.3 %second.1 = (bf16[4,256,512]{2,1,0:T(8,128)(2,1)S(1)}, bf16[256,2048]{1,0:T(8,128)(2,1)}) custom-call(bf16[2048,2048]{1,0:T(8,128)(2,1)S(1)} %copy-done.1, bf16[2048,2048]{1,0:T(8,128)(2,1)S(1)} %copy-done.2, bf16[256,2048]{1,0:T(8,128)(2,1)S(1)} %bitcast.26, f32[256,2048]{1,0:T(8,128)S(1)} %copy-done.6), custom_call_target="tpu_custom_call" | custom-call | flops 4294967296 | bytes 20971520 | tf_op jit(solution)/shard_map/second/pallas_call | solution.py:188
  105.0 18.2 %all_to_all.40.coef_ref = bf16[4,256,512]{2,1,0:T(8,128)(2,1)} all-to-all(bf16[4,256,512]{2,1,0:T(8,128)(2,1)S(1)} %get-tuple-element.10), channel_id=1, replica_groups=mesh['dp'=16,'y'=4,'core'=2] {'y'}, dimensions={0} | all-to-all | bytes 2097152 | tf_op jit(solution)/shard_map/all_to_all | solution.py:317
  123.2 25.3 %all_to_all.41 = bf16[32,8,2048]{2,1,0:T(8,128)(2,1)} all-to-all(bf16[32,8,2048]{2,1,0:T(8,128)(2,1)S(1)} %bitcast.27), channel_id=1, replica_groups=mesh['dp'=16,'y'=4,'core'=2] {'dp','core'}, dimensions={0} | all-to-all | bytes 2097152 | tf_op jit(solution)/shard_map/all_to_all | solution.py:280
  148.5 4.0 %all-to-all-start.4 = ((bf16[32,8,2048]{2,1,0:T(8,128)(2,1)}), bf16[32,8,2048]{2,1,0:T(8,128)(2,1)S(1)}, u32[]{:S(2)}, u32[]{:S(2)}) async-start(bf16[32,8,2048]{2,1,0:T(8,128)(2,1)} %bitcast.14), calls=%async_computation.4 | async-start | bytes 2097152 | tf_op jit(solution)/shard_map/all_to_all | solution.py:280
  152.5 0.4 collective-permute-start.8
  152.9 1.8 collective-permute-start.7
  154.7 0.7 collective-permute-start.6
  155.4 3.2 %scatter_up.1 = bf16[4,64,2048]{2,1,0:T(8,128)(2,1)} custom-call(s32[256,128]{1,0:T(8,128)} %bitcast.34, bf16[256,2048]{1,0:T(8,128)(2,1)} %bitcast.31), custom_call_target="tpu_custom_call" | custom-call | flops 268435456 | bytes 2000000 | tf_op jit(solution)/shard_map/scatter_up/pallas_call | solution.py:225
  158.6 11.1 %all-to-all-done.4 = bf16[32,8,2048]{2,1,0:T(8,128)(2,1)S(1)} async-done(((bf16[32,8,2048]{2,1,0:T(8,128)(2,1)}), bf16[32,8,2048]{2,1,0:T(8,128)(2,1)S(1)}, u32[]{:S(2)}, u32[]{:S(2)}) %all-to-all-start.4) | async-done | bytes 1048608 | tf_op jit(solution)/shard_map/all_to_all | solution.py:280
  169.7 3.5 %all-to-all-start.7 = ((bf16[4,64,2048]{2,1,0:T(8,128)(2,1)}), bf16[4,64,2048]{2,1,0:T(8,128)(2,1)S(1)}, u32[]{:S(2)}, u32[]{:S(2)}) async-start(bf16[4,64,2048]{2,1,0:T(8,128)(2,1)} %scatter_up.1), calls=%async_computation.7 | async-start | bytes 2097152 | tf_op jit(solution)/shard_map/all_to_all | solution.py:312
  173.2 0.6 pad_add_fusion.pos_ref
  173.8 5.1 %collective-permute-done.8.d3 = bf16[256,2048]{1,0:T(8,128)(2,1)} collective-permute-done((bf16[256,2048]{1,0:T(8,128)(2,1)S(1)}, bf16[256,2048]{1,0:T(8,128)(2,1)}, u32[]{:S(2)}, u32[]{:S(2)}) %collective-permute-start.8) | collective-permute-done | bytes 1048608 | tf_op jit(solution)/shard_map/ppermute | solution.py:275
  178.9 21.3 %collective-permute-done.7.d2 = bf16[256,2048]{1,0:T(8,128)(2,1)} collective-permute-done((bf16[256,2048]{1,0:T(8,128)(2,1)S(1)}, bf16[256,2048]{1,0:T(8,128)(2,1)}, u32[]{:S(2)}, u32[]{:S(2)}) %collective-permute-start.7) | collective-permute-done | bytes 1048608 | tf_op jit(solution)/shard_map/ppermute | solution.py:275
  200.2 0.9 collective-permute-done.6.d1
  201.1 6.3 %final.1 = (f32[256,2048]{1,0:T(8,128)}, bf16[256,2048]{1,0:T(8,128)(2,1)}) custom-call(s32[2]{0:T(128)} %pad_add_fusion.pos_ref, bf16[4,256,512]{2,1,0:T(8,128)(2,1)} %all_to_all.40.coef_ref, bf16[256,2048]{1,0:T(8,128)(2,1)} %bitcast.25, bf16[256,2048]{1,0:T(8,128)(2,1)} %collective-permute-done.6.d1, bf16[256,2048]{1,0:T(8,128)(2,1)} %collective-permute-done.7.d2, ...), custom_call_target="tpu_custom_call" | custom-call | flops 2147483648 | bytes 8388608 | tf_op jit(solution)/shard_map/final/pallas_call | solution.py:255
  207.5 2.6 %collective-permute-start.9 = (bf16[256,2048]{1,0:T(8,128)(2,1)}, bf16[256,2048]{1,0:T(8,128)(2,1)S(1)}, u32[]{:S(2)}, u32[]{:S(2)}) collective-permute-start(bf16[256,2048]{1,0:T(8,128)(2,1)} %get-tuple-element.12), channel_id=1, source_target_pairs={{0,1},{1,0},{2,3},{3,2},{4,5},{5,4},{6,7},{7,6},{8,9},{9,8},{10,11... | collective-permute-start | bytes 3145736 | tf_op jit(solution)/shard_map/ppermute | solution.py:319
  210.1 3.2 %scatter_down.1 = bf16[4,64,2048]{2,1,0:T(8,128)(2,1)} custom-call(s32[256,128]{1,0:T(8,128)} %bitcast.35, bf16[256,2048]{1,0:T(8,128)(2,1)} %bitcast.30), custom_call_target="tpu_custom_call" | custom-call | flops 268435456 | bytes 2000000 | tf_op jit(solution)/shard_map/scatter_down/pallas_call | solution.py:225
  213.3 3.5 %all-to-all-start.5 = ((bf16[4,64,2048]{2,1,0:T(8,128)(2,1)}), bf16[4,64,2048]{2,1,0:T(8,128)(2,1)S(1)}, u32[]{:S(2)}, u32[]{:S(2)}) async-start(bf16[4,64,2048]{2,1,0:T(8,128)(2,1)} %scatter_down.1), calls=%async_computation.5 | async-start | bytes 2097152 | tf_op jit(solution)/shard_map/all_to_all | solution.py:312
  216.8 1.0 convert_reduce_fusion
  217.7 13.3 %all-to-all-done.5 = bf16[4,64,2048]{2,1,0:T(8,128)(2,1)S(1)} async-done(((bf16[4,64,2048]{2,1,0:T(8,128)(2,1)}), bf16[4,64,2048]{2,1,0:T(8,128)(2,1)S(1)}, u32[]{:S(2)}, u32[]{:S(2)}) %all-to-all-start.5) | async-done | bytes 1048608 | tf_op jit(solution)/shard_map/all_to_all | solution.py:312
  231.1 0.9 convert_reduce_fusion.1
  232.0 2.8 %add_convert_fusion = bf16[256,2048]{1,0:T(8,128)(2,1)} fusion(f32[256,2048]{1,0:T(8,128)} %get-tuple-element.11, bf16[256,2048]{1,0:T(8,128)(2,1)S(1)} %collective-permute-done.9), kind=kLoop, calls=%fused_computation.2 | loop fusion | flops 1572864 | bytes 4194304 | tf_op jit(solution)/shard_map/convert_element_type | solution.py:320
  (31 shorter events, 0.2 us)
Async XLA Ops:
  0.6 23.9 %collective-permute-start.4 = (bf16[64,2048]{1,0:T(8,128)(2,1)}, bf16[64,2048]{1,0:T(8,128)(2,1)S(1)}, u32[]{:S(2)}, u32[]{:S(2)}) collective-permute-start(bf16[64,2048]{1,0:T(8,128)(2,1)} %t0.3), channel_id=1, source_target_pairs={{0,4},{2,6},{4,0},{6,2},{1,5},{3,7},{5,1},{7,3},{8,12},{10,14},{12... | collective-permute-start | bytes 786440 | tf_op jit(solution)/shard_map/ppermute | solution.py:275
  4.4 20.1 %collective-permute-start.3 = (bf16[64,2048]{1,0:T(8,128)(2,1)}, bf16[64,2048]{1,0:T(8,128)(2,1)S(1)}, u32[]{:S(2)}, u32[]{:S(2)}) collective-permute-start(bf16[64,2048]{1,0:T(8,128)(2,1)} %t0.3), channel_id=1, source_target_pairs={{0,6},{2,0},{4,2},{6,4},{1,7},{3,1},{5,3},{7,5},{8,14},{10,8},{12,... | collective-permute-start | bytes 786440 | tf_op jit(solution)/shard_map/ppermute | solution.py:275
  5.2 19.4 %collective-permute-start.5 = (bf16[64,2048]{1,0:T(8,128)(2,1)}, bf16[64,2048]{1,0:T(8,128)(2,1)S(1)}, u32[]{:S(2)}, u32[]{:S(2)}) collective-permute-start(bf16[64,2048]{1,0:T(8,128)(2,1)} %t0.3), channel_id=1, source_target_pairs={{0,2},{2,4},{4,6},{6,0},{1,3},{3,5},{5,7},{7,1},{8,10},{10,12},{12... | collective-permute-start | bytes 786440 | tf_op jit(solution)/shard_map/ppermute | solution.py:275
  7.5 17.0 %all-to-all-start = ((s32[32,8,128]{2,1,0:T(8,128)}), s32[32,8,128]{2,1,0:T(8,128)S(1)}, u32[]{:S(2)}, u32[]{:S(2)}) async-start(s32[32,8,128]{2,1,0:T(8,128)} %bitcast.36), calls=%async_computation | async-start | bytes 262144 | tf_op jit(solution)/shard_map/all_to_all | solution.py:280
  24.6 0.7 copy-start.8
  24.6 0.7 copy-start.10
  24.6 0.8 copy-start.11
  24.6 0.9 copy-start.12
  25.5 7.5 %copy-start.9 = (bf16[64,2048]{1,0:T(8,128)(2,1)S(1)}, bf16[64,2048]{1,0:T(8,128)(2,1)}, u32[]{:S(2)}) copy-start(bf16[64,2048]{1,0:T(8,128)(2,1)} %t0.2) | copy-start | bytes 786436
  29.0 23.6 %all-to-all-start.2 = ((bf16[32,8,2048]{2,1,0:T(8,128)(2,1)}), bf16[32,8,2048]{2,1,0:T(8,128)(2,1)S(1)}, u32[]{:S(2)}, u32[]{:S(2)}) async-start(bf16[32,8,2048]{2,1,0:T(8,128)(2,1)} %bitcast.28), calls=%async_computation.2 | async-start | bytes 2097152 | tf_op jit(solution)/shard_map/all_to_all | solution.py:280
  33.0 9.1 %collective-permute-start.1 = (bf16[64,2048]{1,0:T(8,128)(2,1)S(1)}, bf16[64,2048]{1,0:T(8,128)(2,1)S(1)}, u32[]{:S(2)}, u32[]{:S(2)}) collective-permute-start(bf16[64,2048]{1,0:T(8,128)(2,1)S(1)} %copy-done.9), channel_id=1, source_target_pairs={{0,4},{2,6},{4,0},{6,2},{1,5},{3,7},{5,1},{7,3},{8,12},{10,14},{12... | collective-permute-start | bytes 786440 | tf_op jit(solution)/shard_map/ppermute | solution.py:275
  33.5 13.8 %collective-permute-start = (bf16[64,2048]{1,0:T(8,128)(2,1)S(1)}, bf16[64,2048]{1,0:T(8,128)(2,1)S(1)}, u32[]{:S(2)}, u32[]{:S(2)}) collective-permute-start(bf16[64,2048]{1,0:T(8,128)(2,1)S(1)} %copy-done.9), channel_id=1, source_target_pairs={{0,6},{2,0},{4,2},{6,4},{1,7},{3,1},{5,3},{7,5},{8,14},{10,8},{12,... | collective-permute-start | bytes 786440 | tf_op jit(solution)/shard_map/ppermute | solution.py:275
  35.8 12.6 %collective-permute-start.2 = (bf16[64,2048]{1,0:T(8,128)(2,1)S(1)}, bf16[64,2048]{1,0:T(8,128)(2,1)S(1)}, u32[]{:S(2)}, u32[]{:S(2)}) collective-permute-start(bf16[64,2048]{1,0:T(8,128)(2,1)S(1)} %copy-done.9), channel_id=1, source_target_pairs={{0,2},{2,4},{4,6},{6,0},{1,3},{3,5},{5,7},{7,1},{8,10},{10,12},{12... | collective-permute-start | bytes 786440 | tf_op jit(solution)/shard_map/ppermute | solution.py:275
  42.1 6.3 %copy-start.13 = (bf16[64,2048]{1,0:T(8,128)(2,1)}, bf16[64,2048]{1,0:T(8,128)(2,1)S(1)}, u32[]{:S(2)}) copy-start(bf16[64,2048]{1,0:T(8,128)(2,1)S(1)} %collective-permute-done.1.t2) | copy-start | bytes 786436
  47.3 1.1 copy-start.14
  48.4 0.7 copy-start.15
  52.5 102.1 %copy-start.4 = (bf16[32,8,2048]{2,1,0:T(8,128)(2,1)}, bf16[32,8,2048]{2,1,0:T(8,128)(2,1)S(1)}, u32[]{:S(2)}) copy-start(bf16[32,8,2048]{2,1,0:T(8,128)(2,1)S(1)} %all-to-all-done.2) | copy-start | bytes 3145732
  52.5 31.9 %all-to-all-start.1 = ((bf16[32,8,2048]{2,1,0:T(8,128)(2,1)}), bf16[32,8,2048]{2,1,0:T(8,128)(2,1)S(1)}, u32[]{:S(2)}, u32[]{:S(2)}) async-start(bf16[32,8,2048]{2,1,0:T(8,128)(2,1)} %bitcast.29), calls=%async_computation.1 | async-start | bytes 2097152 | tf_op jit(solution)/shard_map/all_to_all | solution.py:280
  65.1 3.4 %copy-start = (bf16[2048,2048]{1,0:T(8,128)(2,1)S(1)}, bf16[2048,2048]{1,0:T(8,128)(2,1)}, u32[]{:S(2)}) copy-start(bf16[2048,2048]{1,0:T(8,128)(2,1)} %tok_ref.3) | copy-start | bytes 25165828
  68.5 1.6 copy-start.3
  83.0 1.3 copy-start.5
  84.4 3.4 %copy-start.1 = (bf16[2048,2048]{1,0:T(8,128)(2,1)S(1)}, bf16[2048,2048]{1,0:T(8,128)(2,1)}, u32[]{:S(2)}) copy-start(bf16[2048,2048]{1,0:T(8,128)(2,1)} %tok_ref.3) | copy-start | bytes 25165828
  87.8 3.4 %copy-start.2 = (bf16[2048,2048]{1,0:T(8,128)(2,1)S(1)}, bf16[2048,2048]{1,0:T(8,128)(2,1)}, u32[]{:S(2)}) copy-start(bf16[2048,2048]{1,0:T(8,128)(2,1)} %grad_ref.3) | copy-start | bytes 25165828
  91.2 1.6 copy-start.6
  148.5 21.1 %all-to-all-start.4 = ((bf16[32,8,2048]{2,1,0:T(8,128)(2,1)}), bf16[32,8,2048]{2,1,0:T(8,128)(2,1)S(1)}, u32[]{:S(2)}, u32[]{:S(2)}) async-start(bf16[32,8,2048]{2,1,0:T(8,128)(2,1)} %bitcast.14), calls=%async_computation.4 | async-start | bytes 2097152 | tf_op jit(solution)/shard_map/all_to_all | solution.py:280
  152.5 26.4 %collective-permute-start.8 = (bf16[256,2048]{1,0:T(8,128)(2,1)S(1)}, bf16[256,2048]{1,0:T(8,128)(2,1)}, u32[]{:S(2)}, u32[]{:S(2)}) collective-permute-start(bf16[256,2048]{1,0:T(8,128)(2,1)S(1)} %bitcast.22), channel_id=1, source_target_pairs={{0,2},{2,4},{4,6},{6,0},{1,3},{3,5},{5,7},{7,1},{8,10},{10,12},{12... | collective-permute-start | bytes 3145736 | tf_op jit(solution)/shard_map/ppermute | solution.py:275
  152.9 47.3 %collective-permute-start.7 = (bf16[256,2048]{1,0:T(8,128)(2,1)S(1)}, bf16[256,2048]{1,0:T(8,128)(2,1)}, u32[]{:S(2)}, u32[]{:S(2)}) collective-permute-start(bf16[256,2048]{1,0:T(8,128)(2,1)S(1)} %bitcast.23), channel_id=1, source_target_pairs={{0,4},{2,6},{4,0},{6,2},{1,5},{3,7},{5,1},{7,3},{8,12},{10,14},{12... | collective-permute-start | bytes 3145736 | tf_op jit(solution)/shard_map/ppermute | solution.py:275
  154.7 46.5 %collective-permute-start.6 = (bf16[256,2048]{1,0:T(8,128)(2,1)S(1)}, bf16[256,2048]{1,0:T(8,128)(2,1)}, u32[]{:S(2)}, u32[]{:S(2)}) collective-permute-start(bf16[256,2048]{1,0:T(8,128)(2,1)S(1)} %bitcast.24), channel_id=1, source_target_pairs={{0,6},{2,0},{4,2},{6,4},{1,7},{3,1},{5,3},{7,5},{8,14},{10,8},{12,... | collective-permute-start | bytes 3145736 | tf_op jit(solution)/shard_map/ppermute | solution.py:275
  169.7 37.8 %copy-start.7 = (bf16[32,8,2048]{2,1,0:T(8,128)(2,1)}, bf16[32,8,2048]{2,1,0:T(8,128)(2,1)S(1)}, u32[]{:S(2)}) copy-start(bf16[32,8,2048]{2,1,0:T(8,128)(2,1)S(1)} %all-to-all-done.4) | copy-start | bytes 3145732
  169.7 43.6 %all-to-all-start.7 = ((bf16[4,64,2048]{2,1,0:T(8,128)(2,1)}), bf16[4,64,2048]{2,1,0:T(8,128)(2,1)S(1)}, u32[]{:S(2)}, u32[]{:S(2)}) async-start(bf16[4,64,2048]{2,1,0:T(8,128)(2,1)} %scatter_up.1), calls=%async_computation.7 | async-start | bytes 2097152 | tf_op jit(solution)/shard_map/all_to_all | solution.py:312
  207.5 24.5 %collective-permute-start.9 = (bf16[256,2048]{1,0:T(8,128)(2,1)}, bf16[256,2048]{1,0:T(8,128)(2,1)S(1)}, u32[]{:S(2)}, u32[]{:S(2)}) collective-permute-start(bf16[256,2048]{1,0:T(8,128)(2,1)} %get-tuple-element.12), channel_id=1, source_target_pairs={{0,1},{1,0},{2,3},{3,2},{4,5},{5,4},{6,7},{7,6},{8,9},{9,8},{10,11... | collective-permute-start | bytes 3145736 | tf_op jit(solution)/shard_map/ppermute | solution.py:319
  213.3 17.8 %all-to-all-start.5 = ((bf16[4,64,2048]{2,1,0:T(8,128)(2,1)}), bf16[4,64,2048]{2,1,0:T(8,128)(2,1)S(1)}, u32[]{:S(2)}, u32[]{:S(2)}) async-start(bf16[4,64,2048]{2,1,0:T(8,128)(2,1)} %scatter_down.1), calls=%async_computation.5 | async-start | bytes 2097152 | tf_op jit(solution)/shard_map/all_to_all | solution.py:312

commit v2 on v1

v2 whole, which is shorter than its diff:
```python
import functools
import jax
import jax.numpy as jnp
from jax import lax
from jax.experimental import pallas as pl
from jax.experimental.pallas import tpu as pltpu
from jax.sharding import Mesh, PartitionSpec as P

SQRT_HALF = 0.7071067811865476
INV_ROOT_TAU = 0.3989422804014327
N_Y = 4
N_CORE = 2
F32 = jnp.float32
BF16 = jnp.bfloat16
NT = (((1,), (1,)), ((), ()))
NN = (((1,), (0,)), ((), ()))
TN = (((0,), (0,)), ((), ()))
ANY = pl.BlockSpec(memory_space=pl.ANY)
VMEM = pl.BlockSpec(memory_space=pltpu.VMEM)
DMA = pltpu.SemaphoreType.DMA


def dot(a, b, dims):
    return lax.dot_general(a, b, dims, preferred_element_type=F32)


def iota(shape, axis):
    return lax.broadcasted_iota(jnp.int32, shape, axis)


def cost(flops, bytes_accessed, transcendentals=0):
    return pl.CostEstimate(flops=flops, bytes_accessed=bytes_accessed, transcendentals=transcendentals)


def ids_kernel(req_ref, out_ref):
    capacity, owners = req_ref.shape
    slots = out_ref.shape[0]
    row = iota((slots, owners), 0)
    lane = iota((slots, owners), 1)
    per_peer = N_Y * capacity
    peer = row // per_peer
    owner = (peer // N_CORE) * (N_Y * N_CORE) + ((row % per_peer) // capacity) * N_CORE + peer % N_CORE
    total = jnp.zeros((slots, 1), jnp.int32)
    for r in range(capacity):
        hit = (lane == owner) & (row % capacity == r)
        picked = jnp.where(hit, req_ref[r : r + 1, :], 0)
        total = total + jnp.sum(picked, axis=1, keepdims=True)
    out_ref[...] = jnp.broadcast_to(total, out_ref.shape)


def expand_ids(wanted):
    owners, capacity = wanted.shape
    slots = owners * capacity
    return pl.pallas_call(
        ids_kernel,
        out_shape=jax.ShapeDtypeStruct((slots, 128), jnp.int32),
        in_specs=[VMEM],
        out_specs=VMEM,
        cost_estimate=cost(10**5, 10**5),
        name="ids",
    )(jnp.transpose(wanted))


def copy(src, dst, sem):
    return pltpu.make_async_copy(src, dst, sem)


def params(mib):
    return pltpu.CompilerParams(vmem_limit_bytes=mib << 20)


def column_hits(asked, rows):
    y = lax.axis_index("y")
    slots = asked.shape[0]
    shape = (slots, N_Y * rows)
    at = iota(shape, 1)
    owner_y = (iota(shape, 0) % (N_Y * 2)) // 2
    twice = jnp.concatenate([asked] * (N_Y * rows // asked.shape[1]), axis=1)
    hit = (twice == at % rows) & (owner_y == (y + at // rows) % N_Y)
    return hit.astype(F32).astype(BF16)


def gather_kernel(asked_ref, t0, t1, t2, t3, out_hbm, table, out, sems, out_sems):
    rows = t0.shape[0]
    copies = [
        copy(t, table.at[pl.ds(r * rows, rows), :], sems.at[r]) for r, t in enumerate((t0, t1, t2, t3))
    ]
    for c in copies:
        c.start()
    hits = column_hits(asked_ref[...], rows)
    for c in copies:
        c.wait()
    width = out.shape[1]
    block = width // 4
    sent = []
    for j in range(4):
        cols = pl.ds(j * block, block)
        out[:, cols] = dot(hits, table[:, cols], NN).astype(BF16)
        c = copy(out.at[:, cols], out_hbm.at[:, cols], out_sems.at[j])
        c.start()
        sent.append(c)
    for c in sent:
        c.wait()


def gather_rows(asked, tables):
    slots = asked.shape[0]
    rows, width = tables[0].shape
    return pl.pallas_call(
        gather_kernel,
        out_shape=jax.ShapeDtypeStruct((slots, width), BF16),
        in_specs=[VMEM] + [ANY] * 4,
        out_specs=ANY,
        scratch_shapes=[
            pltpu.VMEM((N_Y * rows, width), BF16),
            pltpu.VMEM((slots, width), BF16),
            DMA((4,)),
            DMA((4,)),
        ],
        compiler_params=params(8),
        cost_estimate=cost(2 * 256 * 256 * 2048, 3 * 10**6),
    )(asked, *tables)


def weight_kernel(places_ref, gates_ref, out_ref):
    topk, block = places_ref.shape
    slots = out_ref.shape[1]
    slot = places_ref[...]
    slot = (slot & ~15) | (((slot >> 1) & 1) << 3) | (((slot >> 2) & 3) << 1) | (slot & 1)
    gates = gates_ref[...]
    for s in range(0, slots, 32):
        row = iota((32, block), 0) + s
        total = jnp.zeros((32, block), F32)
        for k in range(topk):
            total = jnp.where(row == slot[k : k + 1, :], gates[k : k + 1, :], total)
        out_ref[0, s : s + 32, :] = total


def build_weight(places, gates, slots):
    topk, tokens = places.shape
    block = tokens // N_Y
    return pl.pallas_call(
        weight_kernel,
        grid=(N_Y,),
        out_shape=jax.ShapeDtypeStruct((N_Y, slots, block), F32),
        in_specs=[pl.BlockSpec((topk, block), lambda i: (0, i))] * 2,
        out_specs=pl.BlockSpec((1, slots, block), lambda i: (i, 0, 0)),
        compiler_params=params(8),
        cost_estimate=cost(3 * topk * slots * tokens, 4 * slots * tokens),
        name="weight",
    )(places, gates)


def load_rows(src, dst, sems, pieces):
    rows = src.shape[0] // pieces
    return [
        copy(src.at[pl.ds(i * rows, rows), :], dst.at[pl.ds(i * rows, rows), :], sems.at[i])
        for i in range(pieces)
    ]


def part_columns(left, right, part, part_hbm, sems):
    width = part.shape[1]
    block = width // N_Y
    sent = []
    for j in range(N_Y):
        cols = pl.ds(j * block, block)
        part[:, cols] = dot(left[...], right[:, cols], NN).astype(BF16)
        c = copy(part.at[:, cols], part_hbm.at[:, cols], sems.at[j])
        c.start()
        sent.append(c)
    return sent


def first_kernel(
    tok_hbm, grad_hbm, down_hbm, weight_hbm, slope_hbm, part_hbm,
    tok, grad, down, weight, slope, gated, part,
    tok_sems, grad_sems, down_sem, weight_sems, slope_sems, part_sems,
):
    block = weight.shape[2]
    down_in = copy(down_hbm, down, down_sem)
    weight_in = [copy(weight_hbm.at[c], weight.at[c], weight_sems.at[c]) for c in range(N_Y)]
    tok_in = load_rows(tok_hbm, tok, tok_sems, 8)
    grad_in = load_rows(grad_hbm, grad, grad_sems, 8)
    down_in.start()
    for c in range(N_Y):
        tok_in[2 * c].start()
        tok_in[2 * c + 1].start()
        weight_in[c].start()
    for g in grad_in:
        g.start()
    down_in.wait()
    sent = []
    for c in range(N_Y):
        tok_in[2 * c].wait()
        tok_in[2 * c + 1].wait()
        pre = dot(down[...], tok[pl.ds(c * block, block), :], NT)
        weight_in[c].wait()
        here = weight[c]
        cdf = 0.5 * (1.0 + lax.erf(pre * SQRT_HALF))
        density = INV_ROOT_TAU * jnp.exp(-0.5 * pre * pre)
        gated[:, pl.ds(c * block, block)] = (here * (pre * cdf)).astype(BF16)
        slope[c] = here * (cdf + pre * density)
        out = copy(slope.at[c], slope_hbm.at[c], slope_sems.at[c])
        out.start()
        sent.append(out)
    for g in grad_in:
        g.wait()
    sent += part_columns(gated, grad, part, part_hbm, part_sems)
    for s in sent:
        s.wait()


def first_terms(tokens, grads, down, weight):
    count, width = tokens.shape
    slots = down.shape[0]
    return pl.pallas_call(
        first_kernel,
        out_shape=(
            jax.ShapeDtypeStruct(weight.shape, F32),
            jax.ShapeDtypeStruct((slots, width), BF16),
        ),
        in_specs=[ANY] * 4,
        out_specs=(ANY, ANY),
        scratch_shapes=[
            pltpu.VMEM((count, width), BF16),
            pltpu.VMEM((count, width), BF16),
            pltpu.VMEM((slots, width), BF16),
            pltpu.VMEM(weight.shape, F32),
            pltpu.VMEM(weight.shape, F32),
            pltpu.VMEM((slots, count), BF16),
            pltpu.VMEM((slots, width), BF16),
            DMA((8,)), DMA((8,)), DMA, DMA((4,)), DMA((4,)), DMA((4,)),
        ],
        compiler_params=params(56),
        cost_estimate=cost(4 * count * width * slots, 20 << 20),
        name="first",
    )(tokens, grads, down, weight)


def second_kernel(
    tok_hbm, grad_hbm, up_hbm, slope_hbm, c0, c1, c2, c3, part_hbm,
    tok, grad, up, slope, coef, part,
    tok_sems, grad_sems, up_sem, slope_sems, coef_sems, part_sems,
):
    block = slope.shape[2]
    y = lax.axis_index("y")
    up_in = copy(up_hbm, up, up_sem)
    slope_in = [copy(slope_hbm.at[c], slope.at[c], slope_sems.at[c]) for c in range(N_Y)]
    grad_in = load_rows(grad_hbm, grad, grad_sems, 8)
    tok_in = load_rows(tok_hbm, tok, tok_sems, 8)
    up_in.start()
    for c in range(N_Y):
        grad_in[2 * c].start()
        grad_in[2 * c + 1].start()
        slope_in[c].start()
    for t in tok_in:
        t.start()
    up_in.wait()
    for c in range(N_Y):
        grad_in[2 * c].wait()
        grad_in[2 * c + 1].wait()
        back = dot(up[...], grad[pl.ds(c * block, block), :], NT)
        slope_in[c].wait()
        coef[:, pl.ds(c * block, block)] = (slope[c] * back).astype(BF16)
    sent = []
    for r, out in enumerate((c0, c1, c2, c3)):
        start = pl.multiple_of(((y + r) % N_Y) * block, block)
        c = copy(coef.at[:, pl.ds(start, block)], out, coef_sems.at[r])
        c.start()
        sent.append(c)
    for t in tok_in:
        t.wait()
    sent += part_columns(coef, tok, part, part_hbm, part_sems)
    for s in sent:
        s.wait()


def second_terms(tokens, grads, up, slope):
    count, width = tokens.shape
    slots = up.shape[0]
    return pl.pallas_call(
        second_kernel,
        out_shape=tuple(jax.ShapeDtypeStruct((slots, count // N_Y), BF16) for _ in range(N_Y))
        + (jax.ShapeDtypeStruct((slots, width), BF16),),
        in_specs=[ANY] * 4,
        out_specs=(ANY,) * 5,
        scratch_shapes=[
            pltpu.VMEM((count, width), BF16),
            pltpu.VMEM((count, width), BF16),
            pltpu.VMEM((slots, width), BF16),
            pltpu.VMEM(slope.shape, F32),
            pltpu.VMEM((slots, count), BF16),
            pltpu.VMEM((slots, width), BF16),
            DMA((8,)), DMA((8,)), DMA, DMA((4,)), DMA((4,)), DMA((4,)),
        ],
        compiler_params=params(56),
        cost_estimate=cost(4 * count * width * slots, 20 << 20),
        name="second",
    )(tokens, grads, up, slope)


def scatter_kernel(asked_ref, got_hbm, o0, o1, o2, o3, got, sums, sems, out_sems):
    rows = o0.shape[0]
    width = got.shape[1]
    block = width // 4
    copies = [
        copy(got_hbm.at[:, pl.ds(j * block, block)], got.at[:, pl.ds(j * block, block)], sems.at[j])
        for j in range(4)
    ]
    for c in copies:
        c.start()
    hits = column_hits(asked_ref[...], rows)
    for j in range(4):
        copies[j].wait()
        cols = pl.ds(j * block, block)
        sums[:, cols] = dot(hits, got[:, cols], TN).astype(BF16)
    sent = []
    for r, out in enumerate((o0, o1, o2, o3)):
        c = copy(sums.at[pl.ds(r * rows, rows), :], out, out_sems.at[r])
        c.start()
        sent.append(c)
    for c in sent:
        c.wait()


def scatter_rows(asked, got, rows):
    slots, width = got.shape
    return pl.pallas_call(
        scatter_kernel,
        out_shape=tuple(jax.ShapeDtypeStruct((rows, width), BF16) for _ in range(N_Y)),
        in_specs=[VMEM, ANY],
        out_specs=(ANY,) * N_Y,
        scratch_shapes=[
            pltpu.VMEM((slots, width), BF16),
            pltpu.VMEM((N_Y * rows, width), BF16),
            DMA((4,)),
            DMA((4,)),
        ],
        compiler_params=params(8),
        cost_estimate=cost(2 * 256 * 256 * 2048, 2 * 10**6),
    )(asked, got)


def final_kernel(mine, c0, c1, c2, c3, d0, d1, d2, d3, out_hbm, coef, rows, out, c_sems, d_sems, out_sems):
    core = lax.axis_index("core")
    which = core if mine else 1 - core
    slots = c0.shape[0]
    half = out.shape[0]
    loads = []
    for r in range(N_Y):
        cols = pl.ds(pl.multiple_of(which * half, half), half)
        place = pl.ds(r * slots, slots)
        loads.append(copy((c0, c1, c2, c3)[r].at[:, cols], coef.at[place, :], c_sems.at[r]))
        loads.append(copy((d0, d1, d2, d3)[r], rows.at[place, :], d_sems.at[r]))
    for c in loads:
        c.start()
    for c in loads:
        c.wait()
    width = out.shape[1]
    block = width // 4
    sent = []
    for j in range(4):
        cols = pl.ds(j * block, block)
        out[:, cols] = dot(coef[...], rows[:, cols], TN).astype(BF16)
        c = copy(out.at[:, cols], out_hbm.at[:, cols], out_sems.at[j])
        c.start()
        sent.append(c)
    for c in sent:
        c.wait()


def final_product(mine, coef, rows):
    slots, width = rows[0].shape
    half = coef[0].shape[1] // N_CORE
    return pl.pallas_call(
        functools.partial(final_kernel, mine),
        out_shape=jax.ShapeDtypeStruct((half, width), BF16),
        in_specs=[ANY] * 8,
        out_specs=ANY,
        scratch_shapes=[
            pltpu.VMEM((N_Y * slots, half), BF16),
            pltpu.VMEM((N_Y * slots, width), BF16),
            pltpu.VMEM((half, width), BF16),
            DMA((4,)), DMA((4,)), DMA((4,)),
        ],
        compiler_params=params(16),
        cost_estimate=cost(2 * half * 1024 * 2048, 6 << 20),
        name="keep" if mine else "give",
    )(*coef, *rows)


def turn(x, r):
    return lax.ppermute(x, "y", [(i, (i - r) % N_Y) for i in range(N_Y)])


def around(x):
    return (x,) + tuple(turn(x, r) for r in range(1, N_Y))


def exchange(x):
    return lax.all_to_all(x, ("dp", "core"), split_axis=0, concat_axis=0, tiled=True)


def program(tokens, out_grad, down_rows, up_rows, requests, places, gate_weights):
    peers = lax.axis_size("dp") * N_CORE
    row_count, width = down_rows.shape

    down_tables = around(down_rows)
    ids = expand_ids(requests[0])
    slots = ids.shape[0]
    per_peer = slots // peers
    asked = exchange(ids.reshape(peers, per_peer, 128)).reshape(slots, 128)
    up_tables = around(up_rows)
    weight = build_weight(jnp.transpose(places[0]), jnp.transpose(gate_weights[0]), slots)

    def fetch(tables):
        rows = gather_rows(asked, tables)
        return exchange(rows.reshape(peers, per_peer, width)).reshape(slots, width)

    down = fetch(down_tables)
    up = fetch(up_tables)
    down_all = around(down)
    slope, part_up = first_terms(tokens, out_grad, down, weight)
    *coef, part_down = second_terms(tokens, out_grad, up, slope)

    def give_back(part):
        return exchange(part.reshape(peers, per_peer, width)).reshape(slots, width)

    got_up = give_back(part_up)
    got_down = give_back(part_down)
    coef_in = (coef[0],) + tuple(turn(coef[(N_Y - r) % N_Y], r) for r in range(1, N_Y))

    def total(got):
        sums = scatter_rows(asked, got, row_count)
        found = [sums[0]] + [turn(sums[N_Y - r], r) for r in range(1, N_Y)]
        return sum(f.astype(F32) for f in found)

    up_grad = total(got_up)
    give = final_product(False, coef_in, down_all)
    other = lax.ppermute(give, "core", [(0, 1), (1, 0)])
    keep = final_product(True, coef_in, down_all)
    input_grad = (keep.astype(F32) + other.astype(F32)).astype(BF16)
    down_grad = total(got_down)
    return (input_grad, down_grad, up_grad)


def solution(mesh):
    axes = ("dp", "y", "core")
    fine = Mesh(mesh.devices.reshape(mesh.devices.shape[0], N_Y, N_CORE), axes)
    in_specs = (
        P("dp", None),
        P("dp", None),
        P(axes, None),
        P(axes, None),
        P(axes, None, None),
        P(("y", "core"), "dp", None),
        P(("y", "core"), "dp", None),
    )
    out_specs = (P(axes, None), P(axes, None), P(axes, None))
    return jax.shard_map(program, mesh=fine, in_specs=in_specs, out_specs=out_specs, check_vma=False)
```

time: 237 us -> 196 us (0.83)
  blocking collectives: 43.5 us -> 17 us
  local copies, waits for them, and re-layouts: 16.3 us -> 8.98 us
  Pallas kernels: 51.1 us -> 44.5 us
  starting transfers between devices: 45.9 us -> 50.5 us
    all_to_all x1 -> x0, blocking collectives: 18.2 us -> none  [shards(): lax.all_to_all(coef, 'y', split_axis=0, concat_axis=0, tiled=True)]
    ppermute x10 -> x19, waiting for transfers between devices: 39.9 us -> 57 us  [the longest x18 57 us: turn(): return lax.ppermute(x, 'y', [(i, (i - r) % N_Y) for i in range(N_Y)])]
    ppermute x10 -> x19, starting transfers between devices: 13.6 us -> 26.9 us  [the longest x18 24.2 us: turn(): return lax.ppermute(x, 'y', [(i, (i - r) % N_Y) for i in range(N_Y)])]
    all_to_all x2 -> x0, waiting for transfers between devices: 13.3 us -> none  [give_back(): shared = lax.all_to_all(sums, 'y', split_axis=0, concat_axis=0, tiled=True)]
    all_to_all x1, blocking collectives: 25.3 us -> 17 us  [exchange(): lax.all_to_all(x, ('dp', 'core'), split_axis=0, concat_axis=0, tiled=True)]
    unnamed x32 -> x34, local copies, waits for them, and re-layouts: 16.3 us -> 8.98 us
    all_to_all x2 -> x0, starting transfers between devices: 7.03 us -> none  [give_back(): shared = lax.all_to_all(sums, 'y', split_axis=0, concat_axis=0, tiled=True)]
    all_to_all x4, waiting for transfers between devices: 18.7 us -> 12.9 us  [exchange(): lax.all_to_all(x, ('dp', 'core'), split_axis=0, concat_axis=0, tiled=True)]
  transfers between devices with their start and end apart: 16 -> 23, of which waited for: 9 -> 8; matrix products, arithmetic and copies ran while one was open for 1% -> 1% of each run, Pallas kernels for 15% -> 16%
where the time goes in v2:
time: 196 us; the launch traced here: 195 us
  waiting for transfers between devices  69.9 us (36%)
  starting transfers between devices  50.5 us (26%)
  Pallas kernels  44.5 us (23%)
  blocking collectives  17 us (9%)
  local copies, waits for them, and re-layouts  8.98 us (5%)
  other arithmetic  3.2 us (2%)
    ppermute x18, waiting for transfers between devices, turn(): return lax.ppermute(x, 'y', [(i, (i - r) % N_Y) for i in range(N_Y)])  57 us
    ppermute x18, starting transfers between devices, turn(): return lax.ppermute(x, 'y', [(i, (i - r) % N_Y) for i in range(N_Y)])  24.2 us
    all_to_all x4, starting transfers between devices, exchange(): lax.all_to_all(x, ('dp', 'core'), split_axis=0, concat_axis=0, tiled=True)  23.5 us
    all_to_all x1, blocking collectives, exchange(): lax.all_to_all(x, ('dp', 'core'), split_axis=0, concat_axis=0, tiled=True)  17 us
    pallas_call x1, Pallas kernels, first_terms(): pl.pallas_call(first_kernel, out_shape=(jax.ShapeDtypeStruct(weight.shape...  13.3 us
    all_to_all x4, waiting for transfers between devices, exchange(): lax.all_to_all(x, ('dp', 'core'), split_axis=0, concat_axis=0, tiled=True)  12.9 us
    pallas_call x1, Pallas kernels, second_terms(): pl.pallas_call(second_kernel, out_shape=tuple((jax.ShapeDtypeStruct((slot...  12.4 us
    unnamed x34, local copies, waits for them, and re-layouts  8.98 us
  transfers between devices with their start and end apart: 23, of which 8 were waited for; matrix products, arithmetic and copies ran while one was open for 1% of the time, Pallas kernels for 16%

profile of v2, /device:TPU:1, one launch (start us, length us, event | category | flops | bytes accessed | tf_op | source)
XLA Modules:
  0.0 195.0 jit_solution(18111628137521286300)
XLA Ops:
  0.6 3.6 %collective-permute-start.3 = (bf16[64,2048]{1,0:T(8,128)(2,1)}, bf16[64,2048]{1,0:T(8,128)(2,1)S(1)}, u32[]{:S(2)}, u32[]{:S(2)}) collective-permute-start(bf16[64,2048]{1,0:T(8,128)(2,1)} %t0.3), channel_id=1, source_target_pairs={{0,6},{2,0},{4,2},{6,4},{1,7},{3,1},{5,3},{7,5},{8,14},{10,8},{12,... | collective-permute-start | bytes 786440 | tf_op jit(solution)/shard_map/ppermute | solution.py:394
  5.3 1.6 ids.1
  6.9 17.0 %all_to_all.25 = s32[32,8,128]{2,1,0:T(8,128)S(1)} all-to-all(s32[32,8,128]{2,1,0:T(8,128)} %bitcast.36), channel_id=1, replica_groups=mesh['dp'=16,'y'=4,'core'=2] {'dp','core'}, dimensions={0} | all-to-all | bytes 262144 | tf_op jit(solution)/shard_map/all_to_all | solution.py:402
  24.0 0.9 copy-done.10
  24.9 1.5 shard_map.95
  26.4 4.3 %all-to-all-start.2 = ((bf16[32,8,2048]{2,1,0:T(8,128)(2,1)}), bf16[32,8,2048]{2,1,0:T(8,128)(2,1)S(1)}, u32[]{:S(2)}, u32[]{:S(2)}) async-start(bf16[32,8,2048]{2,1,0:T(8,128)(2,1)} %bitcast.6), calls=%async_computation.2 | async-start | bytes 2097152 | tf_op jit(solution)/shard_map/all_to_all | solution.py:402
  30.7 1.8 collective-permute-start
  32.5 1.4 collective-permute-start.1
  33.9 4.5 %collective-permute-done.t1 = bf16[64,2048]{1,0:T(8,128)(2,1)S(1)} collective-permute-done((bf16[64,2048]{1,0:T(8,128)(2,1)S(1)}, bf16[64,2048]{1,0:T(8,128)(2,1)S(1)}, u32[]{:S(2)}, u32[]{:S(2)}) %collective-permute-start) | collective-permute-done | bytes 262176 | tf_op jit(solution)/shard_map/ppermute | solution.py:394
  38.4 2.8 %collective-permute-done.1.t2 = bf16[64,2048]{1,0:T(8,128)(2,1)S(1)} collective-permute-done((bf16[64,2048]{1,0:T(8,128)(2,1)S(1)}, bf16[64,2048]{1,0:T(8,128)(2,1)S(1)}, u32[]{:S(2)}, u32[]{:S(2)}) %collective-permute-start.1) | collective-permute-done | bytes 262176 | tf_op jit(solution)/shard_map/ppermute | solution.py:394
  41.3 6.6 %collective-permute-done.2.t3 = bf16[64,2048]{1,0:T(8,128)(2,1)S(1)} collective-permute-done((bf16[64,2048]{1,0:T(8,128)(2,1)S(1)}, bf16[64,2048]{1,0:T(8,128)(2,1)S(1)}, u32[]{:S(2)}, u32[]{:S(2)}) %collective-permute-start.2) | collective-permute-done | bytes 262176 | tf_op jit(solution)/shard_map/ppermute | solution.py:394
  47.9 1.4 shard_map.94
  49.3 7.6 %all-to-all-start.1 = ((bf16[32,8,2048]{2,1,0:T(8,128)(2,1)}), bf16[32,8,2048]{2,1,0:T(8,128)(2,1)S(1)}, u32[]{:S(2)}, u32[]{:S(2)}) async-start(bf16[32,8,2048]{2,1,0:T(8,128)(2,1)} %bitcast.4), calls=%async_computation.1 | async-start | bytes 2097152 | tf_op jit(solution)/shard_map/all_to_all | solution.py:402
  56.9 2.9 %weight.1.weight_hbm = f32[4,256,512]{2,1,0:T(8,128)S(1)} custom-call(s32[16,2048]{1,0:T(8,128)S(1)} %bitcast.31, f32[16,2048]{1,0:T(8,128)S(1)} %bitcast.32), custom_call_target="tpu_custom_call" | custom-call | flops 25165824 | bytes 2097152 | tf_op jit(solution)/shard_map/weight/pallas_call | solution.py:142
  59.9 1.4 copy-done.2
  61.2 13.3 %first.1 = (f32[4,256,512]{2,1,0:T(8,128)}, bf16[256,2048]{1,0:T(8,128)(2,1)}) custom-call(bf16[2048,2048]{1,0:T(8,128)(2,1)} %tok_hbm.3, bf16[2048,2048]{1,0:T(8,128)(2,1)} %grad_hbm.3, bf16[256,2048]{1,0:T(8,128)(2,1)} %bitcast.19, f32[4,256,512]{2,1,0:T(8,128)} %copy-done.2), custom_call_target="tpu_custom_call" | custom-call | flops 4294967296 | bytes 20971520 | tf_op jit(solution)/shard_map/first/pallas_call | solution.py:217
  74.5 1.0 copy-done.16
  75.5 12.4 %second.1 = (bf16[256,512]{1,0:T(8,128)(2,1)}, bf16[256,512]{1,0:T(8,128)(2,1)}, bf16[256,512]{1,0:T(8,128)(2,1)}, bf16[256,512]{1,0:T(8,128)(2,1)}, bf16[256,2048]{1,0:T(8,128)(2,1)}) custom-call(bf16[2048,2048]{1,0:T(8,128)(2,1)} %tok_hbm.3, bf16[2048,2048]{1,0:T(8,128)(2,1)} %grad_hbm.3, bf16[256,2048]{1,0:T(8,128)(2,1)} %bitcast.33, ...), custom_call_target="tpu_custom_call" | custom-call | flops 4294967296 | bytes 20971520 | tf_op jit(solution)/shard_map/second/pallas_call | solution.py:282
  87.9 7.5 %all-to-all-start.3 = ((bf16[32,8,2048]{2,1,0:T(8,128)(2,1)}), bf16[32,8,2048]{2,1,0:T(8,128)(2,1)S(1)}, u32[]{:S(2)}, u32[]{:S(2)}) async-start(bf16[32,8,2048]{2,1,0:T(8,128)(2,1)} %bitcast.35), calls=%async_computation.3 | async-start | bytes 2097152 | tf_op jit(solution)/shard_map/all_to_all | solution.py:402
  95.4 1.5 collective-permute-start.10
  96.9 2.7 %collective-permute-start.9 = (bf16[256,2048]{1,0:T(8,128)(2,1)S(1)}, bf16[256,2048]{1,0:T(8,128)(2,1)}, u32[]{:S(2)}, u32[]{:S(2)}) collective-permute-start(bf16[256,2048]{1,0:T(8,128)(2,1)S(1)} %bitcast.22), channel_id=1, source_target_pairs={{0,6},{2,0},{4,2},{6,4},{1,7},{3,1},{5,3},{7,5},{8,14},{10,8},{12,... | collective-permute-start | bytes 3145736 | tf_op jit(solution)/shard_map/ppermute | solution.py:394
  99.6 12.9 %all-to-all-done.3 = bf16[32,8,2048]{2,1,0:T(8,128)(2,1)S(1)} async-done(((bf16[32,8,2048]{2,1,0:T(8,128)(2,1)}), bf16[32,8,2048]{2,1,0:T(8,128)(2,1)S(1)}, u32[]{:S(2)}, u32[]{:S(2)}) %all-to-all-start.3) | async-done | bytes 1048608 | tf_op jit(solution)/shard_map/all_to_all | solution.py:402
  112.5 4.1 %all-to-all-start.4 = ((bf16[32,8,2048]{2,1,0:T(8,128)(2,1)}), bf16[32,8,2048]{2,1,0:T(8,128)(2,1)S(1)}, u32[]{:S(2)}, u32[]{:S(2)}) async-start(bf16[32,8,2048]{2,1,0:T(8,128)(2,1)} %bitcast.34), calls=%async_computation.4 | async-start | bytes 2097152 | tf_op jit(solution)/shard_map/all_to_all | solution.py:402
  117.2 1.4 collective-permute-start.7
  118.6 28.9 %collective-permute-done.6.c1 = bf16[256,512]{1,0:T(8,128)(2,1)S(1)} collective-permute-done((bf16[256,512]{1,0:T(8,128)(2,1)}, bf16[256,512]{1,0:T(8,128)(2,1)S(1)}, u32[]{:S(2)}, u32[]{:S(2)}) %collective-permute-start.6) | collective-permute-done | bytes 262176 | tf_op jit(solution)/shard_map/ppermute | solution.py:394
  147.6 0.7 copy-done.4
  148.3 3.1 %collective-permute-start.8 = (bf16[256,512]{1,0:T(8,128)(2,1)}, bf16[256,512]{1,0:T(8,128)(2,1)S(1)}, u32[]{:S(2)}, u32[]{:S(2)}) collective-permute-start(bf16[256,512]{1,0:T(8,128)(2,1)} %get-tuple-element.22), channel_id=1, source_target_pairs={{0,2},{2,4},{4,6},{6,0},{1,3},{3,5},{5,7},{7,1},{8,10},{10,12},{12... | collective-permute-start | bytes 786440 | tf_op jit(solution)/shard_map/ppermute | solution.py:394
  151.4 2.1 %shard_map.96 = (bf16[64,2048]{1,0:T(8,128)(2,1)S(1)}, bf16[64,2048]{1,0:T(8,128)(2,1)}, bf16[64,2048]{1,0:T(8,128)(2,1)}, bf16[64,2048]{1,0:T(8,128)(2,1)}) custom-call(s32[256,128]{1,0:T(8,128)S(1)} %bitcast.29, bf16[256,2048]{1,0:T(8,128)(2,1)S(1)} %bitcast.26), custom_call_target="tpu_custom_call" | custom-call | flops 268435456 | bytes 2000000 | tf_op jit(solution)/shard_map/pallas_call | solution.py:329
  153.5 0.7 copy-done.12
  154.2 0.7 copy-done.6
  154.9 1.4 collective-permute-start.13
  156.3 1.1 collective-permute-done.8.c3
  158.1 1.4 collective-permute-start.14
  159.5 1.0 collective-permute-start.15
  160.5 1.2 shard_map.97
  161.8 1.8 collective-permute-start.16
  163.6 0.9 copy-done.5
  164.5 0.9 copy-done.7
  165.5 0.9 copy-done.9
  166.4 4.1 %give.1 = bf16[256,2048]{1,0:T(8,128)(2,1)S(1)} custom-call(bf16[256,512]{1,0:T(8,128)(2,1)S(1)} %copy-done.3, bf16[256,512]{1,0:T(8,128)(2,1)S(1)} %copy-done.5, bf16[256,512]{1,0:T(8,128)(2,1)S(1)} %copy-done.7, bf16[256,512]{1,0:T(8,128)(2,1)S(1)} %copy-done.9, bf16[256,2048]{1,0:T(8,128)(2,1)S(1)} %bitcast.23, ...), custom_call_target="tpu_custom_call" | custom-call | flops 1073741824 | bytes 6291456 | tf_op jit(solution)/shard_map/give/pallas_call | solution.py:376
  170.5 2.7 %collective-permute-start.12 = (bf16[256,2048]{1,0:T(8,128)(2,1)S(1)}, bf16[256,2048]{1,0:T(8,128)(2,1)S(1)}, u32[]{:S(2)}, u32[]{:S(2)}) collective-permute-start(bf16[256,2048]{1,0:T(8,128)(2,1)S(1)} %give.1), channel_id=1, source_target_pairs={{0,1},{1,0},{2,3},{3,2},{4,5},{5,4},{6,7},{7,6},{8,9},{9,8},{10,11... | collective-permute-start | bytes 3145736 | tf_op jit(solution)/shard_map/ppermute | solution.py:441
  173.2 4.0 %keep.1 = bf16[256,2048]{1,0:T(8,128)(2,1)S(1)} custom-call(bf16[256,512]{1,0:T(8,128)(2,1)S(1)} %copy-done.3, bf16[256,512]{1,0:T(8,128)(2,1)S(1)} %copy-done.5, bf16[256,512]{1,0:T(8,128)(2,1)S(1)} %copy-done.7, bf16[256,512]{1,0:T(8,128)(2,1)S(1)} %copy-done.9, bf16[256,2048]{1,0:T(8,128)(2,1)S(1)} %bitcast.24, ...), custom_call_target="tpu_custom_call" | custom-call | flops 1073741824 | bytes 6291456 | tf_op jit(solution)/shard_map/keep/pallas_call | solution.py:376
  177.7 1.1 collective-permute-start.18
  178.8 0.9 convert_add_fusion.1
  179.7 6.9 %collective-permute-done.17 = bf16[64,2048]{1,0:T(8,128)(2,1)S(1)} collective-permute-done((bf16[64,2048]{1,0:T(8,128)(2,1)S(1)}, bf16[64,2048]{1,0:T(8,128)(2,1)S(1)}, u32[]{:S(2)}, u32[]{:S(2)}) %collective-permute-start.17) | collective-permute-done | bytes 262176 | tf_op jit(solution)/shard_map/ppermute | solution.py:394
  186.7 6.0 %collective-permute-done.18 = bf16[64,2048]{1,0:T(8,128)(2,1)S(1)} collective-permute-done((bf16[64,2048]{1,0:T(8,128)(2,1)S(1)}, bf16[64,2048]{1,0:T(8,128)(2,1)S(1)}, u32[]{:S(2)}, u32[]{:S(2)}) %collective-permute-start.18) | collective-permute-done | bytes 262176 | tf_op jit(solution)/shard_map/ppermute | solution.py:394
  192.7 0.9 convert_add_fusion
  193.6 1.4 add_convert_fusion
  (46 shorter events, 2.9 us)
Async XLA Ops:
  0.6 23.3 %collective-permute-start.3 = (bf16[64,2048]{1,0:T(8,128)(2,1)}, bf16[64,2048]{1,0:T(8,128)(2,1)S(1)}, u32[]{:S(2)}, u32[]{:S(2)}) collective-permute-start(bf16[64,2048]{1,0:T(8,128)(2,1)} %t0.3), channel_id=1, source_target_pairs={{0,6},{2,0},{4,2},{6,4},{1,7},{3,1},{5,3},{7,5},{8,14},{10,8},{12,... | collective-permute-start | bytes 786440 | tf_op jit(solution)/shard_map/ppermute | solution.py:394
  4.3 19.7 %collective-permute-start.4 = (bf16[64,2048]{1,0:T(8,128)(2,1)}, bf16[64,2048]{1,0:T(8,128)(2,1)S(1)}, u32[]{:S(2)}, u32[]{:S(2)}) collective-permute-start(bf16[64,2048]{1,0:T(8,128)(2,1)} %t0.3), channel_id=1, source_target_pairs={{0,4},{2,6},{4,0},{6,2},{1,5},{3,7},{5,1},{7,3},{8,12},{10,14},{12... | collective-permute-start | bytes 786440 | tf_op jit(solution)/shard_map/ppermute | solution.py:394
  4.6 19.3 %collective-permute-start.5 = (bf16[64,2048]{1,0:T(8,128)(2,1)}, bf16[64,2048]{1,0:T(8,128)(2,1)S(1)}, u32[]{:S(2)}, u32[]{:S(2)}) collective-permute-start(bf16[64,2048]{1,0:T(8,128)(2,1)} %t0.3), channel_id=1, source_target_pairs={{0,2},{2,4},{4,6},{6,0},{1,3},{3,5},{5,7},{7,1},{8,10},{10,12},{12... | collective-permute-start | bytes 786440 | tf_op jit(solution)/shard_map/ppermute | solution.py:394
  23.9 1.0 copy-start.10
  24.9 5.8 %copy-start.11 = (bf16[64,2048]{1,0:T(8,128)(2,1)S(1)}, bf16[64,2048]{1,0:T(8,128)(2,1)}, u32[]{:S(2)}) copy-start(bf16[64,2048]{1,0:T(8,128)(2,1)} %t0.2) | copy-start | bytes 786436
  26.4 22.9 %all-to-all-start.2 = ((bf16[32,8,2048]{2,1,0:T(8,128)(2,1)}), bf16[32,8,2048]{2,1,0:T(8,128)(2,1)S(1)}, u32[]{:S(2)}, u32[]{:S(2)}) async-start(bf16[32,8,2048]{2,1,0:T(8,128)(2,1)} %bitcast.6), calls=%async_computation.2 | async-start | bytes 2097152 | tf_op jit(solution)/shard_map/all_to_all | solution.py:402
  30.7 26.2 %copy-start.14 = (s32[1,2048,16]{1,2,0:T(8,128)S(1)}, s32[1,2048,16]{1,2,0:T(8,128)}, u32[]{:S(2)}) copy-start(s32[1,2048,16]{1,2,0:T(8,128)} %param.12) | copy-start | bytes 393220
  30.7 26.2 %copy-start.15 = (f32[1,2048,16]{1,2,0:T(8,128)S(1)}, f32[1,2048,16]{1,2,0:T(8,128)}, u32[]{:S(2)}) copy-start(f32[1,2048,16]{1,2,0:T(8,128)} %param.13) | copy-start | bytes 393220
  30.7 7.7 %collective-permute-start = (bf16[64,2048]{1,0:T(8,128)(2,1)S(1)}, bf16[64,2048]{1,0:T(8,128)(2,1)S(1)}, u32[]{:S(2)}, u32[]{:S(2)}) collective-permute-start(bf16[64,2048]{1,0:T(8,128)(2,1)S(1)} %copy-done.11), channel_id=1, source_target_pairs={{0,6},{2,0},{4,2},{6,4},{1,7},{3,1},{5,3},{7,5},{8,14},{10,8},{12,... | collective-permute-start | bytes 786440 | tf_op jit(solution)/shard_map/ppermute | solution.py:394
  32.5 8.8 %collective-permute-start.1 = (bf16[64,2048]{1,0:T(8,128)(2,1)S(1)}, bf16[64,2048]{1,0:T(8,128)(2,1)S(1)}, u32[]{:S(2)}, u32[]{:S(2)}) collective-permute-start(bf16[64,2048]{1,0:T(8,128)(2,1)S(1)} %copy-done.11), channel_id=1, source_target_pairs={{0,4},{2,6},{4,0},{6,2},{1,5},{3,7},{5,1},{7,3},{8,12},{10,14},{12... | collective-permute-start | bytes 786440 | tf_op jit(solution)/shard_map/ppermute | solution.py:394
  33.9 13.9 %collective-permute-start.2 = (bf16[64,2048]{1,0:T(8,128)(2,1)S(1)}, bf16[64,2048]{1,0:T(8,128)(2,1)S(1)}, u32[]{:S(2)}, u32[]{:S(2)}) collective-permute-start(bf16[64,2048]{1,0:T(8,128)(2,1)S(1)} %copy-done.11), channel_id=1, source_target_pairs={{0,2},{2,4},{4,6},{6,0},{1,3},{3,5},{5,7},{7,1},{8,10},{10,12},{12... | collective-permute-start | bytes 786440 | tf_op jit(solution)/shard_map/ppermute | solution.py:394
  49.3 10.5 %copy-start = (bf16[32,8,2048]{2,1,0:T(8,128)(2,1)}, bf16[32,8,2048]{2,1,0:T(8,128)(2,1)S(1)}, u32[]{:S(2)}) copy-start(bf16[32,8,2048]{2,1,0:T(8,128)(2,1)S(1)} %all-to-all-done.2) | copy-start | bytes 3145732
  49.3 25.2 %all-to-all-start.1 = ((bf16[32,8,2048]{2,1,0:T(8,128)(2,1)}), bf16[32,8,2048]{2,1,0:T(8,128)(2,1)S(1)}, u32[]{:S(2)}, u32[]{:S(2)}) async-start(bf16[32,8,2048]{2,1,0:T(8,128)(2,1)} %bitcast.4), calls=%async_computation.1 | async-start | bytes 2097152 | tf_op jit(solution)/shard_map/all_to_all | solution.py:402
  59.8 1.4 copy-start.2
  74.5 1.0 copy-start.16
  87.9 7.5 %copy-start.1 = (bf16[32,8,2048]{2,1,0:T(8,128)(2,1)S(1)}, bf16[32,8,2048]{2,1,0:T(8,128)(2,1)}, u32[]{:S(2)}) copy-start(bf16[32,8,2048]{2,1,0:T(8,128)(2,1)} %copy-done) | copy-start | bytes 3145732
  87.9 24.6 %all-to-all-start.3 = ((bf16[32,8,2048]{2,1,0:T(8,128)(2,1)}), bf16[32,8,2048]{2,1,0:T(8,128)(2,1)S(1)}, u32[]{:S(2)}, u32[]{:S(2)}) async-start(bf16[32,8,2048]{2,1,0:T(8,128)(2,1)} %bitcast.35), calls=%async_computation.3 | async-start | bytes 2097152 | tf_op jit(solution)/shard_map/all_to_all | solution.py:402
  95.4 64.1 %collective-permute-start.10 = (bf16[256,2048]{1,0:T(8,128)(2,1)S(1)}, bf16[256,2048]{1,0:T(8,128)(2,1)}, u32[]{:S(2)}, u32[]{:S(2)}) collective-permute-start(bf16[256,2048]{1,0:T(8,128)(2,1)S(1)} %bitcast.20), channel_id=1, source_target_pairs={{0,4},{2,6},{4,0},{6,2},{1,5},{3,7},{5,1},{7,3},{8,12},{10,14},{12... | collective-permute-start | bytes 3145736 | tf_op jit(solution)/shard_map/ppermute | solution.py:394
  96.9 64.9 %collective-permute-start.11 = (bf16[256,2048]{1,0:T(8,128)(2,1)S(1)}, bf16[256,2048]{1,0:T(8,128)(2,1)}, u32[]{:S(2)}, u32[]{:S(2)}) collective-permute-start(bf16[256,2048]{1,0:T(8,128)(2,1)S(1)} %bitcast.21), channel_id=1, source_target_pairs={{0,2},{2,4},{4,6},{6,0},{1,3},{3,5},{5,7},{7,1},{8,10},{10,12},{12... | collective-permute-start | bytes 3145736 | tf_op jit(solution)/shard_map/ppermute | solution.py:394
  96.9 66.6 %collective-permute-start.9 = (bf16[256,2048]{1,0:T(8,128)(2,1)S(1)}, bf16[256,2048]{1,0:T(8,128)(2,1)}, u32[]{:S(2)}, u32[]{:S(2)}) collective-permute-start(bf16[256,2048]{1,0:T(8,128)(2,1)S(1)} %bitcast.22), channel_id=1, source_target_pairs={{0,6},{2,0},{4,2},{6,4},{1,7},{3,1},{5,3},{7,5},{8,14},{10,8},{12,... | collective-permute-start | bytes 3145736 | tf_op jit(solution)/shard_map/ppermute | solution.py:394
  112.5 51.1 %copy-start.3 = (bf16[256,512]{1,0:T(8,128)(2,1)S(1)}, bf16[256,512]{1,0:T(8,128)(2,1)}, u32[]{:S(2)}) copy-start(bf16[256,512]{1,0:T(8,128)(2,1)} %get-tuple-element.19.c0) | copy-start | bytes 786436
  112.5 48.1 %all-to-all-start.4 = ((bf16[32,8,2048]{2,1,0:T(8,128)(2,1)}), bf16[32,8,2048]{2,1,0:T(8,128)(2,1)S(1)}, u32[]{:S(2)}, u32[]{:S(2)}) async-start(bf16[32,8,2048]{2,1,0:T(8,128)(2,1)} %bitcast.34), calls=%async_computation.4 | async-start | bytes 2097152 | tf_op jit(solution)/shard_map/all_to_all | solution.py:402
  116.6 31.0 %collective-permute-start.6 = (bf16[256,512]{1,0:T(8,128)(2,1)}, bf16[256,512]{1,0:T(8,128)(2,1)S(1)}, u32[]{:S(2)}, u32[]{:S(2)}) collective-permute-start(bf16[256,512]{1,0:T(8,128)(2,1)} %get-tuple-element.20), channel_id=1, source_target_pairs={{0,6},{2,0},{4,2},{6,4},{1,7},{3,1},{5,3},{7,5},{8,14},{10,8},{12,... | collective-permute-start | bytes 786440 | tf_op jit(solution)/shard_map/ppermute | solution.py:394
  117.2 37.0 %collective-permute-start.7 = (bf16[256,512]{1,0:T(8,128)(2,1)}, bf16[256,512]{1,0:T(8,128)(2,1)S(1)}, u32[]{:S(2)}, u32[]{:S(2)}) collective-permute-start(bf16[256,512]{1,0:T(8,128)(2,1)} %get-tuple-element.21), channel_id=1, source_target_pairs={{0,4},{2,6},{4,0},{6,2},{1,5},{3,7},{5,1},{7,3},{8,12},{10,14},{12... | collective-permute-start | bytes 786440 | tf_op jit(solution)/shard_map/ppermute | solution.py:394
  147.6 0.7 copy-start.4
  148.3 9.1 %collective-permute-start.8 = (bf16[256,512]{1,0:T(8,128)(2,1)}, bf16[256,512]{1,0:T(8,128)(2,1)S(1)}, u32[]{:S(2)}, u32[]{:S(2)}) collective-permute-start(bf16[256,512]{1,0:T(8,128)(2,1)} %get-tuple-element.22), channel_id=1, source_target_pairs={{0,2},{2,4},{4,6},{6,0},{1,3},{3,5},{5,7},{7,1},{8,10},{10,12},{12... | collective-permute-start | bytes 786440 | tf_op jit(solution)/shard_map/ppermute | solution.py:394
  153.5 0.7 copy-start.12
  154.2 0.7 copy-start.6
  154.9 22.3 %collective-permute-start.13 = (bf16[64,2048]{1,0:T(8,128)(2,1)}, bf16[64,2048]{1,0:T(8,128)(2,1)S(1)}, u32[]{:S(2)}, u32[]{:S(2)}) collective-permute-start(bf16[64,2048]{1,0:T(8,128)(2,1)} %get-tuple-element.25), channel_id=1, source_target_pairs={{0,6},{2,0},{4,2},{6,4},{1,7},{3,1},{5,3},{7,5},{8,14},{10,8},{12,... | collective-permute-start | bytes 786440 | tf_op jit(solution)/shard_map/ppermute | solution.py:394
  157.4 0.7 copy-start.8
  158.1 19.6 %collective-permute-start.14 = (bf16[64,2048]{1,0:T(8,128)(2,1)}, bf16[64,2048]{1,0:T(8,128)(2,1)S(1)}, u32[]{:S(2)}, u32[]{:S(2)}) collective-permute-start(bf16[64,2048]{1,0:T(8,128)(2,1)} %get-tuple-element.26), channel_id=1, source_target_pairs={{0,4},{2,6},{4,0},{6,2},{1,5},{3,7},{5,1},{7,3},{8,12},{10,14},{12... | collective-permute-start | bytes 786440 | tf_op jit(solution)/shard_map/ppermute | solution.py:394
  159.5 19.3 %collective-permute-start.15 = (bf16[64,2048]{1,0:T(8,128)(2,1)}, bf16[64,2048]{1,0:T(8,128)(2,1)S(1)}, u32[]{:S(2)}, u32[]{:S(2)}) collective-permute-start(bf16[64,2048]{1,0:T(8,128)(2,1)} %get-tuple-element.27), channel_id=1, source_target_pairs={{0,2},{2,4},{4,6},{6,0},{1,3},{3,5},{5,7},{7,1},{8,10},{10,12},{12... | collective-permute-start | bytes 786440 | tf_op jit(solution)/shard_map/ppermute | solution.py:394
  161.8 17.9 %collective-permute-start.16 = (bf16[64,2048]{1,0:T(8,128)(2,1)S(1)}, bf16[64,2048]{1,0:T(8,128)(2,1)S(1)}, u32[]{:S(2)}, u32[]{:S(2)}) collective-permute-start(bf16[64,2048]{1,0:T(8,128)(2,1)S(1)} %get-tuple-element.30), channel_id=1, source_target_pairs={{0,6},{2,0},{4,2},{6,4},{1,7},{3,1},{5,3},{7,5},{8,14},{10,8},{12,... | collective-permute-start | bytes 786440 | tf_op jit(solution)/shard_map/ppermute | solution.py:394
  163.5 1.0 copy-start.5
  164.5 0.9 copy-start.7
  165.5 0.9 copy-start.9
  170.5 8.3 %copy-start.13 = (bf16[64,2048]{1,0:T(8,128)(2,1)S(1)}, bf16[64,2048]{1,0:T(8,128)(2,1)}, u32[]{:S(2)}) copy-start(bf16[64,2048]{1,0:T(8,128)(2,1)} %copy-done.12) | copy-start | bytes 786436
  170.5 23.1 %collective-permute-start.12 = (bf16[256,2048]{1,0:T(8,128)(2,1)S(1)}, bf16[256,2048]{1,0:T(8,128)(2,1)S(1)}, u32[]{:S(2)}, u32[]{:S(2)}) collective-permute-start(bf16[256,2048]{1,0:T(8,128)(2,1)S(1)} %give.1), channel_id=1, source_target_pairs={{0,1},{1,0},{2,3},{3,2},{4,5},{5,4},{6,7},{7,6},{8,9},{9,8},{10,11... | collective-permute-start | bytes 3145736 | tf_op jit(solution)/shard_map/ppermute | solution.py:441
  177.2 9.4 %collective-permute-start.17 = (bf16[64,2048]{1,0:T(8,128)(2,1)S(1)}, bf16[64,2048]{1,0:T(8,128)(2,1)S(1)}, u32[]{:S(2)}, u32[]{:S(2)}) collective-permute-start(bf16[64,2048]{1,0:T(8,128)(2,1)S(1)} %get-tuple-element.31), channel_id=1, source_target_pairs={{0,4},{2,6},{4,0},{6,2},{1,5},{3,7},{5,1},{7,3},{8,12},{10,14},{12... | collective-permute-start | bytes 786440 | tf_op jit(solution)/shard_map/ppermute | solution.py:394
  177.7 15.0 %collective-permute-start.18 = (bf16[64,2048]{1,0:T(8,128)(2,1)S(1)}, bf16[64,2048]{1,0:T(8,128)(2,1)S(1)}, u32[]{:S(2)}, u32[]{:S(2)}) collective-permute-start(bf16[64,2048]{1,0:T(8,128)(2,1)S(1)} %get-tuple-element.32), channel_id=1, source_target_pairs={{0,2},{2,4},{4,6},{6,0},{1,3},{3,5},{5,7},{7,1},{8,10},{10,12},{12... | collective-permute-start | bytes 786440 | tf_op jit(solution)/shard_map/ppermute | solution.py:394

commit v3 on v2

v3 whole, which is shorter than its diff:
```python
import functools
import jax
import jax.numpy as jnp
from jax import lax
from jax.experimental import pallas as pl
from jax.experimental.pallas import tpu as pltpu
from jax.sharding import Mesh, PartitionSpec as P

SQRT_HALF = 0.7071067811865476
INV_ROOT_TAU = 0.3989422804014327
N_Y = 4
N_CORE = 2
F32 = jnp.float32
BF16 = jnp.bfloat16
NT = (((1,), (1,)), ((), ()))
NN = (((1,), (0,)), ((), ()))
TN = (((0,), (0,)), ((), ()))
ANY = pl.BlockSpec(memory_space=pl.ANY)
VMEM = pl.BlockSpec(memory_space=pltpu.VMEM)
DMA = pltpu.SemaphoreType.DMA


def dot(a, b, dims):
    return lax.dot_general(a, b, dims, preferred_element_type=F32)


def iota(shape, axis):
    return lax.broadcasted_iota(jnp.int32, shape, axis)


def cost(flops, bytes_accessed, transcendentals=0):
    return pl.CostEstimate(flops=flops, bytes_accessed=bytes_accessed, transcendentals=transcendentals)


def copy(src, dst, sem):
    return pltpu.make_async_copy(src, dst, sem)


def params(mib):
    return pltpu.CompilerParams(vmem_limit_bytes=mib << 20)


def load_rows(src, dst, sems, pieces):
    rows = src.shape[0] // pieces
    return [
        copy(src.at[pl.ds(i * rows, rows), :], dst.at[pl.ds(i * rows, rows), :], sems.at[i])
        for i in range(pieces)
    ]


def ids_kernel(req_ref, out_ref):
    capacity, owners = req_ref.shape
    row = iota((owners, owners), 0)
    lane = iota((owners, owners), 1)
    total = jnp.zeros(out_ref.shape, jnp.int32)
    at = iota(out_ref.shape, 1)
    for r in range(capacity):
        picked = jnp.where(lane == row, req_ref[r : r + 1, :], 0)
        column = jnp.sum(picked, axis=1, keepdims=True)
        total = jnp.where(at == r, column, total)
    out_ref[...] = total


def turn_ids(wanted):
    owners, _ = wanted.shape
    return pl.pallas_call(
        ids_kernel,
        out_shape=jax.ShapeDtypeStruct((owners, 128), jnp.int32),
        in_specs=[VMEM],
        out_specs=VMEM,
        cost_estimate=cost(10**5, 10**5),
        name="ids",
    )(jnp.transpose(wanted))


def asked_hits(asked, capacity, rows):
    devices = asked.shape[0]
    slots = devices * capacity
    at = iota((devices, rows), 1)
    place = iota((slots, devices), 0)
    device = iota((slots, devices), 1)
    total = jnp.zeros((slots, rows), F32)
    for r in range(capacity):
        hit = (asked[:, r : r + 1] == at).astype(F32).astype(BF16)
        spread = (place == device * capacity + r).astype(F32).astype(BF16)
        total = total + dot(spread, hit, NN)
    return total.astype(BF16)


def gather_kernel(capacity, asked_ref, down_ref, up_ref, out_hbm, out, out_sems):
    hits = asked_hits(asked_ref[...], capacity, down_ref.shape[0])
    block = 1024
    per_table = down_ref.shape[1] // block
    sent = []
    for j in range(2 * per_table):
        table = (down_ref, up_ref)[j // per_table]
        cols = pl.ds(j * block, block)
        out[:, cols] = dot(hits, table[:, pl.ds(j % per_table * block, block)], NN).astype(BF16)
        c = copy(out.at[:, cols], out_hbm.at[:, cols], out_sems.at[j])
        c.start()
        sent.append(c)
    for c in sent:
        c.wait()


def gather_rows(asked, capacity, down_rows, up_rows):
    slots = asked.shape[0] * capacity
    width = down_rows.shape[1]
    return pl.pallas_call(
        functools.partial(gather_kernel, capacity),
        out_shape=jax.ShapeDtypeStruct((slots, 2 * width), BF16),
        in_specs=[VMEM] * 3,
        out_specs=ANY,
        scratch_shapes=[pltpu.VMEM((slots, 2 * width), BF16), DMA((4,))],
        compiler_params=params(8),
        cost_estimate=cost(2 * 256 * 256 * 2048, 3 * 10**6),
        name="gather",
    )(asked, down_rows, up_rows)


def weight_kernel(places_ref, gates_ref, out_ref):
    topk, block = places_ref.shape
    slots = out_ref.shape[1]
    slot = places_ref[...]
    gates = gates_ref[...]
    for s in range(0, slots, 32):
        row = iota((32, block), 0) + s
        total = jnp.zeros((32, block), F32)
        for k in range(topk):
            total = jnp.where(row == slot[k : k + 1, :], gates[k : k + 1, :], total)
        out_ref[0, s : s + 32, :] = total


def build_weight(places, gates, slots):
    topk, tokens = places.shape
    block = tokens // N_Y
    return pl.pallas_call(
        weight_kernel,
        grid=(N_Y,),
        out_shape=jax.ShapeDtypeStruct((N_Y, slots, block), F32),
        in_specs=[pl.BlockSpec((topk, block), lambda i: (0, i))] * 2,
        out_specs=pl.BlockSpec((1, slots, block), lambda i: (i, 0, 0)),
        compiler_params=params(8),
        cost_estimate=cost(3 * topk * slots * tokens, 4 * slots * tokens),
        name="weight",
    )(places, gates)


def local_kernel(
    tok_hbm, grad_hbm, down_hbm, up_hbm, weight_hbm, places_ref, c0, c1, c2, c3, part_hbm,
    tok, grad, down, up, weight, gated, coef, small, part,
    tok_sems, grad_sems, row_sems, weight_sems, small_sems, part_sems,
):
    block = weight.shape[2]
    topk = places_ref.shape[0]
    slots, width = down.shape
    y = lax.axis_index("y")
    down_in = copy(down_hbm, down, row_sems.at[0])
    up_in = copy(up_hbm, up, row_sems.at[1])
    weight_in = [copy(weight_hbm.at[c], weight.at[c], weight_sems.at[c]) for c in range(N_Y)]
    tok_in = load_rows(tok_hbm, tok, tok_sems, 8)
    grad_in = load_rows(grad_hbm, grad, grad_sems, 8)
    down_in.start()
    for c in range(N_Y):
        tok_in[2 * c].start()
        tok_in[2 * c + 1].start()
        if c == 0:
            up_in.start()
        grad_in[2 * c].start()
        grad_in[2 * c + 1].start()
        weight_in[c].start()
    down_in.wait()
    for c in range(N_Y):
        here = pl.ds(c * block, block)
        tok_in[2 * c].wait()
        tok_in[2 * c + 1].wait()
        pre = dot(down[...], tok[here, :], NT)
        if c == 0:
            up_in.wait()
        grad_in[2 * c].wait()
        grad_in[2 * c + 1].wait()
        back = dot(up[...], grad[here, :], NT)
        weight_in[c].wait()
        gate = weight[c]
        cdf = 0.5 * (1.0 + lax.erf(pre * SQRT_HALF))
        density = INV_ROOT_TAU * jnp.exp(-0.5 * pre * pre)
        gated[:, here] = (gate * (pre * cdf)).astype(BF16)
        product = gate * (cdf + pre * density) * back
        coef[:, here] = product.astype(BF16)
        slot = places_ref[:, here]
        lines = []
        for k in range(topk):
            hit = iota((slots, block), 0) == slot[k : k + 1, :]
            lines.append(jnp.sum(jnp.where(hit, product, 0.0), axis=0, keepdims=True))
        small[c] = jnp.concatenate(lines, axis=0).astype(BF16)
    sent = []
    for r, out in enumerate((c0, c1, c2, c3)):
        c = copy(small.at[(y + r) % N_Y], out, small_sems.at[r])
        c.start()
        sent.append(c)
    step = width // N_Y
    for j in range(2 * N_Y):
        left, right = ((coef, tok), (gated, grad))[j // N_Y]
        cols = pl.ds(j * step, step)
        part[:, cols] = dot(left[...], right[:, pl.ds(j % N_Y * step, step)], NN).astype(BF16)
        c = copy(part.at[:, cols], part_hbm.at[:, cols], part_sems.at[j])
        c.start()
        sent.append(c)
    for s in sent:
        s.wait()


def local_terms(tokens, grads, down, up, weight, places):
    count, width = tokens.shape
    slots = down.shape[0]
    topk = places.shape[0]
    block = count // N_Y
    return pl.pallas_call(
        local_kernel,
        out_shape=tuple(jax.ShapeDtypeStruct((topk, block), BF16) for _ in range(N_Y))
        + (jax.ShapeDtypeStruct((slots, 2 * width), BF16),),
        in_specs=[ANY] * 5 + [VMEM],
        out_specs=(ANY,) * 5,
        scratch_shapes=[
            pltpu.VMEM((count, width), BF16),
            pltpu.VMEM((count, width), BF16),
            pltpu.VMEM((slots, width), BF16),
            pltpu.VMEM((slots, width), BF16),
            pltpu.VMEM(weight.shape, F32),
            pltpu.VMEM((slots, count), BF16),
            pltpu.VMEM((slots, count), BF16),
            pltpu.VMEM((N_Y, topk, block), BF16),
            pltpu.VMEM((slots, 2 * width), BF16),
            DMA((8,)), DMA((8,)), DMA((2,)), DMA((4,)), DMA((4,)), DMA((8,)),
        ],
        compiler_params=params(56),
        cost_estimate=cost(8 * count * width * slots, 24 << 20),
        name="local",
    )(tokens, grads, down, up, weight, places)


def sums_kernel(capacity, asked_ref, got_hbm, down_hbm, up_hbm, got, sums, sems, out_sems):
    rows, width = down_hbm.shape
    block = 1024
    pieces = 2 * width // block
    copies = [
        copy(got_hbm.at[:, pl.ds(j * block, block)], got.at[:, pl.ds(j * block, block)], sems.at[j])
        for j in range(pieces)
    ]
    for c in copies:
        c.start()
    hits = asked_hits(asked_ref[...], capacity, rows)
    sent = []
    for j in range(pieces):
        copies[j].wait()
        cols = pl.ds(j * block, block)
        sums[:, cols] = dot(hits, got[:, cols], TN)
        out = (down_hbm, up_hbm)[2 * j // pieces]
        c = copy(sums.at[:, cols], out.at[:, pl.ds(j * block % width, block)], out_sems.at[j])
        c.start()
        sent.append(c)
    for c in sent:
        c.wait()


def sum_rows(asked, capacity, got, rows):
    slots, both = got.shape
    out = jax.ShapeDtypeStruct((rows, both // 2), F32)
    return pl.pallas_call(
        functools.partial(sums_kernel, capacity),
        out_shape=(out, out),
        in_specs=[VMEM, ANY],
        out_specs=(ANY, ANY),
        scratch_shapes=[
            pltpu.VMEM((slots, both), BF16),
            pltpu.VMEM((rows, both), F32),
            DMA((4,)),
            DMA((4,)),
        ],
        compiler_params=params(8),
        cost_estimate=cost(2 * 256 * 256 * 2048, 4 * 10**6),
        name="sums",
    )(asked, got)


def final_kernel(
    mine, c0, c1, c2, c3, p0, p1, p2, p3, d0, d1, d2a, d2b, d3, out_hbm, coef, rows, out, d_sems, out_sems
):
    core = lax.axis_index("core")
    which = core if mine else 1 - core
    half = out.shape[0]
    slots = coef.shape[0] // N_Y
    topk = c0.shape[0]
    loads = []
    start = 0
    for i, d in enumerate((d0, d1, d2a, d2b, d3)):
        loads.append(copy(d, rows.at[pl.ds(start, d.shape[0]), :], d_sems.at[i]))
        start += d.shape[0]
    for c in loads:
        c.start()
    cols = pl.ds(pl.multiple_of(which * half, half), half)
    for r, (small, places) in enumerate(((c0, p0), (c1, p1), (c2, p2), (c3, p3))):
        values = small[:, cols].astype(F32)
        slot = places[:, cols]
        for s in range(0, slots, 64):
            row = iota((64, half), 0) + s
            total = jnp.zeros((64, half), F32)
            for k in range(topk):
                total = jnp.where(row == slot[k : k + 1, :], values[k : k + 1, :], total)
            coef[r * slots + s : r * slots + s + 64, :] = total.astype(BF16)
    for c in loads:
        c.wait()
    width = out.shape[1]
    block = width // 4
    sent = []
    for j in range(4):
        cols = pl.ds(j * block, block)
        out[:, cols] = dot(coef[...], rows[:, cols], TN).astype(BF16)
        c = copy(out.at[:, cols], out_hbm.at[:, cols], out_sems.at[j])
        c.start()
        sent.append(c)
    for c in sent:
        c.wait()


def final_product(mine, coef, places, rows):
    slots, width = rows[0].shape
    half = coef[0].shape[1] // N_CORE
    return pl.pallas_call(
        functools.partial(final_kernel, mine),
        out_shape=jax.ShapeDtypeStruct((half, width), BF16),
        in_specs=[VMEM] * 8 + [ANY] * 5,
        out_specs=ANY,
        scratch_shapes=[
            pltpu.VMEM((N_Y * slots, half), BF16),
            pltpu.VMEM((N_Y * slots, width), BF16),
            pltpu.VMEM((half, width), BF16),
            DMA((5,)), DMA((4,)),
        ],
        compiler_params=params(16),
        cost_estimate=cost(2 * half * 1024 * 2048, 6 << 20),
        name="keep" if mine else "give",
    )(*coef, *places, *rows)


def turn(x, r):
    return lax.ppermute(x, "y", [(i, (i - r) % N_Y) for i in range(N_Y)])


def gathered(blocks):
    return (blocks[0],) + tuple(turn(blocks[N_Y - r], r) for r in range(1, N_Y))


def exchange(x):
    return lax.all_to_all(x, ("dp", "y", "core"), split_axis=0, concat_axis=0, tiled=True)


def program(tokens, out_grad, down_rows, up_rows, requests, places, gate_weights):
    row_count, width = down_rows.shape
    _, devices, capacity = requests.shape
    slots = devices * capacity
    y = lax.axis_index("y")

    asked = exchange(turn_ids(requests[0]))
    slot_of = jnp.transpose(places[0])
    weight = build_weight(slot_of, jnp.transpose(gate_weights[0]), slots)
    block = slot_of.shape[1] // N_Y
    blocks = [
        lax.dynamic_slice_in_dim(slot_of, ((y + r) & (N_Y - 1)) * block, block, 1) for r in range(N_Y)
    ]
    chip_places = gathered(blocks)
    outgoing = gather_rows(asked, capacity, down_rows, up_rows)
    arrived = exchange(outgoing.reshape(devices, capacity, 2 * width))
    down = arrived[:, :, :width].reshape(slots, width)
    up = arrived[:, :, width:].reshape(slots, width)
    above, below = turn(down, 1), turn(down, 3)
    *coef, part = local_terms(tokens, out_grad, down, up, weight, slot_of)
    chip_coef = gathered(coef)
    got = exchange(part.reshape(devices, capacity, 2 * width)).reshape(slots, 2 * width)
    far = (turn(above[: slots // 2], 1), turn(below[slots // 2 :], 3))
    down_all = (down, above, *far, below)
    give = final_product(False, chip_coef, chip_places, down_all)
    other = lax.ppermute(give, "core", [(0, 1), (1, 0)])
    keep = final_product(True, chip_coef, chip_places, down_all)
    input_grad = (keep.astype(F32) + other.astype(F32)).astype(BF16)
    down_grad, up_grad = sum_rows(asked, capacity, got, row_count)
    return (input_grad, down_grad, up_grad)


def solution(mesh):
    axes = ("dp", "y", "core")
    fine = Mesh(mesh.devices.reshape(mesh.devices.shape[0], N_Y, N_CORE), axes)
    in_specs = (
        P("dp", None),
        P("dp", None),
        P(axes, None),
        P(axes, None),
        P(axes, None, None),
        P(("y", "core"), "dp", None),
        P(("y", "core"), "dp", None),
    )
    out_specs = (P(axes, None), P(axes, None), P(axes, None))
    return jax.shard_map(program, mesh=fine, in_specs=in_specs, out_specs=out_specs, check_vma=False)
```

time: 196 us -> 169 us (0.86)
  starting transfers between devices: 50.5 us -> 24.4 us
  local copies, waits for them, and re-layouts: 8.98 us -> 22 us
  waiting for transfers between devices: 69.9 us -> 57.8 us
  Pallas kernels: 44.5 us -> 39.7 us
  blocking collectives: 17 us -> 21.1 us
    ppermute x18 -> x10, waiting for transfers between devices: 57 us -> 32.1 us  [turn(): return lax.ppermute(x, 'y', [(i, (i - r) % N_Y) for i in range(N_Y)])]
    ppermute x18 -> x10, starting transfers between devices: 24.2 us -> 9.86 us  [turn(): return lax.ppermute(x, 'y', [(i, (i - r) % N_Y) for i in range(N_Y)])]
    all_to_all x4 -> x2, waiting for transfers between devices: 12.9 us -> 25.7 us  [exchange(): lax.all_to_all(x, ('dp', 'y', 'core'), split_axis=0, concat_axis=0, tiled...]
    reshape x0 -> x5, local copies, waits for them, and re-layouts: none -> 12.2 us  [the longest x1 4.4 us: program(): part.reshape(devices, capacity, 2 * width)]
    all_to_all x4 -> x2, starting transfers between devices: 23.5 us -> 11.8 us  [exchange(): lax.all_to_all(x, ('dp', 'y', 'core'), split_axis=0, concat_axis=0, tiled...]
    slice x0 -> x3, local copies, waits for them, and re-layouts: none -> 4.34 us  [the longest x1 2.68 us: program(): up = arrived[:, :, width:].reshape(slots, width)]
    all_to_all x1, blocking collectives: 17 us -> 21.1 us  [exchange(): lax.all_to_all(x, ('dp', 'y', 'core'), split_axis=0, concat_axis=0, tiled...]
    pallas_call x7 -> x4, Pallas kernels: 33.5 us -> 29.6 us  [the longest x1 24.5 us: local_terms(): pl.pallas_call(local_kernel, out_shape=tuple((jax.ShapeDtypeStruct((topk,...]
  transfers between devices with their start and end apart: 23 -> 13, of which waited for: 8 -> 5; matrix products, arithmetic and copies ran while one was open for 1% -> 6% of each run, Pallas kernels for 16% -> 22%
where the time goes in v3:
time: 169 us; the launch traced here: 168 us
  waiting for transfers between devices  57.8 us (34%)
  Pallas kernels  39.7 us (23%)
  starting transfers between devices  24.4 us (14%)
  local copies, waits for them, and re-layouts  22 us (13%)
  blocking collectives  21.1 us (12%)
  other arithmetic  2.59 us (2%)
    ppermute x10, waiting for transfers between devices, turn(): return lax.ppermute(x, 'y', [(i, (i - r) % N_Y) for i in range(N_Y)])  32.1 us
    all_to_all x2, waiting for transfers between devices, exchange(): lax.all_to_all(x, ('dp', 'y', 'core'), split_axis=0, concat_axis=0, tiled...  25.7 us
    pallas_call x1, Pallas kernels, local_terms(): pl.pallas_call(local_kernel, out_shape=tuple((jax.ShapeDtypeStruct((topk,...  24.5 us
    all_to_all x1, blocking collectives, exchange(): lax.all_to_all(x, ('dp', 'y', 'core'), split_axis=0, concat_axis=0, tiled...  21.1 us
    all_to_all x2, starting transfers between devices, exchange(): lax.all_to_all(x, ('dp', 'y', 'core'), split_axis=0, concat_axis=0, tiled...  11.8 us
    ppermute x10, starting transfers between devices, turn(): return lax.ppermute(x, 'y', [(i, (i - r) % N_Y) for i in range(N_Y)])  9.86 us
    pallas_call x2, Pallas kernels, final_product(): pl.pallas_call(functools.partial(final_kernel, mine), out_shape=jax.Shape...  7.34 us
    unnamed x28, local copies, waits for them, and re-layouts  5.38 us
  transfers between devices with their start and end apart: 13, of which 5 were waited for; matrix products, arithmetic and copies ran while one was open for 6% of the time, Pallas kernels for 22%

profile of v3, /device:TPU:1, one launch (start us, length us, event | category | flops | bytes accessed | tf_op | source)
XLA Modules:
  0.0 168.3 jit_solution(18416122845922983470)
XLA Ops:
  0.6 1.5 ids.1
  2.1 21.1 %all_to_all.21 = s32[128,1,128]{2,1,0:T(1,128)S(1)} all-to-all(s32[128,1,128]{2,1,0:T(1,128)} %bitcast.34), channel_id=1, replica_groups=mesh['dp'=16,'y'=4,'core'=2] {'dp','y','core'}, dimensions={0} | all-to-all | bytes 131072 | tf_op jit(solution)/shard_map/all_to_all | solution.py:355
  23.1 0.9 copy-done.7
  24.1 0.9 copy-done.8
  25.0 1.5 gather.1
  26.6 2.6 %reshape.35 = bf16[128,2,4096]{2,1,0:T(2,128)(2,1)} reshape(bf16[256,4096]{1,0:T(8,128)(2,1)S(1)} %gather.1) | data formatting | bytes 4194304 | tf_op jit(solution)/shard_map/reshape | solution.py:373
  29.2 5.4 %all-to-all-start.1 = ((bf16[128,2,4096]{2,1,0:T(2,128)(2,1)}), bf16[128,2,4096]{2,1,0:T(2,128)(2,1)}, u32[]{:S(2)}, u32[]{:S(2)}) async-start(bf16[128,2,4096]{2,1,0:T(2,128)(2,1)} %reshape.35), calls=%async_computation.1 | async-start | bytes 4194304 | tf_op jit(solution)/shard_map/all_to_all | solution.py:355
  34.7 2.8 %weight.1.weight_hbm = f32[4,256,512]{2,1,0:T(8,128)S(1)} custom-call(s32[16,2048]{1,0:T(8,128)S(1)} %bitcast.32, f32[16,2048]{1,0:T(8,128)S(1)} %bitcast.33), custom_call_target="tpu_custom_call" | custom-call | flops 25165824 | bytes 2097152 | tf_op jit(solution)/shard_map/weight/pallas_call | solution.py:137
  37.5 1.4 copy-done
  38.9 25.7 %all-to-all-done.1 = bf16[128,2,4096]{2,1,0:T(2,128)(2,1)} async-done(((bf16[128,2,4096]{2,1,0:T(2,128)(2,1)}), bf16[128,2,4096]{2,1,0:T(2,128)(2,1)}, u32[]{:S(2)}, u32[]{:S(2)}) %all-to-all-start.1) | async-done | bytes 2097184 | tf_op jit(solution)/shard_map/all_to_all | solution.py:355
  64.5 2.7 %fusion = (bf16[128,2,2048]{2,1,0:T(2,128)(2,1)S(1)}, bf16[128,2,2048]{2,1,0:T(2,128)(2,1)S(1)}) fusion(bf16[128,2,4096]{2,1,0:T(2,128)(2,1)} %all-to-all-done.1), kind=kLoop, calls=%fused_computation.5 | loop fusion | bytes 4194304 | tf_op jit(solution)/shard_map/slice | solution.py:375
  67.2 1.2 reshape.36.down_hbm.d0
  68.5 0.0 collective-permute-start.6
  68.5 1.5 collective-permute-start.8
  69.9 1.2 reshape.37.up_hbm
  71.1 24.5 %local.1 = (bf16[16,512]{1,0:T(8,128)(2,1)}, bf16[16,512]{1,0:T(8,128)(2,1)}, bf16[16,512]{1,0:T(8,128)(2,1)}, bf16[16,512]{1,0:T(8,128)(2,1)}, bf16[256,4096]{1,0:T(8,128)(2,1)}) custom-call(bf16[2048,2048]{1,0:T(8,128)(2,1)} %tok_hbm.1, bf16[2048,2048]{1,0:T(8,128)(2,1)} %grad_hbm.1, bf16[256,2048]{1,0:T(8,128)(2,1)} %reshape.36.down_hbm.d0, ...), custom_call_target="tpu_custom_call" | custom-call | flops 8589934592 | bytes 25165824 | tf_op jit(solution)/shard_map/local/pallas_call | solution.py:218
  95.6 4.4 %reshape.42 = bf16[128,2,4096]{2,1,0:T(2,128)(2,1)} reshape(bf16[256,4096]{1,0:T(8,128)(2,1)} %get-tuple-element.14) | data formatting | bytes 4194304 | tf_op jit(solution)/shard_map/reshape | solution.py:379
  100.0 6.4 %all-to-all-start.2 = ((bf16[128,2,4096]{2,1,0:T(2,128)(2,1)}), bf16[128,2,4096]{2,1,0:T(2,128)(2,1)}, u32[]{:S(2)}, u32[]{:S(2)}) async-start(bf16[128,2,4096]{2,1,0:T(2,128)(2,1)} %reshape.42), calls=%async_computation.2 | async-start | bytes 4194304 | tf_op jit(solution)/shard_map/all_to_all | solution.py:355
  106.4 0.0 copy-start.6
  106.5 0.0 collective-permute-done.6.d1
  106.5 0.8 slice.18
  107.3 2.8 %collective-permute-start.7 = (bf16[128,2048]{1,0:T(8,128)(2,1)}, bf16[128,2048]{1,0:T(8,128)(2,1)S(1)}, u32[]{:S(2)}, u32[]{:S(2)}) collective-permute-start(bf16[128,2048]{1,0:T(8,128)(2,1)} %slice.18), channel_id=1, source_target_pairs={{0,6},{2,0},{4,2},{6,4},{1,7},{3,1},{5,3},{7,5},{8,14},{10,8},{12,... | collective-permute-start | bytes 1572872 | tf_op jit(solution)/shard_map/ppermute | solution.py:347
  110.1 0.0 collective-permute-done.8.d3
  110.1 0.8 slice.19
  110.9 0.0 collective-permute-start.9
  110.9 2.7 %collective-permute-start.3 = (s32[16,512]{1,0:T(8,128)S(1)}, s32[16,512]{1,0:T(8,128)S(1)}, u32[]{:S(2)}, u32[]{:S(2)}) collective-permute-start(s32[16,512]{1,0:T(8,128)S(1)} %get-tuple-element.20), channel_id=1, source_target_pairs={{0,6},{2,0},{4,2},{6,4},{1,7},{3,1},{5,3},{7,5},{8,14},{10,8},{12,... | collective-permute-start | bytes 98312 | tf_op jit(solution)/shard_map/ppermute | solution.py:347
  113.7 0.0 collective-permute-start.4
  113.7 0.7 collective-permute-start.5
  114.3 27.5 %collective-permute-done.3.p1 = s32[16,512]{1,0:T(8,128)S(1)} collective-permute-done((s32[16,512]{1,0:T(8,128)S(1)}, s32[16,512]{1,0:T(8,128)S(1)}, u32[]{:S(2)}, u32[]{:S(2)}) %collective-permute-start.3) | collective-permute-done | bytes 32800 | tf_op jit(solution)/shard_map/ppermute | solution.py:347
  141.8 0.8 collective-permute-start
  142.6 1.2 collective-permute-done.4.p2
  143.8 1.0 collective-permute-start.1
  144.9 0.0 collective-permute-done.5.p3
  144.9 0.3 collective-permute-start.2
  145.2 0.0 collective-permute-done.c1
  145.2 2.7 %collective-permute-done.1.c2 = bf16[16,512]{1,0:T(8,128)(2,1)S(1)} collective-permute-done((bf16[16,512]{1,0:T(8,128)(2,1)S(1)}, bf16[16,512]{1,0:T(8,128)(2,1)S(1)}, u32[]{:S(2)}, u32[]{:S(2)}) %collective-permute-start.1) | collective-permute-done | bytes 16416 | tf_op jit(solution)/shard_map/ppermute | solution.py:347
  147.9 0.8 collective-permute-done.2.c3
  148.7 0.0 collective-permute-done.7.d2a
  148.7 0.0 copy-start.3
  148.7 3.7 %give.1 = bf16[256,2048]{1,0:T(8,128)(2,1)} custom-call(bf16[16,512]{1,0:T(8,128)(2,1)S(1)} %copy-done.10, bf16[16,512]{1,0:T(8,128)(2,1)S(1)} %collective-permute-done.c1, bf16[16,512]{1,0:T(8,128)(2,1)S(1)} %collective-permute-done.1.c2, bf16[16,512]{1,0:T(8,128)(2,1)S(1)} %collective-permute-done.2.c3, s32[16,512]{1,0:T(8,128)S(1)} %get-tuple-element.21.p0, ...), custom_call_target="tpu_custom_call" | custom-call | flops 1073741824 | bytes 6291456 | tf_op jit(solution)/shard_map/give/pallas_call | solution.py:329
  152.4 2.7 %collective-permute-start.10 = (bf16[256,2048]{1,0:T(8,128)(2,1)}, bf16[256,2048]{1,0:T(8,128)(2,1)}, u32[]{:S(2)}, u32[]{:S(2)}) collective-permute-start(bf16[256,2048]{1,0:T(8,128)(2,1)} %give.1), channel_id=1, source_target_pairs={{0,1},{1,0},{2,3},{3,2},{4,5},{5,4},{6,7},{7,6},{8,9},{9,8},{10,11... | collective-permute-start | bytes 3145736 | tf_op jit(solution)/shard_map/ppermute | solution.py:383
  155.2 1.0 copy-done.2
  156.2 1.0 copy-done.4
  157.2 3.7 %keep.1 = bf16[256,2048]{1,0:T(8,128)(2,1)S(1)} custom-call(bf16[16,512]{1,0:T(8,128)(2,1)S(1)} %copy-done.10, bf16[16,512]{1,0:T(8,128)(2,1)S(1)} %collective-permute-done.c1, bf16[16,512]{1,0:T(8,128)(2,1)S(1)} %collective-permute-done.1.c2, bf16[16,512]{1,0:T(8,128)(2,1)S(1)} %collective-permute-done.2.c3, s32[16,512]{1,0:T(8,128)S(1)} %get-tuple-element.21.p0, ...), custom_call_target="tpu_custom_call" | custom-call | flops 1073741824 | bytes 6291456 | tf_op jit(solution)/shard_map/keep/pallas_call | solution.py:329
  160.9 0.0 all-to-all-done.2
  160.9 2.7 %reshape.43.got_hbm = bf16[256,4096]{1,0:T(8,128)(2,1)S(1)} reshape(bf16[128,2,4096]{2,1,0:T(2,128)(2,1)} %all-to-all-done.2) | data formatting | bytes 4194304 | tf_op jit(solution)/shard_map/reshape | solution.py:379
  163.7 2.1 %sums.1 = (f32[64,2048]{1,0:T(8,128)}, f32[64,2048]{1,0:T(8,128)}) custom-call(s32[128,128]{1,0:T(8,128)S(1)} %bitcast.30, bf16[256,4096]{1,0:T(8,128)(2,1)S(1)} %reshape.43.got_hbm), custom_call_target="tpu_custom_call" | custom-call | flops 268435456 | bytes 4000000 | tf_op jit(solution)/shard_map/sums/pallas_call | solution.py:269
  165.8 2.6 %add_convert_fusion = bf16[256,2048]{1,0:T(8,128)(2,1)} fusion(bf16[256,2048]{1,0:T(8,128)(2,1)} %collective-permute-done.10, bf16[256,2048]{1,0:T(8,128)(2,1)S(1)} %keep.1), kind=kLoop, calls=%fused_computation | loop fusion | flops 2097152 | bytes 3145728 | tf_op jit(solution)/shard_map/convert_element_type | solution.py:385
  (24 shorter events, 0.1 us)
Async XLA Ops:
  23.1 1.0 copy-start.7
  24.1 0.9 copy-start.8
  29.2 5.4 %copy-start.5 = (s32[1,2048,16]{1,2,0:T(8,128)S(1)}, s32[1,2048,16]{1,2,0:T(8,128)}, u32[]{:S(2)}) copy-start(s32[1,2048,16]{1,2,0:T(8,128)} %param.12) | copy-start | bytes 393220
  29.2 5.4 %copy-start.9 = (f32[1,2048,16]{1,2,0:T(8,128)S(1)}, f32[1,2048,16]{1,2,0:T(8,128)}, u32[]{:S(2)}) copy-start(f32[1,2048,16]{1,2,0:T(8,128)} %param.13) | copy-start | bytes 393220
  29.2 35.3 %all-to-all-start.1 = ((bf16[128,2,4096]{2,1,0:T(2,128)(2,1)}), bf16[128,2,4096]{2,1,0:T(2,128)(2,1)}, u32[]{:S(2)}, u32[]{:S(2)}) async-start(bf16[128,2,4096]{2,1,0:T(2,128)(2,1)} %reshape.35), calls=%async_computation.1 | async-start | bytes 4194304 | tf_op jit(solution)/shard_map/all_to_all | solution.py:355
  37.5 1.4 copy-start
  68.5 38.0 %collective-permute-start.6 = (bf16[256,2048]{1,0:T(8,128)(2,1)}, bf16[256,2048]{1,0:T(8,128)(2,1)S(1)}, u32[]{:S(2)}, u32[]{:S(2)}) collective-permute-start(bf16[256,2048]{1,0:T(8,128)(2,1)} %reshape.36.down_hbm.d0), channel_id=1, source_target_pairs={{0,6},{2,0},{4,2},{6,4},{1,7},{3,1},{5,3},{7,5},{8,14},{10,8},{12,... | collective-permute-start | bytes 3145736 | tf_op jit(solution)/shard_map/ppermute | solution.py:347
  68.5 41.6 %collective-permute-start.8 = (bf16[256,2048]{1,0:T(8,128)(2,1)}, bf16[256,2048]{1,0:T(8,128)(2,1)S(1)}, u32[]{:S(2)}, u32[]{:S(2)}) collective-permute-start(bf16[256,2048]{1,0:T(8,128)(2,1)} %reshape.36.down_hbm.d0), channel_id=1, source_target_pairs={{0,2},{2,4},{4,6},{6,0},{1,3},{3,5},{5,7},{7,1},{8,10},{10,12},{12... | collective-permute-start | bytes 3145736 | tf_op jit(solution)/shard_map/ppermute | solution.py:347
  100.0 60.9 %all-to-all-start.2 = ((bf16[128,2,4096]{2,1,0:T(2,128)(2,1)}), bf16[128,2,4096]{2,1,0:T(2,128)(2,1)}, u32[]{:S(2)}, u32[]{:S(2)}) async-start(bf16[128,2,4096]{2,1,0:T(2,128)(2,1)} %reshape.42), calls=%async_computation.2 | async-start | bytes 4194304 | tf_op jit(solution)/shard_map/all_to_all | solution.py:355
  106.4 4.5 %copy-start.6 = (s32[1,2048,16]{1,2,0:T(8,128)S(1)}, s32[1,2048,16]{1,2,0:T(8,128)}, u32[]{:S(2)}) copy-start(s32[1,2048,16]{1,2,0:T(8,128)} %param.12) | copy-start | bytes 393220
  106.4 35.4 %copy-start.13 = (bf16[16,512]{1,0:T(8,128)(2,1)S(1)}, bf16[16,512]{1,0:T(8,128)(2,1)}, u32[]{:S(2)}) copy-start(bf16[16,512]{1,0:T(8,128)(2,1)} %get-tuple-element.11) | copy-start | bytes 49156
  106.4 37.4 %copy-start.12 = (bf16[16,512]{1,0:T(8,128)(2,1)S(1)}, bf16[16,512]{1,0:T(8,128)(2,1)}, u32[]{:S(2)}) copy-start(bf16[16,512]{1,0:T(8,128)(2,1)} %get-tuple-element.12) | copy-start | bytes 49156
  106.4 38.4 %copy-start.11 = (bf16[16,512]{1,0:T(8,128)(2,1)S(1)}, bf16[16,512]{1,0:T(8,128)(2,1)}, u32[]{:S(2)}) copy-start(bf16[16,512]{1,0:T(8,128)(2,1)} %get-tuple-element.13) | copy-start | bytes 49156
  106.4 42.2 %copy-start.10 = (bf16[16,512]{1,0:T(8,128)(2,1)S(1)}, bf16[16,512]{1,0:T(8,128)(2,1)}, u32[]{:S(2)}) copy-start(bf16[16,512]{1,0:T(8,128)(2,1)} %get-tuple-element.10.c0) | copy-start | bytes 49156
  107.3 41.4 %collective-permute-start.7 = (bf16[128,2048]{1,0:T(8,128)(2,1)}, bf16[128,2048]{1,0:T(8,128)(2,1)S(1)}, u32[]{:S(2)}, u32[]{:S(2)}) collective-permute-start(bf16[128,2048]{1,0:T(8,128)(2,1)} %slice.18), channel_id=1, source_target_pairs={{0,6},{2,0},{4,2},{6,4},{1,7},{3,1},{5,3},{7,5},{8,14},{10,8},{12,... | collective-permute-start | bytes 1572872 | tf_op jit(solution)/shard_map/ppermute | solution.py:347
  110.9 37.8 %collective-permute-start.9 = (bf16[128,2048]{1,0:T(8,128)(2,1)}, bf16[128,2048]{1,0:T(8,128)(2,1)S(1)}, u32[]{:S(2)}, u32[]{:S(2)}) collective-permute-start(bf16[128,2048]{1,0:T(8,128)(2,1)} %slice.19), channel_id=1, source_target_pairs={{0,2},{2,4},{4,6},{6,0},{1,3},{3,5},{5,7},{7,1},{8,10},{10,12},{12... | collective-permute-start | bytes 1572872 | tf_op jit(solution)/shard_map/ppermute | solution.py:347
  110.9 30.9 %collective-permute-start.3 = (s32[16,512]{1,0:T(8,128)S(1)}, s32[16,512]{1,0:T(8,128)S(1)}, u32[]{:S(2)}, u32[]{:S(2)}) collective-permute-start(s32[16,512]{1,0:T(8,128)S(1)} %get-tuple-element.20), channel_id=1, source_target_pairs={{0,6},{2,0},{4,2},{6,4},{1,7},{3,1},{5,3},{7,5},{8,14},{10,8},{12,... | collective-permute-start | bytes 98312 | tf_op jit(solution)/shard_map/ppermute | solution.py:347
  113.7 30.1 %collective-permute-start.4 = (s32[16,512]{1,0:T(8,128)S(1)}, s32[16,512]{1,0:T(8,128)S(1)}, u32[]{:S(2)}, u32[]{:S(2)}) collective-permute-start(s32[16,512]{1,0:T(8,128)S(1)} %get-tuple-element.22), channel_id=1, source_target_pairs={{0,4},{2,6},{4,0},{6,2},{1,5},{3,7},{5,1},{7,3},{8,12},{10,14},{12... | collective-permute-start | bytes 98312 | tf_op jit(solution)/shard_map/ppermute | solution.py:347
  113.7 31.2 %collective-permute-start.5 = (s32[16,512]{1,0:T(8,128)S(1)}, s32[16,512]{1,0:T(8,128)S(1)}, u32[]{:S(2)}, u32[]{:S(2)}) collective-permute-start(s32[16,512]{1,0:T(8,128)S(1)} %get-tuple-element.19), channel_id=1, source_target_pairs={{0,2},{2,4},{4,6},{6,0},{1,3},{3,5},{5,7},{7,1},{8,10},{10,12},{12... | collective-permute-start | bytes 98312 | tf_op jit(solution)/shard_map/ppermute | solution.py:347
  141.8 3.4 %collective-permute-start = (bf16[16,512]{1,0:T(8,128)(2,1)S(1)}, bf16[16,512]{1,0:T(8,128)(2,1)S(1)}, u32[]{:S(2)}, u32[]{:S(2)}) collective-permute-start(bf16[16,512]{1,0:T(8,128)(2,1)S(1)} %copy-done.13), channel_id=1, source_target_pairs={{0,6},{2,0},{4,2},{6,4},{1,7},{3,1},{5,3},{7,5},{8,14},{10,8},{12,... | collective-permute-start | bytes 49160 | tf_op jit(solution)/shard_map/ppermute | solution.py:347
  143.8 4.1 %collective-permute-start.1 = (bf16[16,512]{1,0:T(8,128)(2,1)S(1)}, bf16[16,512]{1,0:T(8,128)(2,1)S(1)}, u32[]{:S(2)}, u32[]{:S(2)}) collective-permute-start(bf16[16,512]{1,0:T(8,128)(2,1)S(1)} %copy-done.12), channel_id=1, source_target_pairs={{0,4},{2,6},{4,0},{6,2},{1,5},{3,7},{5,1},{7,3},{8,12},{10,14},{12... | collective-permute-start | bytes 49160 | tf_op jit(solution)/shard_map/ppermute | solution.py:347
  144.9 3.8 %collective-permute-start.2 = (bf16[16,512]{1,0:T(8,128)(2,1)S(1)}, bf16[16,512]{1,0:T(8,128)(2,1)S(1)}, u32[]{:S(2)}, u32[]{:S(2)}) collective-permute-start(bf16[16,512]{1,0:T(8,128)(2,1)S(1)} %copy-done.11), channel_id=1, source_target_pairs={{0,2},{2,4},{4,6},{6,0},{1,3},{3,5},{5,7},{7,1},{8,10},{10,12},{12... | collective-permute-start | bytes 49160 | tf_op jit(solution)/shard_map/ppermute | solution.py:347
  148.7 3.7 %copy-start.1 = (bf16[128,2048]{1,0:T(8,128)(2,1)}, bf16[128,2048]{1,0:T(8,128)(2,1)S(1)}, u32[]{:S(2)}) copy-start(bf16[128,2048]{1,0:T(8,128)(2,1)S(1)} %collective-permute-done.7.d2a) | copy-start | bytes 1572868
  148.7 3.7 %copy-start.3 = (bf16[128,2048]{1,0:T(8,128)(2,1)}, bf16[128,2048]{1,0:T(8,128)(2,1)S(1)}, u32[]{:S(2)}) copy-start(bf16[128,2048]{1,0:T(8,128)(2,1)S(1)} %collective-permute-done.9.d2b) | copy-start | bytes 1572868
  152.4 13.3 %collective-permute-start.10 = (bf16[256,2048]{1,0:T(8,128)(2,1)}, bf16[256,2048]{1,0:T(8,128)(2,1)}, u32[]{:S(2)}, u32[]{:S(2)}) collective-permute-start(bf16[256,2048]{1,0:T(8,128)(2,1)} %give.1), channel_id=1, source_target_pairs={{0,1},{1,0},{2,3},{3,2},{4,5},{5,4},{6,7},{7,6},{8,9},{9,8},{10,11... | collective-permute-start | bytes 3145736 | tf_op jit(solution)/shard_map/ppermute | solution.py:383
  155.1 1.0 copy-start.2
  156.2 1.0 copy-start.4

commit v4 on v3

v4 whole, which is shorter than its diff:
```python
import functools
import jax
import jax.numpy as jnp
from jax import lax
from jax.experimental import pallas as pl
from jax.experimental.pallas import tpu as pltpu
from jax.sharding import Mesh, PartitionSpec as P

SQRT_HALF = 0.7071067811865476
INV_ROOT_TAU = 0.3989422804014327
N_Y = 4
N_CORE = 2
F32 = jnp.float32
BF16 = jnp.bfloat16
NT = (((1,), (1,)), ((), ()))
NN = (((1,), (0,)), ((), ()))
TN = (((0,), (0,)), ((), ()))
ANY = pl.BlockSpec(memory_space=pl.ANY)
VMEM = pl.BlockSpec(memory_space=pltpu.VMEM)
DMA = pltpu.SemaphoreType.DMA


def dot(a, b, dims):
    return lax.dot_general(a, b, dims, preferred_element_type=F32)


def iota(shape, axis):
    return lax.broadcasted_iota(jnp.int32, shape, axis)


def cost(flops, bytes_accessed, transcendentals=0):
    return pl.CostEstimate(flops=flops, bytes_accessed=bytes_accessed, transcendentals=transcendentals)


def copy(src, dst, sem):
    return pltpu.make_async_copy(src, dst, sem)


def params(mib):
    return pltpu.CompilerParams(vmem_limit_bytes=mib << 20)


def stay(x):
    return pltpu.with_memory_space_constraint(x, pltpu.HBM)


def load_rows(src, dst, sems, pieces):
    rows = src.shape[0] // pieces
    return [
        copy(src.at[pl.ds(i * rows, rows), :], dst.at[pl.ds(i * rows, rows), :], sems.at[i])
        for i in range(pieces)
    ]


def ids_kernel(req_ref, out_ref):
    capacity, owners = req_ref.shape
    slots = out_ref.shape[0]
    row = iota((slots, owners), 0)
    lane = iota((slots, owners), 1)
    per_peer = N_Y * capacity
    peer = row // per_peer
    owner = (peer // N_CORE) * (N_Y * N_CORE) + ((row % per_peer) // capacity) * N_CORE + peer % N_CORE
    total = jnp.zeros((slots, 1), jnp.int32)
    for r in range(capacity):
        hit = (lane == owner) & (row % capacity == r)
        picked = jnp.where(hit, req_ref[r : r + 1, :], 0)
        total = total + jnp.sum(picked, axis=1, keepdims=True)
    out_ref[...] = jnp.broadcast_to(total, out_ref.shape)


def expand_ids(wanted):
    owners, capacity = wanted.shape
    slots = owners * capacity
    return pl.pallas_call(
        ids_kernel,
        out_shape=jax.ShapeDtypeStruct((slots, 128), jnp.int32),
        in_specs=[VMEM],
        out_specs=VMEM,
        cost_estimate=cost(10**5, 10**5),
        name="ids",
    )(jnp.transpose(wanted))


def column_hits(asked, rows):
    y = lax.axis_index("y")
    slots = asked.shape[0]
    shape = (slots, N_Y * rows)
    at = iota(shape, 1)
    owner_y = (iota(shape, 0) % (N_Y * 2)) // 2
    twice = jnp.concatenate([asked] * (N_Y * rows // asked.shape[1]), axis=1)
    hit = (twice == at % rows) & (owner_y == (y + at // rows) % N_Y)
    return hit.astype(F32).astype(BF16)


def gather_kernel(asked_ref, t0, t1, t2, t3, out_hbm, table, out, sems, out_sems):
    rows = t0.shape[0]
    width = out.shape[1]
    copies = [
        copy(t.at[:, pl.ds(0, width)], table.at[pl.ds(r * rows, rows), :], sems.at[r])
        for r, t in enumerate((t0, t1, t2, t3))
    ]
    for c in copies:
        c.start()
    hits = column_hits(asked_ref[...], rows)
    for c in copies:
        c.wait()
    block = width // 4
    sent = []
    for j in range(4):
        cols = pl.ds(j * block, block)
        out[:, cols] = dot(hits, table[:, cols], NN).astype(BF16)
        c = copy(out.at[:, cols], out_hbm.at[:, cols], out_sems.at[j])
        c.start()
        sent.append(c)
    for c in sent:
        c.wait()


def gather_rows(asked, tables, width):
    slots = asked.shape[0]
    rows = tables[0].shape[0]
    return pl.pallas_call(
        gather_kernel,
        out_shape=jax.ShapeDtypeStruct((slots, width), BF16),
        in_specs=[VMEM] + [ANY] * 4,
        out_specs=ANY,
        scratch_shapes=[
            pltpu.VMEM((N_Y * rows, width), BF16),
            pltpu.VMEM((slots, width), BF16),
            DMA((4,)),
            DMA((4,)),
        ],
        compiler_params=params(8),
        cost_estimate=cost(2 * 256 * 256 * 2048, 3 * 10**6),
    )(asked, *tables)


def weight_kernel(places_ref, gates_ref, out_ref):
    topk, block = places_ref.shape
    slots = out_ref.shape[1]
    slot = places_ref[...]
    gates = gates_ref[...]
    for s in range(0, slots, 32):
        row = iota((32, block), 0) + s
        total = jnp.zeros((32, block), F32)
        for k in range(topk):
            total = jnp.where(row == slot[k : k + 1, :], gates[k : k + 1, :], total)
        out_ref[0, s : s + 32, :] = total


def build_weight(places, gates, slots):
    topk, tokens = places.shape
    block = tokens // N_Y
    return pl.pallas_call(
        weight_kernel,
        grid=(N_Y,),
        out_shape=jax.ShapeDtypeStruct((N_Y, slots, block), F32),
        in_specs=[pl.BlockSpec((topk, block), lambda i: (0, i))] * 2,
        out_specs=pl.BlockSpec((1, slots, block), lambda i: (i, 0, 0)),
        compiler_params=params(8),
        cost_estimate=cost(3 * topk * slots * tokens, 4 * slots * tokens),
        name="weight",
    )(places, gates)


def local_kernel(
    tok_hbm, grad_hbm, rows_hbm, weight_hbm, coef_hbm, part_hbm,
    tok, grad, rows, weight, gated, coef, half, part,
    tok_sems, grad_sems, row_sems, weight_sems, coef_sem, part_sems,
):
    block = weight.shape[2]
    width = tok.shape[1]
    down = rows.at[0]
    up = rows.at[1]
    row_in = [
        copy(rows_hbm.at[:, pl.ds(i * width, width)], rows.at[i], row_sems.at[i]) for i in range(2)
    ]
    weight_in = [copy(weight_hbm.at[c], weight.at[c], weight_sems.at[c]) for c in range(N_Y)]
    tok_in = load_rows(tok_hbm, tok, tok_sems, 8)
    grad_in = load_rows(grad_hbm, grad, grad_sems, 8)

    def begin(c):
        tok_in[2 * c].start()
        tok_in[2 * c + 1].start()
        if c == 0:
            row_in[1].start()
        grad_in[2 * c].start()
        grad_in[2 * c + 1].start()
        weight_in[c].start()

    step = width // N_Y
    sent = []

    def parts(tokens, last):
        for j in range(2 * N_Y):
            left, right = ((coef, tok), (gated, grad))[j // N_Y]
            cols = pl.ds(j * step, step)
            here = dot(left[:, tokens], right[tokens, pl.ds(j % N_Y * step, step)], NN)
            if not last:
                half[:, cols] = here
                continue
            part[:, cols] = (half[:, cols] + here).astype(BF16)
            c = copy(part.at[:, cols], part_hbm.at[:, cols], part_sems.at[j])
            c.start()
            sent.append(c)

    row_in[0].start()
    begin(0)
    begin(1)
    row_in[0].wait()
    for c in range(N_Y):
        here = pl.ds(c * block, block)
        tok_in[2 * c].wait()
        tok_in[2 * c + 1].wait()
        pre = dot(down[...], tok[here, :], NT)
        if c == 0:
            row_in[1].wait()
        grad_in[2 * c].wait()
        grad_in[2 * c + 1].wait()
        weight_in[c].wait()
        if c + 2 < N_Y:
            begin(c + 2)
        back = dot(up[...], grad[here, :], NT)
        gate = weight[c]
        cdf = 0.5 * (1.0 + lax.erf(pre * SQRT_HALF))
        density = INV_ROOT_TAU * jnp.exp(-0.5 * pre * pre)
        gated[:, here] = (gate * (pre * cdf)).astype(BF16)
        coef[:, here] = (gate * (cdf + pre * density) * back).astype(BF16)
        if c == N_Y // 2 - 1:
            parts(pl.ds(0, N_Y // 2 * block), False)
    out = copy(coef, coef_hbm, coef_sem)
    out.start()
    sent.append(out)
    parts(pl.ds(N_Y // 2 * block, N_Y // 2 * block), True)
    for c in sent:
        c.wait()


def local_terms(tokens, grads, rows, weight):
    count, width = tokens.shape
    slots = rows.shape[0]
    return pl.pallas_call(
        local_kernel,
        out_shape=(
            jax.ShapeDtypeStruct((slots, count), BF16),
            jax.ShapeDtypeStruct((slots, 2 * width), BF16),
        ),
        in_specs=[ANY] * 4,
        out_specs=(ANY,) * 2,
        scratch_shapes=[
            pltpu.VMEM((count, width), BF16),
            pltpu.VMEM((count, width), BF16),
            pltpu.VMEM((2, slots, width), BF16),
            pltpu.VMEM(weight.shape, F32),
            pltpu.VMEM((slots, count), BF16),
            pltpu.VMEM((slots, count), BF16),
            pltpu.VMEM((slots, 2 * width), F32),
            pltpu.VMEM((slots, 2 * width), BF16),
            DMA((8,)), DMA((8,)), DMA((2,)), DMA((4,)), DMA, DMA((8,)),
        ],
        compiler_params=params(56),
        cost_estimate=cost(8 * count * width * slots, 24 << 20),
        name="local",
    )(tokens, grads, stay(rows), stay(weight))


def compact_kernel(coef_ref, places_ref, c0, c1, c2, c3):
    slots, count = coef_ref.shape
    topk = places_ref.shape[0]
    block = count // N_Y
    y = lax.axis_index("y")
    for r, out in enumerate((c0, c1, c2, c3)):
        here = pl.ds(pl.multiple_of(((y + r) % N_Y) * block, block), block)
        slot = places_ref[:, here]
        lines = []
        row = iota((16, block), 0)
        for k in range(topk):
            want = slot[k : k + 1, :] - row
            found = jnp.zeros((16, block), F32)
            for g in range(0, slots, 16):
                found = jnp.where(want == g, coef_ref[g : g + 16, here].astype(F32), found)
            lines.append(jnp.sum(found, axis=0, keepdims=True))
        out[...] = jnp.concatenate(lines, axis=0).astype(BF16)


def compact(coef, places):
    topk, count = places.shape
    return pl.pallas_call(
        compact_kernel,
        out_shape=tuple(jax.ShapeDtypeStruct((topk, count // N_Y), BF16) for _ in range(N_Y)),
        in_specs=[VMEM] * 2,
        out_specs=(VMEM,) * N_Y,
        compiler_params=params(8),
        cost_estimate=cost(2 * topk * coef.size, 2 * coef.size),
        name="compact",
    )(coef, places)


def own_hits(lists, rows):
    y = lax.axis_index("y")
    slots = lists[0].shape[0]
    i = iota((slots, slots), 0)
    j = iota((slots, slots), 1)
    source = ((i >> 3) << 3) + 2 * y + (i & 1)
    total = jnp.zeros((slots, rows), F32)
    for k, ids in enumerate(lists):
        take = (j == source) & (((i >> 1) & 3) == (y + k) % N_Y)
        hit = (ids[:, :rows] == iota((slots, rows), 1)).astype(F32).astype(BF16)
        total = total + dot(take.astype(F32).astype(BF16), hit, NN)
    return total.astype(BF16)


def sums_kernel(a0, a1, a2, a3, got_hbm, down_hbm, up_hbm, got, sums, sems, out_sems):
    rows, width = down_hbm.shape
    block = 1024
    pieces = 2 * width // block
    copies = [
        copy(got_hbm.at[:, pl.ds(j * block, block)], got.at[:, pl.ds(j * block, block)], sems.at[j])
        for j in range(pieces)
    ]
    for c in copies:
        c.start()
    hits = own_hits([a[...] for a in (a0, a1, a2, a3)], rows)
    sent = []
    for j in range(pieces):
        copies[j].wait()
        cols = pl.ds(j * block, block)
        sums[:, cols] = dot(hits, got[:, cols], TN)
        out = (down_hbm, up_hbm)[2 * j // pieces]
        c = copy(sums.at[:, cols], out.at[:, pl.ds(j * block % width, block)], out_sems.at[j])
        c.start()
        sent.append(c)
    for c in sent:
        c.wait()


def sum_rows(lists, got, rows):
    slots, both = got.shape
    out = jax.ShapeDtypeStruct((rows, both // 2), F32)
    return pl.pallas_call(
        sums_kernel,
        out_shape=(out, out),
        in_specs=[VMEM] * N_Y + [ANY],
        out_specs=(ANY, ANY),
        scratch_shapes=[
            pltpu.VMEM((slots, both), BF16),
            pltpu.VMEM((rows, both), F32),
            DMA((4,)),
            DMA((4,)),
        ],
        compiler_params=params(8),
        cost_estimate=cost(2 * 256 * 256 * 2048, 4 * 10**6),
        name="sums",
    )(*lists, got)


def final_kernel(
    mine, c0, c1, c2, c3, p0, p1, p2, p3, d0, d1, d2, d3, out_hbm, coef, rows, out, d_sems, out_sems
):
    core = lax.axis_index("core")
    which = core if mine else 1 - core
    half = out.shape[0]
    slots = coef.shape[0] // N_Y
    topk = c0.shape[0]
    loads = []
    start = 0
    for i, d in enumerate((d0, d1, d2, d3)):
        loads.append(copy(d, rows.at[pl.ds(start, d.shape[0]), :], d_sems.at[i]))
        start += d.shape[0]
    for c in loads:
        c.start()
    cols = pl.ds(pl.multiple_of(which * half, half), half)
    for r, (small, places) in enumerate(((c0, p0), (c1, p1), (c2, p2), (c3, p3))):
        values = small[:, cols].astype(F32)
        slot = places[:, cols]
        for s in range(0, slots, 64):
            row = iota((64, half), 0) + s
            total = jnp.zeros((64, half), F32)
            for k in range(topk):
                total = jnp.where(row == slot[k : k + 1, :], values[k : k + 1, :], total)
            coef[r * slots + s : r * slots + s + 64, :] = total.astype(BF16)
    for c in loads:
        c.wait()
    width = out.shape[1]
    block = width // 4
    sent = []
    for j in range(4):
        cols = pl.ds(j * block, block)
        out[:, cols] = dot(coef[...], rows[:, cols], TN).astype(BF16)
        c = copy(out.at[:, cols], out_hbm.at[:, cols], out_sems.at[j])
        c.start()
        sent.append(c)
    for c in sent:
        c.wait()


def final_product(mine, coef, places, rows):
    slots, width = rows[0].shape
    half = coef[0].shape[1] // N_CORE
    return pl.pallas_call(
        functools.partial(final_kernel, mine),
        out_shape=jax.ShapeDtypeStruct((half, width), BF16),
        in_specs=[VMEM] * 8 + [ANY] * 4,
        out_specs=ANY,
        scratch_shapes=[
            pltpu.VMEM((N_Y * slots, half), BF16),
            pltpu.VMEM((N_Y * slots, width), BF16),
            pltpu.VMEM((half, width), BF16),
            DMA((4,)), DMA((4,)),
        ],
        compiler_params=params(16),
        cost_estimate=cost(2 * half * 1024 * 2048, 6 << 20),
        name="keep" if mine else "give",
    )(*coef, *places, *rows)


def turn(x, r):
    return lax.ppermute(x, "y", [(i, (i - r) % N_Y) for i in range(N_Y)])


def gathered(blocks):
    return (blocks[0],) + tuple(turn(blocks[N_Y - r], r) for r in range(1, N_Y))


def exchange(x, axes):
    return lax.all_to_all(x, axes, split_axis=0, concat_axis=0, tiled=True)


def program(tokens, out_grad, down_rows, up_rows, requests, places, gate_weights):
    row_count, width = down_rows.shape
    _, devices, capacity = requests.shape
    slots = devices * capacity
    peers = devices // N_Y
    y = lax.axis_index("y")

    def column(x):
        wide = x.reshape(peers, slots // peers, x.shape[1])
        return exchange(wide, ("dp", "core")).reshape(x.shape)

    tables = gathered([jnp.concatenate([down_rows, up_rows], axis=1)] * N_Y)
    asked = column(expand_ids(requests[0]))
    slot_of = jnp.transpose(places[0])
    slot_of = (slot_of & ~15) | ((slot_of & 2) << 2) | ((slot_of & 12) >> 1) | (slot_of & 1)
    weight = build_weight(slot_of, jnp.transpose(gate_weights[0]), slots)
    rows = gather_rows(asked, tables, 2 * width)
    arrived = column(rows)
    lists = gathered([asked] * N_Y)
    block = slot_of.shape[1] // N_Y
    blocks = [
        lax.dynamic_slice_in_dim(slot_of, ((y + r) & (N_Y - 1)) * block, block, 1) for r in range(N_Y)
    ]
    chip_places = gathered(blocks)
    far = gather_rows(lists[2], tables, width)
    opposite = column(far)
    down = arrived[:, :width]
    above, below = turn(down, 1), turn(down, 3)
    coef, part = local_terms(tokens, out_grad, arrived, weight)
    part = part.reshape(devices, capacity, 2 * width)
    got = exchange(part, ("dp", "core", "y")).reshape(slots, 2 * width)
    small = compact(coef, slot_of)
    chip_coef = gathered(small)
    down_all = (down, above, opposite, below)
    give = final_product(False, chip_coef, chip_places, down_all)
    other = lax.ppermute(give, "core", [(0, 1), (1, 0)])
    keep = final_product(True, chip_coef, chip_places, down_all)
    input_grad = (keep.astype(F32) + other.astype(F32)).astype(BF16)
    down_grad, up_grad = sum_rows(lists, got, row_count)
    return (input_grad, down_grad, up_grad)


def solution(mesh):
    axes = ("dp", "y", "core")
    fine = Mesh(mesh.devices.reshape(mesh.devices.shape[0], N_Y, N_CORE), axes)
    in_specs = (
        P("dp", None),
        P("dp", None),
        P(axes, None),
        P(axes, None),
        P(axes, None, None),
        P(("y", "core"), "dp", None),
        P(("y", "core"), "dp", None),
    )
    out_specs = (P(axes, None), P(axes, None), P(axes, None))
    return jax.shard_map(program, mesh=fine, in_specs=in_specs, out_specs=out_specs, check_vma=False)
```

time: 169 us -> 165 us (0.976)
  starting transfers between devices: 24.4 us -> 43.3 us
  waiting for transfers between devices: 57.8 us -> 49.1 us
  local copies, waits for them, and re-layouts: 22 us -> 15 us
  Pallas kernels: 39.7 us -> 35.6 us
  blocking collectives: 21.1 us -> 17 us
    all_to_all x2 -> x3, starting transfers between devices: 11.8 us -> 21.6 us  [exchange(): return lax.all_to_all(x, axes, split_axis=0, concat_axis=0, tiled=True)]
    ppermute x10 -> x14, starting transfers between devices: 9.86 us -> 18.2 us  [turn(): return lax.ppermute(x, 'y', [(i, (i - r) % N_Y) for i in range(N_Y)])]
    reshape x5 -> x2, local copies, waits for them, and re-layouts: 12.2 us -> 7.15 us  [the longest x1 4.41 us: program(): part = part.reshape(devices, capacity, 2 * width)]
    all_to_all x2 -> x3, waiting for transfers between devices: 25.7 us -> 20.7 us  [exchange(): return lax.all_to_all(x, axes, split_axis=0, concat_axis=0, tiled=True)]
    pallas_call x4 -> x6, Pallas kernels: 29.6 us -> 25.5 us  [the longest x1 14.7 us: local_terms(): pl.pallas_call(local_kernel, out_shape=(jax.ShapeDtypeStruct((slots, coun...]
    all_to_all x1, blocking collectives: 21.1 us -> 17 us  [exchange(): return lax.all_to_all(x, axes, split_axis=0, concat_axis=0, tiled=True)]
    ppermute x10 -> x14, waiting for transfers between devices: 32.1 us -> 28.4 us  [turn(): return lax.ppermute(x, 'y', [(i, (i - r) % N_Y) for i in range(N_Y)])]
    slice x3 -> x1, local copies, waits for them, and re-layouts: 4.34 us -> 1.32 us  [program(): down = arrived[:, :width]]
  transfers between devices with their start and end apart: 13 -> 18, of which waited for: 5 -> 7; matrix products, arithmetic and copies ran while one was open for 6% -> 6% of each run, Pallas kernels for 22% -> 20%
where the time goes in v4:
time: 165 us; the launch traced here: 164 us
  waiting for transfers between devices  49.1 us (30%)
  starting transfers between devices  43.3 us (26%)
  Pallas kernels  35.6 us (22%)
  blocking collectives  17 us (10%)
  local copies, waits for them, and re-layouts  15 us (9%)
  other arithmetic  3.29 us (2%)
    ppermute x14, waiting for transfers between devices, turn(): return lax.ppermute(x, 'y', [(i, (i - r) % N_Y) for i in range(N_Y)])  28.4 us
    all_to_all x3, starting transfers between devices, exchange(): return lax.all_to_all(x, axes, split_axis=0, concat_axis=0, tiled=True)  21.6 us
    all_to_all x3, waiting for transfers between devices, exchange(): return lax.all_to_all(x, axes, split_axis=0, concat_axis=0, tiled=True)  20.7 us
    ppermute x14, starting transfers between devices, turn(): return lax.ppermute(x, 'y', [(i, (i - r) % N_Y) for i in range(N_Y)])  18.2 us
    all_to_all x1, blocking collectives, exchange(): return lax.all_to_all(x, axes, split_axis=0, concat_axis=0, tiled=True)  17 us
    pallas_call x1, Pallas kernels, local_terms(): pl.pallas_call(local_kernel, out_shape=(jax.ShapeDtypeStruct((slots, coun...  14.7 us
    pallas_call x2, Pallas kernels, final_product(): pl.pallas_call(functools.partial(final_kernel, mine), out_shape=jax.Shape...  7.29 us
    unnamed x13, local copies, waits for them, and re-layouts  4.74 us
  transfers between devices with their start and end apart: 18, of which 7 were waited for; matrix products, arithmetic and copies ran while one was open for 6% of the time, Pallas kernels for 20%

profile of v4, /device:TPU:1, one launch (start us, length us, event | category | flops | bytes accessed | tf_op | source)
XLA Modules:
  0.0 164.3 jit_solution(9150023347567980409)
XLA Ops:
  0.6 1.0 constant_dynamic-update-slice_fusion.1
  1.6 1.0 constant_dynamic-update-slice_fusion.t0
  2.6 3.6 %collective-permute-start = (bf16[64,4096]{1,0:T(8,128)(2,1)S(1)}, bf16[64,4096]{1,0:T(8,128)(2,1)S(1)}, u32[]{:S(2)}, u32[]{:S(2)}) collective-permute-start(bf16[64,4096]{1,0:T(8,128)(2,1)S(1)} %constant_dynamic-update-slice_fusion.t0), channel_id=1, source_target_pairs={{0,6},{2,0},{4,2},{6,4},{1,7},{3,1},{5,3},{7,5},{8,14},{10,8},{12,... | collective-permute-start | bytes 1572872 | tf_op jit(solution)/shard_map/ppermute | solution.py:418
  6.2 0.3 collective-permute-start.1
  6.5 0.7 collective-permute-start.2
  7.2 1.6 ids.1
  8.8 17.0 %all_to_all.20 = s32[32,8,128]{2,1,0:T(8,128)S(1)} all-to-all(s32[32,8,128]{2,1,0:T(8,128)} %bitcast.40), channel_id=1, replica_groups=mesh['dp'=16,'y'=4,'core'=2] {'dp','core'}, dimensions={0} | all-to-all | bytes 262144 | tf_op jit(solution)/shard_map/all_to_all | solution.py:426
  25.9 2.0 %collective-permute-done.t1 = bf16[64,4096]{1,0:T(8,128)(2,1)S(1)} collective-permute-done((bf16[64,4096]{1,0:T(8,128)(2,1)S(1)}, bf16[64,4096]{1,0:T(8,128)(2,1)S(1)}, u32[]{:S(2)}, u32[]{:S(2)}) %collective-permute-start) | collective-permute-done | bytes 524320 | tf_op jit(solution)/shard_map/ppermute | solution.py:418
  27.9 4.9 %collective-permute-done.2.t3 = bf16[64,4096]{1,0:T(8,128)(2,1)S(1)} collective-permute-done((bf16[64,4096]{1,0:T(8,128)(2,1)S(1)}, bf16[64,4096]{1,0:T(8,128)(2,1)S(1)}, u32[]{:S(2)}, u32[]{:S(2)}) %collective-permute-start.2) | collective-permute-done | bytes 524320 | tf_op jit(solution)/shard_map/ppermute | solution.py:418
  32.8 2.0 %shard_map.94 = bf16[256,4096]{1,0:T(8,128)(2,1)} custom-call(s32[256,128]{1,0:T(8,128)S(1)} %bitcast.34, bf16[64,4096]{1,0:T(8,128)(2,1)S(1)} %constant_dynamic-update-slice_fusion.t0, bf16[64,4096]{1,0:T(8,128)(2,1)S(1)} %collective-permute-done.t1, bf16[64,4096]{1,0:T(8,128)(2,1)S(1)} %collective-permute-done.1.t2, ...), custom_call_target="tpu_custom_call" | custom-call | flops 268435456 | bytes 3000000 | tf_op jit(solution)/shard_map/pallas_call | solution.py:122
  34.8 8.5 %all-to-all-start.1 = ((bf16[32,8,4096]{2,1,0:T(8,128)(2,1)}), bf16[32,8,4096]{2,1,0:T(8,128)(2,1)}, u32[]{:S(2)}, u32[]{:S(2)}) async-start(bf16[32,8,4096]{2,1,0:T(8,128)(2,1)} %bitcast.4), calls=%async_computation.1 | async-start | bytes 4194304 | tf_op jit(solution)/shard_map/all_to_all | solution.py:426
  43.2 0.0 copy-start.5
  43.3 0.0 copy-start.4
  43.3 0.4 collective-permute-start.10
  43.7 6.0 %collective-permute-done.10.asked_ref.a2 = s32[256,128]{1,0:T(8,128)S(1)} collective-permute-done((s32[256,128]{1,0:T(8,128)S(1)}, s32[256,128]{1,0:T(8,128)S(1)}, u32[]{:S(2)}, u32[]{:S(2)}) %collective-permute-start.10) | collective-permute-done | bytes 131104 | tf_op jit(solution)/shard_map/ppermute | solution.py:418
  49.7 1.6 shard_map.95
  51.3 20.7 %all-to-all-done.1 = bf16[32,8,4096]{2,1,0:T(8,128)(2,1)} async-done(((bf16[32,8,4096]{2,1,0:T(8,128)(2,1)}), bf16[32,8,4096]{2,1,0:T(8,128)(2,1)}, u32[]{:S(2)}, u32[]{:S(2)}) %all-to-all-start.1) | async-done | bytes 2097184 | tf_op jit(solution)/shard_map/all_to_all | solution.py:426
  72.0 5.2 %all-to-all-start.2 = ((bf16[32,8,2048]{2,1,0:T(8,128)(2,1)}), bf16[32,8,2048]{2,1,0:T(8,128)(2,1)S(1)}, u32[]{:S(2)}, u32[]{:S(2)}) async-start(bf16[32,8,2048]{2,1,0:T(8,128)(2,1)} %bitcast.18), calls=%async_computation.2 | async-start | bytes 2097152 | tf_op jit(solution)/shard_map/all_to_all | solution.py:426
  77.2 0.7 or_or_fusion
  77.9 2.8 %weight.1.weight_hbm = f32[4,256,512]{2,1,0:T(8,128)S(1)} custom-call(s32[16,2048]{1,0:T(8,128)S(1)} %get-tuple-element.24.places_ref, f32[16,2048]{1,0:T(8,128)S(1)} %bitcast.39), custom_call_target="tpu_custom_call" | custom-call | flops 25165824 | bytes 2097152 | tf_op jit(solution)/shard_map/weight/pallas_call | solution.py:154
  80.7 1.3 copy-done.2
  82.0 1.3 slice.4.d0
  83.4 0.1 collective-permute-start.11
  83.5 2.7 %collective-permute-start.9 = (bf16[256,2048]{1,0:T(8,128)(2,1)S(1)}, bf16[256,2048]{1,0:T(8,128)(2,1)}, u32[]{:S(2)}, u32[]{:S(2)}) collective-permute-start(bf16[256,2048]{1,0:T(8,128)(2,1)S(1)} %slice.4.d0), channel_id=1, source_target_pairs={{0,6},{2,0},{4,2},{6,4},{1,7},{3,1},{5,3},{7,5},{8,14},{10,8},{12,... | collective-permute-start | bytes 3145736 | tf_op jit(solution)/shard_map/ppermute | solution.py:418
  86.1 14.7 %local.1 = (bf16[256,2048]{1,0:T(8,128)(2,1)}, bf16[256,4096]{1,0:T(8,128)(2,1)}) custom-call(bf16[2048,2048]{1,0:T(8,128)(2,1)} %tok_hbm.1, bf16[2048,2048]{1,0:T(8,128)(2,1)} %grad_hbm.1, bf16[256,4096]{1,0:T(8,128)(2,1)} %bitcast.5.rows_hbm, f32[4,256,512]{2,1,0:T(8,128)} %copy-done.2), custom_call_target="tpu_custom_call" | custom-call | flops 8589934592 | bytes 25165824 | tf_op jit(solution)/shard_map/local/pallas_call | solution.py:242
  100.8 4.4 %reshape.49 = bf16[128,2,4096]{2,1,0:T(2,128)(2,1)} reshape(bf16[256,4096]{1,0:T(8,128)(2,1)} %get-tuple-element.16) | data formatting | bytes 4194304 | tf_op jit(solution)/shard_map/reshape | solution.py:458
  105.3 7.9 %all-to-all-start.3 = ((bf16[128,2,4096]{2,1,0:T(2,128)(2,1)}), bf16[128,2,4096]{2,1,0:T(2,128)(2,1)}, u32[]{:S(2)}, u32[]{:S(2)}) async-start(bf16[128,2,4096]{2,1,0:T(2,128)(2,1)} %reshape.49), calls=%async_computation.3 | async-start | bytes 4194304 | tf_op jit(solution)/shard_map/all_to_all | solution.py:426
  113.2 0.8 dynamic-slice_bitcast_fusion
  114.0 2.7 %collective-permute-start.6 = (s32[16,512]{1,0:T(8,128)S(1)}, s32[16,512]{1,0:T(8,128)S(1)}, u32[]{:S(2)}, u32[]{:S(2)}) collective-permute-start(s32[16,512]{1,0:T(8,128)S(1)} %get-tuple-element.21), channel_id=1, source_target_pairs={{0,6},{2,0},{4,2},{6,4},{1,7},{3,1},{5,3},{7,5},{8,14},{10,8},{12,... | collective-permute-start | bytes 98312 | tf_op jit(solution)/shard_map/ppermute | solution.py:418
  116.7 0.5 collective-permute-start.7
  117.2 0.6 collective-permute-start.8
  117.8 1.2 copy-done.3
  119.1 2.6 %compact.1 = (bf16[16,512]{1,0:T(8,128)(2,1)S(1)}, bf16[16,512]{1,0:T(8,128)(2,1)S(1)}, bf16[16,512]{1,0:T(8,128)(2,1)S(1)}, bf16[16,512]{1,0:T(8,128)(2,1)S(1)}) custom-call(bf16[256,2048]{1,0:T(8,128)(2,1)S(1)} %copy-done.3, s32[16,2048]{1,0:T(8,128)S(1)} %get-tuple-element.24.places_ref), custom_call_target="tpu_custom_call" | custom-call | flops 16777216 | bytes 1048576 | tf_op jit(solution)/shard_map/compact/pallas_call | solution.py:288
  121.7 12.6 %collective-permute-done.6.p1 = s32[16,512]{1,0:T(8,128)S(1)} collective-permute-done((s32[16,512]{1,0:T(8,128)S(1)}, s32[16,512]{1,0:T(8,128)S(1)}, u32[]{:S(2)}, u32[]{:S(2)}) %collective-permute-start.6) | collective-permute-done | bytes 32800 | tf_op jit(solution)/shard_map/ppermute | solution.py:418
  134.3 0.0 collective-permute-start.3
  134.3 0.9 collective-permute-done.7.p2
  135.2 0.0 collective-permute-start.4
  135.2 5.1 %collective-permute-start.5 = (bf16[16,512]{1,0:T(8,128)(2,1)S(1)}, bf16[16,512]{1,0:T(8,128)(2,1)S(1)}, u32[]{:S(2)}, u32[]{:S(2)}) collective-permute-start(bf16[16,512]{1,0:T(8,128)(2,1)S(1)} %get-tuple-element.15), channel_id=1, source_target_pairs={{0,2},{2,4},{4,6},{6,0},{1,3},{3,5},{5,7},{7,1},{8,10},{10,12},{12... | collective-permute-start | bytes 49160 | tf_op jit(solution)/shard_map/ppermute | solution.py:418
  140.3 2.0 %collective-permute-done.5.c3 = bf16[16,512]{1,0:T(8,128)(2,1)S(1)} collective-permute-done((bf16[16,512]{1,0:T(8,128)(2,1)S(1)}, bf16[16,512]{1,0:T(8,128)(2,1)S(1)}, u32[]{:S(2)}, u32[]{:S(2)}) %collective-permute-start.5) | collective-permute-done | bytes 16416 | tf_op jit(solution)/shard_map/ppermute | solution.py:418
  142.3 3.7 %give.1 = bf16[256,2048]{1,0:T(8,128)(2,1)} custom-call(bf16[16,512]{1,0:T(8,128)(2,1)S(1)} %get-tuple-element.12.c0, bf16[16,512]{1,0:T(8,128)(2,1)S(1)} %collective-permute-done.3.c1, bf16[16,512]{1,0:T(8,128)(2,1)S(1)} %collective-permute-done.4.c2, bf16[16,512]{1,0:T(8,128)(2,1)S(1)} %collective-permute-done.5.c3, s32[16,512]{1,0:T(8,128)S(1)} %get-tuple-element.22.p0, ...), custom_call_target="tpu_custom_call" | custom-call | flops 1073741824 | bytes 6291456 | tf_op jit(solution)/shard_map/give/pallas_call | solution.py:400
  146.0 3.5 %collective-permute-start.12 = (bf16[256,2048]{1,0:T(8,128)(2,1)}, bf16[256,2048]{1,0:T(8,128)(2,1)}, u32[]{:S(2)}, u32[]{:S(2)}) collective-permute-start(bf16[256,2048]{1,0:T(8,128)(2,1)} %give.1), channel_id=1, source_target_pairs={{0,1},{1,0},{2,3},{3,2},{4,5},{5,4},{6,7},{7,6},{8,9},{9,8},{10,11... | collective-permute-start | bytes 3145736 | tf_op jit(solution)/shard_map/ppermute | solution.py:464
  149.5 1.4 collective-permute-start.13
  150.9 0.1 collective-permute-start.14
  151.0 1.2 copy-done.1
  152.2 3.6 %keep.1 = bf16[256,2048]{1,0:T(8,128)(2,1)S(1)} custom-call(bf16[16,512]{1,0:T(8,128)(2,1)S(1)} %get-tuple-element.12.c0, bf16[16,512]{1,0:T(8,128)(2,1)S(1)} %collective-permute-done.3.c1, bf16[16,512]{1,0:T(8,128)(2,1)S(1)} %collective-permute-done.4.c2, bf16[16,512]{1,0:T(8,128)(2,1)S(1)} %collective-permute-done.5.c3, ...), custom_call_target="tpu_custom_call" | custom-call | flops 1073741824 | bytes 6291456 | tf_op jit(solution)/shard_map/keep/pallas_call | solution.py:400
  155.8 2.7 %reshape.50.got_hbm = bf16[256,4096]{1,0:T(8,128)(2,1)S(1)} reshape(bf16[128,2,4096]{2,1,0:T(2,128)(2,1)} %all-to-all-done.3) | data formatting | bytes 4194304 | tf_op jit(solution)/shard_map/reshape | solution.py:459
  158.6 3.1 %sums.1 = (f32[64,2048]{1,0:T(8,128)}, f32[64,2048]{1,0:T(8,128)}) custom-call(s32[256,128]{1,0:T(8,128)S(1)} %bitcast.38, s32[256,128]{1,0:T(8,128)S(1)} %collective-permute-done.13.a1, s32[256,128]{1,0:T(8,128)S(1)} %collective-permute-done.10.asked_ref.a2, s32[256,128]{1,0:T(8,128)} %collective-permute-done.14.a3, bf16[256,4096]{1,0:T(8,128)(2,1)S(1)} %reshape.50.got_hbm), custom_call_target="tpu_custom_call" | custom-call | flops 268435456 | bytes 4000000 | tf_op jit(solution)/shard_map/sums/pallas_call | solution.py:340
  161.7 2.6 %add_convert_fusion = bf16[256,2048]{1,0:T(8,128)(2,1)} fusion(bf16[256,2048]{1,0:T(8,128)(2,1)} %collective-permute-done.12, bf16[256,2048]{1,0:T(8,128)(2,1)S(1)} %keep.1), kind=kLoop, calls=%fused_computation | loop fusion | flops 2097152 | bytes 3145728 | tf_op jit(solution)/shard_map/convert_element_type | solution.py:466
  (18 shorter events, 0.0 us)
Async XLA Ops:
  2.6 25.3 %collective-permute-start = (bf16[64,4096]{1,0:T(8,128)(2,1)S(1)}, bf16[64,4096]{1,0:T(8,128)(2,1)S(1)}, u32[]{:S(2)}, u32[]{:S(2)}) collective-permute-start(bf16[64,4096]{1,0:T(8,128)(2,1)S(1)} %constant_dynamic-update-slice_fusion.t0), channel_id=1, source_target_pairs={{0,6},{2,0},{4,2},{6,4},{1,7},{3,1},{5,3},{7,5},{8,14},{10,8},{12,... | collective-permute-start | bytes 1572872 | tf_op jit(solution)/shard_map/ppermute | solution.py:418
  6.2 21.7 %collective-permute-start.1 = (bf16[64,4096]{1,0:T(8,128)(2,1)S(1)}, bf16[64,4096]{1,0:T(8,128)(2,1)S(1)}, u32[]{:S(2)}, u32[]{:S(2)}) collective-permute-start(bf16[64,4096]{1,0:T(8,128)(2,1)S(1)} %constant_dynamic-update-slice_fusion.t0), channel_id=1, source_target_pairs={{0,4},{2,6},{4,0},{6,2},{1,5},{3,7},{5,1},{7,3},{8,12},{10,14},{12... | collective-permute-start | bytes 1572872 | tf_op jit(solution)/shard_map/ppermute | solution.py:418
  6.5 26.2 %collective-permute-start.2 = (bf16[64,4096]{1,0:T(8,128)(2,1)S(1)}, bf16[64,4096]{1,0:T(8,128)(2,1)S(1)}, u32[]{:S(2)}, u32[]{:S(2)}) collective-permute-start(bf16[64,4096]{1,0:T(8,128)(2,1)S(1)} %constant_dynamic-update-slice_fusion.t0), channel_id=1, source_target_pairs={{0,2},{2,4},{4,6},{6,0},{1,3},{3,5},{5,7},{7,1},{8,10},{10,12},{12... | collective-permute-start | bytes 1572872 | tf_op jit(solution)/shard_map/ppermute | solution.py:418
  34.8 37.2 %all-to-all-start.1 = ((bf16[32,8,4096]{2,1,0:T(8,128)(2,1)}), bf16[32,8,4096]{2,1,0:T(8,128)(2,1)}, u32[]{:S(2)}, u32[]{:S(2)}) async-start(bf16[32,8,4096]{2,1,0:T(8,128)(2,1)} %bitcast.4), calls=%async_computation.1 | async-start | bytes 4194304 | tf_op jit(solution)/shard_map/all_to_all | solution.py:426
  43.2 33.9 %copy-start.5 = (s32[1,2048,16]{1,2,0:T(8,128)S(1)}, s32[1,2048,16]{1,2,0:T(8,128)}, u32[]{:S(2)}) copy-start(s32[1,2048,16]{1,2,0:T(8,128)} %param.12) | copy-start | bytes 393220
  43.3 34.6 %copy-start.4 = (f32[1,2048,16]{1,2,0:T(8,128)S(1)}, f32[1,2048,16]{1,2,0:T(8,128)}, u32[]{:S(2)}) copy-start(f32[1,2048,16]{1,2,0:T(8,128)} %param.13) | copy-start | bytes 393220
  43.3 6.4 %collective-permute-start.10 = (s32[256,128]{1,0:T(8,128)S(1)}, s32[256,128]{1,0:T(8,128)S(1)}, u32[]{:S(2)}, u32[]{:S(2)}) collective-permute-start(s32[256,128]{1,0:T(8,128)S(1)} %bitcast.35), channel_id=1, source_target_pairs={{0,4},{2,6},{4,0},{6,2},{1,5},{3,7},{5,1},{7,3},{8,12},{10,14},{12... | collective-permute-start | bytes 393224 | tf_op jit(solution)/shard_map/ppermute | solution.py:418
  72.0 33.3 %all-to-all-start.2 = ((bf16[32,8,2048]{2,1,0:T(8,128)(2,1)}), bf16[32,8,2048]{2,1,0:T(8,128)(2,1)S(1)}, u32[]{:S(2)}, u32[]{:S(2)}) async-start(bf16[32,8,2048]{2,1,0:T(8,128)(2,1)} %bitcast.18), calls=%async_computation.2 | async-start | bytes 2097152 | tf_op jit(solution)/shard_map/all_to_all | solution.py:426
  80.7 1.3 copy-start.2
  83.4 58.9 %collective-permute-start.11 = (bf16[256,2048]{1,0:T(8,128)(2,1)S(1)}, bf16[256,2048]{1,0:T(8,128)(2,1)S(1)}, u32[]{:S(2)}, u32[]{:S(2)}) collective-permute-start(bf16[256,2048]{1,0:T(8,128)(2,1)S(1)} %slice.4.d0), channel_id=1, source_target_pairs={{0,2},{2,4},{4,6},{6,0},{1,3},{3,5},{5,7},{7,1},{8,10},{10,12},{12... | collective-permute-start | bytes 3145736 | tf_op jit(solution)/shard_map/ppermute | solution.py:418
  83.5 58.8 %collective-permute-start.9 = (bf16[256,2048]{1,0:T(8,128)(2,1)S(1)}, bf16[256,2048]{1,0:T(8,128)(2,1)}, u32[]{:S(2)}, u32[]{:S(2)}) collective-permute-start(bf16[256,2048]{1,0:T(8,128)(2,1)S(1)} %slice.4.d0), channel_id=1, source_target_pairs={{0,6},{2,0},{4,2},{6,4},{1,7},{3,1},{5,3},{7,5},{8,14},{10,8},{12,... | collective-permute-start | bytes 3145736 | tf_op jit(solution)/shard_map/ppermute | solution.py:418
  105.3 50.5 %all-to-all-start.3 = ((bf16[128,2,4096]{2,1,0:T(2,128)(2,1)}), bf16[128,2,4096]{2,1,0:T(2,128)(2,1)}, u32[]{:S(2)}, u32[]{:S(2)}) async-start(bf16[128,2,4096]{2,1,0:T(2,128)(2,1)} %reshape.49), calls=%async_computation.3 | async-start | bytes 4194304 | tf_op jit(solution)/shard_map/all_to_all | solution.py:426
  114.0 20.2 %collective-permute-start.6 = (s32[16,512]{1,0:T(8,128)S(1)}, s32[16,512]{1,0:T(8,128)S(1)}, u32[]{:S(2)}, u32[]{:S(2)}) collective-permute-start(s32[16,512]{1,0:T(8,128)S(1)} %get-tuple-element.21), channel_id=1, source_target_pairs={{0,6},{2,0},{4,2},{6,4},{1,7},{3,1},{5,3},{7,5},{8,14},{10,8},{12,... | collective-permute-start | bytes 98312 | tf_op jit(solution)/shard_map/ppermute | solution.py:418
  116.7 18.5 %collective-permute-start.7 = (s32[16,512]{1,0:T(8,128)S(1)}, s32[16,512]{1,0:T(8,128)S(1)}, u32[]{:S(2)}, u32[]{:S(2)}) collective-permute-start(s32[16,512]{1,0:T(8,128)S(1)} %get-tuple-element.20), channel_id=1, source_target_pairs={{0,4},{2,6},{4,0},{6,2},{1,5},{3,7},{5,1},{7,3},{8,12},{10,14},{12... | collective-permute-start | bytes 98312 | tf_op jit(solution)/shard_map/ppermute | solution.py:418
  117.2 17.9 %collective-permute-start.8 = (s32[16,512]{1,0:T(8,128)S(1)}, s32[16,512]{1,0:T(8,128)S(1)}, u32[]{:S(2)}, u32[]{:S(2)}) collective-permute-start(s32[16,512]{1,0:T(8,128)S(1)} %get-tuple-element.19), channel_id=1, source_target_pairs={{0,2},{2,4},{4,6},{6,0},{1,3},{3,5},{5,7},{7,1},{8,10},{10,12},{12... | collective-permute-start | bytes 98312 | tf_op jit(solution)/shard_map/ppermute | solution.py:418
  117.8 1.2 copy-start.3
  134.3 6.0 %collective-permute-start.3 = (bf16[16,512]{1,0:T(8,128)(2,1)S(1)}, bf16[16,512]{1,0:T(8,128)(2,1)S(1)}, u32[]{:S(2)}, u32[]{:S(2)}) collective-permute-start(bf16[16,512]{1,0:T(8,128)(2,1)S(1)} %get-tuple-element.13), channel_id=1, source_target_pairs={{0,6},{2,0},{4,2},{6,4},{1,7},{3,1},{5,3},{7,5},{8,14},{10,8},{12,... | collective-permute-start | bytes 49160 | tf_op jit(solution)/shard_map/ppermute | solution.py:418
  135.2 5.1 %collective-permute-start.4 = (bf16[16,512]{1,0:T(8,128)(2,1)S(1)}, bf16[16,512]{1,0:T(8,128)(2,1)S(1)}, u32[]{:S(2)}, u32[]{:S(2)}) collective-permute-start(bf16[16,512]{1,0:T(8,128)(2,1)S(1)} %get-tuple-element.14), channel_id=1, source_target_pairs={{0,4},{2,6},{4,0},{6,2},{1,5},{3,7},{5,1},{7,3},{8,12},{10,14},{12... | collective-permute-start | bytes 49160 | tf_op jit(solution)/shard_map/ppermute | solution.py:418
  135.2 7.1 %collective-permute-start.5 = (bf16[16,512]{1,0:T(8,128)(2,1)S(1)}, bf16[16,512]{1,0:T(8,128)(2,1)S(1)}, u32[]{:S(2)}, u32[]{:S(2)}) collective-permute-start(bf16[16,512]{1,0:T(8,128)(2,1)S(1)} %get-tuple-element.15), channel_id=1, source_target_pairs={{0,2},{2,4},{4,6},{6,0},{1,3},{3,5},{5,7},{7,1},{8,10},{10,12},{12... | collective-permute-start | bytes 49160 | tf_op jit(solution)/shard_map/ppermute | solution.py:418
  142.3 3.7 %copy-start = (bf16[256,2048]{1,0:T(8,128)(2,1)}, bf16[256,2048]{1,0:T(8,128)(2,1)S(1)}, u32[]{:S(2)}) copy-start(bf16[256,2048]{1,0:T(8,128)(2,1)S(1)} %collective-permute-done.11.d3) | copy-start | bytes 3145732
  146.0 15.7 %collective-permute-start.12 = (bf16[256,2048]{1,0:T(8,128)(2,1)}, bf16[256,2048]{1,0:T(8,128)(2,1)}, u32[]{:S(2)}, u32[]{:S(2)}) collective-permute-start(bf16[256,2048]{1,0:T(8,128)(2,1)} %give.1), channel_id=1, source_target_pairs={{0,1},{1,0},{2,3},{3,2},{4,5},{5,4},{6,7},{7,6},{8,9},{9,8},{10,11... | collective-permute-start | bytes 3145736 | tf_op jit(solution)/shard_map/ppermute | solution.py:464
  149.5 9.1 %collective-permute-start.13 = (s32[256,128]{1,0:T(8,128)S(1)}, s32[256,128]{1,0:T(8,128)S(1)}, u32[]{:S(2)}, u32[]{:S(2)}) collective-permute-start(s32[256,128]{1,0:T(8,128)S(1)} %bitcast.36), channel_id=1, source_target_pairs={{0,6},{2,0},{4,2},{6,4},{1,7},{3,1},{5,3},{7,5},{8,14},{10,8},{12,... | collective-permute-start | bytes 393224 | tf_op jit(solution)/shard_map/ppermute | solution.py:418
  150.9 7.7 %collective-permute-start.14 = (s32[256,128]{1,0:T(8,128)S(1)}, s32[256,128]{1,0:T(8,128)}, u32[]{:S(2)}, u32[]{:S(2)}) collective-permute-start(s32[256,128]{1,0:T(8,128)S(1)} %bitcast.37), channel_id=1, source_target_pairs={{0,2},{2,4},{4,6},{6,0},{1,3},{3,5},{5,7},{7,1},{8,10},{10,12},{12... | collective-permute-start | bytes 393224 | tf_op jit(solution)/shard_map/ppermute | solution.py:418
  151.0 1.2 copy-start.1

commit v5 on v4

--- a/solution.py
+++ b/solution.py
@@ -54,26 +54,22 @@
 
 def ids_kernel(req_ref, out_ref):
     capacity, owners = req_ref.shape
-    slots = out_ref.shape[0]
-    row = iota((slots, owners), 0)
-    lane = iota((slots, owners), 1)
-    per_peer = N_Y * capacity
-    peer = row // per_peer
-    owner = (peer // N_CORE) * (N_Y * N_CORE) + ((row % per_peer) // capacity) * N_CORE + peer % N_CORE
-    total = jnp.zeros((slots, 1), jnp.int32)
+    row = iota((owners, owners), 0)
+    lane = iota((owners, owners), 1)
+    total = jnp.zeros(out_ref.shape, jnp.int32)
+    at = iota(out_ref.shape, 1)
     for r in range(capacity):
-        hit = (lane == owner) & (row % capacity == r)
-        picked = jnp.where(hit, req_ref[r : r + 1, :], 0)
-        total = total + jnp.sum(picked, axis=1, keepdims=True)
-    out_ref[...] = jnp.broadcast_to(total, out_ref.shape)
-
-
-def expand_ids(wanted):
-    owners, capacity = wanted.shape
-    slots = owners * capacity
+        picked = jnp.where(lane == row, req_ref[r : r + 1, :], 0)
+        column = jnp.sum(picked, axis=1, keepdims=True)
+        total = jnp.where(at == r, column, total)
+    out_ref[...] = total
+
+
+def turn_ids(wanted):
+    owners, _ = wanted.shape
     return pl.pallas_call(
         ids_kernel,
-        out_shape=jax.ShapeDtypeStruct((slots, 128), jnp.int32),
+        out_shape=jax.ShapeDtypeStruct((owners, 128), jnp.int32),
         in_specs=[VMEM],
         out_specs=VMEM,
         cost_estimate=cost(10**5, 10**5),
@@ -81,58 +77,57 @@
     )(jnp.transpose(wanted))
 
 
-def column_hits(asked, rows):
-    y = lax.axis_index("y")
-    slots = asked.shape[0]
-    shape = (slots, N_Y * rows)
-    at = iota(shape, 1)
-    owner_y = (iota(shape, 0) % (N_Y * 2)) // 2
-    twice = jnp.concatenate([asked] * (N_Y * rows // asked.shape[1]), axis=1)
-    hit = (twice == at % rows) & (owner_y == (y + at // rows) % N_Y)
-    return hit.astype(F32).astype(BF16)
-
-
-def gather_kernel(asked_ref, t0, t1, t2, t3, out_hbm, table, out, sems, out_sems):
-    rows = t0.shape[0]
-    width = out.shape[1]
-    copies = [
-        copy(t.at[:, pl.ds(0, width)], table.at[pl.ds(r * rows, rows), :], sems.at[r])
-        for r, t in enumerate((t0, t1, t2, t3))
-    ]
-    for c in copies:
-        c.start()
-    hits = column_hits(asked_ref[...], rows)
-    for c in copies:
-        c.wait()
-    block = width // 4
+def asked_hits(asked, capacity, rows, flip):
+    devices = asked.shape[0]
+    slots = devices * capacity
+    at = iota((devices, rows), 1)
+    place = iota((slots, devices), 0)
+    device = iota((slots, devices), 1) ^ flip
+    total = jnp.zeros((slots, rows), F32)
+    for r in range(capacity):
+        hit = (asked[:, r : r + 1] == at).astype(F32).astype(BF16)
+        spread = (place == device * capacity + r).astype(F32).astype(BF16)
+        total = total + dot(spread, hit, NN)
+    return total.astype(BF16)
+
+
+def gather_kernel(asked_ref, down_ref, up_ref, out_hbm, far_hbm, out, far, out_sems):
+    devices, capacity, _ = out.shape
+    rows, width = down_ref.shape
+    asked = asked_ref[...]
+    block = 512
     sent = []
-    for j in range(4):
-        cols = pl.ds(j * block, block)
-        out[:, cols] = dot(hits, table[:, cols], NN).astype(BF16)
-        c = copy(out.at[:, cols], out_hbm.at[:, cols], out_sems.at[j])
-        c.start()
-        sent.append(c)
+
+    def fill(hits, tables, buf, hbm, base):
+        for j in range(buf.shape[2] // block):
+            table = tables[j * block // width]
+            cols = pl.ds(j * block, block)
+            found = dot(hits, table[:, pl.ds(j * block % width, block)], NN).astype(BF16)
+            buf[:, :, cols] = found.reshape(devices, capacity, block)
+            c = copy(buf.at[:, :, cols], hbm.at[:, :, cols], out_sems.at[base + j])
+            c.start()
+            sent.append(c)
+
+    fill(asked_hits(asked, capacity, rows, 0), (down_ref, up_ref), out, out_hbm, 0)
+    fill(asked_hits(asked, capacity, rows, 2 * N_CORE), (down_ref,), far, far_hbm, 8)
     for c in sent:
         c.wait()
 
 
-def gather_rows(asked, tables, width):
-    slots = asked.shape[0]
-    rows = tables[0].shape[0]
+def gather_rows(asked, capacity, down_rows, up_rows):
+    devices = asked.shape[0]
+    width = down_rows.shape[1]
+    shapes = ((devices, capacity, 2 * width), (devices, capacity, width))
     return pl.pallas_call(
         gather_kernel,
-        out_shape=jax.ShapeDtypeStruct((slots, width), BF16),
-        in_specs=[VMEM] + [ANY] * 4,
-        out_specs=ANY,
-        scratch_shapes=[
-            pltpu.VMEM((N_Y * rows, width), BF16),
-            pltpu.VMEM((slots, width), BF16),
-            DMA((4,)),
-            DMA((4,)),
-        ],
+        out_shape=tuple(jax.ShapeDtypeStruct(x, BF16) for x in shapes),
+        in_specs=[VMEM] * 3,
+        out_specs=(ANY, ANY),
+        scratch_shapes=[pltpu.VMEM(x, BF16) for x in shapes] + [DMA((12,))],
         compiler_params=params(8),
-        cost_estimate=cost(2 * 256 * 256 * 2048, 3 * 10**6),
-    )(asked, *tables)
+        cost_estimate=cost(3 * 256 * 256 * 2048, 4 * 10**6),
+        name="gather",
+    )(asked, stay(down_rows), stay(up_rows))
 
 
 def weight_kernel(places_ref, gates_ref, out_ref):
@@ -165,7 +160,7 @@
 
 def local_kernel(
     tok_hbm, grad_hbm, rows_hbm, weight_hbm, coef_hbm, part_hbm,
-    tok, grad, rows, weight, gated, coef, half, part,
+    tok, grad, raw, rows, weight, gated, coef, half, part,
     tok_sems, grad_sems, row_sems, weight_sems, coef_sem, part_sems,
 ):
     block = weight.shape[2]
@@ -173,7 +168,7 @@
     down = rows.at[0]
     up = rows.at[1]
     row_in = [
-        copy(rows_hbm.at[:, pl.ds(i * width, width)], rows.at[i], row_sems.at[i]) for i in range(2)
+        copy(rows_hbm.at[:, :, pl.ds(i * width, width)], raw.at[i], row_sems.at[i]) for i in range(2)
     ]
     weight_in = [copy(weight_hbm.at[c], weight.at[c], weight_sems.at[c]) for c in range(N_Y)]
     tok_in = load_rows(tok_hbm, tok, tok_sems, 8)
@@ -189,7 +184,15 @@
         weight_in[c].start()
 
     step = width // N_Y
+    slots = rows.shape[1]
+    chunk = part.shape[:2] + (step,)
     sent = []
+
+    def unpack(i):
+        row_in[i].wait()
+        for j in range(N_Y):
+            cols = pl.ds(j * step, step)
+            rows[i, :, cols] = raw[i, :, :, cols].reshape(slots, step)
 
     def parts(tokens, last):
         for j in range(2 * N_Y):
@@ -199,22 +202,22 @@
             if not last:
                 half[:, cols] = here
                 continue
-            part[:, cols] = (half[:, cols] + here).astype(BF16)
-            c = copy(part.at[:, cols], part_hbm.at[:, cols], part_sems.at[j])
+            part[:, :, cols] = (half[:, cols] + here).astype(BF16).reshape(chunk)
+            c = copy(part.at[:, :, cols], part_hbm.at[:, :, cols], part_sems.at[j])
             c.start()
             sent.append(c)
 
     row_in[0].start()
     begin(0)
     begin(1)
-    row_in[0].wait()
+    unpack(0)
     for c in range(N_Y):
         here = pl.ds(c * block, block)
         tok_in[2 * c].wait()
         tok_in[2 * c + 1].wait()
         pre = dot(down[...], tok[here, :], NT)
         if c == 0:
-            row_in[1].wait()
+            unpack(1)
         grad_in[2 * c].wait()
         grad_in[2 * c + 1].wait()
         weight_in[c].wait()
@@ -238,24 +241,25 @@
 
 def local_terms(tokens, grads, rows, weight):
     count, width = tokens.shape
-    slots = rows.shape[0]
+    slots = rows.shape[0] * rows.shape[1]
     return pl.pallas_call(
         local_kernel,
         out_shape=(
             jax.ShapeDtypeStruct((slots, count), BF16),
-            jax.ShapeDtypeStruct((slots, 2 * width), BF16),
+            jax.ShapeDtypeStruct(rows.shape, BF16),
         ),
         in_specs=[ANY] * 4,
         out_specs=(ANY,) * 2,
         scratch_shapes=[
             pltpu.VMEM((count, width), BF16),
             pltpu.VMEM((count, width), BF16),
+            pltpu.VMEM((2,) + rows.shape[:2] + (width,), BF16),
             pltpu.VMEM((2, slots, width), BF16),
             pltpu.VMEM(weight.shape, F32),
             pltpu.VMEM((slots, count), BF16),
             pltpu.VMEM((slots, count), BF16),
             pltpu.VMEM((slots, 2 * width), F32),
-            pltpu.VMEM((slots, 2 * width), BF16),
+            pltpu.VMEM(rows.shape, BF16),
             DMA((8,)), DMA((8,)), DMA((2,)), DMA((4,)), DMA, DMA((8,)),
         ],
         compiler_params=params(56),
@@ -296,36 +300,22 @@
     )(coef, places)
 
 
-def own_hits(lists, rows):
-    y = lax.axis_index("y")
-    slots = lists[0].shape[0]
-    i = iota((slots, slots), 0)
-    j = iota((slots, slots), 1)
-    source = ((i >> 3) << 3) + 2 * y + (i & 1)
-    total = jnp.zeros((slots, rows), F32)
-    for k, ids in enumerate(lists):
-        take = (j == source) & (((i >> 1) & 3) == (y + k) % N_Y)
-        hit = (ids[:, :rows] == iota((slots, rows), 1)).astype(F32).astype(BF16)
-        total = total + dot(take.astype(F32).astype(BF16), hit, NN)
-    return total.astype(BF16)
-
-
-def sums_kernel(a0, a1, a2, a3, got_hbm, down_hbm, up_hbm, got, sums, sems, out_sems):
+def sums_kernel(asked_ref, got_hbm, down_hbm, up_hbm, got, sums, sems, out_sems):
     rows, width = down_hbm.shape
-    block = 1024
-    pieces = 2 * width // block
-    copies = [
-        copy(got_hbm.at[:, pl.ds(j * block, block)], got.at[:, pl.ds(j * block, block)], sems.at[j])
-        for j in range(pieces)
-    ]
-    for c in copies:
-        c.start()
-    hits = own_hits([a[...] for a in (a0, a1, a2, a3)], rows)
+    devices, capacity, both = got.shape
+    block = 512
+    pieces = both // block
+    copies = []
+    for j in range(pieces):
+        cols = pl.ds(j * block, block)
+        copies.append(copy(got_hbm.at[:, :, cols], got.at[:, :, cols], sems.at[j]))
+        copies[j].start()
+    hits = asked_hits(asked_ref[...], capacity, rows, 0)
     sent = []
     for j in range(pieces):
         copies[j].wait()
         cols = pl.ds(j * block, block)
-        sums[:, cols] = dot(hits, got[:, cols], TN)
+        sums[:, cols] = dot(hits, got[:, :, cols].reshape(devices * capacity, block), TN)
         out = (down_hbm, up_hbm)[2 * j // pieces]
         c = copy(sums.at[:, cols], out.at[:, pl.ds(j * block % width, block)], out_sems.at[j])
         c.start()
@@ -334,24 +324,24 @@
         c.wait()
 
 
-def sum_rows(lists, got, rows):
-    slots, both = got.shape
+def sum_rows(asked, got, rows):
+    both = got.shape[2]
     out = jax.ShapeDtypeStruct((rows, both // 2), F32)
     return pl.pallas_call(
         sums_kernel,
         out_shape=(out, out),
-        in_specs=[VMEM] * N_Y + [ANY],
+        in_specs=[VMEM, ANY],
         out_specs=(ANY, ANY),
         scratch_shapes=[
-            pltpu.VMEM((slots, both), BF16),
+            pltpu.VMEM(got.shape, BF16),
             pltpu.VMEM((rows, both), F32),
-            DMA((4,)),
-            DMA((4,)),
+            DMA((8,)),
+            DMA((8,)),
         ],
-        compiler_params=params(8),
+        compiler_params=params(12),
         cost_estimate=cost(2 * 256 * 256 * 2048, 4 * 10**6),
         name="sums",
-    )(*lists, got)
+    )(asked, stay(got))
 
 
 def final_kernel(
@@ -422,49 +412,39 @@
     return (blocks[0],) + tuple(turn(blocks[N_Y - r], r) for r in range(1, N_Y))
 
 
-def exchange(x, axes):
-    return lax.all_to_all(x, axes, split_axis=0, concat_axis=0, tiled=True)
+def exchange(x):
+    return lax.all_to_all(x, ("dp", "y", "core"), split_axis=0, concat_axis=0, tiled=True)
 
 
 def program(tokens, out_grad, down_rows, up_rows, requests, places, gate_weights):
     row_count, width = down_rows.shape
     _, devices, capacity = requests.shape
     slots = devices * capacity
-    peers = devices // N_Y
     y = lax.axis_index("y")
 
-    def column(x):
-        wide = x.reshape(peers, slots // peers, x.shape[1])
-        return exchange(wide, ("dp", "core")).reshape(x.shape)
-
-    tables = gathered([jnp.concatenate([down_rows, up_rows], axis=1)] * N_Y)
-    asked = column(expand_ids(requests[0]))
+    asked = exchange(turn_ids(requests[0]))
     slot_of = jnp.transpose(places[0])
-    slot_of = (slot_of & ~15) | ((slot_of & 2) << 2) | ((slot_of & 12) >> 1) | (slot_of & 1)
     weight = build_weight(slot_of, jnp.transpose(gate_weights[0]), slots)
-    rows = gather_rows(asked, tables, 2 * width)
-    arrived = column(rows)
-    lists = gathered([asked] * N_Y)
     block = slot_of.shape[1] // N_Y
     blocks = [
         lax.dynamic_slice_in_dim(slot_of, ((y + r) & (N_Y - 1)) * block, block, 1) for r in range(N_Y)
     ]
     chip_places = gathered(blocks)
-    far = gather_rows(lists[2], tables, width)
-    opposite = column(far)
-    down = arrived[:, :width]
+    outgoing, far = gather_rows(asked, capacity, down_rows, up_rows)
+    arrived = exchange(outgoing)
+    down = arrived[:, :, :width]
     above, below = turn(down, 1), turn(down, 3)
+    opposite = exchange(far)
     coef, part = local_terms(tokens, out_grad, arrived, weight)
-    part = part.reshape(devices, capacity, 2 * width)
-    got = exchange(part, ("dp", "core", "y")).reshape(slots, 2 * width)
     small = compact(coef, slot_of)
     chip_coef = gathered(small)
-    down_all = (down, above, opposite, below)
+    got = exchange(part)
+    down_all = [x.reshape(slots, width) for x in (down, above, opposite, below)]
     give = final_product(False, chip_coef, chip_places, down_all)
     other = lax.ppermute(give, "core", [(0, 1), (1, 0)])
     keep = final_product(True, chip_coef, chip_places, down_all)
     input_grad = (keep.astype(F32) + other.astype(F32)).astype(BF16)
-    down_grad, up_grad = sum_rows(lists, got, row_count)
+    down_grad, up_grad = sum_rows(asked, got, row_count)
     return (input_grad, down_grad, up_grad)
 
 

time: 165 us -> 156 us (0.945)
  blocking collectives: 17 us -> 55.4 us
  waiting for transfers between devices: 49.1 us -> 10.9 us
  starting transfers between devices: 43.3 us -> 34.7 us
  Pallas kernels: 35.6 us -> 38.1 us
  local copies, waits for them, and re-layouts: 15 us -> 12.9 us
    all_to_all x1 -> x2, blocking collectives: 17 us -> 55.4 us  [exchange(): lax.all_to_all(x, ('dp', 'y', 'core'), split_axis=0, concat_axis=0, tiled...]
    all_to_all x3 -> x2, waiting for transfers between devices: 20.7 us -> 0.01 us  [exchange(): lax.all_to_all(x, ('dp', 'y', 'core'), split_axis=0, concat_axis=0, tiled...]
    ppermute x14 -> x8, waiting for transfers between devices: 28.4 us -> 10.9 us  [turn(): return lax.ppermute(x, 'y', [(i, (i - r) % N_Y) for i in range(N_Y)])]
    all_to_all x3 -> x2, starting transfers between devices: 21.6 us -> 16.6 us  [exchange(): lax.all_to_all(x, ('dp', 'y', 'core'), split_axis=0, concat_axis=0, tiled...]
    ppermute x14 -> x8, starting transfers between devices: 18.2 us -> 13.7 us  [turn(): return lax.ppermute(x, 'y', [(i, (i - r) % N_Y) for i in range(N_Y)])]
    pallas_call x4 -> x3, Pallas kernels: 8.2 us -> 10.2 us  [the longest x1 5.2 us: gather_rows(): pl.pallas_call(gather_kernel, out_shape=tuple((jax.ShapeDtypeStruct(x, BF...]
    unnamed x13 -> x20, local copies, waits for them, and re-layouts: 4.74 us -> 3.56 us
    reshape x2 -> x4, local copies, waits for them, and re-layouts: 7.15 us -> 6.64 us  [program(): down_all = [x.reshape(slots, width) for x in (down, above, opposite, below)]]
  transfers between devices with their start and end apart: 18 -> 11, of which waited for: 7 -> 1; matrix products, arithmetic and copies ran while one was open for 6% -> 6% of each run, Pallas kernels for 20% -> 20%
where the time goes in v5:
time: 156 us; the launch traced here: 155 us
  blocking collectives  55.4 us (36%)
  Pallas kernels  38.1 us (24%)
  starting transfers between devices  34.7 us (22%)
  local copies, waits for them, and re-layouts  12.9 us (8%)
  waiting for transfers between devices  10.9 us (7%)
  other arithmetic  2.59 us (2%)
    all_to_all x2, blocking collectives, exchange(): lax.all_to_all(x, ('dp', 'y', 'core'), split_axis=0, concat_axis=0, tiled...  55.4 us
    all_to_all x2, starting transfers between devices, exchange(): lax.all_to_all(x, ('dp', 'y', 'core'), split_axis=0, concat_axis=0, tiled...  16.6 us
    pallas_call x1, Pallas kernels, local_terms(): pl.pallas_call(local_kernel, out_shape=(jax.ShapeDtypeStruct((slots, coun...  15.1 us
    ppermute x8, starting transfers between devices, turn(): return lax.ppermute(x, 'y', [(i, (i - r) % N_Y) for i in range(N_Y)])  13.7 us
    ppermute x8, waiting for transfers between devices, turn(): return lax.ppermute(x, 'y', [(i, (i - r) % N_Y) for i in range(N_Y)])  10.9 us
    pallas_call x2, Pallas kernels, final_product(): pl.pallas_call(functools.partial(final_kernel, mine), out_shape=jax.Shape...  7.38 us
    reshape x4, local copies, waits for them, and re-layouts, program(): down_all = [x.reshape(slots, width) for x in (down, above, opposite, below)]  6.64 us
    pallas_call x1, Pallas kernels, gather_rows(): pl.pallas_call(gather_kernel, out_shape=tuple((jax.ShapeDtypeStruct(x, BF...  5.2 us
  transfers between devices with their start and end apart: 11, of which 1 were waited for; matrix products, arithmetic and copies ran while one was open for 6% of the time, Pallas kernels for 20%

profile of v5, /device:TPU:1, one launch (start us, length us, event | category | flops | bytes accessed | tf_op | source)
XLA Modules:
  0.0 155.4 jit_solution(2061903033073457986)
XLA Ops:
  0.6 1.5 ids.1
  2.1 21.1 %all_to_all.26 = s32[128,1,128]{2,1,0:T(1,128)S(1)} all-to-all(s32[128,1,128]{2,1,0:T(1,128)} %bitcast.34), channel_id=1, replica_groups=mesh['dp'=16,'y'=4,'core'=2] {'dp','y','core'}, dimensions={0} | all-to-all | bytes 131072 | tf_op jit(solution)/shard_map/all_to_all | solution.py:416
  23.1 5.2 %gather.1 = (bf16[128,2,4096]{2,1,0:T(2,128)(2,1)S(1)}, bf16[128,2,2048]{2,1,0:T(2,128)(2,1)}) custom-call(s32[128,128]{1,0:T(8,128)S(1)} %bitcast.31, bf16[64,2048]{1,0:T(8,128)(2,1)} %down_ref.1, bf16[64,2048]{1,0:T(8,128)(2,1)} %up_ref.1), custom_call_target="tpu_custom_call" | custom-call | flops 402653184 | bytes 4000000 | tf_op jit(solution)/shard_map/gather/pallas_call | solution.py:121
  28.3 34.3 %all_to_all.27.rows_hbm = bf16[128,2,4096]{2,1,0:T(2,128)(2,1)S(1)} all-to-all(bf16[128,2,4096]{2,1,0:T(2,128)(2,1)S(1)} %get-tuple-element.13), channel_id=1, replica_groups=mesh['dp'=16,'y'=4,'core'=2] {'dp','y','core'}, dimensions={0} | all-to-all | bytes 4194304 | tf_op jit(solution)/shard_map/all_to_all | solution.py:416
  62.7 5.9 %all-to-all-start.2 = ((bf16[128,2,2048]{2,1,0:T(2,128)(2,1)}), bf16[128,2,2048]{2,1,0:T(2,128)(2,1)}, u32[]{:S(2)}, u32[]{:S(2)}) async-start(bf16[128,2,2048]{2,1,0:T(2,128)(2,1)} %get-tuple-element.19), calls=%async_computation.2 | async-start | bytes 2097152 | tf_op jit(solution)/shard_map/all_to_all | solution.py:416
  68.6 0.0 copy-done.4
  68.6 0.0 copy-done.6
  68.6 2.8 %weight.1.weight_hbm = f32[4,256,512]{2,1,0:T(8,128)S(1)} custom-call(s32[16,2048]{1,0:T(8,128)S(1)} %bitcast.29, f32[16,2048]{1,0:T(8,128)S(1)} %bitcast.33), custom_call_target="tpu_custom_call" | custom-call | flops 25165824 | bytes 2097152 | tf_op jit(solution)/shard_map/weight/pallas_call | solution.py:149
  71.5 0.0 copy-done.7
  71.5 0.0 copy-start.3
  71.5 1.3 copy-done.3
  72.9 2.0 %slice.4 = bf16[128,2,2048]{2,1,0:T(2,128)(2,1)} slice(bf16[128,2,4096]{2,1,0:T(2,128)(2,1)S(1)} %all_to_all.27.rows_hbm), slice={[0:128], [0:2], [0:2048]} | slice | bytes 2097152 | tf_op jit(solution)/shard_map/slice | solution.py:435
  74.9 2.8 %collective-permute-start.6 = (bf16[128,2,2048]{2,1,0:T(2,128)(2,1)}, bf16[128,2,2048]{2,1,0:T(2,128)(2,1)S(1)}, u32[]{:S(2)}, u32[]{:S(2)}) collective-permute-start(bf16[128,2,2048]{2,1,0:T(2,128)(2,1)} %slice.4), channel_id=1, source_target_pairs={{0,6},{2,0},{4,2},{6,4},{1,7},{3,1},{5,3},{7,5},{8,14},{10,8},{12,... | collective-permute-start | bytes 3145736 | tf_op jit(solution)/shard_map/ppermute | solution.py:408
  77.6 0.0 collective-permute-start.7
  77.6 15.1 %local.1 = (bf16[256,2048]{1,0:T(8,128)(2,1)}, bf16[128,2,4096]{2,1,0:T(2,128)(2,1)}) custom-call(bf16[2048,2048]{1,0:T(8,128)(2,1)} %tok_hbm.1, bf16[2048,2048]{1,0:T(8,128)(2,1)} %grad_hbm.1, bf16[128,2,4096]{2,1,0:T(2,128)(2,1)} %copy-done.7, f32[4,256,512]{2,1,0:T(8,128)} %copy-done.3), custom_call_target="tpu_custom_call" | custom-call | flops 8589934592 | bytes 25165824 | tf_op jit(solution)/shard_map/local/pallas_call | solution.py:245
  92.7 0.0 all-to-all-done.2
  92.7 10.6 %all-to-all-start.3 = ((bf16[128,2,4096]{2,1,0:T(2,128)(2,1)}), bf16[128,2,4096]{2,1,0:T(2,128)(2,1)}, u32[]{:S(2)}, u32[]{:S(2)}) async-start(bf16[128,2,4096]{2,1,0:T(2,128)(2,1)} %get-tuple-element.20), calls=%async_computation.3 | async-start | bytes 4194304 | tf_op jit(solution)/shard_map/all_to_all | solution.py:416
  103.4 0.6 dynamic-slice_bitcast_fusion
  104.0 2.6 %collective-permute-start.3 = (s32[16,512]{1,0:T(8,128)S(1)}, s32[16,512]{1,0:T(8,128)S(1)}, u32[]{:S(2)}, u32[]{:S(2)}) collective-permute-start(s32[16,512]{1,0:T(8,128)S(1)} %get-tuple-element.24), channel_id=1, source_target_pairs={{0,6},{2,0},{4,2},{6,4},{1,7},{3,1},{5,3},{7,5},{8,14},{10,8},{12,... | collective-permute-start | bytes 98312 | tf_op jit(solution)/shard_map/ppermute | solution.py:408
  106.6 0.5 collective-permute-start.4
  107.1 0.6 collective-permute-start.5
  107.7 2.6 %compact.1 = (bf16[16,512]{1,0:T(8,128)(2,1)S(1)}, bf16[16,512]{1,0:T(8,128)(2,1)S(1)}, bf16[16,512]{1,0:T(8,128)(2,1)S(1)}, bf16[16,512]{1,0:T(8,128)(2,1)S(1)}) custom-call(bf16[256,2048]{1,0:T(8,128)(2,1)S(1)} %copy-done.5, s32[16,2048]{1,0:T(8,128)S(1)} %bitcast.30), custom_call_target="tpu_custom_call" | custom-call | flops 16777216 | bytes 1048576 | tf_op jit(solution)/shard_map/compact/pallas_call | solution.py:292
  110.3 10.9 %collective-permute-done.3.p1 = s32[16,512]{1,0:T(8,128)S(1)} collective-permute-done((s32[16,512]{1,0:T(8,128)S(1)}, s32[16,512]{1,0:T(8,128)S(1)}, u32[]{:S(2)}, u32[]{:S(2)}) %collective-permute-start.3) | collective-permute-done | bytes 32800 | tf_op jit(solution)/shard_map/ppermute | solution.py:408
  121.2 5.9 %collective-permute-start = (bf16[16,512]{1,0:T(8,128)(2,1)S(1)}, bf16[16,512]{1,0:T(8,128)(2,1)S(1)}, u32[]{:S(2)}, u32[]{:S(2)}) collective-permute-start(bf16[16,512]{1,0:T(8,128)(2,1)S(1)} %get-tuple-element.16), channel_id=1, source_target_pairs={{0,6},{2,0},{4,2},{6,4},{1,7},{3,1},{5,3},{7,5},{8,14},{10,8},{12,... | collective-permute-start | bytes 49160 | tf_op jit(solution)/shard_map/ppermute | solution.py:408
  127.1 0.0 collective-permute-done.6
  127.1 0.6 collective-permute-start.1
  127.7 0.0 collective-permute-done.7
  127.7 0.8 collective-permute-start.2
  128.4 1.5 reshape.38.d2
  129.9 0.0 copy-done.9
  129.9 1.5 reshape.36.d0
  131.4 1.5 reshape.37.d1
  132.9 2.2 %reshape.39.d3 = bf16[256,2048]{1,0:T(8,128)(2,1)} reshape(bf16[128,2,2048]{2,1,0:T(2,128)(2,1)} %copy-done.9) | data formatting | bytes 2097152 | tf_op jit(solution)/shard_map/reshape | solution.py:442
  135.1 0.0 collective-permute-done.4.p2
  135.1 0.0 collective-permute-done.5.p3
  135.1 0.0 collective-permute-done.c1
  135.1 0.0 collective-permute-done.1.c2
  135.1 0.0 collective-permute-done.2.c3
  135.2 0.0 copy-start
  135.2 1.2 copy-done
  136.4 3.7 %give.1 = bf16[256,2048]{1,0:T(8,128)(2,1)} custom-call(bf16[16,512]{1,0:T(8,128)(2,1)S(1)} %get-tuple-element.15.c0, bf16[16,512]{1,0:T(8,128)(2,1)S(1)} %collective-permute-done.c1, bf16[16,512]{1,0:T(8,128)(2,1)S(1)} %collective-permute-done.1.c2, bf16[16,512]{1,0:T(8,128)(2,1)S(1)} %collective-permute-done.2.c3, s32[16,512]{1,0:T(8,128)S(1)} %get-tuple-element.25.p0, ...), custom_call_target="tpu_custom_call" | custom-call | flops 1073741824 | bytes 6291456 | tf_op jit(solution)/shard_map/give/pallas_call | solution.py:390
  140.1 4.4 %collective-permute-start.8 = (bf16[256,2048]{1,0:T(8,128)(2,1)}, bf16[256,2048]{1,0:T(8,128)(2,1)}, u32[]{:S(2)}, u32[]{:S(2)}) collective-permute-start(bf16[256,2048]{1,0:T(8,128)(2,1)} %give.1), channel_id=1, source_target_pairs={{0,1},{1,0},{2,3},{3,2},{4,5},{5,4},{6,7},{7,6},{8,9},{9,8},{10,11... | collective-permute-start | bytes 3145736 | tf_op jit(solution)/shard_map/ppermute | solution.py:444
  144.5 3.7 %keep.1 = bf16[256,2048]{1,0:T(8,128)(2,1)S(1)} custom-call(bf16[16,512]{1,0:T(8,128)(2,1)S(1)} %get-tuple-element.15.c0, bf16[16,512]{1,0:T(8,128)(2,1)S(1)} %collective-permute-done.c1, bf16[16,512]{1,0:T(8,128)(2,1)S(1)} %collective-permute-done.1.c2, bf16[16,512]{1,0:T(8,128)(2,1)S(1)} %collective-permute-done.2.c3, s32[16,512]{1,0:T(8,128)S(1)} %get-tuple-element.25.p0, ...), custom_call_target="tpu_custom_call" | custom-call | flops 1073741824 | bytes 6291456 | tf_op jit(solution)/shard_map/keep/pallas_call | solution.py:390
  148.2 1.0 copy-done.1
  149.2 0.0 all-to-all-done.3.got_hbm
  149.2 3.6 %sums.1 = (f32[64,2048]{1,0:T(8,128)}, f32[64,2048]{1,0:T(8,128)}) custom-call(s32[128,128]{1,0:T(8,128)S(1)} %bitcast.32, bf16[128,2,4096]{2,1,0:T(2,128)(2,1)} %all-to-all-done.3.got_hbm), custom_call_target="tpu_custom_call" | custom-call | flops 268435456 | bytes 4000000 | tf_op jit(solution)/shard_map/sums/pallas_call | solution.py:330
  152.8 0.0 collective-permute-done.8
  152.8 2.6 %add_convert_fusion = bf16[256,2048]{1,0:T(8,128)(2,1)} fusion(bf16[256,2048]{1,0:T(8,128)(2,1)} %collective-permute-done.8, bf16[256,2048]{1,0:T(8,128)(2,1)S(1)} %copy-done.2), kind=kLoop, calls=%fused_computation | loop fusion | flops 2097152 | bytes 3145728 | tf_op jit(solution)/shard_map/convert_element_type | solution.py:446
  (11 shorter events, 0.0 us)
Async XLA Ops:
  62.7 8.8 %copy-start.7 = (bf16[128,2,4096]{2,1,0:T(2,128)(2,1)}, bf16[128,2,4096]{2,1,0:T(2,128)(2,1)S(1)}, u32[]{:S(2)}) copy-start(bf16[128,2,4096]{2,1,0:T(2,128)(2,1)S(1)} %all_to_all.27.rows_hbm) | copy-start | bytes 6291460
  62.7 6.0 %copy-start.4 = (s32[1,2048,16]{1,2,0:T(8,128)S(1)}, s32[1,2048,16]{1,2,0:T(8,128)}, u32[]{:S(2)}) copy-start(s32[1,2048,16]{1,2,0:T(8,128)} %param.12) | copy-start | bytes 393220
  62.7 6.0 %copy-start.6 = (f32[1,2048,16]{1,2,0:T(8,128)S(1)}, f32[1,2048,16]{1,2,0:T(8,128)}, u32[]{:S(2)}) copy-start(f32[1,2048,16]{1,2,0:T(8,128)} %param.13) | copy-start | bytes 393220
  62.7 30.0 %all-to-all-start.2 = ((bf16[128,2,2048]{2,1,0:T(2,128)(2,1)}), bf16[128,2,2048]{2,1,0:T(2,128)(2,1)}, u32[]{:S(2)}, u32[]{:S(2)}) async-start(bf16[128,2,2048]{2,1,0:T(2,128)(2,1)} %get-tuple-element.19), calls=%async_computation.2 | async-start | bytes 2097152 | tf_op jit(solution)/shard_map/all_to_all | solution.py:416
  71.5 1.4 copy-start.3
  74.9 52.2 %collective-permute-start.6 = (bf16[128,2,2048]{2,1,0:T(2,128)(2,1)}, bf16[128,2,2048]{2,1,0:T(2,128)(2,1)S(1)}, u32[]{:S(2)}, u32[]{:S(2)}) collective-permute-start(bf16[128,2,2048]{2,1,0:T(2,128)(2,1)} %slice.4), channel_id=1, source_target_pairs={{0,6},{2,0},{4,2},{6,4},{1,7},{3,1},{5,3},{7,5},{8,14},{10,8},{12,... | collective-permute-start | bytes 3145736 | tf_op jit(solution)/shard_map/ppermute | solution.py:408
  77.6 50.0 %collective-permute-start.7 = (bf16[128,2,2048]{2,1,0:T(2,128)(2,1)}, bf16[128,2,2048]{2,1,0:T(2,128)(2,1)S(1)}, u32[]{:S(2)}, u32[]{:S(2)}) collective-permute-start(bf16[128,2,2048]{2,1,0:T(2,128)(2,1)} %slice.4), channel_id=1, source_target_pairs={{0,2},{2,4},{4,6},{6,0},{1,3},{3,5},{5,7},{7,1},{8,10},{10,12},{12... | collective-permute-start | bytes 3145736 | tf_op jit(solution)/shard_map/ppermute | solution.py:408
  92.7 15.0 %copy-start.5 = (bf16[256,2048]{1,0:T(8,128)(2,1)S(1)}, bf16[256,2048]{1,0:T(8,128)(2,1)}, u32[]{:S(2)}) copy-start(bf16[256,2048]{1,0:T(8,128)(2,1)} %get-tuple-element.14.coef_ref) | copy-start | bytes 3145732
  92.7 56.5 %all-to-all-start.3 = ((bf16[128,2,4096]{2,1,0:T(2,128)(2,1)}), bf16[128,2,4096]{2,1,0:T(2,128)(2,1)}, u32[]{:S(2)}, u32[]{:S(2)}) async-start(bf16[128,2,4096]{2,1,0:T(2,128)(2,1)} %get-tuple-element.20), calls=%async_computation.3 | async-start | bytes 4194304 | tf_op jit(solution)/shard_map/all_to_all | solution.py:416
  104.0 17.2 %collective-permute-start.3 = (s32[16,512]{1,0:T(8,128)S(1)}, s32[16,512]{1,0:T(8,128)S(1)}, u32[]{:S(2)}, u32[]{:S(2)}) collective-permute-start(s32[16,512]{1,0:T(8,128)S(1)} %get-tuple-element.24), channel_id=1, source_target_pairs={{0,6},{2,0},{4,2},{6,4},{1,7},{3,1},{5,3},{7,5},{8,14},{10,8},{12,... | collective-permute-start | bytes 98312 | tf_op jit(solution)/shard_map/ppermute | solution.py:408
  106.6 28.5 %collective-permute-start.4 = (s32[16,512]{1,0:T(8,128)}, s32[16,512]{1,0:T(8,128)S(1)}, u32[]{:S(2)}, u32[]{:S(2)}) collective-permute-start(s32[16,512]{1,0:T(8,128)} %get-tuple-element.26), channel_id=1, source_target_pairs={{0,4},{2,6},{4,0},{6,2},{1,5},{3,7},{5,1},{7,3},{8,12},{10,14},{12... | collective-permute-start | bytes 98312 | tf_op jit(solution)/shard_map/ppermute | solution.py:408
  107.1 28.0 %collective-permute-start.5 = (s32[16,512]{1,0:T(8,128)}, s32[16,512]{1,0:T(8,128)S(1)}, u32[]{:S(2)}, u32[]{:S(2)}) collective-permute-start(s32[16,512]{1,0:T(8,128)} %get-tuple-element.23), channel_id=1, source_target_pairs={{0,2},{2,4},{4,6},{6,0},{1,3},{3,5},{5,7},{7,1},{8,10},{10,12},{12... | collective-permute-start | bytes 98312 | tf_op jit(solution)/shard_map/ppermute | solution.py:408
  121.2 13.9 %collective-permute-start = (bf16[16,512]{1,0:T(8,128)(2,1)S(1)}, bf16[16,512]{1,0:T(8,128)(2,1)S(1)}, u32[]{:S(2)}, u32[]{:S(2)}) collective-permute-start(bf16[16,512]{1,0:T(8,128)(2,1)S(1)} %get-tuple-element.16), channel_id=1, source_target_pairs={{0,6},{2,0},{4,2},{6,4},{1,7},{3,1},{5,3},{7,5},{8,14},{10,8},{12,... | collective-permute-start | bytes 49160 | tf_op jit(solution)/shard_map/ppermute | solution.py:408
  127.1 1.3 copy-start.8
  127.1 8.0 %collective-permute-start.1 = (bf16[16,512]{1,0:T(8,128)(2,1)S(1)}, bf16[16,512]{1,0:T(8,128)(2,1)S(1)}, u32[]{:S(2)}, u32[]{:S(2)}) collective-permute-start(bf16[16,512]{1,0:T(8,128)(2,1)S(1)} %get-tuple-element.17), channel_id=1, source_target_pairs={{0,4},{2,6},{4,0},{6,2},{1,5},{3,7},{5,1},{7,3},{8,12},{10,14},{12... | collective-permute-start | bytes 49160 | tf_op jit(solution)/shard_map/ppermute | solution.py:408
  127.7 2.3 %copy-start.9 = (bf16[128,2,2048]{2,1,0:T(2,128)(2,1)}, bf16[128,2,2048]{2,1,0:T(2,128)(2,1)S(1)}, u32[]{:S(2)}) copy-start(bf16[128,2,2048]{2,1,0:T(2,128)(2,1)S(1)} %collective-permute-done.7) | copy-start | bytes 3145732
  127.7 7.5 %collective-permute-start.2 = (bf16[16,512]{1,0:T(8,128)(2,1)S(1)}, bf16[16,512]{1,0:T(8,128)(2,1)S(1)}, u32[]{:S(2)}, u32[]{:S(2)}) collective-permute-start(bf16[16,512]{1,0:T(8,128)(2,1)S(1)} %get-tuple-element.18), channel_id=1, source_target_pairs={{0,2},{2,4},{4,6},{6,0},{1,3},{3,5},{5,7},{7,1},{8,10},{10,12},{12... | collective-permute-start | bytes 49160 | tf_op jit(solution)/shard_map/ppermute | solution.py:408
  135.2 1.2 copy-start
  140.1 12.7 %collective-permute-start.8 = (bf16[256,2048]{1,0:T(8,128)(2,1)}, bf16[256,2048]{1,0:T(8,128)(2,1)}, u32[]{:S(2)}, u32[]{:S(2)}) collective-permute-start(bf16[256,2048]{1,0:T(8,128)(2,1)} %give.1), channel_id=1, source_target_pairs={{0,1},{1,0},{2,3},{3,2},{4,5},{5,4},{6,7},{7,6},{8,9},{9,8},{10,11... | collective-permute-start | bytes 3145736 | tf_op jit(solution)/shard_map/ppermute | solution.py:444
  148.2 1.0 copy-start.1
  149.2 3.6 %copy-start.2 = (bf16[256,2048]{1,0:T(8,128)(2,1)S(1)}, bf16[256,2048]{1,0:T(8,128)(2,1)}, u32[]{:S(2)}) copy-start(bf16[256,2048]{1,0:T(8,128)(2,1)} %copy-done.1) | copy-start | bytes 3145732

commit v6 on v4

--- a/solution.py
+++ b/solution.py
@@ -163,105 +163,98 @@
     )(places, gates)
 
 
-def local_kernel(
-    tok_hbm, grad_hbm, rows_hbm, weight_hbm, coef_hbm, part_hbm,
-    tok, grad, rows, weight, gated, coef, half, part,
-    tok_sems, grad_sems, row_sems, weight_sems, coef_sem, part_sems,
+def half_kernel(
+    first, lead_hbm, other_hbm, rows_hbm, side_hbm, extra_hbm, part_hbm,
+    lead, other, rows, side, left, slope, half, part,
+    lead_sems, other_sems, row_sem, side_sems, extra_sems, part_sems,
 ):
-    block = weight.shape[2]
-    width = tok.shape[1]
-    down = rows.at[0]
-    up = rows.at[1]
-    row_in = [
-        copy(rows_hbm.at[:, pl.ds(i * width, width)], rows.at[i], row_sems.at[i]) for i in range(2)
-    ]
-    weight_in = [copy(weight_hbm.at[c], weight.at[c], weight_sems.at[c]) for c in range(N_Y)]
-    tok_in = load_rows(tok_hbm, tok, tok_sems, 8)
-    grad_in = load_rows(grad_hbm, grad, grad_sems, 8)
+    block = side.shape[2]
+    width = lead.shape[1]
+    step = width // N_Y
+    chunk = part.shape[:2] + (step,)
+    rows_in = copy(rows_hbm, rows, row_sem)
+    side_in = [copy(side_hbm.at[c], side.at[c], side_sems.at[c]) for c in range(N_Y)]
+    lead_in = load_rows(lead_hbm, lead, lead_sems, 8)
+    other_in = load_rows(other_hbm, other, other_sems, 8)
+    sent = []
 
     def begin(c):
-        tok_in[2 * c].start()
-        tok_in[2 * c + 1].start()
-        if c == 0:
-            row_in[1].start()
-        grad_in[2 * c].start()
-        grad_in[2 * c + 1].start()
-        weight_in[c].start()
-
-    step = width // N_Y
-    sent = []
-
-    def parts(tokens, last):
-        for j in range(2 * N_Y):
-            left, right = ((coef, tok), (gated, grad))[j // N_Y]
+        for i in (2 * c, 2 * c + 1):
+            lead_in[i].start()
+        side_in[c].start()
+        for i in (2 * c, 2 * c + 1):
+            other_in[i].start()
+
+    def parts(c, last):
+        tokens = pl.ds((c - 1) * block, 2 * block)
+        for i in range(2 * c - 2, 2 * c + 2):
+            other_in[i].wait()
+        for j in range(N_Y):
             cols = pl.ds(j * step, step)
-            here = dot(left[:, tokens], right[tokens, pl.ds(j % N_Y * step, step)], NN)
+            here = dot(left[:, tokens], other[tokens, cols], NN)
             if not last:
                 half[:, cols] = here
                 continue
-            part[:, cols] = (half[:, cols] + here).astype(BF16)
-            c = copy(part.at[:, cols], part_hbm.at[:, cols], part_sems.at[j])
-            c.start()
-            sent.append(c)
-
-    row_in[0].start()
+            part[:, :, cols] = (half[:, cols] + here).astype(BF16).reshape(chunk)
+            out = copy(part.at[:, :, cols], part_hbm.at[:, :, cols], part_sems.at[j])
+            out.start()
+            sent.append(out)
+
+    rows_in.start()
     begin(0)
     begin(1)
-    row_in[0].wait()
+    rows_in.wait()
     for c in range(N_Y):
         here = pl.ds(c * block, block)
-        tok_in[2 * c].wait()
-        tok_in[2 * c + 1].wait()
-        pre = dot(down[...], tok[here, :], NT)
-        if c == 0:
-            row_in[1].wait()
-        grad_in[2 * c].wait()
-        grad_in[2 * c + 1].wait()
-        weight_in[c].wait()
+        lead_in[2 * c].wait()
+        lead_in[2 * c + 1].wait()
+        side_in[c].wait()
         if c + 2 < N_Y:
             begin(c + 2)
-        back = dot(up[...], grad[here, :], NT)
-        gate = weight[c]
-        cdf = 0.5 * (1.0 + lax.erf(pre * SQRT_HALF))
-        density = INV_ROOT_TAU * jnp.exp(-0.5 * pre * pre)
-        gated[:, here] = (gate * (pre * cdf)).astype(BF16)
-        coef[:, here] = (gate * (cdf + pre * density) * back).astype(BF16)
+        found = dot(rows[...], lead[here, :], NT)
+        if first:
+            cdf = 0.5 * (1.0 + lax.erf(found * SQRT_HALF))
+            density = INV_ROOT_TAU * jnp.exp(-0.5 * found * found)
+            left[:, here] = (side[c] * (found * cdf)).astype(BF16)
+            slope[c] = side[c] * (cdf + found * density)
+            out = copy(slope.at[c], extra_hbm.at[c], extra_sems.at[c])
+        else:
+            left[:, here] = (side[c] * found).astype(BF16)
+            out = copy(left.at[:, here], extra_hbm.at[:, here], extra_sems.at[c])
+        out.start()
+        sent.append(out)
         if c == N_Y // 2 - 1:
-            parts(pl.ds(0, N_Y // 2 * block), False)
-    out = copy(coef, coef_hbm, coef_sem)
-    out.start()
-    sent.append(out)
-    parts(pl.ds(N_Y // 2 * block, N_Y // 2 * block), True)
-    for c in sent:
-        c.wait()
-
-
-def local_terms(tokens, grads, rows, weight):
-    count, width = tokens.shape
+            parts(c, False)
+    parts(N_Y - 1, True)
+    for out in sent:
+        out.wait()
+
+
+def half_terms(first, lead, other, rows, side, devices):
+    count, width = lead.shape
     slots = rows.shape[0]
-    return pl.pallas_call(
-        local_kernel,
-        out_shape=(
-            jax.ShapeDtypeStruct((slots, count), BF16),
-            jax.ShapeDtypeStruct((slots, 2 * width), BF16),
-        ),
+    chunks = (devices, slots // devices, width)
+    extra = (side.shape, F32) if first else ((slots, count), BF16)
+    return pl.pallas_call(
+        functools.partial(half_kernel, first),
+        out_shape=(jax.ShapeDtypeStruct(*extra), jax.ShapeDtypeStruct(chunks, BF16)),
         in_specs=[ANY] * 4,
         out_specs=(ANY,) * 2,
         scratch_shapes=[
             pltpu.VMEM((count, width), BF16),
             pltpu.VMEM((count, width), BF16),
-            pltpu.VMEM((2, slots, width), BF16),
-            pltpu.VMEM(weight.shape, F32),
+            pltpu.VMEM((slots, width), BF16),
+            pltpu.VMEM(side.shape, F32),
             pltpu.VMEM((slots, count), BF16),
-            pltpu.VMEM((slots, count), BF16),
-            pltpu.VMEM((slots, 2 * width), F32),
-            pltpu.VMEM((slots, 2 * width), BF16),
-            DMA((8,)), DMA((8,)), DMA((2,)), DMA((4,)), DMA, DMA((8,)),
+            pltpu.VMEM(side.shape, F32),
+            pltpu.VMEM((slots, width), F32),
+            pltpu.VMEM(chunks, BF16),
+            DMA((8,)), DMA((8,)), DMA, DMA((4,)), DMA((4,)), DMA((4,)),
         ],
         compiler_params=params(56),
-        cost_estimate=cost(8 * count * width * slots, 24 << 20),
-        name="local",
-    )(tokens, grads, stay(rows), stay(weight))
+        cost_estimate=cost(4 * count * width * slots, 24 << 20),
+        name="first" if first else "second",
+    )(lead, other, stay(rows), stay(side))
 
 
 def compact_kernel(coef_ref, places_ref, c0, c1, c2, c3):
@@ -310,24 +303,22 @@
     return total.astype(BF16)
 
 
-def sums_kernel(a0, a1, a2, a3, got_hbm, down_hbm, up_hbm, got, sums, sems, out_sems):
-    rows, width = down_hbm.shape
-    block = 1024
-    pieces = 2 * width // block
-    copies = [
-        copy(got_hbm.at[:, pl.ds(j * block, block)], got.at[:, pl.ds(j * block, block)], sems.at[j])
-        for j in range(pieces)
-    ]
-    for c in copies:
-        c.start()
+def sums_kernel(a0, a1, a2, a3, got_hbm, out_hbm, got, sums, sems, out_sems):
+    rows, width = sums.shape
+    devices, capacity, _ = got.shape
+    block = 512
+    copies = []
+    for j in range(width // block):
+        cols = pl.ds(j * block, block)
+        copies.append(copy(got_hbm.at[:, :, cols], got.at[:, :, cols], sems.at[j]))
+        copies[j].start()
     hits = own_hits([a[...] for a in (a0, a1, a2, a3)], rows)
     sent = []
-    for j in range(pieces):
+    for j in range(width // block):
         copies[j].wait()
         cols = pl.ds(j * block, block)
-        sums[:, cols] = dot(hits, got[:, cols], TN)
-        out = (down_hbm, up_hbm)[2 * j // pieces]
-        c = copy(sums.at[:, cols], out.at[:, pl.ds(j * block % width, block)], out_sems.at[j])
+        sums[:, cols] = dot(hits, got[:, :, cols].reshape(devices * capacity, block), TN)
+        c = copy(sums.at[:, cols], out_hbm.at[:, cols], out_sems.at[j])
         c.start()
         sent.append(c)
     for c in sent:
@@ -335,27 +326,25 @@
 
 
 def sum_rows(lists, got, rows):
-    slots, both = got.shape
-    out = jax.ShapeDtypeStruct((rows, both // 2), F32)
+    width = got.shape[2]
     return pl.pallas_call(
         sums_kernel,
-        out_shape=(out, out),
+        out_shape=jax.ShapeDtypeStruct((rows, width), F32),
         in_specs=[VMEM] * N_Y + [ANY],
-        out_specs=(ANY, ANY),
+        out_specs=ANY,
         scratch_shapes=[
-            pltpu.VMEM((slots, both), BF16),
-            pltpu.VMEM((rows, both), F32),
+            pltpu.VMEM(got.shape, BF16),
+            pltpu.VMEM((rows, width), F32),
             DMA((4,)),
             DMA((4,)),
         ],
-        compiler_params=params(8),
-        cost_estimate=cost(2 * 256 * 256 * 2048, 4 * 10**6),
-        name="sums",
-    )(*lists, got)
+        compiler_params=params(12),
+        cost_estimate=cost(2 * 256 * 256 * 2048, 2 * 10**6),
+    )(*lists, stay(got))
 
 
 def final_kernel(
-    mine, c0, c1, c2, c3, p0, p1, p2, p3, d0, d1, d2, d3, out_hbm, coef, rows, out, d_sems, out_sems
+    mine, c0, c1, c2, c3, p0, p1, p2, p3, d0, d1, d2a, d2b, d3, out_hbm, coef, rows, out, d_sems, out_sems
 ):
     core = lax.axis_index("core")
     which = core if mine else 1 - core
@@ -364,7 +353,7 @@
     topk = c0.shape[0]
     loads = []
     start = 0
-    for i, d in enumerate((d0, d1, d2, d3)):
+    for i, d in enumerate((d0, d1, d2a, d2b, d3)):
         loads.append(copy(d, rows.at[pl.ds(start, d.shape[0]), :], d_sems.at[i]))
         start += d.shape[0]
     for c in loads:
@@ -400,13 +389,13 @@
     return pl.pallas_call(
         functools.partial(final_kernel, mine),
         out_shape=jax.ShapeDtypeStruct((half, width), BF16),
-        in_specs=[VMEM] * 8 + [ANY] * 4,
+        in_specs=[VMEM] * 8 + [ANY] * 5,
         out_specs=ANY,
         scratch_shapes=[
             pltpu.VMEM((N_Y * slots, half), BF16),
             pltpu.VMEM((N_Y * slots, width), BF16),
             pltpu.VMEM((half, width), BF16),
-            DMA((4,)), DMA((4,)),
+            DMA((5,)), DMA((4,)),
         ],
         compiler_params=params(16),
         cost_estimate=cost(2 * half * 1024 * 2048, 6 << 20),
@@ -437,34 +426,35 @@
         wide = x.reshape(peers, slots // peers, x.shape[1])
         return exchange(wide, ("dp", "core")).reshape(x.shape)
 
-    tables = gathered([jnp.concatenate([down_rows, up_rows], axis=1)] * N_Y)
+    down_tables = gathered([down_rows] * N_Y)
     asked = column(expand_ids(requests[0]))
+    up_tables = gathered([up_rows] * N_Y)
     slot_of = jnp.transpose(places[0])
     slot_of = (slot_of & ~15) | ((slot_of & 2) << 2) | ((slot_of & 12) >> 1) | (slot_of & 1)
     weight = build_weight(slot_of, jnp.transpose(gate_weights[0]), slots)
-    rows = gather_rows(asked, tables, 2 * width)
-    arrived = column(rows)
+    down = column(gather_rows(asked, down_tables, width))
     lists = gathered([asked] * N_Y)
     block = slot_of.shape[1] // N_Y
     blocks = [
         lax.dynamic_slice_in_dim(slot_of, ((y + r) & (N_Y - 1)) * block, block, 1) for r in range(N_Y)
     ]
     chip_places = gathered(blocks)
-    far = gather_rows(lists[2], tables, width)
-    opposite = column(far)
-    down = arrived[:, :width]
+    up = column(gather_rows(asked, up_tables, width))
     above, below = turn(down, 1), turn(down, 3)
-    coef, part = local_terms(tokens, out_grad, arrived, weight)
-    part = part.reshape(devices, capacity, 2 * width)
-    got = exchange(part, ("dp", "core", "y")).reshape(slots, 2 * width)
+    slope, part_up = half_terms(True, tokens, out_grad, down, weight, devices)
+    got_up = exchange(part_up, ("dp", "core", "y"))
+    far = (turn(above[: slots // 2], 1), turn(below[slots // 2 :], 3))
+    coef, part_down = half_terms(False, out_grad, tokens, up, slope, devices)
     small = compact(coef, slot_of)
     chip_coef = gathered(small)
-    down_all = (down, above, opposite, below)
+    got_down = exchange(part_down, ("dp", "core", "y"))
+    up_grad = sum_rows(lists, got_up, row_count)
+    down_all = (down, above, *far, below)
     give = final_product(False, chip_coef, chip_places, down_all)
     other = lax.ppermute(give, "core", [(0, 1), (1, 0)])
     keep = final_product(True, chip_coef, chip_places, down_all)
     input_grad = (keep.astype(F32) + other.astype(F32)).astype(BF16)
-    down_grad, up_grad = sum_rows(lists, got, row_count)
+    down_grad = sum_rows(lists, got_down, row_count)
     return (input_grad, down_grad, up_grad)
 
 

time: 165 us -> 161 us (0.976)
  waiting for transfers between devices: 49.1 us -> 33.4 us
  starting transfers between devices: 43.3 us -> 51.9 us
  Pallas kernels: 35.6 us -> 42.4 us
  local copies, waits for them, and re-layouts: 15 us -> 10.1 us
    all_to_all x3 -> x4, waiting for transfers between devices: 20.7 us -> 3.37 us  [exchange(): return lax.all_to_all(x, axes, split_axis=0, concat_axis=0, tiled=True)]
    pallas_call x2 -> x4, Pallas kernels: 17.8 us -> 25.2 us  [the longest x2 20.2 us: half_terms(): pl.pallas_call(functools.partial(half_kernel, first), out_shape=(jax.Shap...]
    reshape x2 -> x0, local copies, waits for them, and re-layouts: 7.15 us -> none  [the longest x1 4.41 us: program(): part = part.reshape(devices, capacity, 2 * width)]
    all_to_all x3 -> x4, starting transfers between devices: 21.6 us -> 27.3 us  [exchange(): return lax.all_to_all(x, axes, split_axis=0, concat_axis=0, tiled=True)]
    ppermute x14 -> x19, starting transfers between devices: 18.2 us -> 23.4 us  [turn(): return lax.ppermute(x, 'y', [(i, (i - r) % N_Y) for i in range(N_Y)])]
    ppermute x1, starting transfers between devices: 3.52 us -> 1.27 us  [program(): other = lax.ppermute(give, 'core', [(0, 1), (1, 0)])]
    unnamed x13 -> x56, local copies, waits for them, and re-layouts: 4.74 us -> 6.96 us
    ppermute x14 -> x19, waiting for transfers between devices: 28.4 us -> 30 us  [turn(): return lax.ppermute(x, 'y', [(i, (i - r) % N_Y) for i in range(N_Y)])]
  transfers between devices with their start and end apart: 18 -> 24, of which waited for: 7 -> 12; matrix products, arithmetic and copies ran while one was open for 6% -> 2% of each run, Pallas kernels for 20% -> 26%
where the time goes in v6:
time: 161 us; the launch traced here: 159 us
  starting transfers between devices  51.9 us (32%)
  Pallas kernels  42.4 us (26%)
  waiting for transfers between devices  33.4 us (21%)
  blocking collectives  17 us (11%)
  local copies, waits for them, and re-layouts  10.1 us (6%)
  other arithmetic  3.3 us (2%)
    ppermute x19, waiting for transfers between devices, turn(): return lax.ppermute(x, 'y', [(i, (i - r) % N_Y) for i in range(N_Y)])  30 us
    all_to_all x4, starting transfers between devices, exchange(): return lax.all_to_all(x, axes, split_axis=0, concat_axis=0, tiled=True)  27.3 us
    ppermute x19, starting transfers between devices, turn(): return lax.ppermute(x, 'y', [(i, (i - r) % N_Y) for i in range(N_Y)])  23.4 us
    pallas_call x2, Pallas kernels, half_terms(): pl.pallas_call(functools.partial(half_kernel, first), out_shape=(jax.Shap...  20.2 us
    all_to_all x1, blocking collectives, exchange(): return lax.all_to_all(x, axes, split_axis=0, concat_axis=0, tiled=True)  17 us
    pallas_call x2, Pallas kernels, final_product(): pl.pallas_call(functools.partial(final_kernel, mine), out_shape=jax.Shape...  7.24 us
    unnamed x56, local copies, waits for them, and re-layouts  6.96 us
    pallas_call x2, Pallas kernels, sum_rows(): pl.pallas_call(sums_kernel, out_shape=jax.ShapeDtypeStruct((rows, width),...  4.99 us
  transfers between devices with their start and end apart: 24, of which 12 were waited for; matrix products, arithmetic and copies ran while one was open for 2% of the time, Pallas kernels for 26%

profile of v6, /device:TPU:1, one launch (start us, length us, event | category | flops | bytes accessed | tf_op | source)
XLA Modules:
  0.0 159.1 jit_solution(14137187121372873876)
XLA Ops:
  0.6 3.6 %collective-permute-start.3 = (bf16[64,2048]{1,0:T(8,128)(2,1)}, bf16[64,2048]{1,0:T(8,128)(2,1)S(1)}, u32[]{:S(2)}, u32[]{:S(2)}) collective-permute-start(bf16[64,2048]{1,0:T(8,128)(2,1)} %t0.3), channel_id=1, source_target_pairs={{0,6},{2,0},{4,2},{6,4},{1,7},{3,1},{5,3},{7,5},{8,14},{10,8},{12,... | collective-permute-start | bytes 786440 | tf_op jit(solution)/shard_map/ppermute | solution.py:407
  4.6 0.7 collective-permute-start.5
  5.3 1.6 %ids.1 = s32[256,128]{1,0:T(8,128)} custom-call(s32[2,128]{1,0:T(2,128)} %bitcast.41), custom_call_target="tpu_custom_call" | custom-call | flops 100000 | bytes 100000 | tf_op jit(solution)/shard_map/ids/pallas_call | solution.py:74
  6.9 17.0 %all_to_all.25 = s32[32,8,128]{2,1,0:T(8,128)S(1)} all-to-all(s32[32,8,128]{2,1,0:T(8,128)} %bitcast.40), channel_id=1, replica_groups=mesh['dp'=16,'y'=4,'core'=2] {'dp','core'}, dimensions={0} | all-to-all | bytes 262144 | tf_op jit(solution)/shard_map/all_to_all | solution.py:415
  24.0 0.9 copy-done.6
  24.9 1.5 shard_map.95
  26.4 4.7 %all-to-all-start.2 = ((bf16[32,8,2048]{2,1,0:T(8,128)(2,1)}), bf16[32,8,2048]{2,1,0:T(8,128)(2,1)}, u32[]{:S(2)}, u32[]{:S(2)}) async-start(bf16[32,8,2048]{2,1,0:T(8,128)(2,1)} %bitcast.6), calls=%async_computation.2 | async-start | bytes 2097152 | tf_op jit(solution)/shard_map/all_to_all | solution.py:415
  31.1 2.1 %collective-permute-start = (bf16[64,2048]{1,0:T(8,128)(2,1)S(1)}, bf16[64,2048]{1,0:T(8,128)(2,1)S(1)}, u32[]{:S(2)}, u32[]{:S(2)}) collective-permute-start(bf16[64,2048]{1,0:T(8,128)(2,1)S(1)} %copy-done.7), channel_id=1, source_target_pairs={{0,6},{2,0},{4,2},{6,4},{1,7},{3,1},{5,3},{7,5},{8,14},{10,8},{12,... | collective-permute-start | bytes 786440 | tf_op jit(solution)/shard_map/ppermute | solution.py:407
  33.2 1.4 collective-permute-start.1
  34.6 4.4 %collective-permute-done.t1 = bf16[64,2048]{1,0:T(8,128)(2,1)S(1)} collective-permute-done((bf16[64,2048]{1,0:T(8,128)(2,1)S(1)}, bf16[64,2048]{1,0:T(8,128)(2,1)S(1)}, u32[]{:S(2)}, u32[]{:S(2)}) %collective-permute-start) | collective-permute-done | bytes 262176 | tf_op jit(solution)/shard_map/ppermute | solution.py:407
  39.0 3.0 %collective-permute-done.1.t2 = bf16[64,2048]{1,0:T(8,128)(2,1)S(1)} collective-permute-done((bf16[64,2048]{1,0:T(8,128)(2,1)S(1)}, bf16[64,2048]{1,0:T(8,128)(2,1)S(1)}, u32[]{:S(2)}, u32[]{:S(2)}) %collective-permute-start.1) | collective-permute-done | bytes 262176 | tf_op jit(solution)/shard_map/ppermute | solution.py:407
  42.0 6.5 %collective-permute-done.2.t3 = bf16[64,2048]{1,0:T(8,128)(2,1)S(1)} collective-permute-done((bf16[64,2048]{1,0:T(8,128)(2,1)S(1)}, bf16[64,2048]{1,0:T(8,128)(2,1)S(1)}, u32[]{:S(2)}, u32[]{:S(2)}) %collective-permute-start.2) | collective-permute-done | bytes 262176 | tf_op jit(solution)/shard_map/ppermute | solution.py:407
  48.5 1.4 shard_map.94
  50.0 7.7 %all-to-all-start.1 = ((bf16[32,8,2048]{2,1,0:T(8,128)(2,1)}), bf16[32,8,2048]{2,1,0:T(8,128)(2,1)}, u32[]{:S(2)}, u32[]{:S(2)}) async-start(bf16[32,8,2048]{2,1,0:T(8,128)(2,1)} %bitcast.4), calls=%async_computation.1 | async-start | bytes 2097152 | tf_op jit(solution)/shard_map/all_to_all | solution.py:415
  57.6 0.7 or_or_fusion
  58.4 2.8 %weight.1.side_hbm = f32[4,256,512]{2,1,0:T(8,128)S(1)} custom-call(s32[16,2048]{1,0:T(8,128)S(1)} %get-tuple-element.24.places_ref, f32[16,2048]{1,0:T(8,128)S(1)} %bitcast.39), custom_call_target="tpu_custom_call" | custom-call | flops 25165824 | bytes 2097152 | tf_op jit(solution)/shard_map/weight/pallas_call | solution.py:154
  61.2 1.4 copy-done
  62.9 1.1 collective-permute-start.14
  64.0 10.5 %first.1 = (f32[4,256,512]{2,1,0:T(8,128)}, bf16[128,2,2048]{2,1,0:T(2,128)(2,1)}) custom-call(bf16[2048,2048]{1,0:T(8,128)(2,1)} %other_hbm.3, bf16[2048,2048]{1,0:T(8,128)(2,1)} %lead_hbm.3, bf16[256,2048]{1,0:T(8,128)(2,1)} %bitcast.7.rows_hbm.d0, f32[4,256,512]{2,1,0:T(8,128)} %copy-done), custom_call_target="tpu_custom_call" | custom-call | flops 4294967296 | bytes 25165824 | tf_op jit(solution)/shard_map/first/pallas_call | solution.py:238
  74.7 9.7 %second.1 = (bf16[256,2048]{1,0:T(8,128)(2,1)}, bf16[128,2,2048]{2,1,0:T(2,128)(2,1)}) custom-call(bf16[2048,2048]{1,0:T(8,128)(2,1)} %lead_hbm.3, bf16[2048,2048]{1,0:T(8,128)(2,1)} %other_hbm.3, bf16[256,2048]{1,0:T(8,128)(2,1)} %bitcast.5.rows_hbm, f32[4,256,512]{2,1,0:T(8,128)} %get-tuple-element.11.side_hbm), custom_call_target="tpu_custom_call" | custom-call | flops 4294967296 | bytes 25165824 | tf_op jit(solution)/shard_map/second/pallas_call | solution.py:238
  84.5 8.9 %all-to-all-start.3 = ((bf16[128,2,2048]{2,1,0:T(2,128)(2,1)}), bf16[128,2,2048]{2,1,0:T(2,128)(2,1)}, u32[]{:S(2)}, u32[]{:S(2)}) async-start(bf16[128,2,2048]{2,1,0:T(2,128)(2,1)} %get-tuple-element.17), calls=%async_computation.3 | async-start | bytes 2097152 | tf_op jit(solution)/shard_map/all_to_all | solution.py:415
  93.4 0.8 slice.8
  94.3 2.6 %collective-permute-start.13 = (bf16[128,2048]{1,0:T(8,128)(2,1)}, bf16[128,2048]{1,0:T(8,128)(2,1)S(1)}, u32[]{:S(2)}, u32[]{:S(2)}) collective-permute-start(bf16[128,2048]{1,0:T(8,128)(2,1)} %slice.8), channel_id=1, source_target_pairs={{0,6},{2,0},{4,2},{6,4},{1,7},{3,1},{5,3},{7,5},{8,14},{10,8},{12,... | collective-permute-start | bytes 1572872 | tf_op jit(solution)/shard_map/ppermute | solution.py:407
  96.9 0.8 slice.9
  97.7 1.5 dynamic-slice_bitcast_fusion
  99.2 1.7 %collective-permute-start.10 = (s32[16,512]{1,0:T(8,128)}, s32[16,512]{1,0:T(8,128)S(1)}, u32[]{:S(2)}, u32[]{:S(2)}) collective-permute-start(s32[16,512]{1,0:T(8,128)} %get-tuple-element.20), channel_id=1, source_target_pairs={{0,4},{2,6},{4,0},{6,2},{1,5},{3,7},{5,1},{7,3},{8,12},{10,14},{12... | collective-permute-start | bytes 98312 | tf_op jit(solution)/shard_map/ppermute | solution.py:407
  100.9 1.5 collective-permute-start.11
  102.4 1.1 collective-permute-start.9
  103.6 1.2 copy-done.1
  104.8 2.6 %compact.1 = (bf16[16,512]{1,0:T(8,128)(2,1)S(1)}, bf16[16,512]{1,0:T(8,128)(2,1)S(1)}, bf16[16,512]{1,0:T(8,128)(2,1)S(1)}, bf16[16,512]{1,0:T(8,128)(2,1)S(1)}) custom-call(bf16[256,2048]{1,0:T(8,128)(2,1)S(1)} %copy-done.1, s32[16,2048]{1,0:T(8,128)S(1)} %get-tuple-element.24.places_ref), custom_call_target="tpu_custom_call" | custom-call | flops 16777216 | bytes 1048576 | tf_op jit(solution)/shard_map/compact/pallas_call | solution.py:281
  109.2 3.1 %all-to-all-done.3.got_hbm = bf16[128,2,2048]{2,1,0:T(2,128)(2,1)} async-done(((bf16[128,2,2048]{2,1,0:T(2,128)(2,1)}), bf16[128,2,2048]{2,1,0:T(2,128)(2,1)}, u32[]{:S(2)}, u32[]{:S(2)}) %all-to-all-start.3) | async-done | bytes 1048608 | tf_op jit(solution)/shard_map/all_to_all | solution.py:415
  112.4 6.0 %all-to-all-start.4 = ((bf16[128,2,2048]{2,1,0:T(2,128)(2,1)}), bf16[128,2,2048]{2,1,0:T(2,128)(2,1)}, u32[]{:S(2)}, u32[]{:S(2)}) async-start(bf16[128,2,2048]{2,1,0:T(2,128)(2,1)} %get-tuple-element.18), calls=%async_computation.4 | async-start | bytes 2097152 | tf_op jit(solution)/shard_map/all_to_all | solution.py:415
  118.8 2.3 %collective-permute-start.6 = (bf16[16,512]{1,0:T(8,128)(2,1)S(1)}, bf16[16,512]{1,0:T(8,128)(2,1)S(1)}, u32[]{:S(2)}, u32[]{:S(2)}) collective-permute-start(bf16[16,512]{1,0:T(8,128)(2,1)S(1)} %copy-done.26), channel_id=1, source_target_pairs={{0,6},{2,0},{4,2},{6,4},{1,7},{3,1},{5,3},{7,5},{8,14},{10,8},{12,... | collective-permute-start | bytes 49160 | tf_op jit(solution)/shard_map/ppermute | solution.py:407
  122.4 4.1 %collective-permute-done.6.c1 = bf16[16,512]{1,0:T(8,128)(2,1)S(1)} collective-permute-done((bf16[16,512]{1,0:T(8,128)(2,1)S(1)}, bf16[16,512]{1,0:T(8,128)(2,1)S(1)}, u32[]{:S(2)}, u32[]{:S(2)}) %collective-permute-start.6) | collective-permute-done | bytes 16416 | tf_op jit(solution)/shard_map/ppermute | solution.py:407
  126.5 1.0 collective-permute-done.7.c2
  127.5 1.6 %collective-permute-done.8.c3 = bf16[16,512]{1,0:T(8,128)(2,1)S(1)} collective-permute-done((bf16[16,512]{1,0:T(8,128)(2,1)S(1)}, bf16[16,512]{1,0:T(8,128)(2,1)S(1)}, u32[]{:S(2)}, u32[]{:S(2)}) %collective-permute-start.8) | collective-permute-done | bytes 16416 | tf_op jit(solution)/shard_map/ppermute | solution.py:407
  129.1 3.6 %give.1 = bf16[256,2048]{1,0:T(8,128)(2,1)} custom-call(bf16[16,512]{1,0:T(8,128)(2,1)S(1)} %get-tuple-element.13.c0, bf16[16,512]{1,0:T(8,128)(2,1)S(1)} %collective-permute-done.6.c1, bf16[16,512]{1,0:T(8,128)(2,1)S(1)} %collective-permute-done.7.c2, bf16[16,512]{1,0:T(8,128)(2,1)S(1)} %collective-permute-done.8.c3, s32[16,512]{1,0:T(8,128)S(1)} %get-tuple-element.22.p0, ...), custom_call_target="tpu_custom_call" | custom-call | flops 1073741824 | bytes 6291456 | tf_op jit(solution)/shard_map/give/pallas_call | solution.py:389
  132.8 1.3 collective-permute-start.16
  134.0 2.6 %collective-permute-start.17 = (s32[256,128]{1,0:T(8,128)S(1)}, s32[256,128]{1,0:T(8,128)S(1)}, u32[]{:S(2)}, u32[]{:S(2)}) collective-permute-start(s32[256,128]{1,0:T(8,128)S(1)} %bitcast.34), channel_id=1, source_target_pairs={{0,6},{2,0},{4,2},{6,4},{1,7},{3,1},{5,3},{7,5},{8,14},{10,8},{12,... | collective-permute-start | bytes 393224 | tf_op jit(solution)/shard_map/ppermute | solution.py:407
  137.3 4.9 %collective-permute-done.17.a1 = s32[256,128]{1,0:T(8,128)S(1)} collective-permute-done((s32[256,128]{1,0:T(8,128)S(1)}, s32[256,128]{1,0:T(8,128)S(1)}, u32[]{:S(2)}, u32[]{:S(2)}) %collective-permute-start.17) | collective-permute-done | bytes 131104 | tf_op jit(solution)/shard_map/ppermute | solution.py:407
  142.1 0.8 collective-permute-done.18.a2
  142.9 3.3 %collective-permute-done.19.a3 = s32[256,128]{1,0:T(8,128)S(1)} collective-permute-done((s32[256,128]{1,0:T(8,128)S(1)}, s32[256,128]{1,0:T(8,128)S(1)}, u32[]{:S(2)}, u32[]{:S(2)}) %collective-permute-start.19) | collective-permute-done | bytes 131104 | tf_op jit(solution)/shard_map/ppermute | solution.py:407
  146.2 2.5 %shard_map.96 = f32[64,2048]{1,0:T(8,128)} custom-call(s32[256,128]{1,0:T(8,128)S(1)} %bitcast.37, s32[256,128]{1,0:T(8,128)S(1)} %collective-permute-done.17.a1, s32[256,128]{1,0:T(8,128)S(1)} %collective-permute-done.18.a2, s32[256,128]{1,0:T(8,128)S(1)} %collective-permute-done.19.a3, bf16[128,2,2048]{2,1,0:T(2,128)(2,1)} %all-to-all-done.3.got_hbm), custom_call_target="tpu_custom_call" | custom-call | flops 268435456 | bytes 2000000 | tf_op jit(solution)/shard_map/pallas_call | solution.py:330
  148.7 0.6 copy-done.2
  149.4 0.9 copy-done.3
  150.3 2.5 %shard_map.97 = f32[64,2048]{1,0:T(8,128)} custom-call(s32[256,128]{1,0:T(8,128)S(1)} %bitcast.38, s32[256,128]{1,0:T(8,128)S(1)} %collective-permute-done.17.a1, s32[256,128]{1,0:T(8,128)S(1)} %collective-permute-done.18.a2, s32[256,128]{1,0:T(8,128)S(1)} %copy-done.3, bf16[128,2,2048]{2,1,0:T(2,128)(2,1)} %all-to-all-done.4.got_hbm), custom_call_target="tpu_custom_call" | custom-call | flops 268435456 | bytes 2000000 | tf_op jit(solution)/shard_map/pallas_call | solution.py:330
  152.9 3.6 %keep.1 = bf16[256,2048]{1,0:T(8,128)(2,1)S(1)} custom-call(bf16[16,512]{1,0:T(8,128)(2,1)S(1)} %get-tuple-element.13.c0, bf16[16,512]{1,0:T(8,128)(2,1)S(1)} %copy-done.16, bf16[16,512]{1,0:T(8,128)(2,1)S(1)} %copy-done.18, bf16[16,512]{1,0:T(8,128)(2,1)S(1)} %copy-done.20, s32[16,512]{1,0:T(8,128)S(1)} %copy-done.5, s32[16,512]{1,0:T(8,128)S(1)} %copy-done.13, ...), custom_call_target="tpu_custom_call" | custom-call | flops 1073741824 | bytes 6291456 | tf_op jit(solution)/shard_map/keep/pallas_call | solution.py:389
  156.5 2.6 %add_convert_fusion = bf16[256,2048]{1,0:T(8,128)(2,1)} fusion(bf16[256,2048]{1,0:T(8,128)(2,1)} %collective-permute-done.16, bf16[256,2048]{1,0:T(8,128)(2,1)S(1)} %keep.1), kind=kLoop, calls=%fused_computation | loop fusion | flops 2097152 | bytes 3145728 | tf_op jit(solution)/shard_map/convert_element_type | solution.py:456
  (73 shorter events, 5.0 us)
Async XLA Ops:
  0.6 23.3 %collective-permute-start.3 = (bf16[64,2048]{1,0:T(8,128)(2,1)}, bf16[64,2048]{1,0:T(8,128)(2,1)S(1)}, u32[]{:S(2)}, u32[]{:S(2)}) collective-permute-start(bf16[64,2048]{1,0:T(8,128)(2,1)} %t0.3), channel_id=1, source_target_pairs={{0,6},{2,0},{4,2},{6,4},{1,7},{3,1},{5,3},{7,5},{8,14},{10,8},{12,... | collective-permute-start | bytes 786440 | tf_op jit(solution)/shard_map/ppermute | solution.py:407
  4.3 19.7 %collective-permute-start.4 = (bf16[64,2048]{1,0:T(8,128)(2,1)}, bf16[64,2048]{1,0:T(8,128)(2,1)S(1)}, u32[]{:S(2)}, u32[]{:S(2)}) collective-permute-start(bf16[64,2048]{1,0:T(8,128)(2,1)} %t0.3), channel_id=1, source_target_pairs={{0,4},{2,6},{4,0},{6,2},{1,5},{3,7},{5,1},{7,3},{8,12},{10,14},{12... | collective-permute-start | bytes 786440 | tf_op jit(solution)/shard_map/ppermute | solution.py:407
  4.6 19.3 %collective-permute-start.5 = (bf16[64,2048]{1,0:T(8,128)(2,1)}, bf16[64,2048]{1,0:T(8,128)(2,1)S(1)}, u32[]{:S(2)}, u32[]{:S(2)}) collective-permute-start(bf16[64,2048]{1,0:T(8,128)(2,1)} %t0.3), channel_id=1, source_target_pairs={{0,2},{2,4},{4,6},{6,0},{1,3},{3,5},{5,7},{7,1},{8,10},{10,12},{12... | collective-permute-start | bytes 786440 | tf_op jit(solution)/shard_map/ppermute | solution.py:407
  23.9 1.0 copy-start.6
  24.9 6.2 %copy-start.7 = (bf16[64,2048]{1,0:T(8,128)(2,1)S(1)}, bf16[64,2048]{1,0:T(8,128)(2,1)}, u32[]{:S(2)}) copy-start(bf16[64,2048]{1,0:T(8,128)(2,1)} %t0.2) | copy-start | bytes 786436
  26.4 23.6 %all-to-all-start.2 = ((bf16[32,8,2048]{2,1,0:T(8,128)(2,1)}), bf16[32,8,2048]{2,1,0:T(8,128)(2,1)}, u32[]{:S(2)}, u32[]{:S(2)}) async-start(bf16[32,8,2048]{2,1,0:T(8,128)(2,1)} %bitcast.6), calls=%async_computation.2 | async-start | bytes 2097152 | tf_op jit(solution)/shard_map/all_to_all | solution.py:415
  31.1 26.5 %copy-start.27 = (s32[1,2048,16]{1,2,0:T(8,128)S(1)}, s32[1,2048,16]{1,2,0:T(8,128)}, u32[]{:S(2)}) copy-start(s32[1,2048,16]{1,2,0:T(8,128)} %param.12) | copy-start | bytes 393220
  31.1 27.3 %copy-start.14 = (f32[1,2048,16]{1,2,0:T(8,128)S(1)}, f32[1,2048,16]{1,2,0:T(8,128)}, u32[]{:S(2)}) copy-start(f32[1,2048,16]{1,2,0:T(8,128)} %param.13) | copy-start | bytes 393220
  31.1 7.9 %collective-permute-start = (bf16[64,2048]{1,0:T(8,128)(2,1)S(1)}, bf16[64,2048]{1,0:T(8,128)(2,1)S(1)}, u32[]{:S(2)}, u32[]{:S(2)}) collective-permute-start(bf16[64,2048]{1,0:T(8,128)(2,1)S(1)} %copy-done.7), channel_id=1, source_target_pairs={{0,6},{2,0},{4,2},{6,4},{1,7},{3,1},{5,3},{7,5},{8,14},{10,8},{12,... | collective-permute-start | bytes 786440 | tf_op jit(solution)/shard_map/ppermute | solution.py:407
  33.2 8.8 %collective-permute-start.1 = (bf16[64,2048]{1,0:T(8,128)(2,1)S(1)}, bf16[64,2048]{1,0:T(8,128)(2,1)S(1)}, u32[]{:S(2)}, u32[]{:S(2)}) collective-permute-start(bf16[64,2048]{1,0:T(8,128)(2,1)S(1)} %copy-done.7), channel_id=1, source_target_pairs={{0,4},{2,6},{4,0},{6,2},{1,5},{3,7},{5,1},{7,3},{8,12},{10,14},{12... | collective-permute-start | bytes 786440 | tf_op jit(solution)/shard_map/ppermute | solution.py:407
  34.6 13.9 %collective-permute-start.2 = (bf16[64,2048]{1,0:T(8,128)(2,1)S(1)}, bf16[64,2048]{1,0:T(8,128)(2,1)S(1)}, u32[]{:S(2)}, u32[]{:S(2)}) collective-permute-start(bf16[64,2048]{1,0:T(8,128)(2,1)S(1)} %copy-done.7), channel_id=1, source_target_pairs={{0,2},{2,4},{4,6},{6,0},{1,3},{3,5},{5,7},{7,1},{8,10},{10,12},{12... | collective-permute-start | bytes 786440 | tf_op jit(solution)/shard_map/ppermute | solution.py:407
  50.0 24.8 %all-to-all-start.1 = ((bf16[32,8,2048]{2,1,0:T(8,128)(2,1)}), bf16[32,8,2048]{2,1,0:T(8,128)(2,1)}, u32[]{:S(2)}, u32[]{:S(2)}) async-start(bf16[32,8,2048]{2,1,0:T(8,128)(2,1)} %bitcast.4), calls=%async_computation.1 | async-start | bytes 2097152 | tf_op jit(solution)/shard_map/all_to_all | solution.py:415
  61.2 1.4 copy-start
  62.6 30.8 %collective-permute-start.12 = (bf16[256,2048]{1,0:T(8,128)(2,1)}, bf16[256,2048]{1,0:T(8,128)(2,1)S(1)}, u32[]{:S(2)}, u32[]{:S(2)}) collective-permute-start(bf16[256,2048]{1,0:T(8,128)(2,1)} %bitcast.7.rows_hbm.d0), channel_id=1, source_target_pairs={{0,6},{2,0},{4,2},{6,4},{1,7},{3,1},{5,3},{7,5},{8,14},{10,8},{12,... | collective-permute-start | bytes 3145736 | tf_op jit(solution)/shard_map/ppermute | solution.py:407
  62.9 34.0 %collective-permute-start.14 = (bf16[256,2048]{1,0:T(8,128)(2,1)}, bf16[256,2048]{1,0:T(8,128)(2,1)S(1)}, u32[]{:S(2)}, u32[]{:S(2)}) collective-permute-start(bf16[256,2048]{1,0:T(8,128)(2,1)} %bitcast.7.rows_hbm.d0), channel_id=1, source_target_pairs={{0,2},{2,4},{4,6},{6,0},{1,3},{3,5},{5,7},{7,1},{8,10},{10,12},{12... | collective-permute-start | bytes 3145736 | tf_op jit(solution)/shard_map/ppermute | solution.py:407
  84.5 27.9 %all-to-all-start.3 = ((bf16[128,2,2048]{2,1,0:T(2,128)(2,1)}), bf16[128,2,2048]{2,1,0:T(2,128)(2,1)}, u32[]{:S(2)}, u32[]{:S(2)}) async-start(bf16[128,2,2048]{2,1,0:T(2,128)(2,1)} %get-tuple-element.17), calls=%async_computation.3 | async-start | bytes 2097152 | tf_op jit(solution)/shard_map/all_to_all | solution.py:415
  94.3 34.8 %collective-permute-start.13 = (bf16[128,2048]{1,0:T(8,128)(2,1)}, bf16[128,2048]{1,0:T(8,128)(2,1)S(1)}, u32[]{:S(2)}, u32[]{:S(2)}) collective-permute-start(bf16[128,2048]{1,0:T(8,128)(2,1)} %slice.8), channel_id=1, source_target_pairs={{0,6},{2,0},{4,2},{6,4},{1,7},{3,1},{5,3},{7,5},{8,14},{10,8},{12,... | collective-permute-start | bytes 1572872 | tf_op jit(solution)/shard_map/ppermute | solution.py:407
  97.7 31.3 %collective-permute-start.15 = (bf16[128,2048]{1,0:T(8,128)(2,1)}, bf16[128,2048]{1,0:T(8,128)(2,1)S(1)}, u32[]{:S(2)}, u32[]{:S(2)}) collective-permute-start(bf16[128,2048]{1,0:T(8,128)(2,1)} %slice.9), channel_id=1, source_target_pairs={{0,2},{2,4},{4,6},{6,0},{1,3},{3,5},{5,7},{7,1},{8,10},{10,12},{12... | collective-permute-start | bytes 1572872 | tf_op jit(solution)/shard_map/ppermute | solution.py:407
  99.2 33.5 %copy-start.4 = (s32[16,512]{1,0:T(8,128)}, s32[16,512]{1,0:T(8,128)S(1)}, u32[]{:S(2)}) copy-start(s32[16,512]{1,0:T(8,128)S(1)} %get-tuple-element.22.p0) | copy-start | bytes 98308
  99.2 19.6 %collective-permute-start.10 = (s32[16,512]{1,0:T(8,128)}, s32[16,512]{1,0:T(8,128)S(1)}, u32[]{:S(2)}, u32[]{:S(2)}) collective-permute-start(s32[16,512]{1,0:T(8,128)} %get-tuple-element.20), channel_id=1, source_target_pairs={{0,4},{2,6},{4,0},{6,2},{1,5},{3,7},{5,1},{7,3},{8,12},{10,14},{12... | collective-permute-start | bytes 98312 | tf_op jit(solution)/shard_map/ppermute | solution.py:407
  100.9 20.2 %collective-permute-start.11 = (s32[16,512]{1,0:T(8,128)}, s32[16,512]{1,0:T(8,128)S(1)}, u32[]{:S(2)}, u32[]{:S(2)}) collective-permute-start(s32[16,512]{1,0:T(8,128)} %get-tuple-element.19), channel_id=1, source_target_pairs={{0,2},{2,4},{4,6},{6,0},{1,3},{3,5},{5,7},{7,1},{8,10},{10,12},{12... | collective-permute-start | bytes 98312 | tf_op jit(solution)/shard_map/ppermute | solution.py:407
  102.4 19.3 %collective-permute-start.9 = (s32[16,512]{1,0:T(8,128)}, s32[16,512]{1,0:T(8,128)S(1)}, u32[]{:S(2)}, u32[]{:S(2)}) collective-permute-start(s32[16,512]{1,0:T(8,128)} %get-tuple-element.21), channel_id=1, source_target_pairs={{0,6},{2,0},{4,2},{6,4},{1,7},{3,1},{5,3},{7,5},{8,14},{10,8},{12,... | collective-permute-start | bytes 98312 | tf_op jit(solution)/shard_map/ppermute | solution.py:407
  103.6 1.2 copy-start.1
  112.3 6.4 %copy-start.26 = (bf16[16,512]{1,0:T(8,128)(2,1)S(1)}, bf16[16,512]{1,0:T(8,128)(2,1)}, u32[]{:S(2)}) copy-start(bf16[16,512]{1,0:T(8,128)(2,1)} %copy-done.25) | copy-start | bytes 49156
  112.3 8.8 %copy-start.24 = (bf16[16,512]{1,0:T(8,128)(2,1)S(1)}, bf16[16,512]{1,0:T(8,128)(2,1)}, u32[]{:S(2)}) copy-start(bf16[16,512]{1,0:T(8,128)(2,1)} %copy-done.23) | copy-start | bytes 49156
  112.4 9.4 %copy-start.22 = (bf16[16,512]{1,0:T(8,128)(2,1)S(1)}, bf16[16,512]{1,0:T(8,128)(2,1)}, u32[]{:S(2)}) copy-start(bf16[16,512]{1,0:T(8,128)(2,1)} %copy-done.21) | copy-start | bytes 49156
  112.4 37.0 %all-to-all-start.4 = ((bf16[128,2,2048]{2,1,0:T(2,128)(2,1)}), bf16[128,2,2048]{2,1,0:T(2,128)(2,1)}, u32[]{:S(2)}, u32[]{:S(2)}) async-start(bf16[128,2,2048]{2,1,0:T(2,128)(2,1)} %get-tuple-element.18), calls=%async_computation.4 | async-start | bytes 2097152 | tf_op jit(solution)/shard_map/all_to_all | solution.py:415
  118.8 13.9 %copy-start.8 = (s32[16,512]{1,0:T(8,128)}, s32[16,512]{1,0:T(8,128)S(1)}, u32[]{:S(2)}) copy-start(s32[16,512]{1,0:T(8,128)S(1)} %collective-permute-done.10.p2) | copy-start | bytes 98308
  118.8 7.7 %collective-permute-start.6 = (bf16[16,512]{1,0:T(8,128)(2,1)S(1)}, bf16[16,512]{1,0:T(8,128)(2,1)S(1)}, u32[]{:S(2)}, u32[]{:S(2)}) collective-permute-start(bf16[16,512]{1,0:T(8,128)(2,1)S(1)} %copy-done.26), channel_id=1, source_target_pairs={{0,6},{2,0},{4,2},{6,4},{1,7},{3,1},{5,3},{7,5},{8,14},{10,8},{12,... | collective-permute-start | bytes 49160 | tf_op jit(solution)/shard_map/ppermute | solution.py:407
  121.1 11.6 %copy-start.10 = (s32[16,512]{1,0:T(8,128)}, s32[16,512]{1,0:T(8,128)S(1)}, u32[]{:S(2)}) copy-start(s32[16,512]{1,0:T(8,128)S(1)} %collective-permute-done.11.p3) | copy-start | bytes 98308
  121.1 6.4 %collective-permute-start.7 = (bf16[16,512]{1,0:T(8,128)(2,1)S(1)}, bf16[16,512]{1,0:T(8,128)(2,1)S(1)}, u32[]{:S(2)}, u32[]{:S(2)}) collective-permute-start(bf16[16,512]{1,0:T(8,128)(2,1)S(1)} %copy-done.24), channel_id=1, source_target_pairs={{0,4},{2,6},{4,0},{6,2},{1,5},{3,7},{5,1},{7,3},{8,12},{10,14},{12... | collective-permute-start | bytes 49160 | tf_op jit(solution)/shard_map/ppermute | solution.py:407
  121.7 11.0 %copy-start.12 = (s32[16,512]{1,0:T(8,128)}, s32[16,512]{1,0:T(8,128)S(1)}, u32[]{:S(2)}) copy-start(s32[16,512]{1,0:T(8,128)S(1)} %collective-permute-done.9.p1) | copy-start | bytes 98308
  121.7 7.3 %collective-permute-start.8 = (bf16[16,512]{1,0:T(8,128)(2,1)S(1)}, bf16[16,512]{1,0:T(8,128)(2,1)S(1)}, u32[]{:S(2)}, u32[]{:S(2)}) collective-permute-start(bf16[16,512]{1,0:T(8,128)(2,1)S(1)} %copy-done.22), channel_id=1, source_target_pairs={{0,2},{2,4},{4,6},{6,0},{1,3},{3,5},{5,7},{7,1},{8,10},{10,12},{12... | collective-permute-start | bytes 49160 | tf_op jit(solution)/shard_map/ppermute | solution.py:407
  126.5 6.3 %copy-start.15 = (bf16[16,512]{1,0:T(8,128)(2,1)}, bf16[16,512]{1,0:T(8,128)(2,1)S(1)}, u32[]{:S(2)}) copy-start(bf16[16,512]{1,0:T(8,128)(2,1)S(1)} %collective-permute-done.6.c1) | copy-start | bytes 49156
  127.5 5.3 %copy-start.17 = (bf16[16,512]{1,0:T(8,128)(2,1)}, bf16[16,512]{1,0:T(8,128)(2,1)S(1)}, u32[]{:S(2)}) copy-start(bf16[16,512]{1,0:T(8,128)(2,1)S(1)} %collective-permute-done.7.c2) | copy-start | bytes 49156
  129.1 3.7 %copy-start.19 = (bf16[16,512]{1,0:T(8,128)(2,1)}, bf16[16,512]{1,0:T(8,128)(2,1)S(1)}, u32[]{:S(2)}) copy-start(bf16[16,512]{1,0:T(8,128)(2,1)S(1)} %collective-permute-done.8.c3) | copy-start | bytes 49156
  132.8 23.7 %collective-permute-start.16 = (bf16[256,2048]{1,0:T(8,128)(2,1)}, bf16[256,2048]{1,0:T(8,128)(2,1)}, u32[]{:S(2)}, u32[]{:S(2)}) collective-permute-start(bf16[256,2048]{1,0:T(8,128)(2,1)} %give.1), channel_id=1, source_target_pairs={{0,1},{1,0},{2,3},{3,2},{4,5},{5,4},{6,7},{7,6},{8,9},{9,8},{10,11... | collective-permute-start | bytes 3145736 | tf_op jit(solution)/shard_map/ppermute | solution.py:454
  134.0 8.1 %collective-permute-start.17 = (s32[256,128]{1,0:T(8,128)S(1)}, s32[256,128]{1,0:T(8,128)S(1)}, u32[]{:S(2)}, u32[]{:S(2)}) collective-permute-start(s32[256,128]{1,0:T(8,128)S(1)} %bitcast.34), channel_id=1, source_target_pairs={{0,6},{2,0},{4,2},{6,4},{1,7},{3,1},{5,3},{7,5},{8,14},{10,8},{12,... | collective-permute-start | bytes 393224 | tf_op jit(solution)/shard_map/ppermute | solution.py:407
  136.7 6.2 %collective-permute-start.18 = (s32[256,128]{1,0:T(8,128)S(1)}, s32[256,128]{1,0:T(8,128)S(1)}, u32[]{:S(2)}, u32[]{:S(2)}) collective-permute-start(s32[256,128]{1,0:T(8,128)S(1)} %bitcast.35), channel_id=1, source_target_pairs={{0,4},{2,6},{4,0},{6,2},{1,5},{3,7},{5,1},{7,3},{8,12},{10,14},{12... | collective-permute-start | bytes 393224 | tf_op jit(solution)/shard_map/ppermute | solution.py:407
  136.9 9.3 %collective-permute-start.19 = (s32[256,128]{1,0:T(8,128)S(1)}, s32[256,128]{1,0:T(8,128)S(1)}, u32[]{:S(2)}, u32[]{:S(2)}) collective-permute-start(s32[256,128]{1,0:T(8,128)S(1)} %bitcast.36), channel_id=1, source_target_pairs={{0,2},{2,4},{4,6},{6,0},{1,3},{3,5},{5,7},{7,1},{8,10},{10,12},{12... | collective-permute-start | bytes 393224 | tf_op jit(solution)/shard_map/ppermute | solution.py:407
  149.4 0.9 copy-start.3
  150.3 2.5 %copy-start.5 = (s32[16,512]{1,0:T(8,128)S(1)}, s32[16,512]{1,0:T(8,128)}, u32[]{:S(2)}) copy-start(s32[16,512]{1,0:T(8,128)} %copy-done.4) | copy-start | bytes 98308
  150.3 2.6 %copy-start.9 = (s32[16,512]{1,0:T(8,128)S(1)}, s32[16,512]{1,0:T(8,128)}, u32[]{:S(2)}) copy-start(s32[16,512]{1,0:T(8,128)} %copy-done.8) | copy-start | bytes 98308
  150.3 2.6 %copy-start.11 = (s32[16,512]{1,0:T(8,128)S(1)}, s32[16,512]{1,0:T(8,128)}, u32[]{:S(2)}) copy-start(s32[16,512]{1,0:T(8,128)} %copy-done.10) | copy-start | bytes 98308
  150.3 2.6 %copy-start.13 = (s32[16,512]{1,0:T(8,128)S(1)}, s32[16,512]{1,0:T(8,128)}, u32[]{:S(2)}) copy-start(s32[16,512]{1,0:T(8,128)} %copy-done.12) | copy-start | bytes 98308
  150.3 2.6 %copy-start.16 = (bf16[16,512]{1,0:T(8,128)(2,1)S(1)}, bf16[16,512]{1,0:T(8,128)(2,1)}, u32[]{:S(2)}) copy-start(bf16[16,512]{1,0:T(8,128)(2,1)} %copy-done.15) | copy-start | bytes 49156
  150.3 2.6 %copy-start.18 = (bf16[16,512]{1,0:T(8,128)(2,1)S(1)}, bf16[16,512]{1,0:T(8,128)(2,1)}, u32[]{:S(2)}) copy-start(bf16[16,512]{1,0:T(8,128)(2,1)} %copy-done.17) | copy-start | bytes 49156
  150.3 2.6 %copy-start.20 = (bf16[16,512]{1,0:T(8,128)(2,1)S(1)}, bf16[16,512]{1,0:T(8,128)(2,1)}, u32[]{:S(2)}) copy-start(bf16[16,512]{1,0:T(8,128)(2,1)} %copy-done.19) | copy-start | bytes 49156
  (4 other events, 2.5 us)

commit v7 on v6

--- a/solution.py
+++ b/solution.py
@@ -132,7 +132,7 @@
         ],
         compiler_params=params(8),
         cost_estimate=cost(2 * 256 * 256 * 2048, 3 * 10**6),
-    )(asked, *tables)
+    )(asked, stay(tables[0]), *tables[1:])
 
 
 def weight_kernel(places_ref, gates_ref, out_ref):
@@ -163,11 +163,26 @@
     )(places, gates)
 
 
-def half_kernel(
-    first, lead_hbm, other_hbm, rows_hbm, side_hbm, extra_hbm, part_hbm,
-    lead, other, rows, side, left, slope, half, part,
-    lead_sems, other_sems, row_sem, side_sems, extra_sems, part_sems,
-):
+def at_places(left, here, slot):
+    topk, block = slot.shape
+    row = iota((16, block), 0)
+    lines = []
+    for k in range(topk):
+        want = slot[k : k + 1, :] - row
+        found = jnp.zeros((16, block), F32)
+        for g in range(0, left.shape[0], 16):
+            found = jnp.where(want == g, left[g : g + 16, here].astype(F32), found)
+        lines.append(jnp.sum(found, axis=0, keepdims=True))
+    return jnp.concatenate(lines, axis=0).astype(BF16)
+
+
+def half_kernel(first, lead_hbm, other_hbm, rows_hbm, side_hbm, *refs):
+    places = None if first else refs[0]
+    extra_hbm = refs[:1] if first else refs[1 : 1 + N_Y]
+    (
+        part_hbm, lead, other, rows, side, left, extra, half, part,
+        lead_sems, other_sems, row_sem, side_sems, extra_sems, part_sems,
+    ) = refs[-15:]
     block = side.shape[2]
     width = lead.shape[1]
     step = width // N_Y
@@ -216,77 +231,58 @@
             cdf = 0.5 * (1.0 + lax.erf(found * SQRT_HALF))
             density = INV_ROOT_TAU * jnp.exp(-0.5 * found * found)
             left[:, here] = (side[c] * (found * cdf)).astype(BF16)
-            slope[c] = side[c] * (cdf + found * density)
-            out = copy(slope.at[c], extra_hbm.at[c], extra_sems.at[c])
+            extra[c] = side[c] * (cdf + found * density)
+            out = copy(extra.at[c], extra_hbm[0].at[c], extra_sems.at[c])
+            out.start()
+            sent.append(out)
         else:
             left[:, here] = (side[c] * found).astype(BF16)
-            out = copy(left.at[:, here], extra_hbm.at[:, here], extra_sems.at[c])
-        out.start()
-        sent.append(out)
+            extra[c] = at_places(left, here, places[:, here])
         if c == N_Y // 2 - 1:
             parts(c, False)
+    if not first:
+        y = lax.axis_index("y")
+        for r in range(N_Y):
+            out = copy(extra.at[(y + r) % N_Y], extra_hbm[r], extra_sems.at[r])
+            out.start()
+            sent.append(out)
     parts(N_Y - 1, True)
     for out in sent:
         out.wait()
 
 
-def half_terms(first, lead, other, rows, side, devices):
+def half_terms(lead, other, rows, side, devices, places=None):
+    first = places is None
     count, width = lead.shape
     slots = rows.shape[0]
-    chunks = (devices, slots // devices, width)
-    extra = (side.shape, F32) if first else ((slots, count), BF16)
+    chunks = jax.ShapeDtypeStruct((devices, slots // devices, width), BF16)
+    if first:
+        extra = (jax.ShapeDtypeStruct(side.shape, F32),)
+        held = pltpu.VMEM(side.shape, F32)
+    else:
+        topk = places.shape[0]
+        extra = (jax.ShapeDtypeStruct((topk, count // N_Y), BF16),) * N_Y
+        held = pltpu.VMEM((N_Y, topk, count // N_Y), BF16)
     return pl.pallas_call(
         functools.partial(half_kernel, first),
-        out_shape=(jax.ShapeDtypeStruct(*extra), jax.ShapeDtypeStruct(chunks, BF16)),
-        in_specs=[ANY] * 4,
-        out_specs=(ANY,) * 2,
+        out_shape=extra + (chunks,),
+        in_specs=[ANY] * 4 + ([] if first else [VMEM]),
+        out_specs=(ANY,) * (len(extra) + 1),
         scratch_shapes=[
             pltpu.VMEM((count, width), BF16),
             pltpu.VMEM((count, width), BF16),
             pltpu.VMEM((slots, width), BF16),
             pltpu.VMEM(side.shape, F32),
             pltpu.VMEM((slots, count), BF16),
-            pltpu.VMEM(side.shape, F32),
+            held,
             pltpu.VMEM((slots, width), F32),
-            pltpu.VMEM(chunks, BF16),
+            pltpu.VMEM(chunks.shape, BF16),
             DMA((8,)), DMA((8,)), DMA, DMA((4,)), DMA((4,)), DMA((4,)),
         ],
         compiler_params=params(56),
         cost_estimate=cost(4 * count * width * slots, 24 << 20),
         name="first" if first else "second",
-    )(lead, other, stay(rows), stay(side))
-
-
-def compact_kernel(coef_ref, places_ref, c0, c1, c2, c3):
-    slots, count = coef_ref.shape
-    topk = places_ref.shape[0]
-    block = count // N_Y
-    y = lax.axis_index("y")
-    for r, out in enumerate((c0, c1, c2, c3)):
-        here = pl.ds(pl.multiple_of(((y + r) % N_Y) * block, block), block)
-        slot = places_ref[:, here]
-        lines = []
-        row = iota((16, block), 0)
-        for k in range(topk):
-            want = slot[k : k + 1, :] - row
-            found = jnp.zeros((16, block), F32)
-            for g in range(0, slots, 16):
-                found = jnp.where(want == g, coef_ref[g : g + 16, here].astype(F32), found)
-            lines.append(jnp.sum(found, axis=0, keepdims=True))
-        out[...] = jnp.concatenate(lines, axis=0).astype(BF16)
-
-
-def compact(coef, places):
-    topk, count = places.shape
-    return pl.pallas_call(
-        compact_kernel,
-        out_shape=tuple(jax.ShapeDtypeStruct((topk, count // N_Y), BF16) for _ in range(N_Y)),
-        in_specs=[VMEM] * 2,
-        out_specs=(VMEM,) * N_Y,
-        compiler_params=params(8),
-        cost_estimate=cost(2 * topk * coef.size, 2 * coef.size),
-        name="compact",
-    )(coef, places)
+    )(lead, other, stay(rows), stay(side), *(() if first else (places,)))
 
 
 def own_hits(lists, rows):
@@ -303,8 +299,24 @@
     return total.astype(BF16)
 
 
-def sums_kernel(a0, a1, a2, a3, got_hbm, out_hbm, got, sums, sems, out_sems):
-    rows, width = sums.shape
+def hits_kernel(a0, a1, a2, a3, out_ref):
+    out_ref[...] = own_hits([a[...] for a in (a0, a1, a2, a3)], out_ref.shape[1])
+
+
+def hit_rows(lists, rows):
+    return pl.pallas_call(
+        hits_kernel,
+        out_shape=jax.ShapeDtypeStruct((lists[0].shape[0], rows), BF16),
+        in_specs=[VMEM] * N_Y,
+        out_specs=VMEM,
+        compiler_params=params(8),
+        cost_estimate=cost(10**7, 10**6),
+        name="hits",
+    )(*lists)
+
+
+def sums_kernel(hits_ref, got_hbm, out_hbm, got, sums, sems, out_sems):
+    _, width = sums.shape
     devices, capacity, _ = got.shape
     block = 512
     copies = []
@@ -312,7 +324,7 @@
         cols = pl.ds(j * block, block)
         copies.append(copy(got_hbm.at[:, :, cols], got.at[:, :, cols], sems.at[j]))
         copies[j].start()
-    hits = own_hits([a[...] for a in (a0, a1, a2, a3)], rows)
+    hits = hits_ref[...]
     sent = []
     for j in range(width // block):
         copies[j].wait()
@@ -325,12 +337,13 @@
         c.wait()
 
 
-def sum_rows(lists, got, rows):
+def sum_rows(hits, got):
     width = got.shape[2]
+    rows = hits.shape[1]
     return pl.pallas_call(
         sums_kernel,
         out_shape=jax.ShapeDtypeStruct((rows, width), F32),
-        in_specs=[VMEM] * N_Y + [ANY],
+        in_specs=[VMEM, ANY],
         out_specs=ANY,
         scratch_shapes=[
             pltpu.VMEM(got.shape, BF16),
@@ -340,7 +353,7 @@
         ],
         compiler_params=params(12),
         cost_estimate=cost(2 * 256 * 256 * 2048, 2 * 10**6),
-    )(*lists, stay(got))
+    )(hits, stay(got))
 
 
 def final_kernel(
@@ -434,6 +447,7 @@
     weight = build_weight(slot_of, jnp.transpose(gate_weights[0]), slots)
     down = column(gather_rows(asked, down_tables, width))
     lists = gathered([asked] * N_Y)
+    hits = hit_rows(lists, row_count)
     block = slot_of.shape[1] // N_Y
     blocks = [
         lax.dynamic_slice_in_dim(slot_of, ((y + r) & (N_Y - 1)) * block, block, 1) for r in range(N_Y)
@@ -441,20 +455,19 @@
     chip_places = gathered(blocks)
     up = column(gather_rows(asked, up_tables, width))
     above, below = turn(down, 1), turn(down, 3)
-    slope, part_up = half_terms(True, tokens, out_grad, down, weight, devices)
+    slope, part_up = half_terms(tokens, out_grad, down, weight, devices)
     got_up = exchange(part_up, ("dp", "core", "y"))
     far = (turn(above[: slots // 2], 1), turn(below[slots // 2 :], 3))
-    coef, part_down = half_terms(False, out_grad, tokens, up, slope, devices)
-    small = compact(coef, slot_of)
+    *small, part_down = half_terms(out_grad, tokens, up, slope, devices, slot_of)
     chip_coef = gathered(small)
     got_down = exchange(part_down, ("dp", "core", "y"))
-    up_grad = sum_rows(lists, got_up, row_count)
+    up_grad = sum_rows(hits, got_up)
     down_all = (down, above, *far, below)
     give = final_product(False, chip_coef, chip_places, down_all)
     other = lax.ppermute(give, "core", [(0, 1), (1, 0)])
     keep = final_product(True, chip_coef, chip_places, down_all)
     input_grad = (keep.astype(F32) + other.astype(F32)).astype(BF16)
-    down_grad = sum_rows(lists, got_down, row_count)
+    down_grad = sum_rows(hits, got_down)
     return (input_grad, down_grad, up_grad)
 
 

time: 161 us -> 163 us (1.012)
  waiting for transfers between devices: 33.4 us -> 42.5 us
  local copies, waits for them, and re-layouts: 10.1 us -> 3.99 us
  Pallas kernels: 42.4 us -> 45.9 us
  starting transfers between devices: 51.9 us -> 48.9 us
    all_to_all x4, waiting for transfers between devices: 3.37 us -> 11 us  [exchange(): return lax.all_to_all(x, axes, split_axis=0, concat_axis=0, tiled=True)]
    unnamed x56 -> x14, local copies, waits for them, and re-layouts: 6.96 us -> 2.32 us
    pallas_call x3, Pallas kernels: 22.8 us -> 24.9 us  [the longest x2 24.6 us: half_terms(): pl.pallas_call(functools.partial(half_kernel, first), out_shape=extra + (...]
    all_to_all x4, starting transfers between devices: 27.3 us -> 25.5 us  [exchange(): return lax.all_to_all(x, axes, split_axis=0, concat_axis=0, tiled=True)]
  transfers between devices with their start and end apart: 24 -> 24, of which waited for: 12 -> 12; matrix products, arithmetic and copies ran while one was open for 2% -> 1% of each run, Pallas kernels for 26% -> 27%
where the time goes in v7:
time: 163 us; the launch traced here: 162 us
  starting transfers between devices  48.9 us (30%)
  Pallas kernels  45.9 us (28%)
  waiting for transfers between devices  42.5 us (26%)
  blocking collectives  17 us (10%)
  local copies, waits for them, and re-layouts  3.99 us (2%)
  other arithmetic  2.63 us (2%)
    ppermute x19, waiting for transfers between devices, turn(): return lax.ppermute(x, 'y', [(i, (i - r) % N_Y) for i in range(N_Y)])  31.5 us
    all_to_all x4, starting transfers between devices, exchange(): return lax.all_to_all(x, axes, split_axis=0, concat_axis=0, tiled=True)  25.5 us
    pallas_call x2, Pallas kernels, half_terms(): pl.pallas_call(functools.partial(half_kernel, first), out_shape=extra + (...  24.6 us
    ppermute x19, starting transfers between devices, turn(): return lax.ppermute(x, 'y', [(i, (i - r) % N_Y) for i in range(N_Y)])  22.7 us
    all_to_all x1, blocking collectives, exchange(): return lax.all_to_all(x, axes, split_axis=0, concat_axis=0, tiled=True)  17 us
    all_to_all x4, waiting for transfers between devices, exchange(): return lax.all_to_all(x, axes, split_axis=0, concat_axis=0, tiled=True)  11 us
    pallas_call x2, Pallas kernels, final_product(): pl.pallas_call(functools.partial(final_kernel, mine), out_shape=jax.Shape...  7.22 us
    pallas_call x2, Pallas kernels, sum_rows(): pl.pallas_call(sums_kernel, out_shape=jax.ShapeDtypeStruct((rows, width),...  4.78 us
  transfers between devices with their start and end apart: 24, of which 12 were waited for; matrix products, arithmetic and copies ran while one was open for 1% of the time, Pallas kernels for 27%

profile of v7, /device:TPU:1, one launch (start us, length us, event | category | flops | bytes accessed | tf_op | source)
XLA Modules:
  0.0 161.8 jit_solution(6510315118082675355)
XLA Ops:
  0.6 3.6 %collective-permute-start.3 = (bf16[64,2048]{1,0:T(8,128)(2,1)}, bf16[64,2048]{1,0:T(8,128)(2,1)S(1)}, u32[]{:S(2)}, u32[]{:S(2)}) collective-permute-start(bf16[64,2048]{1,0:T(8,128)(2,1)} %t0.3), channel_id=1, source_target_pairs={{0,6},{2,0},{4,2},{6,4},{1,7},{3,1},{5,3},{7,5},{8,14},{10,8},{12,... | collective-permute-start | bytes 786440 | tf_op jit(solution)/shard_map/ppermute | solution.py:420
  4.3 0.3 collective-permute-start.4
  4.6 0.7 collective-permute-start.5
  5.3 1.6 ids.1
  6.9 17.0 %all_to_all.25 = s32[32,8,128]{2,1,0:T(8,128)S(1)} all-to-all(s32[32,8,128]{2,1,0:T(8,128)} %bitcast.40), channel_id=1, replica_groups=mesh['dp'=16,'y'=4,'core'=2] {'dp','core'}, dimensions={0} | all-to-all | bytes 262144 | tf_op jit(solution)/shard_map/all_to_all | solution.py:428
  24.0 2.3 %shard_map.95 = bf16[256,2048]{1,0:T(8,128)(2,1)} custom-call(s32[256,128]{1,0:T(8,128)S(1)} %bitcast.32, bf16[64,2048]{1,0:T(8,128)(2,1)} %t0.3, bf16[64,2048]{1,0:T(8,128)(2,1)S(1)} %collective-permute-done.3.t1, bf16[64,2048]{1,0:T(8,128)(2,1)S(1)} %collective-permute-done.4.t2, bf16[64,2048]{1,0:T(8,128)(2,1)S(1)} %collective-permute-done.5.t3), custom_call_target="tpu_custom_call" | custom-call | flops 268435456 | bytes 3000000 | tf_op jit(solution)/shard_map/pallas_call | solution.py:122
  26.3 4.7 %all-to-all-start.2 = ((bf16[32,8,2048]{2,1,0:T(8,128)(2,1)}), bf16[32,8,2048]{2,1,0:T(8,128)(2,1)}, u32[]{:S(2)}, u32[]{:S(2)}) async-start(bf16[32,8,2048]{2,1,0:T(8,128)(2,1)} %bitcast.6), calls=%async_computation.2 | async-start | bytes 2097152 | tf_op jit(solution)/shard_map/all_to_all | solution.py:428
  31.0 2.1 %collective-permute-start = (bf16[64,2048]{1,0:T(8,128)(2,1)S(1)}, bf16[64,2048]{1,0:T(8,128)(2,1)S(1)}, u32[]{:S(2)}, u32[]{:S(2)}) collective-permute-start(bf16[64,2048]{1,0:T(8,128)(2,1)S(1)} %copy-done.5), channel_id=1, source_target_pairs={{0,6},{2,0},{4,2},{6,4},{1,7},{3,1},{5,3},{7,5},{8,14},{10,8},{12,... | collective-permute-start | bytes 786440 | tf_op jit(solution)/shard_map/ppermute | solution.py:420
  33.0 1.4 collective-permute-start.1
  34.5 4.4 %collective-permute-done.t1 = bf16[64,2048]{1,0:T(8,128)(2,1)S(1)} collective-permute-done((bf16[64,2048]{1,0:T(8,128)(2,1)S(1)}, bf16[64,2048]{1,0:T(8,128)(2,1)S(1)}, u32[]{:S(2)}, u32[]{:S(2)}) %collective-permute-start) | collective-permute-done | bytes 262176 | tf_op jit(solution)/shard_map/ppermute | solution.py:420
  38.9 3.0 %collective-permute-done.1.t2 = bf16[64,2048]{1,0:T(8,128)(2,1)S(1)} collective-permute-done((bf16[64,2048]{1,0:T(8,128)(2,1)S(1)}, bf16[64,2048]{1,0:T(8,128)(2,1)S(1)}, u32[]{:S(2)}, u32[]{:S(2)}) %collective-permute-start.1) | collective-permute-done | bytes 262176 | tf_op jit(solution)/shard_map/ppermute | solution.py:420
  41.9 6.5 %collective-permute-done.2.t3 = bf16[64,2048]{1,0:T(8,128)(2,1)S(1)} collective-permute-done((bf16[64,2048]{1,0:T(8,128)(2,1)S(1)}, bf16[64,2048]{1,0:T(8,128)(2,1)S(1)}, u32[]{:S(2)}, u32[]{:S(2)}) %collective-permute-start.2) | collective-permute-done | bytes 262176 | tf_op jit(solution)/shard_map/ppermute | solution.py:420
  48.4 2.2 %shard_map.94 = bf16[256,2048]{1,0:T(8,128)(2,1)} custom-call(s32[256,128]{1,0:T(8,128)S(1)} %bitcast.33, bf16[64,2048]{1,0:T(8,128)(2,1)} %t0.2, bf16[64,2048]{1,0:T(8,128)(2,1)S(1)} %collective-permute-done.t1, bf16[64,2048]{1,0:T(8,128)(2,1)S(1)} %collective-permute-done.1.t2, bf16[64,2048]{1,0:T(8,128)(2,1)S(1)} %collective-permute-done.2.t3), custom_call_target="tpu_custom_call" | custom-call | flops 268435456 | bytes 3000000 | tf_op jit(solution)/shard_map/pallas_call | solution.py:122
  50.6 7.6 %all-to-all-start.1 = ((bf16[32,8,2048]{2,1,0:T(8,128)(2,1)}), bf16[32,8,2048]{2,1,0:T(8,128)(2,1)S(1)}, u32[]{:S(2)}, u32[]{:S(2)}) async-start(bf16[32,8,2048]{2,1,0:T(8,128)(2,1)} %bitcast.4), calls=%async_computation.1 | async-start | bytes 2097152 | tf_op jit(solution)/shard_map/all_to_all | solution.py:428
  58.3 2.8 %weight.1.side_hbm = f32[4,256,512]{2,1,0:T(8,128)S(1)} custom-call(s32[16,2048]{1,0:T(8,128)S(1)} %get-tuple-element.22.places_ref.refs_0_, f32[16,2048]{1,0:T(8,128)S(1)} %bitcast.38), custom_call_target="tpu_custom_call" | custom-call | flops 25165824 | bytes 2097152 | tf_op jit(solution)/shard_map/weight/pallas_call | solution.py:154
  61.2 1.3 copy-done
  62.8 1.1 collective-permute-start.14
  64.0 10.5 %first.1 = (f32[4,256,512]{2,1,0:T(8,128)}, bf16[128,2,2048]{2,1,0:T(2,128)(2,1)}) custom-call(bf16[2048,2048]{1,0:T(8,128)(2,1)} %other_hbm.3, bf16[2048,2048]{1,0:T(8,128)(2,1)} %lead_hbm.3, bf16[256,2048]{1,0:T(8,128)(2,1)} %bitcast.7.rows_hbm.d0, f32[4,256,512]{2,1,0:T(8,128)} %copy-done), custom_call_target="tpu_custom_call" | custom-call | flops 4294967296 | bytes 25165824 | tf_op jit(solution)/shard_map/first/pallas_call | solution.py:266
  74.5 0.8 all-to-all-done.1
  75.3 1.0 copy-done.4
  76.3 14.1 %second.1 = (bf16[16,512]{1,0:T(8,128)(2,1)}, bf16[16,512]{1,0:T(8,128)(2,1)}, bf16[16,512]{1,0:T(8,128)(2,1)}, bf16[16,512]{1,0:T(8,128)(2,1)}, bf16[128,2,2048]{2,1,0:T(2,128)(2,1)}) custom-call(bf16[2048,2048]{1,0:T(8,128)(2,1)} %lead_hbm.3, bf16[2048,2048]{1,0:T(8,128)(2,1)} %other_hbm.3, bf16[256,2048]{1,0:T(8,128)(2,1)} %bitcast.39, ...), custom_call_target="tpu_custom_call" | custom-call | flops 4294967296 | bytes 25165824 | tf_op jit(solution)/shard_map/second/pallas_call | solution.py:266
  90.4 8.3 %all-to-all-start.3 = ((bf16[128,2,2048]{2,1,0:T(2,128)(2,1)}), bf16[128,2,2048]{2,1,0:T(2,128)(2,1)}, u32[]{:S(2)}, u32[]{:S(2)}) async-start(bf16[128,2,2048]{2,1,0:T(2,128)(2,1)} %get-tuple-element.15), calls=%async_computation.3 | async-start | bytes 2097152 | tf_op jit(solution)/shard_map/all_to_all | solution.py:428
  98.7 0.8 slice.8
  99.6 2.6 %collective-permute-start.13 = (bf16[128,2048]{1,0:T(8,128)(2,1)}, bf16[128,2048]{1,0:T(8,128)(2,1)S(1)}, u32[]{:S(2)}, u32[]{:S(2)}) collective-permute-start(bf16[128,2048]{1,0:T(8,128)(2,1)} %slice.8), channel_id=1, source_target_pairs={{0,6},{2,0},{4,2},{6,4},{1,7},{3,1},{5,3},{7,5},{8,14},{10,8},{12,... | collective-permute-start | bytes 1572872 | tf_op jit(solution)/shard_map/ppermute | solution.py:420
  102.2 0.8 slice.9
  103.0 1.8 %collective-permute-start.10 = (s32[16,512]{1,0:T(8,128)S(1)}, s32[16,512]{1,0:T(8,128)S(1)}, u32[]{:S(2)}, u32[]{:S(2)}) collective-permute-start(s32[16,512]{1,0:T(8,128)S(1)} %get-tuple-element.18), channel_id=1, source_target_pairs={{0,4},{2,6},{4,0},{6,2},{1,5},{3,7},{5,1},{7,3},{8,12},{10,14},{12... | collective-permute-start | bytes 98312 | tf_op jit(solution)/shard_map/ppermute | solution.py:420
  104.8 1.5 collective-permute-start.11
  106.4 1.1 collective-permute-start.9
  107.5 10.2 %all-to-all-done.3.got_hbm = bf16[128,2,2048]{2,1,0:T(2,128)(2,1)} async-done(((bf16[128,2,2048]{2,1,0:T(2,128)(2,1)}), bf16[128,2,2048]{2,1,0:T(2,128)(2,1)}, u32[]{:S(2)}, u32[]{:S(2)}) %all-to-all-start.3) | async-done | bytes 1048608 | tf_op jit(solution)/shard_map/all_to_all | solution.py:428
  117.7 4.9 %all-to-all-start.4 = ((bf16[128,2,2048]{2,1,0:T(2,128)(2,1)}), bf16[128,2,2048]{2,1,0:T(2,128)(2,1)}, u32[]{:S(2)}, u32[]{:S(2)}) async-start(bf16[128,2,2048]{2,1,0:T(2,128)(2,1)} %get-tuple-element.16), calls=%async_computation.4 | async-start | bytes 2097152 | tf_op jit(solution)/shard_map/all_to_all | solution.py:428
  122.5 1.6 collective-permute-done.10.p2
  124.1 1.3 collective-permute-start.6
  125.4 0.7 collective-permute-start.7
  126.1 0.3 collective-permute-start.8
  126.5 4.2 %collective-permute-done.6.c1 = bf16[16,512]{1,0:T(8,128)(2,1)S(1)} collective-permute-done((bf16[16,512]{1,0:T(8,128)(2,1)}, bf16[16,512]{1,0:T(8,128)(2,1)S(1)}, u32[]{:S(2)}, u32[]{:S(2)}) %collective-permute-start.6) | collective-permute-done | bytes 16416 | tf_op jit(solution)/shard_map/ppermute | solution.py:420
  130.7 1.1 collective-permute-done.7.c2
  131.8 1.6 collective-permute-done.8.c3
  133.4 3.6 %give.1 = bf16[256,2048]{1,0:T(8,128)(2,1)} custom-call(bf16[16,512]{1,0:T(8,128)(2,1)S(1)} %copy-done.3, bf16[16,512]{1,0:T(8,128)(2,1)S(1)} %collective-permute-done.6.c1, bf16[16,512]{1,0:T(8,128)(2,1)S(1)} %collective-permute-done.7.c2, bf16[16,512]{1,0:T(8,128)(2,1)S(1)} %collective-permute-done.8.c3, s32[16,512]{1,0:T(8,128)S(1)} %get-tuple-element.20.p0, ...), custom_call_target="tpu_custom_call" | custom-call | flops 1073741824 | bytes 6291456 | tf_op jit(solution)/shard_map/give/pallas_call | solution.py:402
  137.0 0.7 collective-permute-start.16
  137.8 3.1 %collective-permute-start.17 = (s32[256,128]{1,0:T(8,128)S(1)}, s32[256,128]{1,0:T(8,128)S(1)}, u32[]{:S(2)}, u32[]{:S(2)}) collective-permute-start(s32[256,128]{1,0:T(8,128)S(1)} %bitcast.34), channel_id=1, source_target_pairs={{0,6},{2,0},{4,2},{6,4},{1,7},{3,1},{5,3},{7,5},{8,14},{10,8},{12,... | collective-permute-start | bytes 393224 | tf_op jit(solution)/shard_map/ppermute | solution.py:420
  141.1 0.3 collective-permute-start.19
  141.4 4.9 %collective-permute-done.17.a1 = s32[256,128]{1,0:T(8,128)S(1)} collective-permute-done((s32[256,128]{1,0:T(8,128)S(1)}, s32[256,128]{1,0:T(8,128)S(1)}, u32[]{:S(2)}, u32[]{:S(2)}) %collective-permute-start.17) | collective-permute-done | bytes 131104 | tf_op jit(solution)/shard_map/ppermute | solution.py:420
  146.3 0.8 collective-permute-done.18.a2
  147.1 3.4 %collective-permute-done.19.a3 = s32[256,128]{1,0:T(8,128)S(1)} collective-permute-done((s32[256,128]{1,0:T(8,128)S(1)}, s32[256,128]{1,0:T(8,128)S(1)}, u32[]{:S(2)}, u32[]{:S(2)}) %collective-permute-start.19) | collective-permute-done | bytes 131104 | tf_op jit(solution)/shard_map/ppermute | solution.py:420
  150.8 2.4 %shard_map.96 = f32[64,2048]{1,0:T(8,128)} custom-call(bf16[256,64]{1,0:T(8,128)(2,1)S(1)} %hits.1.hits_ref, bf16[128,2,2048]{2,1,0:T(2,128)(2,1)} %all-to-all-done.3.got_hbm), custom_call_target="tpu_custom_call" | custom-call | flops 268435456 | bytes 2000000 | tf_op jit(solution)/shard_map/pallas_call | solution.py:343
  153.2 2.4 %shard_map.97 = f32[64,2048]{1,0:T(8,128)} custom-call(bf16[256,64]{1,0:T(8,128)(2,1)S(1)} %hits.1.hits_ref, bf16[128,2,2048]{2,1,0:T(2,128)(2,1)} %all-to-all-done.4.got_hbm), custom_call_target="tpu_custom_call" | custom-call | flops 268435456 | bytes 2000000 | tf_op jit(solution)/shard_map/pallas_call | solution.py:343
  155.6 3.6 %keep.1 = bf16[256,2048]{1,0:T(8,128)(2,1)S(1)} custom-call(bf16[16,512]{1,0:T(8,128)(2,1)S(1)} %copy-done.3, bf16[16,512]{1,0:T(8,128)(2,1)S(1)} %collective-permute-done.6.c1, bf16[16,512]{1,0:T(8,128)(2,1)S(1)} %collective-permute-done.7.c2, bf16[16,512]{1,0:T(8,128)(2,1)S(1)} %collective-permute-done.8.c3, s32[16,512]{1,0:T(8,128)S(1)} %get-tuple-element.20.p0, ...), custom_call_target="tpu_custom_call" | custom-call | flops 1073741824 | bytes 6291456 | tf_op jit(solution)/shard_map/keep/pallas_call | solution.py:402
  159.2 2.6 %add_convert_fusion = bf16[256,2048]{1,0:T(8,128)(2,1)} fusion(bf16[256,2048]{1,0:T(8,128)(2,1)} %collective-permute-done.16, bf16[256,2048]{1,0:T(8,128)(2,1)S(1)} %keep.1), kind=kLoop, calls=%fused_computation | loop fusion | flops 2097152 | bytes 3145728 | tf_op jit(solution)/shard_map/convert_element_type | solution.py:469
  (31 shorter events, 1.0 us)
Async XLA Ops:
  0.6 23.3 %collective-permute-start.3 = (bf16[64,2048]{1,0:T(8,128)(2,1)}, bf16[64,2048]{1,0:T(8,128)(2,1)S(1)}, u32[]{:S(2)}, u32[]{:S(2)}) collective-permute-start(bf16[64,2048]{1,0:T(8,128)(2,1)} %t0.3), channel_id=1, source_target_pairs={{0,6},{2,0},{4,2},{6,4},{1,7},{3,1},{5,3},{7,5},{8,14},{10,8},{12,... | collective-permute-start | bytes 786440 | tf_op jit(solution)/shard_map/ppermute | solution.py:420
  4.3 19.7 %collective-permute-start.4 = (bf16[64,2048]{1,0:T(8,128)(2,1)}, bf16[64,2048]{1,0:T(8,128)(2,1)S(1)}, u32[]{:S(2)}, u32[]{:S(2)}) collective-permute-start(bf16[64,2048]{1,0:T(8,128)(2,1)} %t0.3), channel_id=1, source_target_pairs={{0,4},{2,6},{4,0},{6,2},{1,5},{3,7},{5,1},{7,3},{8,12},{10,14},{12... | collective-permute-start | bytes 786440 | tf_op jit(solution)/shard_map/ppermute | solution.py:420
  4.6 19.3 %collective-permute-start.5 = (bf16[64,2048]{1,0:T(8,128)(2,1)}, bf16[64,2048]{1,0:T(8,128)(2,1)S(1)}, u32[]{:S(2)}, u32[]{:S(2)}) collective-permute-start(bf16[64,2048]{1,0:T(8,128)(2,1)} %t0.3), channel_id=1, source_target_pairs={{0,2},{2,4},{4,6},{6,0},{1,3},{3,5},{5,7},{7,1},{8,10},{10,12},{12... | collective-permute-start | bytes 786440 | tf_op jit(solution)/shard_map/ppermute | solution.py:420
  23.9 7.0 %copy-start.5 = (bf16[64,2048]{1,0:T(8,128)(2,1)S(1)}, bf16[64,2048]{1,0:T(8,128)(2,1)}, u32[]{:S(2)}) copy-start(bf16[64,2048]{1,0:T(8,128)(2,1)} %t0.2) | copy-start | bytes 786436
  26.3 24.4 %all-to-all-start.2 = ((bf16[32,8,2048]{2,1,0:T(8,128)(2,1)}), bf16[32,8,2048]{2,1,0:T(8,128)(2,1)}, u32[]{:S(2)}, u32[]{:S(2)}) async-start(bf16[32,8,2048]{2,1,0:T(8,128)(2,1)} %bitcast.6), calls=%async_computation.2 | async-start | bytes 2097152 | tf_op jit(solution)/shard_map/all_to_all | solution.py:428
  31.0 27.3 %copy-start.6 = (s32[1,2048,16]{1,2,0:T(8,128)S(1)}, s32[1,2048,16]{1,2,0:T(8,128)}, u32[]{:S(2)}) copy-start(s32[1,2048,16]{1,2,0:T(8,128)} %param.12) | copy-start | bytes 393220
  31.0 27.4 %copy-start.2 = (f32[1,2048,16]{1,2,0:T(8,128)S(1)}, f32[1,2048,16]{1,2,0:T(8,128)}, u32[]{:S(2)}) copy-start(f32[1,2048,16]{1,2,0:T(8,128)} %param.13) | copy-start | bytes 393220
  31.0 7.9 %collective-permute-start = (bf16[64,2048]{1,0:T(8,128)(2,1)S(1)}, bf16[64,2048]{1,0:T(8,128)(2,1)S(1)}, u32[]{:S(2)}, u32[]{:S(2)}) collective-permute-start(bf16[64,2048]{1,0:T(8,128)(2,1)S(1)} %copy-done.5), channel_id=1, source_target_pairs={{0,6},{2,0},{4,2},{6,4},{1,7},{3,1},{5,3},{7,5},{8,14},{10,8},{12,... | collective-permute-start | bytes 786440 | tf_op jit(solution)/shard_map/ppermute | solution.py:420
  33.0 8.8 %collective-permute-start.1 = (bf16[64,2048]{1,0:T(8,128)(2,1)S(1)}, bf16[64,2048]{1,0:T(8,128)(2,1)S(1)}, u32[]{:S(2)}, u32[]{:S(2)}) collective-permute-start(bf16[64,2048]{1,0:T(8,128)(2,1)S(1)} %copy-done.5), channel_id=1, source_target_pairs={{0,4},{2,6},{4,0},{6,2},{1,5},{3,7},{5,1},{7,3},{8,12},{10,14},{12... | collective-permute-start | bytes 786440 | tf_op jit(solution)/shard_map/ppermute | solution.py:420
  34.5 13.9 %collective-permute-start.2 = (bf16[64,2048]{1,0:T(8,128)(2,1)S(1)}, bf16[64,2048]{1,0:T(8,128)(2,1)S(1)}, u32[]{:S(2)}, u32[]{:S(2)}) collective-permute-start(bf16[64,2048]{1,0:T(8,128)(2,1)S(1)} %copy-done.5), channel_id=1, source_target_pairs={{0,2},{2,4},{4,6},{6,0},{1,3},{3,5},{5,7},{7,1},{8,10},{10,12},{12... | collective-permute-start | bytes 786440 | tf_op jit(solution)/shard_map/ppermute | solution.py:420
  50.6 24.7 %all-to-all-start.1 = ((bf16[32,8,2048]{2,1,0:T(8,128)(2,1)}), bf16[32,8,2048]{2,1,0:T(8,128)(2,1)S(1)}, u32[]{:S(2)}, u32[]{:S(2)}) async-start(bf16[32,8,2048]{2,1,0:T(8,128)(2,1)} %bitcast.4), calls=%async_computation.1 | async-start | bytes 2097152 | tf_op jit(solution)/shard_map/all_to_all | solution.py:428
  58.3 16.2 %copy-start.1 = (s32[16,2048]{1,0:T(8,128)}, s32[16,2048]{1,0:T(8,128)S(1)}, u32[]{:S(2)}) copy-start(s32[16,2048]{1,0:T(8,128)S(1)} %get-tuple-element.22.places_ref.refs_0_) | copy-start | bytes 393220
  61.2 1.3 copy-start
  62.5 36.2 %collective-permute-start.12 = (bf16[256,2048]{1,0:T(8,128)(2,1)}, bf16[256,2048]{1,0:T(8,128)(2,1)S(1)}, u32[]{:S(2)}, u32[]{:S(2)}) collective-permute-start(bf16[256,2048]{1,0:T(8,128)(2,1)} %bitcast.7.rows_hbm.d0), channel_id=1, source_target_pairs={{0,6},{2,0},{4,2},{6,4},{1,7},{3,1},{5,3},{7,5},{8,14},{10,8},{12,... | collective-permute-start | bytes 3145736 | tf_op jit(solution)/shard_map/ppermute | solution.py:420
  62.8 39.3 %collective-permute-start.14 = (bf16[256,2048]{1,0:T(8,128)(2,1)}, bf16[256,2048]{1,0:T(8,128)(2,1)S(1)}, u32[]{:S(2)}, u32[]{:S(2)}) collective-permute-start(bf16[256,2048]{1,0:T(8,128)(2,1)} %bitcast.7.rows_hbm.d0), channel_id=1, source_target_pairs={{0,2},{2,4},{4,6},{6,0},{1,3},{3,5},{5,7},{7,1},{8,10},{10,12},{12... | collective-permute-start | bytes 3145736 | tf_op jit(solution)/shard_map/ppermute | solution.py:420
  75.3 1.0 copy-start.4
  90.4 27.3 %all-to-all-start.3 = ((bf16[128,2,2048]{2,1,0:T(2,128)(2,1)}), bf16[128,2,2048]{2,1,0:T(2,128)(2,1)}, u32[]{:S(2)}, u32[]{:S(2)}) async-start(bf16[128,2,2048]{2,1,0:T(2,128)(2,1)} %get-tuple-element.15), calls=%async_computation.3 | async-start | bytes 2097152 | tf_op jit(solution)/shard_map/all_to_all | solution.py:428
  98.7 34.7 %copy-start.3 = (bf16[16,512]{1,0:T(8,128)(2,1)S(1)}, bf16[16,512]{1,0:T(8,128)(2,1)}, u32[]{:S(2)}) copy-start(bf16[16,512]{1,0:T(8,128)(2,1)} %get-tuple-element.11.c0) | copy-start | bytes 49156
  99.6 33.8 %collective-permute-start.13 = (bf16[128,2048]{1,0:T(8,128)(2,1)}, bf16[128,2048]{1,0:T(8,128)(2,1)S(1)}, u32[]{:S(2)}, u32[]{:S(2)}) collective-permute-start(bf16[128,2048]{1,0:T(8,128)(2,1)} %slice.8), channel_id=1, source_target_pairs={{0,6},{2,0},{4,2},{6,4},{1,7},{3,1},{5,3},{7,5},{8,14},{10,8},{12,... | collective-permute-start | bytes 1572872 | tf_op jit(solution)/shard_map/ppermute | solution.py:420
  103.0 30.4 %collective-permute-start.15 = (bf16[128,2048]{1,0:T(8,128)(2,1)}, bf16[128,2048]{1,0:T(8,128)(2,1)S(1)}, u32[]{:S(2)}, u32[]{:S(2)}) collective-permute-start(bf16[128,2048]{1,0:T(8,128)(2,1)} %slice.9), channel_id=1, source_target_pairs={{0,2},{2,4},{4,6},{6,0},{1,3},{3,5},{5,7},{7,1},{8,10},{10,12},{12... | collective-permute-start | bytes 1572872 | tf_op jit(solution)/shard_map/ppermute | solution.py:420
  103.0 21.1 %collective-permute-start.10 = (s32[16,512]{1,0:T(8,128)S(1)}, s32[16,512]{1,0:T(8,128)S(1)}, u32[]{:S(2)}, u32[]{:S(2)}) collective-permute-start(s32[16,512]{1,0:T(8,128)S(1)} %get-tuple-element.18), channel_id=1, source_target_pairs={{0,4},{2,6},{4,0},{6,2},{1,5},{3,7},{5,1},{7,3},{8,12},{10,14},{12... | collective-permute-start | bytes 98312 | tf_op jit(solution)/shard_map/ppermute | solution.py:420
  104.8 20.6 %collective-permute-start.11 = (s32[16,512]{1,0:T(8,128)S(1)}, s32[16,512]{1,0:T(8,128)S(1)}, u32[]{:S(2)}, u32[]{:S(2)}) collective-permute-start(s32[16,512]{1,0:T(8,128)S(1)} %get-tuple-element.17), channel_id=1, source_target_pairs={{0,2},{2,4},{4,6},{6,0},{1,3},{3,5},{5,7},{7,1},{8,10},{10,12},{12... | collective-permute-start | bytes 98312 | tf_op jit(solution)/shard_map/ppermute | solution.py:420
  106.4 19.8 %collective-permute-start.9 = (s32[16,512]{1,0:T(8,128)S(1)}, s32[16,512]{1,0:T(8,128)S(1)}, u32[]{:S(2)}, u32[]{:S(2)}) collective-permute-start(s32[16,512]{1,0:T(8,128)S(1)} %get-tuple-element.19), channel_id=1, source_target_pairs={{0,6},{2,0},{4,2},{6,4},{1,7},{3,1},{5,3},{7,5},{8,14},{10,8},{12,... | collective-permute-start | bytes 98312 | tf_op jit(solution)/shard_map/ppermute | solution.py:420
  117.7 35.5 %all-to-all-start.4 = ((bf16[128,2,2048]{2,1,0:T(2,128)(2,1)}), bf16[128,2,2048]{2,1,0:T(2,128)(2,1)}, u32[]{:S(2)}, u32[]{:S(2)}) async-start(bf16[128,2,2048]{2,1,0:T(2,128)(2,1)} %get-tuple-element.16), calls=%async_computation.4 | async-start | bytes 2097152 | tf_op jit(solution)/shard_map/all_to_all | solution.py:428
  124.1 6.6 %collective-permute-start.6 = (bf16[16,512]{1,0:T(8,128)(2,1)}, bf16[16,512]{1,0:T(8,128)(2,1)S(1)}, u32[]{:S(2)}, u32[]{:S(2)}) collective-permute-start(bf16[16,512]{1,0:T(8,128)(2,1)} %get-tuple-element.12), channel_id=1, source_target_pairs={{0,6},{2,0},{4,2},{6,4},{1,7},{3,1},{5,3},{7,5},{8,14},{10,8},{12,... | collective-permute-start | bytes 49160 | tf_op jit(solution)/shard_map/ppermute | solution.py:420
  125.4 6.4 %collective-permute-start.7 = (bf16[16,512]{1,0:T(8,128)(2,1)}, bf16[16,512]{1,0:T(8,128)(2,1)S(1)}, u32[]{:S(2)}, u32[]{:S(2)}) collective-permute-start(bf16[16,512]{1,0:T(8,128)(2,1)} %get-tuple-element.13), channel_id=1, source_target_pairs={{0,4},{2,6},{4,0},{6,2},{1,5},{3,7},{5,1},{7,3},{8,12},{10,14},{12... | collective-permute-start | bytes 49160 | tf_op jit(solution)/shard_map/ppermute | solution.py:420
  126.1 7.3 %collective-permute-start.8 = (bf16[16,512]{1,0:T(8,128)(2,1)}, bf16[16,512]{1,0:T(8,128)(2,1)S(1)}, u32[]{:S(2)}, u32[]{:S(2)}) collective-permute-start(bf16[16,512]{1,0:T(8,128)(2,1)} %get-tuple-element.14), channel_id=1, source_target_pairs={{0,2},{2,4},{4,6},{6,0},{1,3},{3,5},{5,7},{7,1},{8,10},{10,12},{12... | collective-permute-start | bytes 49160 | tf_op jit(solution)/shard_map/ppermute | solution.py:420
  137.0 22.1 %collective-permute-start.16 = (bf16[256,2048]{1,0:T(8,128)(2,1)}, bf16[256,2048]{1,0:T(8,128)(2,1)}, u32[]{:S(2)}, u32[]{:S(2)}) collective-permute-start(bf16[256,2048]{1,0:T(8,128)(2,1)} %give.1), channel_id=1, source_target_pairs={{0,1},{1,0},{2,3},{3,2},{4,5},{5,4},{6,7},{7,6},{8,9},{9,8},{10,11... | collective-permute-start | bytes 3145736 | tf_op jit(solution)/shard_map/ppermute | solution.py:467
  137.8 8.5 %collective-permute-start.17 = (s32[256,128]{1,0:T(8,128)S(1)}, s32[256,128]{1,0:T(8,128)S(1)}, u32[]{:S(2)}, u32[]{:S(2)}) collective-permute-start(s32[256,128]{1,0:T(8,128)S(1)} %bitcast.34), channel_id=1, source_target_pairs={{0,6},{2,0},{4,2},{6,4},{1,7},{3,1},{5,3},{7,5},{8,14},{10,8},{12,... | collective-permute-start | bytes 393224 | tf_op jit(solution)/shard_map/ppermute | solution.py:420
  140.8 6.2 %collective-permute-start.18 = (s32[256,128]{1,0:T(8,128)S(1)}, s32[256,128]{1,0:T(8,128)S(1)}, u32[]{:S(2)}, u32[]{:S(2)}) collective-permute-start(s32[256,128]{1,0:T(8,128)S(1)} %bitcast.35), channel_id=1, source_target_pairs={{0,4},{2,6},{4,0},{6,2},{1,5},{3,7},{5,1},{7,3},{8,12},{10,14},{12... | collective-permute-start | bytes 393224 | tf_op jit(solution)/shard_map/ppermute | solution.py:420
  141.1 9.4 %collective-permute-start.19 = (s32[256,128]{1,0:T(8,128)S(1)}, s32[256,128]{1,0:T(8,128)S(1)}, u32[]{:S(2)}, u32[]{:S(2)}) collective-permute-start(s32[256,128]{1,0:T(8,128)S(1)} %bitcast.36), channel_id=1, source_target_pairs={{0,2},{2,4},{4,6},{6,0},{1,3},{3,5},{5,7},{7,1},{8,10},{10,12},{12... | collective-permute-start | bytes 393224 | tf_op jit(solution)/shard_map/ppermute | solution.py:420

commit v8 on v6

--- a/solution.py
+++ b/solution.py
@@ -132,7 +132,7 @@
         ],
         compiler_params=params(8),
         cost_estimate=cost(2 * 256 * 256 * 2048, 3 * 10**6),
-    )(asked, *tables)
+    )(asked, stay(tables[0]), *tables[1:])
 
 
 def weight_kernel(places_ref, gates_ref, out_ref):
@@ -164,10 +164,12 @@
 
 
 def half_kernel(
-    first, lead_hbm, other_hbm, rows_hbm, side_hbm, extra_hbm, part_hbm,
-    lead, other, rows, side, left, slope, half, part,
-    lead_sems, other_sems, row_sem, side_sems, extra_sems, part_sems,
+    first, lead_hbm, other_hbm, rows_hbm, side_hbm, *refs
 ):
+    (
+        extra_hbm, part_hbm, lead, other, rows, side, left, slope, half, part,
+        lead_sems, other_sems, row_sem, side_sems, extra_sems, part_sems,
+    ) = refs[-16:]
     block = side.shape[2]
     width = lead.shape[1]
     step = width // N_Y
@@ -196,7 +198,8 @@
                 half[:, cols] = here
                 continue
             part[:, :, cols] = (half[:, cols] + here).astype(BF16).reshape(chunk)
-            out = copy(part.at[:, :, cols], part_hbm.at[:, :, cols], part_sems.at[j])
+            there = pl.ds((width if first else 0) + j * step, step)
+            out = copy(part.at[:, :, cols], part_hbm.at[:, :, there], part_sems.at[j])
             out.start()
             sent.append(out)
 
@@ -230,15 +233,19 @@
         out.wait()
 
 
-def half_terms(first, lead, other, rows, side, devices):
+def half_terms(lead, other, rows, side, devices, parts=None):
+    first = parts is None
     count, width = lead.shape
     slots = rows.shape[0]
-    chunks = (devices, slots // devices, width)
+    capacity = slots // devices
     extra = (side.shape, F32) if first else ((slots, count), BF16)
     return pl.pallas_call(
         functools.partial(half_kernel, first),
-        out_shape=(jax.ShapeDtypeStruct(*extra), jax.ShapeDtypeStruct(chunks, BF16)),
-        in_specs=[ANY] * 4,
+        out_shape=(
+            jax.ShapeDtypeStruct(*extra),
+            jax.ShapeDtypeStruct((devices, capacity, 2 * width), BF16),
+        ),
+        in_specs=[ANY] * (4 if first else 5),
         out_specs=(ANY,) * 2,
         scratch_shapes=[
             pltpu.VMEM((count, width), BF16),
@@ -248,13 +255,14 @@
             pltpu.VMEM((slots, count), BF16),
             pltpu.VMEM(side.shape, F32),
             pltpu.VMEM((slots, width), F32),
-            pltpu.VMEM(chunks, BF16),
+            pltpu.VMEM((devices, capacity, width), BF16),
             DMA((8,)), DMA((8,)), DMA, DMA((4,)), DMA((4,)), DMA((4,)),
         ],
+        input_output_aliases={} if first else {4: 1},
         compiler_params=params(56),
         cost_estimate=cost(4 * count * width * slots, 24 << 20),
         name="first" if first else "second",
-    )(lead, other, stay(rows), stay(side))
+    )(lead, other, stay(rows), stay(side), *(() if first else (parts,)))
 
 
 def compact_kernel(coef_ref, places_ref, c0, c1, c2, c3):
@@ -286,7 +294,7 @@
         compiler_params=params(8),
         cost_estimate=cost(2 * topk * coef.size, 2 * coef.size),
         name="compact",
-    )(coef, places)
+    )(stay(coef), places)
 
 
 def own_hits(lists, rows):
@@ -303,48 +311,69 @@
     return total.astype(BF16)
 
 
-def sums_kernel(a0, a1, a2, a3, got_hbm, out_hbm, got, sums, sems, out_sems):
-    rows, width = sums.shape
-    devices, capacity, _ = got.shape
+def hits_kernel(a0, a1, a2, a3, out_ref):
+    out_ref[...] = own_hits([a[...] for a in (a0, a1, a2, a3)], out_ref.shape[1])
+
+
+def hit_rows(lists, rows):
+    return pl.pallas_call(
+        hits_kernel,
+        out_shape=jax.ShapeDtypeStruct((lists[0].shape[0], rows), BF16),
+        in_specs=[VMEM] * N_Y,
+        out_specs=VMEM,
+        compiler_params=params(8),
+        cost_estimate=cost(10**7, 10**6),
+        name="hits",
+    )(*lists)
+
+
+def sums_kernel(hits_ref, got_hbm, down_hbm, up_hbm, got, sums, sems, out_sems):
+    width = down_hbm.shape[1]
+    devices, capacity, both = got.shape
     block = 512
+    pieces = both // block
     copies = []
-    for j in range(width // block):
+    for j in range(pieces):
         cols = pl.ds(j * block, block)
         copies.append(copy(got_hbm.at[:, :, cols], got.at[:, :, cols], sems.at[j]))
         copies[j].start()
-    hits = own_hits([a[...] for a in (a0, a1, a2, a3)], rows)
+    hits = hits_ref[...]
     sent = []
-    for j in range(width // block):
+    for j in range(pieces):
         copies[j].wait()
         cols = pl.ds(j * block, block)
         sums[:, cols] = dot(hits, got[:, :, cols].reshape(devices * capacity, block), TN)
-        c = copy(sums.at[:, cols], out_hbm.at[:, cols], out_sems.at[j])
+        out = (down_hbm, up_hbm)[2 * j // pieces]
+        c = copy(sums.at[:, cols], out.at[:, pl.ds(j * block % width, block)], out_sems.at[j])
         c.start()
         sent.append(c)
     for c in sent:
         c.wait()
 
 
-def sum_rows(lists, got, rows):
-    width = got.shape[2]
+def sum_rows(hits, got):
+    both = got.shape[2]
+    rows = hits.shape[1]
+    out = jax.ShapeDtypeStruct((rows, both // 2), F32)
     return pl.pallas_call(
         sums_kernel,
-        out_shape=jax.ShapeDtypeStruct((rows, width), F32),
-        in_specs=[VMEM] * N_Y + [ANY],
-        out_specs=ANY,
+        out_shape=(out, out),
+        in_specs=[VMEM, ANY],
+        out_specs=(ANY, ANY),
         scratch_shapes=[
             pltpu.VMEM(got.shape, BF16),
-            pltpu.VMEM((rows, width), F32),
-            DMA((4,)),
-            DMA((4,)),
+            pltpu.VMEM((rows, both), F32),
+            DMA((8,)),
+            DMA((8,)),
         ],
         compiler_params=params(12),
-        cost_estimate=cost(2 * 256 * 256 * 2048, 2 * 10**6),
-    )(*lists, stay(got))
+        cost_estimate=cost(2 * 256 * 256 * 2048, 4 * 10**6),
+        name="sums",
+    )(hits, stay(got))
 
 
 def final_kernel(
-    mine, c0, c1, c2, c3, p0, p1, p2, p3, d0, d1, d2a, d2b, d3, out_hbm, coef, rows, out, d_sems, out_sems
+    mine, c0, c1, c2, c3, p0, p1, p2, p3, d0, d1, d2, d3, out_hbm, coef, rows, out, d_sems, out_sems
 ):
     core = lax.axis_index("core")
     which = core if mine else 1 - core
@@ -353,7 +382,7 @@
     topk = c0.shape[0]
     loads = []
     start = 0
-    for i, d in enumerate((d0, d1, d2a, d2b, d3)):
+    for i, d in enumerate((d0, d1, d2, d3)):
         loads.append(copy(d, rows.at[pl.ds(start, d.shape[0]), :], d_sems.at[i]))
         start += d.shape[0]
     for c in loads:
@@ -389,13 +418,13 @@
     return pl.pallas_call(
         functools.partial(final_kernel, mine),
         out_shape=jax.ShapeDtypeStruct((half, width), BF16),
-        in_specs=[VMEM] * 8 + [ANY] * 5,
+        in_specs=[VMEM] * 8 + [ANY] * 4,
         out_specs=ANY,
         scratch_shapes=[
             pltpu.VMEM((N_Y * slots, half), BF16),
             pltpu.VMEM((N_Y * slots, width), BF16),
             pltpu.VMEM((half, width), BF16),
-            DMA((5,)), DMA((4,)),
+            DMA((4,)), DMA((4,)),
         ],
         compiler_params=params(16),
         cost_estimate=cost(2 * half * 1024 * 2048, 6 << 20),
@@ -440,21 +469,18 @@
     ]
     chip_places = gathered(blocks)
     up = column(gather_rows(asked, up_tables, width))
-    above, below = turn(down, 1), turn(down, 3)
-    slope, part_up = half_terms(True, tokens, out_grad, down, weight, devices)
-    got_up = exchange(part_up, ("dp", "core", "y"))
-    far = (turn(above[: slots // 2], 1), turn(below[slots // 2 :], 3))
-    coef, part_down = half_terms(False, out_grad, tokens, up, slope, devices)
+    down_all = gathered([down] * N_Y)
+    hits = hit_rows(lists, row_count)
+    slope, parts = half_terms(tokens, out_grad, down, weight, devices)
+    coef, parts = half_terms(out_grad, tokens, up, slope, devices, parts)
+    got = exchange(parts, ("dp", "core", "y"))
     small = compact(coef, slot_of)
     chip_coef = gathered(small)
-    got_down = exchange(part_down, ("dp", "core", "y"))
-    up_grad = sum_rows(lists, got_up, row_count)
-    down_all = (down, above, *far, below)
     give = final_product(False, chip_coef, chip_places, down_all)
     other = lax.ppermute(give, "core", [(0, 1), (1, 0)])
     keep = final_product(True, chip_coef, chip_places, down_all)
     input_grad = (keep.astype(F32) + other.astype(F32)).astype(BF16)
-    down_grad = sum_rows(lists, got_down, row_count)
+    down_grad, up_grad = sum_rows(hits, got)
     return (input_grad, down_grad, up_grad)
 
 

time: 161 us -> 176 us (1.093)
  waiting for transfers between devices: 33.4 us -> 62.1 us
  local copies, waits for them, and re-layouts: 10.1 us -> 2.64 us
  starting transfers between devices: 51.9 us -> 46.3 us
    ppermute x19 -> x18, waiting for transfers between devices: 30 us -> 62 us  [turn(): return lax.ppermute(x, 'y', [(i, (i - r) % N_Y) for i in range(N_Y)])]
    unnamed x56 -> x12, local copies, waits for them, and re-layouts: 6.96 us -> 2.62 us
    all_to_all x4 -> x3, starting transfers between devices: 27.3 us -> 22.9 us  [exchange(): return lax.all_to_all(x, axes, split_axis=0, concat_axis=0, tiled=True)]
    ppermute x19 -> x18, starting transfers between devices: 23.4 us -> 19.7 us  [turn(): return lax.ppermute(x, 'y', [(i, (i - r) % N_Y) for i in range(N_Y)])]
    all_to_all x4 -> x3, waiting for transfers between devices: 3.37 us -> 0.03 us  [exchange(): return lax.all_to_all(x, axes, split_axis=0, concat_axis=0, tiled=True)]
    ppermute x1, starting transfers between devices: 1.27 us -> 3.72 us  [program(): other = lax.ppermute(give, 'core', [(0, 1), (1, 0)])]
  transfers between devices with their start and end apart: 24 -> 22, of which waited for: 12 -> 10; matrix products, arithmetic and copies ran while one was open for 2% -> 0% of each run, Pallas kernels for 26% -> 24%
where the time goes in v8:
time: 176 us
  waiting for transfers between devices  62.1 us (35%)
  starting transfers between devices  46.3 us (26%)
  Pallas kernels  44.1 us (25%)
  blocking collectives  17 us (10%)
  local copies, waits for them, and re-layouts  2.64 us (2%)
  other arithmetic  2.63 us (1%)
    ppermute x18, waiting for transfers between devices, turn(): return lax.ppermute(x, 'y', [(i, (i - r) % N_Y) for i in range(N_Y)])  62 us
    all_to_all x3, starting transfers between devices, exchange(): return lax.all_to_all(x, axes, split_axis=0, concat_axis=0, tiled=True)  22.9 us
    pallas_call x2, Pallas kernels, half_terms(): pl.pallas_call(functools.partial(half_kernel, first), out_shape=(jax.Shap...  20.3 us
    ppermute x18, starting transfers between devices, turn(): return lax.ppermute(x, 'y', [(i, (i - r) % N_Y) for i in range(N_Y)])  19.7 us
    all_to_all x1, blocking collectives, exchange(): return lax.all_to_all(x, axes, split_axis=0, concat_axis=0, tiled=True)  17 us
    pallas_call x2, Pallas kernels, final_product(): pl.pallas_call(functools.partial(final_kernel, mine), out_shape=jax.Shape...  7.3 us
    pallas_call x2, Pallas kernels, gather_rows(): pl.pallas_call(gather_kernel, out_shape=jax.ShapeDtypeStruct((slots, widt...  4.53 us
    pallas_call x1, Pallas kernels, compact(): pl.pallas_call(compact_kernel, out_shape=tuple((jax.ShapeDtypeStruct((top...  3.83 us
  transfers between devices with their start and end apart: 22, of which 10 were waited for; matrix products, arithmetic and copies ran while one was open for 0% of the time, Pallas kernels for 24%

profile of v8, /device:TPU:1, one launch (start us, length us, event | category | flops | bytes accessed | tf_op | source)
XLA Modules:
  0.0 175.7 jit_solution(13189809709602248264)
XLA Ops:
  0.6 3.6 %collective-permute-start.3 = (bf16[64,2048]{1,0:T(8,128)(2,1)}, bf16[64,2048]{1,0:T(8,128)(2,1)S(1)}, u32[]{:S(2)}, u32[]{:S(2)}) collective-permute-start(bf16[64,2048]{1,0:T(8,128)(2,1)} %t0.3), channel_id=1, source_target_pairs={{0,6},{2,0},{4,2},{6,4},{1,7},{3,1},{5,3},{7,5},{8,14},{10,8},{12,... | collective-permute-start | bytes 786440 | tf_op jit(solution)/shard_map/ppermute | solution.py:436
  4.3 0.3 collective-permute-start.4
  4.6 0.7 collective-permute-start.5
  5.3 1.6 ids.1
  6.9 17.0 %all_to_all.20 = s32[32,8,128]{2,1,0:T(8,128)S(1)} all-to-all(s32[32,8,128]{2,1,0:T(8,128)} %bitcast.39), channel_id=1, replica_groups=mesh['dp'=16,'y'=4,'core'=2] {'dp','core'}, dimensions={0} | all-to-all | bytes 262144 | tf_op jit(solution)/shard_map/all_to_all | solution.py:444
  23.9 0.0 copy-start.4
  24.0 2.3 %shard_map.95 = bf16[256,2048]{1,0:T(8,128)(2,1)} custom-call(s32[256,128]{1,0:T(8,128)S(1)} %bitcast.32, bf16[64,2048]{1,0:T(8,128)(2,1)} %t0.3, bf16[64,2048]{1,0:T(8,128)(2,1)S(1)} %collective-permute-done.3.t1, bf16[64,2048]{1,0:T(8,128)(2,1)S(1)} %collective-permute-done.4.t2, bf16[64,2048]{1,0:T(8,128)(2,1)S(1)} %collective-permute-done.5.t3), custom_call_target="tpu_custom_call" | custom-call | flops 268435456 | bytes 3000000 | tf_op jit(solution)/shard_map/pallas_call | solution.py:122
  26.3 4.7 %all-to-all-start.2 = ((bf16[32,8,2048]{2,1,0:T(8,128)(2,1)}), bf16[32,8,2048]{2,1,0:T(8,128)(2,1)}, u32[]{:S(2)}, u32[]{:S(2)}) async-start(bf16[32,8,2048]{2,1,0:T(8,128)(2,1)} %bitcast.6), calls=%async_computation.2 | async-start | bytes 2097152 | tf_op jit(solution)/shard_map/all_to_all | solution.py:444
  31.0 2.1 %collective-permute-start = (bf16[64,2048]{1,0:T(8,128)(2,1)S(1)}, bf16[64,2048]{1,0:T(8,128)(2,1)S(1)}, u32[]{:S(2)}, u32[]{:S(2)}) collective-permute-start(bf16[64,2048]{1,0:T(8,128)(2,1)S(1)} %copy-done.4), channel_id=1, source_target_pairs={{0,6},{2,0},{4,2},{6,4},{1,7},{3,1},{5,3},{7,5},{8,14},{10,8},{12,... | collective-permute-start | bytes 786440 | tf_op jit(solution)/shard_map/ppermute | solution.py:436
  33.0 1.4 collective-permute-start.1
  34.4 4.4 %collective-permute-done.t1 = bf16[64,2048]{1,0:T(8,128)(2,1)S(1)} collective-permute-done((bf16[64,2048]{1,0:T(8,128)(2,1)S(1)}, bf16[64,2048]{1,0:T(8,128)(2,1)S(1)}, u32[]{:S(2)}, u32[]{:S(2)}) %collective-permute-start) | collective-permute-done | bytes 262176 | tf_op jit(solution)/shard_map/ppermute | solution.py:436
  38.9 3.0 %collective-permute-done.1.t2 = bf16[64,2048]{1,0:T(8,128)(2,1)S(1)} collective-permute-done((bf16[64,2048]{1,0:T(8,128)(2,1)S(1)}, bf16[64,2048]{1,0:T(8,128)(2,1)S(1)}, u32[]{:S(2)}, u32[]{:S(2)}) %collective-permute-start.1) | collective-permute-done | bytes 262176 | tf_op jit(solution)/shard_map/ppermute | solution.py:436
  41.9 6.5 %collective-permute-done.2.t3 = bf16[64,2048]{1,0:T(8,128)(2,1)S(1)} collective-permute-done((bf16[64,2048]{1,0:T(8,128)(2,1)S(1)}, bf16[64,2048]{1,0:T(8,128)(2,1)S(1)}, u32[]{:S(2)}, u32[]{:S(2)}) %collective-permute-start.2) | collective-permute-done | bytes 262176 | tf_op jit(solution)/shard_map/ppermute | solution.py:436
  48.4 2.2 %shard_map.94 = bf16[256,2048]{1,0:T(8,128)(2,1)} custom-call(s32[256,128]{1,0:T(8,128)S(1)} %bitcast.33, bf16[64,2048]{1,0:T(8,128)(2,1)} %t0.2, bf16[64,2048]{1,0:T(8,128)(2,1)S(1)} %collective-permute-done.t1, bf16[64,2048]{1,0:T(8,128)(2,1)S(1)} %collective-permute-done.1.t2, bf16[64,2048]{1,0:T(8,128)(2,1)S(1)} %collective-permute-done.2.t3), custom_call_target="tpu_custom_call" | custom-call | flops 268435456 | bytes 3000000 | tf_op jit(solution)/shard_map/pallas_call | solution.py:122
  50.6 7.7 %all-to-all-start.1 = ((bf16[32,8,2048]{2,1,0:T(8,128)(2,1)}), bf16[32,8,2048]{2,1,0:T(8,128)(2,1)}, u32[]{:S(2)}, u32[]{:S(2)}) async-start(bf16[32,8,2048]{2,1,0:T(8,128)(2,1)} %bitcast.4), calls=%async_computation.1 | async-start | bytes 2097152 | tf_op jit(solution)/shard_map/all_to_all | solution.py:444
  58.4 2.8 %weight.1.side_hbm = f32[4,256,512]{2,1,0:T(8,128)S(1)} custom-call(s32[16,2048]{1,0:T(8,128)S(1)} %get-tuple-element.28.places_ref, f32[16,2048]{1,0:T(8,128)S(1)} %bitcast.38), custom_call_target="tpu_custom_call" | custom-call | flops 25165824 | bytes 2097152 | tf_op jit(solution)/shard_map/weight/pallas_call | solution.py:154
  61.2 1.4 copy-done
  62.6 0.3 collective-permute-start.12
  62.9 1.4 collective-permute-start.13
  64.3 0.5 collective-permute-start.14
  64.9 10.5 %first.1 = (f32[4,256,512]{2,1,0:T(8,128)}, bf16[128,2,4096]{2,1,0:T(2,128)(2,1)}) custom-call(bf16[2048,2048]{1,0:T(8,128)(2,1)} %other_hbm.3, bf16[2048,2048]{1,0:T(8,128)(2,1)} %lead_hbm.3, bf16[256,2048]{1,0:T(8,128)(2,1)} %bitcast.7.rows_hbm.d0, f32[4,256,512]{2,1,0:T(8,128)} %copy-done), custom_call_target="tpu_custom_call" | custom-call | flops 4294967296 | bytes 25165824 | tf_op jit(solution)/shard_map/first/pallas_call | solution.py:242
  75.4 0.0 all-to-all-done.1
  75.4 9.8 %second.1 = (bf16[256,2048]{1,0:T(8,128)(2,1)}, bf16[128,2,4096]{2,1,0:T(2,128)(2,1)}) custom-call(bf16[2048,2048]{1,0:T(8,128)(2,1)} %lead_hbm.3, bf16[2048,2048]{1,0:T(8,128)(2,1)} %other_hbm.3, bf16[256,2048]{1,0:T(8,128)(2,1)} %bitcast.5.rows_hbm, f32[4,256,512]{2,1,0:T(8,128)} %get-tuple-element.13.side_hbm, ...), custom_call_target="tpu_custom_call", output_to_operand_aliasing={{1}: (4, {})} | custom-call | flops 4294967296 | bytes 25165824 | tf_op jit(solution)/shard_map/second/pallas_call | solution.py:242
  85.2 10.6 %all-to-all-start.3 = ((bf16[128,2,4096]{2,1,0:T(2,128)(2,1)}), bf16[128,2,4096]{2,1,0:T(2,128)(2,1)}, u32[]{:S(2)}, u32[]{:S(2)}) async-start(bf16[128,2,4096]{2,1,0:T(2,128)(2,1)} %get-tuple-element.20), calls=%async_computation.3 | async-start | bytes 4194304 | tf_op jit(solution)/shard_map/all_to_all | solution.py:444
  95.8 2.9 %collective-permute-start.10 = (s32[16,512]{1,0:T(8,128)S(1)}, s32[16,512]{1,0:T(8,128)S(1)}, u32[]{:S(2)}, u32[]{:S(2)}) collective-permute-start(s32[16,512]{1,0:T(8,128)S(1)} %get-tuple-element.24), channel_id=1, source_target_pairs={{0,4},{2,6},{4,0},{6,2},{1,5},{3,7},{5,1},{7,3},{8,12},{10,14},{12... | collective-permute-start | bytes 98312 | tf_op jit(solution)/shard_map/ppermute | solution.py:436
  98.8 0.3 collective-permute-start.11
  99.1 35.5 %collective-permute-done.10.p2 = s32[16,512]{1,0:T(8,128)S(1)} collective-permute-done((s32[16,512]{1,0:T(8,128)S(1)}, s32[16,512]{1,0:T(8,128)S(1)}, u32[]{:S(2)}, u32[]{:S(2)}) %collective-permute-start.10) | collective-permute-done | bytes 32800 | tf_op jit(solution)/shard_map/ppermute | solution.py:436
  134.6 0.9 collective-permute-start.9
  135.5 3.8 %compact.1 = (bf16[16,512]{1,0:T(8,128)(2,1)S(1)}, bf16[16,512]{1,0:T(8,128)(2,1)S(1)}, bf16[16,512]{1,0:T(8,128)(2,1)S(1)}, bf16[16,512]{1,0:T(8,128)(2,1)S(1)}) custom-call(bf16[256,2048]{1,0:T(8,128)(2,1)} %get-tuple-element.15.coef_ref, s32[16,2048]{1,0:T(8,128)S(1)} %get-tuple-element.28.places_ref), custom_call_target="tpu_custom_call" | custom-call | flops 16777216 | bytes 1048576 | tf_op jit(solution)/shard_map/compact/pallas_call | solution.py:289
  139.3 0.9 collective-permute-start.6
  140.2 1.6 collective-permute-start.7
  141.7 0.2 collective-permute-done.6.c1
  142.0 0.6 collective-permute-start.8
  142.5 1.7 collective-permute-done.7.c2
  144.3 1.5 collective-permute-done.8.c3
  145.8 3.7 %give.1 = bf16[256,2048]{1,0:T(8,128)(2,1)} custom-call(bf16[16,512]{1,0:T(8,128)(2,1)S(1)} %get-tuple-element.16.c0, bf16[16,512]{1,0:T(8,128)(2,1)S(1)} %collective-permute-done.6.c1, bf16[16,512]{1,0:T(8,128)(2,1)S(1)} %collective-permute-done.7.c2, bf16[16,512]{1,0:T(8,128)(2,1)S(1)} %collective-permute-done.8.c3, s32[16,512]{1,0:T(8,128)S(1)} %get-tuple-element.26.p0, ...), custom_call_target="tpu_custom_call" | custom-call | flops 1073741824 | bytes 6291456 | tf_op jit(solution)/shard_map/give/pallas_call | solution.py:418
  149.5 3.7 %collective-permute-start.15 = (bf16[256,2048]{1,0:T(8,128)(2,1)}, bf16[256,2048]{1,0:T(8,128)(2,1)}, u32[]{:S(2)}, u32[]{:S(2)}) collective-permute-start(bf16[256,2048]{1,0:T(8,128)(2,1)} %give.1), channel_id=1, source_target_pairs={{0,1},{1,0},{2,3},{3,2},{4,5},{5,4},{6,7},{7,6},{8,9},{9,8},{10,11... | collective-permute-start | bytes 3145736 | tf_op jit(solution)/shard_map/ppermute | solution.py:480
  153.2 1.5 collective-permute-start.16
  154.7 0.4 collective-permute-start.17
  155.1 0.2 collective-permute-start.18
  155.3 2.9 %collective-permute-done.16.a1 = s32[256,128]{1,0:T(8,128)S(1)} collective-permute-done((s32[256,128]{1,0:T(8,128)S(1)}, s32[256,128]{1,0:T(8,128)S(1)}, u32[]{:S(2)}, u32[]{:S(2)}) %collective-permute-start.16) | collective-permute-done | bytes 131104 | tf_op jit(solution)/shard_map/ppermute | solution.py:436
  158.2 2.8 %collective-permute-done.17.a2 = s32[256,128]{1,0:T(8,128)S(1)} collective-permute-done((s32[256,128]{1,0:T(8,128)S(1)}, s32[256,128]{1,0:T(8,128)S(1)}, u32[]{:S(2)}, u32[]{:S(2)}) %collective-permute-start.17) | collective-permute-done | bytes 131104 | tf_op jit(solution)/shard_map/ppermute | solution.py:436
  161.0 3.5 %collective-permute-done.18.a3 = s32[256,128]{1,0:T(8,128)S(1)} collective-permute-done((s32[256,128]{1,0:T(8,128)S(1)}, s32[256,128]{1,0:T(8,128)S(1)}, u32[]{:S(2)}, u32[]{:S(2)}) %collective-permute-start.18) | collective-permute-done | bytes 131104 | tf_op jit(solution)/shard_map/ppermute | solution.py:436
  164.5 0.3 hits.1.hits_ref
  164.8 1.2 copy-done.2
  166.0 3.6 %keep.1 = bf16[256,2048]{1,0:T(8,128)(2,1)S(1)} custom-call(bf16[16,512]{1,0:T(8,128)(2,1)S(1)} %get-tuple-element.16.c0, bf16[16,512]{1,0:T(8,128)(2,1)S(1)} %collective-permute-done.6.c1, bf16[16,512]{1,0:T(8,128)(2,1)S(1)} %collective-permute-done.7.c2, bf16[16,512]{1,0:T(8,128)(2,1)S(1)} %collective-permute-done.8.c3, ...), custom_call_target="tpu_custom_call" | custom-call | flops 1073741824 | bytes 6291456 | tf_op jit(solution)/shard_map/keep/pallas_call | solution.py:418
  169.6 3.4 %sums.1 = (f32[64,2048]{1,0:T(8,128)}, f32[64,2048]{1,0:T(8,128)}) custom-call(bf16[256,64]{1,0:T(8,128)(2,1)S(1)} %hits.1.hits_ref, bf16[128,2,4096]{2,1,0:T(2,128)(2,1)} %all-to-all-done.3.got_hbm), custom_call_target="tpu_custom_call" | custom-call | flops 268435456 | bytes 4000000 | tf_op jit(solution)/shard_map/sums/pallas_call | solution.py:358
  173.1 2.6 %add_convert_fusion = bf16[256,2048]{1,0:T(8,128)(2,1)} fusion(bf16[256,2048]{1,0:T(8,128)(2,1)} %collective-permute-done.15, bf16[256,2048]{1,0:T(8,128)(2,1)S(1)} %keep.1), kind=kLoop, calls=%fused_computation | loop fusion | flops 2097152 | bytes 3145728 | tf_op jit(solution)/shard_map/convert_element_type | solution.py:482
  (23 shorter events, 0.1 us)
Async XLA Ops:
  0.6 23.3 %collective-permute-start.3 = (bf16[64,2048]{1,0:T(8,128)(2,1)}, bf16[64,2048]{1,0:T(8,128)(2,1)S(1)}, u32[]{:S(2)}, u32[]{:S(2)}) collective-permute-start(bf16[64,2048]{1,0:T(8,128)(2,1)} %t0.3), channel_id=1, source_target_pairs={{0,6},{2,0},{4,2},{6,4},{1,7},{3,1},{5,3},{7,5},{8,14},{10,8},{12,... | collective-permute-start | bytes 786440 | tf_op jit(solution)/shard_map/ppermute | solution.py:436
  4.3 19.7 %collective-permute-start.4 = (bf16[64,2048]{1,0:T(8,128)(2,1)}, bf16[64,2048]{1,0:T(8,128)(2,1)S(1)}, u32[]{:S(2)}, u32[]{:S(2)}) collective-permute-start(bf16[64,2048]{1,0:T(8,128)(2,1)} %t0.3), channel_id=1, source_target_pairs={{0,4},{2,6},{4,0},{6,2},{1,5},{3,7},{5,1},{7,3},{8,12},{10,14},{12... | collective-permute-start | bytes 786440 | tf_op jit(solution)/shard_map/ppermute | solution.py:436
  4.6 19.3 %collective-permute-start.5 = (bf16[64,2048]{1,0:T(8,128)(2,1)}, bf16[64,2048]{1,0:T(8,128)(2,1)S(1)}, u32[]{:S(2)}, u32[]{:S(2)}) collective-permute-start(bf16[64,2048]{1,0:T(8,128)(2,1)} %t0.3), channel_id=1, source_target_pairs={{0,2},{2,4},{4,6},{6,0},{1,3},{3,5},{5,7},{7,1},{8,10},{10,12},{12... | collective-permute-start | bytes 786440 | tf_op jit(solution)/shard_map/ppermute | solution.py:436
  23.9 7.0 %copy-start.4 = (bf16[64,2048]{1,0:T(8,128)(2,1)S(1)}, bf16[64,2048]{1,0:T(8,128)(2,1)}, u32[]{:S(2)}) copy-start(bf16[64,2048]{1,0:T(8,128)(2,1)} %t0.2) | copy-start | bytes 786436
  26.3 24.4 %all-to-all-start.2 = ((bf16[32,8,2048]{2,1,0:T(8,128)(2,1)}), bf16[32,8,2048]{2,1,0:T(8,128)(2,1)}, u32[]{:S(2)}, u32[]{:S(2)}) async-start(bf16[32,8,2048]{2,1,0:T(8,128)(2,1)} %bitcast.6), calls=%async_computation.2 | async-start | bytes 2097152 | tf_op jit(solution)/shard_map/all_to_all | solution.py:444
  31.0 27.4 %copy-start.5 = (s32[1,2048,16]{1,2,0:T(8,128)S(1)}, s32[1,2048,16]{1,2,0:T(8,128)}, u32[]{:S(2)}) copy-start(s32[1,2048,16]{1,2,0:T(8,128)} %param.12) | copy-start | bytes 393220
  31.0 27.4 %copy-start.3 = (f32[1,2048,16]{1,2,0:T(8,128)S(1)}, f32[1,2048,16]{1,2,0:T(8,128)}, u32[]{:S(2)}) copy-start(f32[1,2048,16]{1,2,0:T(8,128)} %param.13) | copy-start | bytes 393220
  31.0 7.9 %collective-permute-start = (bf16[64,2048]{1,0:T(8,128)(2,1)S(1)}, bf16[64,2048]{1,0:T(8,128)(2,1)S(1)}, u32[]{:S(2)}, u32[]{:S(2)}) collective-permute-start(bf16[64,2048]{1,0:T(8,128)(2,1)S(1)} %copy-done.4), channel_id=1, source_target_pairs={{0,6},{2,0},{4,2},{6,4},{1,7},{3,1},{5,3},{7,5},{8,14},{10,8},{12,... | collective-permute-start | bytes 786440 | tf_op jit(solution)/shard_map/ppermute | solution.py:436
  33.0 8.8 %collective-permute-start.1 = (bf16[64,2048]{1,0:T(8,128)(2,1)S(1)}, bf16[64,2048]{1,0:T(8,128)(2,1)S(1)}, u32[]{:S(2)}, u32[]{:S(2)}) collective-permute-start(bf16[64,2048]{1,0:T(8,128)(2,1)S(1)} %copy-done.4), channel_id=1, source_target_pairs={{0,4},{2,6},{4,0},{6,2},{1,5},{3,7},{5,1},{7,3},{8,12},{10,14},{12... | collective-permute-start | bytes 786440 | tf_op jit(solution)/shard_map/ppermute | solution.py:436
  34.4 13.9 %collective-permute-start.2 = (bf16[64,2048]{1,0:T(8,128)(2,1)S(1)}, bf16[64,2048]{1,0:T(8,128)(2,1)S(1)}, u32[]{:S(2)}, u32[]{:S(2)}) collective-permute-start(bf16[64,2048]{1,0:T(8,128)(2,1)S(1)} %copy-done.4), channel_id=1, source_target_pairs={{0,2},{2,4},{4,6},{6,0},{1,3},{3,5},{5,7},{7,1},{8,10},{10,12},{12... | collective-permute-start | bytes 786440 | tf_op jit(solution)/shard_map/ppermute | solution.py:436
  50.6 24.8 %all-to-all-start.1 = ((bf16[32,8,2048]{2,1,0:T(8,128)(2,1)}), bf16[32,8,2048]{2,1,0:T(8,128)(2,1)}, u32[]{:S(2)}, u32[]{:S(2)}) async-start(bf16[32,8,2048]{2,1,0:T(8,128)(2,1)} %bitcast.4), calls=%async_computation.1 | async-start | bytes 2097152 | tf_op jit(solution)/shard_map/all_to_all | solution.py:444
  61.2 1.4 copy-start
  62.6 83.2 %collective-permute-start.12 = (bf16[256,2048]{1,0:T(8,128)(2,1)}, bf16[256,2048]{1,0:T(8,128)(2,1)S(1)}, u32[]{:S(2)}, u32[]{:S(2)}) collective-permute-start(bf16[256,2048]{1,0:T(8,128)(2,1)} %bitcast.7.rows_hbm.d0), channel_id=1, source_target_pairs={{0,6},{2,0},{4,2},{6,4},{1,7},{3,1},{5,3},{7,5},{8,14},{10,8},{12,... | collective-permute-start | bytes 3145736 | tf_op jit(solution)/shard_map/ppermute | solution.py:436
  62.9 82.8 %collective-permute-start.13 = (bf16[256,2048]{1,0:T(8,128)(2,1)}, bf16[256,2048]{1,0:T(8,128)(2,1)S(1)}, u32[]{:S(2)}, u32[]{:S(2)}) collective-permute-start(bf16[256,2048]{1,0:T(8,128)(2,1)} %bitcast.7.rows_hbm.d0), channel_id=1, source_target_pairs={{0,4},{2,6},{4,0},{6,2},{1,5},{3,7},{5,1},{7,3},{8,12},{10,14},{12... | collective-permute-start | bytes 3145736 | tf_op jit(solution)/shard_map/ppermute | solution.py:436
  64.3 81.4 %collective-permute-start.14 = (bf16[256,2048]{1,0:T(8,128)(2,1)}, bf16[256,2048]{1,0:T(8,128)(2,1)S(1)}, u32[]{:S(2)}, u32[]{:S(2)}) collective-permute-start(bf16[256,2048]{1,0:T(8,128)(2,1)} %bitcast.7.rows_hbm.d0), channel_id=1, source_target_pairs={{0,2},{2,4},{4,6},{6,0},{1,3},{3,5},{5,7},{7,1},{8,10},{10,12},{12... | collective-permute-start | bytes 3145736 | tf_op jit(solution)/shard_map/ppermute | solution.py:436
  85.2 84.5 %all-to-all-start.3 = ((bf16[128,2,4096]{2,1,0:T(2,128)(2,1)}), bf16[128,2,4096]{2,1,0:T(2,128)(2,1)}, u32[]{:S(2)}, u32[]{:S(2)}) async-start(bf16[128,2,4096]{2,1,0:T(2,128)(2,1)} %get-tuple-element.20), calls=%async_computation.3 | async-start | bytes 4194304 | tf_op jit(solution)/shard_map/all_to_all | solution.py:444
  95.8 38.8 %collective-permute-start.10 = (s32[16,512]{1,0:T(8,128)S(1)}, s32[16,512]{1,0:T(8,128)S(1)}, u32[]{:S(2)}, u32[]{:S(2)}) collective-permute-start(s32[16,512]{1,0:T(8,128)S(1)} %get-tuple-element.24), channel_id=1, source_target_pairs={{0,4},{2,6},{4,0},{6,2},{1,5},{3,7},{5,1},{7,3},{8,12},{10,14},{12... | collective-permute-start | bytes 98312 | tf_op jit(solution)/shard_map/ppermute | solution.py:436
  98.8 40.5 %collective-permute-start.11 = (s32[16,512]{1,0:T(8,128)S(1)}, s32[16,512]{1,0:T(8,128)S(1)}, u32[]{:S(2)}, u32[]{:S(2)}) collective-permute-start(s32[16,512]{1,0:T(8,128)S(1)} %get-tuple-element.23), channel_id=1, source_target_pairs={{0,2},{2,4},{4,6},{6,0},{1,3},{3,5},{5,7},{7,1},{8,10},{10,12},{12... | collective-permute-start | bytes 98312 | tf_op jit(solution)/shard_map/ppermute | solution.py:436
  134.6 5.6 %collective-permute-start.9 = (s32[16,512]{1,0:T(8,128)S(1)}, s32[16,512]{1,0:T(8,128)S(1)}, u32[]{:S(2)}, u32[]{:S(2)}) collective-permute-start(s32[16,512]{1,0:T(8,128)S(1)} %get-tuple-element.25), channel_id=1, source_target_pairs={{0,6},{2,0},{4,2},{6,4},{1,7},{3,1},{5,3},{7,5},{8,14},{10,8},{12,... | collective-permute-start | bytes 98312 | tf_op jit(solution)/shard_map/ppermute | solution.py:436
  139.3 2.7 %collective-permute-start.6 = (bf16[16,512]{1,0:T(8,128)(2,1)S(1)}, bf16[16,512]{1,0:T(8,128)(2,1)S(1)}, u32[]{:S(2)}, u32[]{:S(2)}) collective-permute-start(bf16[16,512]{1,0:T(8,128)(2,1)S(1)} %get-tuple-element.17), channel_id=1, source_target_pairs={{0,6},{2,0},{4,2},{6,4},{1,7},{3,1},{5,3},{7,5},{8,14},{10,8},{12,... | collective-permute-start | bytes 49160 | tf_op jit(solution)/shard_map/ppermute | solution.py:436
  140.2 4.1 %collective-permute-start.7 = (bf16[16,512]{1,0:T(8,128)(2,1)S(1)}, bf16[16,512]{1,0:T(8,128)(2,1)S(1)}, u32[]{:S(2)}, u32[]{:S(2)}) collective-permute-start(bf16[16,512]{1,0:T(8,128)(2,1)S(1)} %get-tuple-element.18), channel_id=1, source_target_pairs={{0,4},{2,6},{4,0},{6,2},{1,5},{3,7},{5,1},{7,3},{8,12},{10,14},{12... | collective-permute-start | bytes 49160 | tf_op jit(solution)/shard_map/ppermute | solution.py:436
  142.0 3.8 %collective-permute-start.8 = (bf16[16,512]{1,0:T(8,128)(2,1)S(1)}, bf16[16,512]{1,0:T(8,128)(2,1)S(1)}, u32[]{:S(2)}, u32[]{:S(2)}) collective-permute-start(bf16[16,512]{1,0:T(8,128)(2,1)S(1)} %get-tuple-element.19), channel_id=1, source_target_pairs={{0,2},{2,4},{4,6},{6,0},{1,3},{3,5},{5,7},{7,1},{8,10},{10,12},{12... | collective-permute-start | bytes 49160 | tf_op jit(solution)/shard_map/ppermute | solution.py:436
  145.8 3.7 %copy-start.1 = (bf16[256,2048]{1,0:T(8,128)(2,1)}, bf16[256,2048]{1,0:T(8,128)(2,1)S(1)}, u32[]{:S(2)}) copy-start(bf16[256,2048]{1,0:T(8,128)(2,1)S(1)} %collective-permute-done.14.d3) | copy-start | bytes 3145732
  149.5 23.6 %collective-permute-start.15 = (bf16[256,2048]{1,0:T(8,128)(2,1)}, bf16[256,2048]{1,0:T(8,128)(2,1)}, u32[]{:S(2)}, u32[]{:S(2)}) collective-permute-start(bf16[256,2048]{1,0:T(8,128)(2,1)} %give.1), channel_id=1, source_target_pairs={{0,1},{1,0},{2,3},{3,2},{4,5},{5,4},{6,7},{7,6},{8,9},{9,8},{10,11... | collective-permute-start | bytes 3145736 | tf_op jit(solution)/shard_map/ppermute | solution.py:480
  153.2 5.0 %collective-permute-start.16 = (s32[256,128]{1,0:T(8,128)S(1)}, s32[256,128]{1,0:T(8,128)S(1)}, u32[]{:S(2)}, u32[]{:S(2)}) collective-permute-start(s32[256,128]{1,0:T(8,128)S(1)} %bitcast.34), channel_id=1, source_target_pairs={{0,6},{2,0},{4,2},{6,4},{1,7},{3,1},{5,3},{7,5},{8,14},{10,8},{12,... | collective-permute-start | bytes 393224 | tf_op jit(solution)/shard_map/ppermute | solution.py:436
  154.7 6.2 %collective-permute-start.17 = (s32[256,128]{1,0:T(8,128)S(1)}, s32[256,128]{1,0:T(8,128)S(1)}, u32[]{:S(2)}, u32[]{:S(2)}) collective-permute-start(s32[256,128]{1,0:T(8,128)S(1)} %bitcast.35), channel_id=1, source_target_pairs={{0,4},{2,6},{4,0},{6,2},{1,5},{3,7},{5,1},{7,3},{8,12},{10,14},{12... | collective-permute-start | bytes 393224 | tf_op jit(solution)/shard_map/ppermute | solution.py:436
  155.1 9.3 %collective-permute-start.18 = (s32[256,128]{1,0:T(8,128)S(1)}, s32[256,128]{1,0:T(8,128)S(1)}, u32[]{:S(2)}, u32[]{:S(2)}) collective-permute-start(s32[256,128]{1,0:T(8,128)S(1)} %bitcast.36), channel_id=1, source_target_pairs={{0,2},{2,4},{4,6},{6,0},{1,3},{3,5},{5,7},{7,1},{8,10},{10,12},{12... | collective-permute-start | bytes 393224 | tf_op jit(solution)/shard_map/ppermute | solution.py:436
  164.8 1.2 copy-start.2

commit v9 on v7

--- a/solution.py
+++ b/solution.py
@@ -176,9 +176,11 @@
     return jnp.concatenate(lines, axis=0).astype(BF16)
 
 
-def half_kernel(first, lead_hbm, other_hbm, rows_hbm, side_hbm, *refs):
+def half_kernel(
+    first, lead_hbm, other_hbm, rows_hbm, side_hbm, *refs
+):
     places = None if first else refs[0]
-    extra_hbm = refs[:1] if first else refs[1 : 1 + N_Y]
+    extra_hbm = refs[:1] if first else refs[2 : 2 + N_Y]
     (
         part_hbm, lead, other, rows, side, left, extra, half, part,
         lead_sems, other_sems, row_sem, side_sems, extra_sems, part_sems,
@@ -207,11 +209,16 @@
         for j in range(N_Y):
             cols = pl.ds(j * step, step)
             here = dot(left[:, tokens], other[tokens, cols], NN)
+            if not first and j % 2 == 0:
+                at_chunk = c - 1 + j // 2
+                mine = pl.ds(at_chunk * block, block)
+                extra[at_chunk] = at_places(left, mine, places[:, mine])
             if not last:
                 half[:, cols] = here
                 continue
             part[:, :, cols] = (half[:, cols] + here).astype(BF16).reshape(chunk)
-            out = copy(part.at[:, :, cols], part_hbm.at[:, :, cols], part_sems.at[j])
+            there = pl.ds((width if first else 0) + j * step, step)
+            out = copy(part.at[:, :, cols], part_hbm.at[:, :, there], part_sems.at[j])
             out.start()
             sent.append(out)
 
@@ -237,25 +244,24 @@
             sent.append(out)
         else:
             left[:, here] = (side[c] * found).astype(BF16)
-            extra[c] = at_places(left, here, places[:, here])
         if c == N_Y // 2 - 1:
             parts(c, False)
+    parts(N_Y - 1, True)
     if not first:
         y = lax.axis_index("y")
         for r in range(N_Y):
             out = copy(extra.at[(y + r) % N_Y], extra_hbm[r], extra_sems.at[r])
             out.start()
             sent.append(out)
-    parts(N_Y - 1, True)
     for out in sent:
         out.wait()
 
 
-def half_terms(lead, other, rows, side, devices, places=None):
-    first = places is None
+def half_terms(lead, other, rows, side, devices, places=None, parts=None):
+    first = parts is None
     count, width = lead.shape
     slots = rows.shape[0]
-    chunks = jax.ShapeDtypeStruct((devices, slots // devices, width), BF16)
+    capacity = slots // devices
     if first:
         extra = (jax.ShapeDtypeStruct(side.shape, F32),)
         held = pltpu.VMEM(side.shape, F32)
@@ -265,8 +271,8 @@
         held = pltpu.VMEM((N_Y, topk, count // N_Y), BF16)
     return pl.pallas_call(
         functools.partial(half_kernel, first),
-        out_shape=extra + (chunks,),
-        in_specs=[ANY] * 4 + ([] if first else [VMEM]),
+        out_shape=extra + (jax.ShapeDtypeStruct((devices, capacity, 2 * width), BF16),),
+        in_specs=[ANY] * 4 + ([] if first else [VMEM, ANY]),
         out_specs=(ANY,) * (len(extra) + 1),
         scratch_shapes=[
             pltpu.VMEM((count, width), BF16),
@@ -276,13 +282,14 @@
             pltpu.VMEM((slots, count), BF16),
             held,
             pltpu.VMEM((slots, width), F32),
-            pltpu.VMEM(chunks.shape, BF16),
+            pltpu.VMEM((devices, capacity, width), BF16),
             DMA((8,)), DMA((8,)), DMA, DMA((4,)), DMA((4,)), DMA((4,)),
         ],
+        input_output_aliases={} if first else {5: N_Y},
         compiler_params=params(56),
         cost_estimate=cost(4 * count * width * slots, 24 << 20),
         name="first" if first else "second",
-    )(lead, other, stay(rows), stay(side), *(() if first else (places,)))
+    )(lead, other, stay(rows), stay(side), *(() if first else (places, parts)))
 
 
 def own_hits(lists, rows):
@@ -315,22 +322,24 @@
     )(*lists)
 
 
-def sums_kernel(hits_ref, got_hbm, out_hbm, got, sums, sems, out_sems):
-    _, width = sums.shape
-    devices, capacity, _ = got.shape
+def sums_kernel(hits_ref, got_hbm, down_hbm, up_hbm, got, sums, sems, out_sems):
+    width = down_hbm.shape[1]
+    devices, capacity, both = got.shape
     block = 512
+    pieces = both // block
     copies = []
-    for j in range(width // block):
+    for j in range(pieces):
         cols = pl.ds(j * block, block)
         copies.append(copy(got_hbm.at[:, :, cols], got.at[:, :, cols], sems.at[j]))
         copies[j].start()
     hits = hits_ref[...]
     sent = []
-    for j in range(width // block):
+    for j in range(pieces):
         copies[j].wait()
         cols = pl.ds(j * block, block)
         sums[:, cols] = dot(hits, got[:, :, cols].reshape(devices * capacity, block), TN)
-        c = copy(sums.at[:, cols], out_hbm.at[:, cols], out_sems.at[j])
+        out = (down_hbm, up_hbm)[2 * j // pieces]
+        c = copy(sums.at[:, cols], out.at[:, pl.ds(j * block % width, block)], out_sems.at[j])
         c.start()
         sent.append(c)
     for c in sent:
@@ -338,26 +347,28 @@
 
 
 def sum_rows(hits, got):
-    width = got.shape[2]
+    both = got.shape[2]
     rows = hits.shape[1]
+    out = jax.ShapeDtypeStruct((rows, both // 2), F32)
     return pl.pallas_call(
         sums_kernel,
-        out_shape=jax.ShapeDtypeStruct((rows, width), F32),
+        out_shape=(out, out),
         in_specs=[VMEM, ANY],
-        out_specs=ANY,
+        out_specs=(ANY, ANY),
         scratch_shapes=[
             pltpu.VMEM(got.shape, BF16),
-            pltpu.VMEM((rows, width), F32),
-            DMA((4,)),
-            DMA((4,)),
+            pltpu.VMEM((rows, both), F32),
+            DMA((8,)),
+            DMA((8,)),
         ],
         compiler_params=params(12),
-        cost_estimate=cost(2 * 256 * 256 * 2048, 2 * 10**6),
+        cost_estimate=cost(2 * 256 * 256 * 2048, 4 * 10**6),
+        name="sums",
     )(hits, stay(got))
 
 
 def final_kernel(
-    mine, c0, c1, c2, c3, p0, p1, p2, p3, d0, d1, d2a, d2b, d3, out_hbm, coef, rows, out, d_sems, out_sems
+    mine, c0, c1, c2, c3, p0, p1, p2, p3, d0, d1, d2, d3, out_hbm, coef, rows, out, d_sems, out_sems
 ):
     core = lax.axis_index("core")
     which = core if mine else 1 - core
@@ -366,7 +377,7 @@
     topk = c0.shape[0]
     loads = []
     start = 0
-    for i, d in enumerate((d0, d1, d2a, d2b, d3)):
+    for i, d in enumerate((d0, d1, d2, d3)):
         loads.append(copy(d, rows.at[pl.ds(start, d.shape[0]), :], d_sems.at[i]))
         start += d.shape[0]
     for c in loads:
@@ -402,13 +413,13 @@
     return pl.pallas_call(
         functools.partial(final_kernel, mine),
         out_shape=jax.ShapeDtypeStruct((half, width), BF16),
-        in_specs=[VMEM] * 8 + [ANY] * 5,
+        in_specs=[VMEM] * 8 + [ANY] * 4,
         out_specs=ANY,
         scratch_shapes=[
             pltpu.VMEM((N_Y * slots, half), BF16),
             pltpu.VMEM((N_Y * slots, width), BF16),
             pltpu.VMEM((half, width), BF16),
-            DMA((5,)), DMA((4,)),
+            DMA((4,)), DMA((4,)),
         ],
         compiler_params=params(16),
         cost_estimate=cost(2 * half * 1024 * 2048, 6 << 20),
@@ -447,27 +458,23 @@
     weight = build_weight(slot_of, jnp.transpose(gate_weights[0]), slots)
     down = column(gather_rows(asked, down_tables, width))
     lists = gathered([asked] * N_Y)
-    hits = hit_rows(lists, row_count)
     block = slot_of.shape[1] // N_Y
     blocks = [
         lax.dynamic_slice_in_dim(slot_of, ((y + r) & (N_Y - 1)) * block, block, 1) for r in range(N_Y)
     ]
     chip_places = gathered(blocks)
     up = column(gather_rows(asked, up_tables, width))
-    above, below = turn(down, 1), turn(down, 3)
-    slope, part_up = half_terms(tokens, out_grad, down, weight, devices)
-    got_up = exchange(part_up, ("dp", "core", "y"))
-    far = (turn(above[: slots // 2], 1), turn(below[slots // 2 :], 3))
-    *small, part_down = half_terms(out_grad, tokens, up, slope, devices, slot_of)
+    down_all = gathered([down] * N_Y)
+    hits = hit_rows(lists, row_count)
+    slope, parts = half_terms(tokens, out_grad, down, weight, devices)
+    *small, parts = half_terms(out_grad, tokens, up, slope, devices, slot_of, parts)
     chip_coef = gathered(small)
-    got_down = exchange(part_down, ("dp", "core", "y"))
-    up_grad = sum_rows(hits, got_up)
-    down_all = (down, above, *far, below)
+    got = exchange(parts, ("dp", "core", "y"))
     give = final_product(False, chip_coef, chip_places, down_all)
     other = lax.ppermute(give, "core", [(0, 1), (1, 0)])
     keep = final_product(True, chip_coef, chip_places, down_all)
     input_grad = (keep.astype(F32) + other.astype(F32)).astype(BF16)
-    down_grad = sum_rows(hits, got_down)
+    down_grad, up_grad = sum_rows(hits, got)
     return (input_grad, down_grad, up_grad)
 
 

time: 163 us -> 172 us (1.055)
  waiting for transfers between devices: 42.5 us -> 59.1 us
  starting transfers between devices: 48.9 us -> 45.8 us
  Pallas kernels: 45.9 us -> 43.5 us
    ppermute x19 -> x18, waiting for transfers between devices: 31.5 us -> 59.1 us  [turn(): return lax.ppermute(x, 'y', [(i, (i - r) % N_Y) for i in range(N_Y)])]
    all_to_all x4 -> x3, waiting for transfers between devices: 11 us -> 0.01 us  [exchange(): return lax.all_to_all(x, axes, split_axis=0, concat_axis=0, tiled=True)]
    ppermute x19 -> x18, starting transfers between devices: 22.7 us -> 18.8 us  [turn(): return lax.ppermute(x, 'y', [(i, (i - r) % N_Y) for i in range(N_Y)])]
    ppermute x1, starting transfers between devices: 0.72 us -> 4.05 us  [program(): other = lax.ppermute(give, 'core', [(0, 1), (1, 0)])]
    all_to_all x4 -> x3, starting transfers between devices: 25.5 us -> 22.9 us  [exchange(): return lax.all_to_all(x, axes, split_axis=0, concat_axis=0, tiled=True)]
    pallas_call x2 -> x1, Pallas kernels: 4.78 us -> 3.43 us  [sum_rows(): pl.pallas_call(sums_kernel, out_shape=(out, out), in_specs=[VMEM, ANY], o...]
  transfers between devices with their start and end apart: 24 -> 22, of which waited for: 12 -> 11; matrix products, arithmetic and copies ran while one was open for 1% -> 0% of each run, Pallas kernels for 27% -> 24%
where the time goes in v9:
time: 172 us
  waiting for transfers between devices  59.1 us (34%)
  starting transfers between devices  45.8 us (27%)
  Pallas kernels  43.5 us (25%)
  blocking collectives  17 us (10%)
  local copies, waits for them, and re-layouts  2.67 us (2%)
  other arithmetic  2.63 us (2%)
    ppermute x18, waiting for transfers between devices, turn(): return lax.ppermute(x, 'y', [(i, (i - r) % N_Y) for i in range(N_Y)])  59.1 us
    pallas_call x2, Pallas kernels, half_terms(): pl.pallas_call(functools.partial(half_kernel, first), out_shape=extra + (...  23.6 us
    all_to_all x3, starting transfers between devices, exchange(): return lax.all_to_all(x, axes, split_axis=0, concat_axis=0, tiled=True)  22.9 us
    ppermute x18, starting transfers between devices, turn(): return lax.ppermute(x, 'y', [(i, (i - r) % N_Y) for i in range(N_Y)])  18.8 us
    all_to_all x1, blocking collectives, exchange(): return lax.all_to_all(x, axes, split_axis=0, concat_axis=0, tiled=True)  17 us
    pallas_call x2, Pallas kernels, final_product(): pl.pallas_call(functools.partial(final_kernel, mine), out_shape=jax.Shape...  7.24 us
    pallas_call x2, Pallas kernels, gather_rows(): pl.pallas_call(gather_kernel, out_shape=jax.ShapeDtypeStruct((slots, widt...  4.53 us
    ppermute x1, starting transfers between devices, program(): other = lax.ppermute(give, 'core', [(0, 1), (1, 0)])  4.05 us
  transfers between devices with their start and end apart: 22, of which 11 were waited for; matrix products, arithmetic and copies ran while one was open for 0% of the time, Pallas kernels for 24%

profile of v9, /device:TPU:1, one launch (start us, length us, event | category | flops | bytes accessed | tf_op | source)
XLA Modules:
  0.0 171.7 jit_solution(5082817912644340377)
XLA Ops:
  0.6 3.6 %collective-permute-start.3 = (bf16[64,2048]{1,0:T(8,128)(2,1)}, bf16[64,2048]{1,0:T(8,128)(2,1)S(1)}, u32[]{:S(2)}, u32[]{:S(2)}) collective-permute-start(bf16[64,2048]{1,0:T(8,128)(2,1)} %t0.3), channel_id=1, source_target_pairs={{0,6},{2,0},{4,2},{6,4},{1,7},{3,1},{5,3},{7,5},{8,14},{10,8},{12,... | collective-permute-start | bytes 786440 | tf_op jit(solution)/shard_map/ppermute | solution.py:431
  4.3 0.3 collective-permute-start.4
  4.6 0.7 collective-permute-start.5
  5.3 1.6 ids.1
  6.9 17.0 %all_to_all.20 = s32[32,8,128]{2,1,0:T(8,128)S(1)} all-to-all(s32[32,8,128]{2,1,0:T(8,128)} %bitcast.39), channel_id=1, replica_groups=mesh['dp'=16,'y'=4,'core'=2] {'dp','core'}, dimensions={0} | all-to-all | bytes 262144 | tf_op jit(solution)/shard_map/all_to_all | solution.py:439
  23.9 0.0 copy-start.6
  24.0 2.3 %shard_map.95 = bf16[256,2048]{1,0:T(8,128)(2,1)} custom-call(s32[256,128]{1,0:T(8,128)S(1)} %bitcast.32, bf16[64,2048]{1,0:T(8,128)(2,1)} %t0.3, bf16[64,2048]{1,0:T(8,128)(2,1)S(1)} %collective-permute-done.3.t1, bf16[64,2048]{1,0:T(8,128)(2,1)S(1)} %collective-permute-done.4.t2, bf16[64,2048]{1,0:T(8,128)(2,1)S(1)} %collective-permute-done.5.t3), custom_call_target="tpu_custom_call" | custom-call | flops 268435456 | bytes 3000000 | tf_op jit(solution)/shard_map/pallas_call | solution.py:122
  26.3 4.7 %all-to-all-start.2 = ((bf16[32,8,2048]{2,1,0:T(8,128)(2,1)}), bf16[32,8,2048]{2,1,0:T(8,128)(2,1)}, u32[]{:S(2)}, u32[]{:S(2)}) async-start(bf16[32,8,2048]{2,1,0:T(8,128)(2,1)} %bitcast.6), calls=%async_computation.2 | async-start | bytes 2097152 | tf_op jit(solution)/shard_map/all_to_all | solution.py:439
  31.0 2.1 %collective-permute-start = (bf16[64,2048]{1,0:T(8,128)(2,1)S(1)}, bf16[64,2048]{1,0:T(8,128)(2,1)S(1)}, u32[]{:S(2)}, u32[]{:S(2)}) collective-permute-start(bf16[64,2048]{1,0:T(8,128)(2,1)S(1)} %copy-done.6), channel_id=1, source_target_pairs={{0,6},{2,0},{4,2},{6,4},{1,7},{3,1},{5,3},{7,5},{8,14},{10,8},{12,... | collective-permute-start | bytes 786440 | tf_op jit(solution)/shard_map/ppermute | solution.py:431
  33.0 1.4 collective-permute-start.1
  34.4 4.4 %collective-permute-done.t1 = bf16[64,2048]{1,0:T(8,128)(2,1)S(1)} collective-permute-done((bf16[64,2048]{1,0:T(8,128)(2,1)S(1)}, bf16[64,2048]{1,0:T(8,128)(2,1)S(1)}, u32[]{:S(2)}, u32[]{:S(2)}) %collective-permute-start) | collective-permute-done | bytes 262176 | tf_op jit(solution)/shard_map/ppermute | solution.py:431
  38.9 3.0 %collective-permute-done.1.t2 = bf16[64,2048]{1,0:T(8,128)(2,1)S(1)} collective-permute-done((bf16[64,2048]{1,0:T(8,128)(2,1)S(1)}, bf16[64,2048]{1,0:T(8,128)(2,1)S(1)}, u32[]{:S(2)}, u32[]{:S(2)}) %collective-permute-start.1) | collective-permute-done | bytes 262176 | tf_op jit(solution)/shard_map/ppermute | solution.py:431
  41.8 6.5 %collective-permute-done.2.t3 = bf16[64,2048]{1,0:T(8,128)(2,1)S(1)} collective-permute-done((bf16[64,2048]{1,0:T(8,128)(2,1)S(1)}, bf16[64,2048]{1,0:T(8,128)(2,1)S(1)}, u32[]{:S(2)}, u32[]{:S(2)}) %collective-permute-start.2) | collective-permute-done | bytes 262176 | tf_op jit(solution)/shard_map/ppermute | solution.py:431
  48.4 2.2 %shard_map.94 = bf16[256,2048]{1,0:T(8,128)(2,1)} custom-call(s32[256,128]{1,0:T(8,128)S(1)} %bitcast.33, bf16[64,2048]{1,0:T(8,128)(2,1)} %t0.2, bf16[64,2048]{1,0:T(8,128)(2,1)S(1)} %collective-permute-done.t1, bf16[64,2048]{1,0:T(8,128)(2,1)S(1)} %collective-permute-done.1.t2, bf16[64,2048]{1,0:T(8,128)(2,1)S(1)} %collective-permute-done.2.t3), custom_call_target="tpu_custom_call" | custom-call | flops 268435456 | bytes 3000000 | tf_op jit(solution)/shard_map/pallas_call | solution.py:122
  50.6 7.7 %all-to-all-start.1 = ((bf16[32,8,2048]{2,1,0:T(8,128)(2,1)}), bf16[32,8,2048]{2,1,0:T(8,128)(2,1)}, u32[]{:S(2)}, u32[]{:S(2)}) async-start(bf16[32,8,2048]{2,1,0:T(8,128)(2,1)} %bitcast.4), calls=%async_computation.1 | async-start | bytes 2097152 | tf_op jit(solution)/shard_map/all_to_all | solution.py:439
  58.4 2.8 %weight.1.side_hbm = f32[4,256,512]{2,1,0:T(8,128)S(1)} custom-call(s32[16,2048]{1,0:T(8,128)S(1)} %get-tuple-element.26.places_ref.refs_0_, f32[16,2048]{1,0:T(8,128)S(1)} %bitcast.38), custom_call_target="tpu_custom_call" | custom-call | flops 25165824 | bytes 2097152 | tf_op jit(solution)/shard_map/weight/pallas_call | solution.py:154
  61.2 1.4 copy-done
  62.6 0.3 collective-permute-start.12
  62.9 1.4 collective-permute-start.13
  64.3 0.5 collective-permute-start.14
  64.9 10.5 %first.1 = (f32[4,256,512]{2,1,0:T(8,128)}, bf16[128,2,4096]{2,1,0:T(2,128)(2,1)}) custom-call(bf16[2048,2048]{1,0:T(8,128)(2,1)} %other_hbm.3, bf16[2048,2048]{1,0:T(8,128)(2,1)} %lead_hbm.3, bf16[256,2048]{1,0:T(8,128)(2,1)} %bitcast.7.rows_hbm.d0, f32[4,256,512]{2,1,0:T(8,128)} %copy-done), custom_call_target="tpu_custom_call" | custom-call | flops 4294967296 | bytes 25165824 | tf_op jit(solution)/shard_map/first/pallas_call | solution.py:272
  75.4 0.0 all-to-all-done.1
  75.4 13.1 %second.1 = (bf16[16,512]{1,0:T(8,128)(2,1)}, bf16[16,512]{1,0:T(8,128)(2,1)}, bf16[16,512]{1,0:T(8,128)(2,1)}, bf16[16,512]{1,0:T(8,128)(2,1)}, bf16[128,2,4096]{2,1,0:T(2,128)(2,1)}) custom-call(bf16[2048,2048]{1,0:T(8,128)(2,1)} %lead_hbm.3, bf16[2048,2048]{1,0:T(8,128)(2,1)} %other_hbm.3, ...), custom_call_target="tpu_custom_call", output_to_operand_aliasing={{4}: (5, {})} | custom-call | flops 4294967296 | bytes 25165824 | tf_op jit(solution)/shard_map/second/pallas_call | solution.py:272
  88.6 10.6 %all-to-all-start.3 = ((bf16[128,2,4096]{2,1,0:T(2,128)(2,1)}), bf16[128,2,4096]{2,1,0:T(2,128)(2,1)}, u32[]{:S(2)}, u32[]{:S(2)}) async-start(bf16[128,2,4096]{2,1,0:T(2,128)(2,1)} %get-tuple-element.18), calls=%async_computation.3 | async-start | bytes 4194304 | tf_op jit(solution)/shard_map/all_to_all | solution.py:439
  99.2 2.9 %collective-permute-start.10 = (s32[16,512]{1,0:T(8,128)S(1)}, s32[16,512]{1,0:T(8,128)S(1)}, u32[]{:S(2)}, u32[]{:S(2)}) collective-permute-start(s32[16,512]{1,0:T(8,128)S(1)} %get-tuple-element.22), channel_id=1, source_target_pairs={{0,4},{2,6},{4,0},{6,2},{1,5},{3,7},{5,1},{7,3},{8,12},{10,14},{12... | collective-permute-start | bytes 98312 | tf_op jit(solution)/shard_map/ppermute | solution.py:431
  102.2 0.3 collective-permute-start.11
  102.5 32.0 %collective-permute-done.10.p2 = s32[16,512]{1,0:T(8,128)S(1)} collective-permute-done((s32[16,512]{1,0:T(8,128)S(1)}, s32[16,512]{1,0:T(8,128)S(1)}, u32[]{:S(2)}, u32[]{:S(2)}) %collective-permute-start.10) | collective-permute-done | bytes 32800 | tf_op jit(solution)/shard_map/ppermute | solution.py:431
  134.6 0.9 collective-permute-start.9
  135.5 0.7 collective-permute-done.11.p3
  136.2 0.1 collective-permute-start.6
  136.3 1.1 collective-permute-done.9.p1
  137.3 1.8 %collective-permute-start.7 = (bf16[16,512]{1,0:T(8,128)(2,1)S(1)}, bf16[16,512]{1,0:T(8,128)(2,1)S(1)}, u32[]{:S(2)}, u32[]{:S(2)}) collective-permute-start(bf16[16,512]{1,0:T(8,128)(2,1)S(1)} %copy-done.9), channel_id=1, source_target_pairs={{0,4},{2,6},{4,0},{6,2},{1,5},{3,7},{5,1},{7,3},{8,12},{10,14},{12... | collective-permute-start | bytes 49160 | tf_op jit(solution)/shard_map/ppermute | solution.py:431
  139.2 0.9 collective-permute-start.8
  140.0 1.4 collective-permute-done.7.c2
  141.4 1.5 collective-permute-done.8.c3
  143.0 3.7 %give.1 = bf16[256,2048]{1,0:T(8,128)(2,1)} custom-call(bf16[16,512]{1,0:T(8,128)(2,1)S(1)} %copy-done.5, bf16[16,512]{1,0:T(8,128)(2,1)S(1)} %collective-permute-done.6.c1, bf16[16,512]{1,0:T(8,128)(2,1)S(1)} %collective-permute-done.7.c2, bf16[16,512]{1,0:T(8,128)(2,1)S(1)} %collective-permute-done.8.c3, s32[16,512]{1,0:T(8,128)S(1)} %get-tuple-element.24.p0, ...), custom_call_target="tpu_custom_call" | custom-call | flops 1073741824 | bytes 6291456 | tf_op jit(solution)/shard_map/give/pallas_call | solution.py:413
  146.7 4.0 %collective-permute-start.15 = (bf16[256,2048]{1,0:T(8,128)(2,1)}, bf16[256,2048]{1,0:T(8,128)(2,1)}, u32[]{:S(2)}, u32[]{:S(2)}) collective-permute-start(bf16[256,2048]{1,0:T(8,128)(2,1)} %give.1), channel_id=1, source_target_pairs={{0,1},{1,0},{2,3},{3,2},{4,5},{5,4},{6,7},{7,6},{8,9},{9,8},{10,11... | collective-permute-start | bytes 3145736 | tf_op jit(solution)/shard_map/ppermute | solution.py:474
  150.7 0.1 collective-permute-start.16
  150.8 1.0 collective-permute-start.17
  151.8 0.3 collective-permute-start.18
  152.2 3.5 %collective-permute-done.16.a1 = s32[256,128]{1,0:T(8,128)S(1)} collective-permute-done((s32[256,128]{1,0:T(8,128)S(1)}, s32[256,128]{1,0:T(8,128)S(1)}, u32[]{:S(2)}, u32[]{:S(2)}) %collective-permute-start.16) | collective-permute-done | bytes 131104 | tf_op jit(solution)/shard_map/ppermute | solution.py:431
  155.7 1.3 collective-permute-done.17.a2
  157.0 3.5 %collective-permute-done.18.a3 = s32[256,128]{1,0:T(8,128)S(1)} collective-permute-done((s32[256,128]{1,0:T(8,128)S(1)}, s32[256,128]{1,0:T(8,128)S(1)}, u32[]{:S(2)}, u32[]{:S(2)}) %collective-permute-start.18) | collective-permute-done | bytes 131104 | tf_op jit(solution)/shard_map/ppermute | solution.py:431
  160.6 0.3 hits.1.hits_ref
  160.9 1.2 copy-done.2
  162.1 3.6 %keep.1 = bf16[256,2048]{1,0:T(8,128)(2,1)S(1)} custom-call(bf16[16,512]{1,0:T(8,128)(2,1)S(1)} %copy-done.5, bf16[16,512]{1,0:T(8,128)(2,1)S(1)} %collective-permute-done.6.c1, bf16[16,512]{1,0:T(8,128)(2,1)S(1)} %collective-permute-done.7.c2, bf16[16,512]{1,0:T(8,128)(2,1)S(1)} %collective-permute-done.8.c3, s32[16,512]{1,0:T(8,128)S(1)} %get-tuple-element.24.p0, ...), custom_call_target="tpu_custom_call" | custom-call | flops 1073741824 | bytes 6291456 | tf_op jit(solution)/shard_map/keep/pallas_call | solution.py:413
  165.7 3.4 %sums.1 = (f32[64,2048]{1,0:T(8,128)}, f32[64,2048]{1,0:T(8,128)}) custom-call(bf16[256,64]{1,0:T(8,128)(2,1)S(1)} %hits.1.hits_ref, bf16[128,2,4096]{2,1,0:T(2,128)(2,1)} %all-to-all-done.3.got_hbm), custom_call_target="tpu_custom_call" | custom-call | flops 268435456 | bytes 4000000 | tf_op jit(solution)/shard_map/sums/pallas_call | solution.py:353
  169.1 2.6 %add_convert_fusion = bf16[256,2048]{1,0:T(8,128)(2,1)} fusion(bf16[256,2048]{1,0:T(8,128)(2,1)} %collective-permute-done.15, bf16[256,2048]{1,0:T(8,128)(2,1)S(1)} %keep.1), kind=kLoop, calls=%fused_computation | loop fusion | flops 2097152 | bytes 3145728 | tf_op jit(solution)/shard_map/convert_element_type | solution.py:476
  (32 shorter events, 0.1 us)
Async XLA Ops:
  0.6 23.3 %collective-permute-start.3 = (bf16[64,2048]{1,0:T(8,128)(2,1)}, bf16[64,2048]{1,0:T(8,128)(2,1)S(1)}, u32[]{:S(2)}, u32[]{:S(2)}) collective-permute-start(bf16[64,2048]{1,0:T(8,128)(2,1)} %t0.3), channel_id=1, source_target_pairs={{0,6},{2,0},{4,2},{6,4},{1,7},{3,1},{5,3},{7,5},{8,14},{10,8},{12,... | collective-permute-start | bytes 786440 | tf_op jit(solution)/shard_map/ppermute | solution.py:431
  4.3 19.7 %collective-permute-start.4 = (bf16[64,2048]{1,0:T(8,128)(2,1)}, bf16[64,2048]{1,0:T(8,128)(2,1)S(1)}, u32[]{:S(2)}, u32[]{:S(2)}) collective-permute-start(bf16[64,2048]{1,0:T(8,128)(2,1)} %t0.3), channel_id=1, source_target_pairs={{0,4},{2,6},{4,0},{6,2},{1,5},{3,7},{5,1},{7,3},{8,12},{10,14},{12... | collective-permute-start | bytes 786440 | tf_op jit(solution)/shard_map/ppermute | solution.py:431
  4.6 19.3 %collective-permute-start.5 = (bf16[64,2048]{1,0:T(8,128)(2,1)}, bf16[64,2048]{1,0:T(8,128)(2,1)S(1)}, u32[]{:S(2)}, u32[]{:S(2)}) collective-permute-start(bf16[64,2048]{1,0:T(8,128)(2,1)} %t0.3), channel_id=1, source_target_pairs={{0,2},{2,4},{4,6},{6,0},{1,3},{3,5},{5,7},{7,1},{8,10},{10,12},{12... | collective-permute-start | bytes 786440 | tf_op jit(solution)/shard_map/ppermute | solution.py:431
  23.9 7.0 %copy-start.6 = (bf16[64,2048]{1,0:T(8,128)(2,1)S(1)}, bf16[64,2048]{1,0:T(8,128)(2,1)}, u32[]{:S(2)}) copy-start(bf16[64,2048]{1,0:T(8,128)(2,1)} %t0.2) | copy-start | bytes 786436
  26.3 24.3 %all-to-all-start.2 = ((bf16[32,8,2048]{2,1,0:T(8,128)(2,1)}), bf16[32,8,2048]{2,1,0:T(8,128)(2,1)}, u32[]{:S(2)}, u32[]{:S(2)}) async-start(bf16[32,8,2048]{2,1,0:T(8,128)(2,1)} %bitcast.6), calls=%async_computation.2 | async-start | bytes 2097152 | tf_op jit(solution)/shard_map/all_to_all | solution.py:439
  30.9 27.4 %copy-start.7 = (s32[1,2048,16]{1,2,0:T(8,128)S(1)}, s32[1,2048,16]{1,2,0:T(8,128)}, u32[]{:S(2)}) copy-start(s32[1,2048,16]{1,2,0:T(8,128)} %param.12) | copy-start | bytes 393220
  31.0 27.4 %copy-start.4 = (f32[1,2048,16]{1,2,0:T(8,128)S(1)}, f32[1,2048,16]{1,2,0:T(8,128)}, u32[]{:S(2)}) copy-start(f32[1,2048,16]{1,2,0:T(8,128)} %param.13) | copy-start | bytes 393220
  31.0 7.9 %collective-permute-start = (bf16[64,2048]{1,0:T(8,128)(2,1)S(1)}, bf16[64,2048]{1,0:T(8,128)(2,1)S(1)}, u32[]{:S(2)}, u32[]{:S(2)}) collective-permute-start(bf16[64,2048]{1,0:T(8,128)(2,1)S(1)} %copy-done.6), channel_id=1, source_target_pairs={{0,6},{2,0},{4,2},{6,4},{1,7},{3,1},{5,3},{7,5},{8,14},{10,8},{12,... | collective-permute-start | bytes 786440 | tf_op jit(solution)/shard_map/ppermute | solution.py:431
  33.0 8.8 %collective-permute-start.1 = (bf16[64,2048]{1,0:T(8,128)(2,1)S(1)}, bf16[64,2048]{1,0:T(8,128)(2,1)S(1)}, u32[]{:S(2)}, u32[]{:S(2)}) collective-permute-start(bf16[64,2048]{1,0:T(8,128)(2,1)S(1)} %copy-done.6), channel_id=1, source_target_pairs={{0,4},{2,6},{4,0},{6,2},{1,5},{3,7},{5,1},{7,3},{8,12},{10,14},{12... | collective-permute-start | bytes 786440 | tf_op jit(solution)/shard_map/ppermute | solution.py:431
  34.4 13.9 %collective-permute-start.2 = (bf16[64,2048]{1,0:T(8,128)(2,1)S(1)}, bf16[64,2048]{1,0:T(8,128)(2,1)S(1)}, u32[]{:S(2)}, u32[]{:S(2)}) collective-permute-start(bf16[64,2048]{1,0:T(8,128)(2,1)S(1)} %copy-done.6), channel_id=1, source_target_pairs={{0,2},{2,4},{4,6},{6,0},{1,3},{3,5},{5,7},{7,1},{8,10},{10,12},{12... | collective-permute-start | bytes 786440 | tf_op jit(solution)/shard_map/ppermute | solution.py:431
  50.6 24.8 %all-to-all-start.1 = ((bf16[32,8,2048]{2,1,0:T(8,128)(2,1)}), bf16[32,8,2048]{2,1,0:T(8,128)(2,1)}, u32[]{:S(2)}, u32[]{:S(2)}) async-start(bf16[32,8,2048]{2,1,0:T(8,128)(2,1)} %bitcast.4), calls=%async_computation.1 | async-start | bytes 2097152 | tf_op jit(solution)/shard_map/all_to_all | solution.py:439
  58.4 17.0 %copy-start.3 = (s32[16,2048]{1,0:T(8,128)}, s32[16,2048]{1,0:T(8,128)S(1)}, u32[]{:S(2)}) copy-start(s32[16,2048]{1,0:T(8,128)S(1)} %get-tuple-element.26.places_ref.refs_0_) | copy-start | bytes 393220
  61.2 1.4 copy-start
  62.6 80.4 %collective-permute-start.12 = (bf16[256,2048]{1,0:T(8,128)(2,1)}, bf16[256,2048]{1,0:T(8,128)(2,1)S(1)}, u32[]{:S(2)}, u32[]{:S(2)}) collective-permute-start(bf16[256,2048]{1,0:T(8,128)(2,1)} %bitcast.7.rows_hbm.d0), channel_id=1, source_target_pairs={{0,6},{2,0},{4,2},{6,4},{1,7},{3,1},{5,3},{7,5},{8,14},{10,8},{12,... | collective-permute-start | bytes 3145736 | tf_op jit(solution)/shard_map/ppermute | solution.py:431
  62.9 80.0 %collective-permute-start.13 = (bf16[256,2048]{1,0:T(8,128)(2,1)}, bf16[256,2048]{1,0:T(8,128)(2,1)S(1)}, u32[]{:S(2)}, u32[]{:S(2)}) collective-permute-start(bf16[256,2048]{1,0:T(8,128)(2,1)} %bitcast.7.rows_hbm.d0), channel_id=1, source_target_pairs={{0,4},{2,6},{4,0},{6,2},{1,5},{3,7},{5,1},{7,3},{8,12},{10,14},{12... | collective-permute-start | bytes 3145736 | tf_op jit(solution)/shard_map/ppermute | solution.py:431
  64.3 78.6 %collective-permute-start.14 = (bf16[256,2048]{1,0:T(8,128)(2,1)}, bf16[256,2048]{1,0:T(8,128)(2,1)S(1)}, u32[]{:S(2)}, u32[]{:S(2)}) collective-permute-start(bf16[256,2048]{1,0:T(8,128)(2,1)} %bitcast.7.rows_hbm.d0), channel_id=1, source_target_pairs={{0,2},{2,4},{4,6},{6,0},{1,3},{3,5},{5,7},{7,1},{8,10},{10,12},{12... | collective-permute-start | bytes 3145736 | tf_op jit(solution)/shard_map/ppermute | solution.py:431
  88.5 47.6 %copy-start.10 = (bf16[16,512]{1,0:T(8,128)(2,1)S(1)}, bf16[16,512]{1,0:T(8,128)(2,1)}, u32[]{:S(2)}) copy-start(bf16[16,512]{1,0:T(8,128)(2,1)} %get-tuple-element.15) | copy-start | bytes 49156
  88.6 48.8 %copy-start.9 = (bf16[16,512]{1,0:T(8,128)(2,1)S(1)}, bf16[16,512]{1,0:T(8,128)(2,1)}, u32[]{:S(2)}) copy-start(bf16[16,512]{1,0:T(8,128)(2,1)} %get-tuple-element.16) | copy-start | bytes 49156
  88.6 50.6 %copy-start.8 = (bf16[16,512]{1,0:T(8,128)(2,1)S(1)}, bf16[16,512]{1,0:T(8,128)(2,1)}, u32[]{:S(2)}) copy-start(bf16[16,512]{1,0:T(8,128)(2,1)} %get-tuple-element.17) | copy-start | bytes 49156
  88.6 54.4 %copy-start.5 = (bf16[16,512]{1,0:T(8,128)(2,1)S(1)}, bf16[16,512]{1,0:T(8,128)(2,1)}, u32[]{:S(2)}) copy-start(bf16[16,512]{1,0:T(8,128)(2,1)} %get-tuple-element.14.c0) | copy-start | bytes 49156
  88.6 77.1 %all-to-all-start.3 = ((bf16[128,2,4096]{2,1,0:T(2,128)(2,1)}), bf16[128,2,4096]{2,1,0:T(2,128)(2,1)}, u32[]{:S(2)}, u32[]{:S(2)}) async-start(bf16[128,2,4096]{2,1,0:T(2,128)(2,1)} %get-tuple-element.18), calls=%async_computation.3 | async-start | bytes 4194304 | tf_op jit(solution)/shard_map/all_to_all | solution.py:439
  99.2 35.3 %collective-permute-start.10 = (s32[16,512]{1,0:T(8,128)S(1)}, s32[16,512]{1,0:T(8,128)S(1)}, u32[]{:S(2)}, u32[]{:S(2)}) collective-permute-start(s32[16,512]{1,0:T(8,128)S(1)} %get-tuple-element.22), channel_id=1, source_target_pairs={{0,4},{2,6},{4,0},{6,2},{1,5},{3,7},{5,1},{7,3},{8,12},{10,14},{12... | collective-permute-start | bytes 98312 | tf_op jit(solution)/shard_map/ppermute | solution.py:431
  102.2 34.0 %collective-permute-start.11 = (s32[16,512]{1,0:T(8,128)S(1)}, s32[16,512]{1,0:T(8,128)S(1)}, u32[]{:S(2)}, u32[]{:S(2)}) collective-permute-start(s32[16,512]{1,0:T(8,128)S(1)} %get-tuple-element.21), channel_id=1, source_target_pairs={{0,2},{2,4},{4,6},{6,0},{1,3},{3,5},{5,7},{7,1},{8,10},{10,12},{12... | collective-permute-start | bytes 98312 | tf_op jit(solution)/shard_map/ppermute | solution.py:431
  134.6 2.8 %collective-permute-start.9 = (s32[16,512]{1,0:T(8,128)S(1)}, s32[16,512]{1,0:T(8,128)S(1)}, u32[]{:S(2)}, u32[]{:S(2)}) collective-permute-start(s32[16,512]{1,0:T(8,128)S(1)} %get-tuple-element.23), channel_id=1, source_target_pairs={{0,6},{2,0},{4,2},{6,4},{1,7},{3,1},{5,3},{7,5},{8,14},{10,8},{12,... | collective-permute-start | bytes 98312 | tf_op jit(solution)/shard_map/ppermute | solution.py:431
  136.2 3.0 %collective-permute-start.6 = (bf16[16,512]{1,0:T(8,128)(2,1)S(1)}, bf16[16,512]{1,0:T(8,128)(2,1)S(1)}, u32[]{:S(2)}, u32[]{:S(2)}) collective-permute-start(bf16[16,512]{1,0:T(8,128)(2,1)S(1)} %copy-done.10), channel_id=1, source_target_pairs={{0,6},{2,0},{4,2},{6,4},{1,7},{3,1},{5,3},{7,5},{8,14},{10,8},{12,... | collective-permute-start | bytes 49160 | tf_op jit(solution)/shard_map/ppermute | solution.py:431
  137.3 4.1 %collective-permute-start.7 = (bf16[16,512]{1,0:T(8,128)(2,1)S(1)}, bf16[16,512]{1,0:T(8,128)(2,1)S(1)}, u32[]{:S(2)}, u32[]{:S(2)}) collective-permute-start(bf16[16,512]{1,0:T(8,128)(2,1)S(1)} %copy-done.9), channel_id=1, source_target_pairs={{0,4},{2,6},{4,0},{6,2},{1,5},{3,7},{5,1},{7,3},{8,12},{10,14},{12... | collective-permute-start | bytes 49160 | tf_op jit(solution)/shard_map/ppermute | solution.py:431
  139.2 3.8 %collective-permute-start.8 = (bf16[16,512]{1,0:T(8,128)(2,1)S(1)}, bf16[16,512]{1,0:T(8,128)(2,1)S(1)}, u32[]{:S(2)}, u32[]{:S(2)}) collective-permute-start(bf16[16,512]{1,0:T(8,128)(2,1)S(1)} %copy-done.8), channel_id=1, source_target_pairs={{0,2},{2,4},{4,6},{6,0},{1,3},{3,5},{5,7},{7,1},{8,10},{10,12},{12... | collective-permute-start | bytes 49160 | tf_op jit(solution)/shard_map/ppermute | solution.py:431
  143.0 3.7 %copy-start.1 = (bf16[256,2048]{1,0:T(8,128)(2,1)}, bf16[256,2048]{1,0:T(8,128)(2,1)S(1)}, u32[]{:S(2)}) copy-start(bf16[256,2048]{1,0:T(8,128)(2,1)S(1)} %collective-permute-done.14.d3) | copy-start | bytes 3145732
  146.7 22.4 %collective-permute-start.15 = (bf16[256,2048]{1,0:T(8,128)(2,1)}, bf16[256,2048]{1,0:T(8,128)(2,1)}, u32[]{:S(2)}, u32[]{:S(2)}) collective-permute-start(bf16[256,2048]{1,0:T(8,128)(2,1)} %give.1), channel_id=1, source_target_pairs={{0,1},{1,0},{2,3},{3,2},{4,5},{5,4},{6,7},{7,6},{8,9},{9,8},{10,11... | collective-permute-start | bytes 3145736 | tf_op jit(solution)/shard_map/ppermute | solution.py:474
  150.7 5.0 %collective-permute-start.16 = (s32[256,128]{1,0:T(8,128)S(1)}, s32[256,128]{1,0:T(8,128)S(1)}, u32[]{:S(2)}, u32[]{:S(2)}) collective-permute-start(s32[256,128]{1,0:T(8,128)S(1)} %bitcast.34), channel_id=1, source_target_pairs={{0,6},{2,0},{4,2},{6,4},{1,7},{3,1},{5,3},{7,5},{8,14},{10,8},{12,... | collective-permute-start | bytes 393224 | tf_op jit(solution)/shard_map/ppermute | solution.py:431
  150.8 6.2 %collective-permute-start.17 = (s32[256,128]{1,0:T(8,128)S(1)}, s32[256,128]{1,0:T(8,128)S(1)}, u32[]{:S(2)}, u32[]{:S(2)}) collective-permute-start(s32[256,128]{1,0:T(8,128)S(1)} %bitcast.35), channel_id=1, source_target_pairs={{0,4},{2,6},{4,0},{6,2},{1,5},{3,7},{5,1},{7,3},{8,12},{10,14},{12... | collective-permute-start | bytes 393224 | tf_op jit(solution)/shard_map/ppermute | solution.py:431
  151.8 8.7 %collective-permute-start.18 = (s32[256,128]{1,0:T(8,128)S(1)}, s32[256,128]{1,0:T(8,128)S(1)}, u32[]{:S(2)}, u32[]{:S(2)}) collective-permute-start(s32[256,128]{1,0:T(8,128)S(1)} %bitcast.36), channel_id=1, source_target_pairs={{0,2},{2,4},{4,6},{6,0},{1,3},{3,5},{5,7},{7,1},{8,10},{10,12},{12... | collective-permute-start | bytes 393224 | tf_op jit(solution)/shard_map/ppermute | solution.py:431
  160.9 1.2 copy-start.2

commit v10 on v9

--- a/solution.py
+++ b/solution.py
@@ -168,11 +168,11 @@
     row = iota((16, block), 0)
     lines = []
     for k in range(topk):
-        want = slot[k : k + 1, :] - row
-        found = jnp.zeros((16, block), F32)
+        want = (slot[k : k + 1, :] - row).astype(jnp.int16)
+        found = jnp.zeros((16, block), BF16)
         for g in range(0, left.shape[0], 16):
-            found = jnp.where(want == g, left[g : g + 16, here].astype(F32), found)
-        lines.append(jnp.sum(found, axis=0, keepdims=True))
+            found = jnp.where(want == jnp.int16(g), left[g : g + 16, here], found)
+        lines.append(jnp.sum(found.astype(F32), axis=0, keepdims=True))
     return jnp.concatenate(lines, axis=0).astype(BF16)
 
 
@@ -368,8 +368,10 @@
 
 
 def final_kernel(
-    mine, c0, c1, c2, c3, p0, p1, p2, p3, d0, d1, d2, d3, out_hbm, coef, rows, out, d_sems, out_sems
+    mine, c0, c1, c2, c3, p0, p1, p2, p3, *refs
 ):
+    blocks = refs[:-6]
+    out_hbm, coef, rows, out, d_sems, out_sems = refs[-6:]
     core = lax.axis_index("core")
     which = core if mine else 1 - core
     half = out.shape[0]
@@ -377,7 +379,7 @@
     topk = c0.shape[0]
     loads = []
     start = 0
-    for i, d in enumerate((d0, d1, d2, d3)):
+    for i, d in enumerate(blocks):
         loads.append(copy(d, rows.at[pl.ds(start, d.shape[0]), :], d_sems.at[i]))
         start += d.shape[0]
     for c in loads:
@@ -413,13 +415,13 @@
     return pl.pallas_call(
         functools.partial(final_kernel, mine),
         out_shape=jax.ShapeDtypeStruct((half, width), BF16),
-        in_specs=[VMEM] * 8 + [ANY] * 4,
+        in_specs=[VMEM] * 8 + [ANY] * len(rows),
         out_specs=ANY,
         scratch_shapes=[
             pltpu.VMEM((N_Y * slots, half), BF16),
             pltpu.VMEM((N_Y * slots, width), BF16),
             pltpu.VMEM((half, width), BF16),
-            DMA((4,)), DMA((4,)),
+            DMA((len(rows),)), DMA((4,)),
         ],
         compiler_params=params(16),
         cost_estimate=cost(2 * half * 1024 * 2048, 6 << 20),
@@ -464,7 +466,11 @@
     ]
     chip_places = gathered(blocks)
     up = column(gather_rows(asked, up_tables, width))
-    down_all = gathered([down] * N_Y)
+    head, tail = down[: slots // 2], down[slots // 2 :]
+    above_head, below_tail = turn(head, 1), turn(tail, 3)
+    above_tail, below_head = turn(tail, 1), turn(head, 3)
+    far_head, far_tail = turn(above_head, 1), turn(below_tail, 3)
+    down_all = (down, above_head, above_tail, far_head, far_tail, below_head, below_tail)
     hits = hit_rows(lists, row_count)
     slope, parts = half_terms(tokens, out_grad, down, weight, devices)
     *small, parts = half_terms(out_grad, tokens, up, slope, devices, slot_of, parts)

time: 172 us -> 195 us (1.13)
  waiting for transfers between devices: 59.1 us -> 79.4 us
    ppermute x18 -> x21, waiting for transfers between devices: 59.1 us -> 79.4 us  [turn(): return lax.ppermute(x, 'y', [(i, (i - r) % N_Y) for i in range(N_Y)])]
    ppermute x1, starting transfers between devices: 4.05 us -> 6.95 us  [program(): other = lax.ppermute(give, 'core', [(0, 1), (1, 0)])]
    ppermute x18 -> x21, starting transfers between devices: 18.8 us -> 19.6 us  [turn(): return lax.ppermute(x, 'y', [(i, (i - r) % N_Y) for i in range(N_Y)])]
  transfers between devices with their start and end apart: 22 -> 25, of which waited for: 11 -> 12; matrix products, arithmetic and copies ran while one was open for 0% -> 0% of each run, Pallas kernels for 24% -> 21%
where the time goes in v10:
time: 195 us; the launch traced here: 194 us
  waiting for transfers between devices  79.4 us (41%)
  starting transfers between devices  47.6 us (24%)
  Pallas kernels  42.5 us (22%)
  blocking collectives  17 us (9%)
  local copies, waits for them, and re-layouts  4.23 us (2%)
  other arithmetic  2.63 us (1%)
    ppermute x21, waiting for transfers between devices, turn(): return lax.ppermute(x, 'y', [(i, (i - r) % N_Y) for i in range(N_Y)])  79.4 us
    pallas_call x2, Pallas kernels, half_terms(): pl.pallas_call(functools.partial(half_kernel, first), out_shape=extra + (...  22.5 us
    all_to_all x3, starting transfers between devices, exchange(): return lax.all_to_all(x, axes, split_axis=0, concat_axis=0, tiled=True)  21 us
    ppermute x21, starting transfers between devices, turn(): return lax.ppermute(x, 'y', [(i, (i - r) % N_Y) for i in range(N_Y)])  19.6 us
    all_to_all x1, blocking collectives, exchange(): return lax.all_to_all(x, axes, split_axis=0, concat_axis=0, tiled=True)  17 us
    pallas_call x2, Pallas kernels, final_product(): pl.pallas_call(functools.partial(final_kernel, mine), out_shape=jax.Shape...  7.26 us
    ppermute x1, starting transfers between devices, program(): other = lax.ppermute(give, 'core', [(0, 1), (1, 0)])  6.95 us
    pallas_call x2, Pallas kernels, gather_rows(): pl.pallas_call(gather_kernel, out_shape=jax.ShapeDtypeStruct((slots, widt...  4.57 us
  transfers between devices with their start and end apart: 25, of which 12 were waited for; matrix products, arithmetic and copies ran while one was open for 0% of the time, Pallas kernels for 21%

profile of v10, /device:TPU:1, one launch (start us, length us, event | category | flops | bytes accessed | tf_op | source)
XLA Modules:
  0.0 194.4 jit_solution(6972646303728780862)
XLA Ops:
  0.6 3.6 %collective-permute-start.3 = (bf16[64,2048]{1,0:T(8,128)(2,1)}, bf16[64,2048]{1,0:T(8,128)(2,1)S(1)}, u32[]{:S(2)}, u32[]{:S(2)}) collective-permute-start(bf16[64,2048]{1,0:T(8,128)(2,1)} %t0.3), channel_id=1, source_target_pairs={{0,6},{2,0},{4,2},{6,4},{1,7},{3,1},{5,3},{7,5},{8,14},{10,8},{12,... | collective-permute-start | bytes 786440 | tf_op jit(solution)/shard_map/ppermute | solution.py:433
  4.3 0.3 collective-permute-start.4
  4.6 0.7 collective-permute-start.5
  5.3 1.6 ids.1
  6.9 17.0 %all_to_all.20 = s32[32,8,128]{2,1,0:T(8,128)S(1)} all-to-all(s32[32,8,128]{2,1,0:T(8,128)} %bitcast.47), channel_id=1, replica_groups=mesh['dp'=16,'y'=4,'core'=2] {'dp','core'}, dimensions={0} | all-to-all | bytes 262144 | tf_op jit(solution)/shard_map/all_to_all | solution.py:441
  23.9 0.0 copy-start.9
  24.0 2.3 %shard_map.95 = bf16[256,2048]{1,0:T(8,128)(2,1)} custom-call(s32[256,128]{1,0:T(8,128)S(1)} %bitcast.39, bf16[64,2048]{1,0:T(8,128)(2,1)} %t0.3, bf16[64,2048]{1,0:T(8,128)(2,1)S(1)} %collective-permute-done.3.t1, bf16[64,2048]{1,0:T(8,128)(2,1)S(1)} %collective-permute-done.4.t2, bf16[64,2048]{1,0:T(8,128)(2,1)S(1)} %collective-permute-done.5.t3), custom_call_target="tpu_custom_call" | custom-call | flops 268435456 | bytes 3000000 | tf_op jit(solution)/shard_map/pallas_call | solution.py:122
  26.3 4.3 %all-to-all-start.2 = ((bf16[32,8,2048]{2,1,0:T(8,128)(2,1)}), bf16[32,8,2048]{2,1,0:T(8,128)(2,1)S(1)}, u32[]{:S(2)}, u32[]{:S(2)}) async-start(bf16[32,8,2048]{2,1,0:T(8,128)(2,1)} %bitcast.6), calls=%async_computation.2 | async-start | bytes 2097152 | tf_op jit(solution)/shard_map/all_to_all | solution.py:441
  30.6 1.8 collective-permute-start
  32.4 1.4 collective-permute-start.1
  33.8 4.5 %collective-permute-done.t1 = bf16[64,2048]{1,0:T(8,128)(2,1)S(1)} collective-permute-done((bf16[64,2048]{1,0:T(8,128)(2,1)S(1)}, bf16[64,2048]{1,0:T(8,128)(2,1)S(1)}, u32[]{:S(2)}, u32[]{:S(2)}) %collective-permute-start) | collective-permute-done | bytes 262176 | tf_op jit(solution)/shard_map/ppermute | solution.py:433
  38.3 2.8 %collective-permute-done.1.t2 = bf16[64,2048]{1,0:T(8,128)(2,1)S(1)} collective-permute-done((bf16[64,2048]{1,0:T(8,128)(2,1)S(1)}, bf16[64,2048]{1,0:T(8,128)(2,1)S(1)}, u32[]{:S(2)}, u32[]{:S(2)}) %collective-permute-start.1) | collective-permute-done | bytes 262176 | tf_op jit(solution)/shard_map/ppermute | solution.py:433
  41.2 6.6 %collective-permute-done.2.t3 = bf16[64,2048]{1,0:T(8,128)(2,1)S(1)} collective-permute-done((bf16[64,2048]{1,0:T(8,128)(2,1)S(1)}, bf16[64,2048]{1,0:T(8,128)(2,1)S(1)}, u32[]{:S(2)}, u32[]{:S(2)}) %collective-permute-start.2) | collective-permute-done | bytes 262176 | tf_op jit(solution)/shard_map/ppermute | solution.py:433
  47.8 2.2 %shard_map.94 = bf16[256,2048]{1,0:T(8,128)(2,1)} custom-call(s32[256,128]{1,0:T(8,128)S(1)} %bitcast.40, bf16[64,2048]{1,0:T(8,128)(2,1)} %t0.2, bf16[64,2048]{1,0:T(8,128)(2,1)S(1)} %collective-permute-done.t1, bf16[64,2048]{1,0:T(8,128)(2,1)S(1)} %collective-permute-done.1.t2, bf16[64,2048]{1,0:T(8,128)(2,1)S(1)} %collective-permute-done.2.t3), custom_call_target="tpu_custom_call" | custom-call | flops 268435456 | bytes 3000000 | tf_op jit(solution)/shard_map/pallas_call | solution.py:122
  50.0 7.6 %all-to-all-start.1 = ((bf16[32,8,2048]{2,1,0:T(8,128)(2,1)}), bf16[32,8,2048]{2,1,0:T(8,128)(2,1)S(1)}, u32[]{:S(2)}, u32[]{:S(2)}) async-start(bf16[32,8,2048]{2,1,0:T(8,128)(2,1)} %bitcast.4), calls=%async_computation.1 | async-start | bytes 2097152 | tf_op jit(solution)/shard_map/all_to_all | solution.py:441
  57.7 2.8 %weight.1.side_hbm = f32[4,256,512]{2,1,0:T(8,128)S(1)} custom-call(s32[16,2048]{1,0:T(8,128)S(1)} %get-tuple-element.28.places_ref.refs_0_, f32[16,2048]{1,0:T(8,128)S(1)} %bitcast.45), custom_call_target="tpu_custom_call" | custom-call | flops 25165824 | bytes 2097152 | tf_op jit(solution)/shard_map/weight/pallas_call | solution.py:154
  60.6 1.3 copy-done.2
  61.9 0.9 slice_bitcast_fusion
  62.7 0.3 collective-permute-start.12
  63.1 1.1 collective-permute-start.15
  64.2 10.5 %first.1 = (f32[4,256,512]{2,1,0:T(8,128)}, bf16[128,2,4096]{2,1,0:T(2,128)(2,1)}) custom-call(bf16[2048,2048]{1,0:T(8,128)(2,1)} %other_hbm.3, bf16[2048,2048]{1,0:T(8,128)(2,1)} %lead_hbm.3, bf16[256,2048]{1,0:T(8,128)(2,1)} %bitcast.36, f32[4,256,512]{2,1,0:T(8,128)} %copy-done.2), custom_call_target="tpu_custom_call" | custom-call | flops 4294967296 | bytes 25165824 | tf_op jit(solution)/shard_map/first/pallas_call | solution.py:272
  74.8 1.0 copy-done.8
  75.7 12.0 %second.1 = (bf16[16,512]{1,0:T(8,128)(2,1)}, bf16[16,512]{1,0:T(8,128)(2,1)}, bf16[16,512]{1,0:T(8,128)(2,1)}, bf16[16,512]{1,0:T(8,128)(2,1)}, bf16[128,2,4096]{2,1,0:T(2,128)(2,1)}) custom-call(bf16[2048,2048]{1,0:T(8,128)(2,1)} %lead_hbm.3, bf16[2048,2048]{1,0:T(8,128)(2,1)} %other_hbm.3, ...), custom_call_target="tpu_custom_call", output_to_operand_aliasing={{4}: (5, {})} | custom-call | flops 4294967296 | bytes 25165824 | tf_op jit(solution)/shard_map/second/pallas_call | solution.py:272
  87.8 9.1 %all-to-all-start.3 = ((bf16[128,2,4096]{2,1,0:T(2,128)(2,1)}), bf16[128,2,4096]{2,1,0:T(2,128)(2,1)}, u32[]{:S(2)}, u32[]{:S(2)}) async-start(bf16[128,2,4096]{2,1,0:T(2,128)(2,1)} %get-tuple-element.18), calls=%async_computation.3 | async-start | bytes 4194304 | tf_op jit(solution)/shard_map/all_to_all | solution.py:441
  96.9 2.7 %collective-permute-start.13 = (bf16[128,2048]{1,0:T(8,128)(2,1)}, bf16[128,2048]{1,0:T(8,128)(2,1)S(1)}, u32[]{:S(2)}, u32[]{:S(2)}) collective-permute-start(bf16[128,2048]{1,0:T(8,128)(2,1)} %get-tuple-element.21), channel_id=1, source_target_pairs={{0,6},{2,0},{4,2},{6,4},{1,7},{3,1},{5,3},{7,5},{8,14},{10,8},{12,... | collective-permute-start | bytes 1572872 | tf_op jit(solution)/shard_map/ppermute | solution.py:433
  99.6 2.7 %collective-permute-start.14 = (bf16[128,2048]{1,0:T(8,128)(2,1)S(1)}, bf16[128,2048]{1,0:T(8,128)(2,1)}, u32[]{:S(2)}, u32[]{:S(2)}) collective-permute-start(bf16[128,2048]{1,0:T(8,128)(2,1)S(1)} %collective-permute-done.12.refs_1_), channel_id=1, source_target_pairs={{0,6},{2,0},{4,2},{6,4},{1,7},{3,1},{5,3},{7,5},{8,14},{10,8},{12,... | collective-permute-start | bytes 1572872 | tf_op jit(solution)/shard_map/ppermute | solution.py:433
  102.3 1.3 collective-permute-start.10
  103.6 41.0 %collective-permute-done.10.p2 = s32[16,512]{1,0:T(8,128)S(1)} collective-permute-done((s32[16,512]{1,0:T(8,128)S(1)}, s32[16,512]{1,0:T(8,128)S(1)}, u32[]{:S(2)}, u32[]{:S(2)}) %collective-permute-start.10) | collective-permute-done | bytes 32800 | tf_op jit(solution)/shard_map/ppermute | solution.py:433
  144.6 0.4 collective-permute-start.11
  145.0 3.6 %collective-permute-done.11.p3 = s32[16,512]{1,0:T(8,128)S(1)} collective-permute-done((s32[16,512]{1,0:T(8,128)S(1)}, s32[16,512]{1,0:T(8,128)S(1)}, u32[]{:S(2)}, u32[]{:S(2)}) %collective-permute-start.11) | collective-permute-done | bytes 32800 | tf_op jit(solution)/shard_map/ppermute | solution.py:433
  148.6 2.8 %collective-permute-done.9.p1 = s32[16,512]{1,0:T(8,128)S(1)} collective-permute-done((s32[16,512]{1,0:T(8,128)S(1)}, s32[16,512]{1,0:T(8,128)S(1)}, u32[]{:S(2)}, u32[]{:S(2)}) %collective-permute-start.9) | collective-permute-done | bytes 32800 | tf_op jit(solution)/shard_map/ppermute | solution.py:433
  151.4 1.2 collective-permute-start.6
  152.6 1.7 collective-permute-done.6.c1
  154.3 0.6 collective-permute-start.7
  154.9 3.5 %collective-permute-done.7.c2 = bf16[16,512]{1,0:T(8,128)(2,1)S(1)} collective-permute-done((bf16[16,512]{1,0:T(8,128)(2,1)S(1)}, bf16[16,512]{1,0:T(8,128)(2,1)S(1)}, u32[]{:S(2)}, u32[]{:S(2)}) %collective-permute-start.7) | collective-permute-done | bytes 16416 | tf_op jit(solution)/shard_map/ppermute | solution.py:433
  158.4 3.8 %collective-permute-done.8.c3 = bf16[16,512]{1,0:T(8,128)(2,1)S(1)} collective-permute-done((bf16[16,512]{1,0:T(8,128)(2,1)S(1)}, bf16[16,512]{1,0:T(8,128)(2,1)S(1)}, u32[]{:S(2)}, u32[]{:S(2)}) %collective-permute-start.8) | collective-permute-done | bytes 16416 | tf_op jit(solution)/shard_map/ppermute | solution.py:433
  162.3 3.6 %give.1 = bf16[256,2048]{1,0:T(8,128)(2,1)} custom-call(bf16[16,512]{1,0:T(8,128)(2,1)S(1)} %copy-done.7, bf16[16,512]{1,0:T(8,128)(2,1)S(1)} %collective-permute-done.6.c1, bf16[16,512]{1,0:T(8,128)(2,1)S(1)} %collective-permute-done.7.c2, bf16[16,512]{1,0:T(8,128)(2,1)S(1)} %collective-permute-done.8.c3, s32[16,512]{1,0:T(8,128)S(1)} %get-tuple-element.26.p0, ...), custom_call_target="tpu_custom_call" | custom-call | flops 1073741824 | bytes 6291456 | tf_op jit(solution)/shard_map/give/pallas_call | solution.py:415
  165.9 7.0 %collective-permute-start.18 = (bf16[256,2048]{1,0:T(8,128)(2,1)}, bf16[256,2048]{1,0:T(8,128)(2,1)}, u32[]{:S(2)}, u32[]{:S(2)}) collective-permute-start(bf16[256,2048]{1,0:T(8,128)(2,1)} %give.1), channel_id=1, source_target_pairs={{0,1},{1,0},{2,3},{3,2},{4,5},{5,4},{6,7},{7,6},{8,9},{9,8},{10,11... | collective-permute-start | bytes 3145736 | tf_op jit(solution)/shard_map/ppermute | solution.py:480
  172.9 0.7 collective-permute-start.19
  173.6 0.7 collective-permute-start.21
  174.3 3.5 %collective-permute-done.19.a1 = s32[256,128]{1,0:T(8,128)S(1)} collective-permute-done((s32[256,128]{1,0:T(8,128)S(1)}, s32[256,128]{1,0:T(8,128)S(1)}, u32[]{:S(2)}, u32[]{:S(2)}) %collective-permute-start.19) | collective-permute-done | bytes 131104 | tf_op jit(solution)/shard_map/ppermute | solution.py:433
  177.8 2.0 %collective-permute-done.20.a2 = s32[256,128]{1,0:T(8,128)S(1)} collective-permute-done((s32[256,128]{1,0:T(8,128)S(1)}, s32[256,128]{1,0:T(8,128)S(1)}, u32[]{:S(2)}, u32[]{:S(2)}) %collective-permute-start.20) | collective-permute-done | bytes 131104 | tf_op jit(solution)/shard_map/ppermute | solution.py:433
  179.8 3.5 %collective-permute-done.21.a3 = s32[256,128]{1,0:T(8,128)S(1)} collective-permute-done((s32[256,128]{1,0:T(8,128)S(1)}, s32[256,128]{1,0:T(8,128)S(1)}, u32[]{:S(2)}, u32[]{:S(2)}) %collective-permute-start.21) | collective-permute-done | bytes 131104 | tf_op jit(solution)/shard_map/ppermute | solution.py:433
  183.4 0.3 hits.1.hits_ref
  183.7 1.0 copy-done.4
  184.7 3.6 %keep.1 = bf16[256,2048]{1,0:T(8,128)(2,1)S(1)} custom-call(bf16[16,512]{1,0:T(8,128)(2,1)S(1)} %copy-done.7, bf16[16,512]{1,0:T(8,128)(2,1)S(1)} %collective-permute-done.6.c1, bf16[16,512]{1,0:T(8,128)(2,1)S(1)} %collective-permute-done.7.c2, bf16[16,512]{1,0:T(8,128)(2,1)S(1)} %collective-permute-done.8.c3, s32[16,512]{1,0:T(8,128)S(1)} %get-tuple-element.26.p0, ...), custom_call_target="tpu_custom_call" | custom-call | flops 1073741824 | bytes 6291456 | tf_op jit(solution)/shard_map/keep/pallas_call | solution.py:415
  188.4 3.4 %sums.1 = (f32[64,2048]{1,0:T(8,128)}, f32[64,2048]{1,0:T(8,128)}) custom-call(bf16[256,64]{1,0:T(8,128)(2,1)S(1)} %hits.1.hits_ref, bf16[128,2,4096]{2,1,0:T(2,128)(2,1)} %all-to-all-done.3.got_hbm), custom_call_target="tpu_custom_call" | custom-call | flops 268435456 | bytes 4000000 | tf_op jit(solution)/shard_map/sums/pallas_call | solution.py:353
  191.8 2.6 %add_convert_fusion = bf16[256,2048]{1,0:T(8,128)(2,1)} fusion(bf16[256,2048]{1,0:T(8,128)(2,1)} %collective-permute-done.18, bf16[256,2048]{1,0:T(8,128)(2,1)S(1)} %keep.1), kind=kLoop, calls=%fused_computation | loop fusion | flops 2097152 | bytes 3145728 | tf_op jit(solution)/shard_map/convert_element_type | solution.py:482
  (45 shorter events, 0.2 us)
Async XLA Ops:
  0.6 23.3 %collective-permute-start.3 = (bf16[64,2048]{1,0:T(8,128)(2,1)}, bf16[64,2048]{1,0:T(8,128)(2,1)S(1)}, u32[]{:S(2)}, u32[]{:S(2)}) collective-permute-start(bf16[64,2048]{1,0:T(8,128)(2,1)} %t0.3), channel_id=1, source_target_pairs={{0,6},{2,0},{4,2},{6,4},{1,7},{3,1},{5,3},{7,5},{8,14},{10,8},{12,... | collective-permute-start | bytes 786440 | tf_op jit(solution)/shard_map/ppermute | solution.py:433
  4.3 19.7 %collective-permute-start.4 = (bf16[64,2048]{1,0:T(8,128)(2,1)}, bf16[64,2048]{1,0:T(8,128)(2,1)S(1)}, u32[]{:S(2)}, u32[]{:S(2)}) collective-permute-start(bf16[64,2048]{1,0:T(8,128)(2,1)} %t0.3), channel_id=1, source_target_pairs={{0,4},{2,6},{4,0},{6,2},{1,5},{3,7},{5,1},{7,3},{8,12},{10,14},{12... | collective-permute-start | bytes 786440 | tf_op jit(solution)/shard_map/ppermute | solution.py:433
  4.6 19.3 %collective-permute-start.5 = (bf16[64,2048]{1,0:T(8,128)(2,1)}, bf16[64,2048]{1,0:T(8,128)(2,1)S(1)}, u32[]{:S(2)}, u32[]{:S(2)}) collective-permute-start(bf16[64,2048]{1,0:T(8,128)(2,1)} %t0.3), channel_id=1, source_target_pairs={{0,2},{2,4},{4,6},{6,0},{1,3},{3,5},{5,7},{7,1},{8,10},{10,12},{12... | collective-permute-start | bytes 786440 | tf_op jit(solution)/shard_map/ppermute | solution.py:433
  23.9 6.7 %copy-start.9 = (bf16[64,2048]{1,0:T(8,128)(2,1)S(1)}, bf16[64,2048]{1,0:T(8,128)(2,1)}, u32[]{:S(2)}) copy-start(bf16[64,2048]{1,0:T(8,128)(2,1)} %t0.2) | copy-start | bytes 786436
  26.3 23.7 %all-to-all-start.2 = ((bf16[32,8,2048]{2,1,0:T(8,128)(2,1)}), bf16[32,8,2048]{2,1,0:T(8,128)(2,1)S(1)}, u32[]{:S(2)}, u32[]{:S(2)}) async-start(bf16[32,8,2048]{2,1,0:T(8,128)(2,1)} %bitcast.6), calls=%async_computation.2 | async-start | bytes 2097152 | tf_op jit(solution)/shard_map/all_to_all | solution.py:441
  30.6 27.0 %copy-start.10 = (s32[1,2048,16]{1,2,0:T(8,128)S(1)}, s32[1,2048,16]{1,2,0:T(8,128)}, u32[]{:S(2)}) copy-start(s32[1,2048,16]{1,2,0:T(8,128)} %param.12) | copy-start | bytes 393220
  30.6 27.1 %copy-start.6 = (f32[1,2048,16]{1,2,0:T(8,128)S(1)}, f32[1,2048,16]{1,2,0:T(8,128)}, u32[]{:S(2)}) copy-start(f32[1,2048,16]{1,2,0:T(8,128)} %param.13) | copy-start | bytes 393220
  30.6 7.7 %collective-permute-start = (bf16[64,2048]{1,0:T(8,128)(2,1)S(1)}, bf16[64,2048]{1,0:T(8,128)(2,1)S(1)}, u32[]{:S(2)}, u32[]{:S(2)}) collective-permute-start(bf16[64,2048]{1,0:T(8,128)(2,1)S(1)} %copy-done.9), channel_id=1, source_target_pairs={{0,6},{2,0},{4,2},{6,4},{1,7},{3,1},{5,3},{7,5},{8,14},{10,8},{12,... | collective-permute-start | bytes 786440 | tf_op jit(solution)/shard_map/ppermute | solution.py:433
  32.4 8.8 %collective-permute-start.1 = (bf16[64,2048]{1,0:T(8,128)(2,1)S(1)}, bf16[64,2048]{1,0:T(8,128)(2,1)S(1)}, u32[]{:S(2)}, u32[]{:S(2)}) collective-permute-start(bf16[64,2048]{1,0:T(8,128)(2,1)S(1)} %copy-done.9), channel_id=1, source_target_pairs={{0,4},{2,6},{4,0},{6,2},{1,5},{3,7},{5,1},{7,3},{8,12},{10,14},{12... | collective-permute-start | bytes 786440 | tf_op jit(solution)/shard_map/ppermute | solution.py:433
  33.8 13.9 %collective-permute-start.2 = (bf16[64,2048]{1,0:T(8,128)(2,1)S(1)}, bf16[64,2048]{1,0:T(8,128)(2,1)S(1)}, u32[]{:S(2)}, u32[]{:S(2)}) collective-permute-start(bf16[64,2048]{1,0:T(8,128)(2,1)S(1)} %copy-done.9), channel_id=1, source_target_pairs={{0,2},{2,4},{4,6},{6,0},{1,3},{3,5},{5,7},{7,1},{8,10},{10,12},{12... | collective-permute-start | bytes 786440 | tf_op jit(solution)/shard_map/ppermute | solution.py:433
  50.0 10.6 %copy-start = (bf16[32,8,2048]{2,1,0:T(8,128)(2,1)}, bf16[32,8,2048]{2,1,0:T(8,128)(2,1)S(1)}, u32[]{:S(2)}) copy-start(bf16[32,8,2048]{2,1,0:T(8,128)(2,1)S(1)} %all-to-all-done.2) | copy-start | bytes 3145732
  50.0 24.7 %all-to-all-start.1 = ((bf16[32,8,2048]{2,1,0:T(8,128)(2,1)}), bf16[32,8,2048]{2,1,0:T(8,128)(2,1)S(1)}, u32[]{:S(2)}, u32[]{:S(2)}) async-start(bf16[32,8,2048]{2,1,0:T(8,128)(2,1)} %bitcast.4), calls=%async_computation.1 | async-start | bytes 2097152 | tf_op jit(solution)/shard_map/all_to_all | solution.py:441
  57.7 5.1 %copy-start.5 = (s32[16,2048]{1,0:T(8,128)}, s32[16,2048]{1,0:T(8,128)S(1)}, u32[]{:S(2)}) copy-start(s32[16,2048]{1,0:T(8,128)S(1)} %get-tuple-element.28.places_ref.refs_0_) | copy-start | bytes 393220
  60.6 1.3 copy-start.2
  62.7 36.8 %collective-permute-start.12 = (bf16[128,2048]{1,0:T(8,128)(2,1)S(1)}, bf16[128,2048]{1,0:T(8,128)(2,1)S(1)}, u32[]{:S(2)}, u32[]{:S(2)}) collective-permute-start(bf16[128,2048]{1,0:T(8,128)(2,1)S(1)} %get-tuple-element.22), channel_id=1, source_target_pairs={{0,6},{2,0},{4,2},{6,4},{1,7},{3,1},{5,3},{7,5},{8,14},{10,8},{12,... | collective-permute-start | bytes 1572872 | tf_op jit(solution)/shard_map/ppermute | solution.py:433
  63.1 39.2 %collective-permute-start.15 = (bf16[128,2048]{1,0:T(8,128)(2,1)}, bf16[128,2048]{1,0:T(8,128)(2,1)S(1)}, u32[]{:S(2)}, u32[]{:S(2)}) collective-permute-start(bf16[128,2048]{1,0:T(8,128)(2,1)} %get-tuple-element.21), channel_id=1, source_target_pairs={{0,2},{2,4},{4,6},{6,0},{1,3},{3,5},{5,7},{7,1},{8,10},{10,12},{12... | collective-permute-start | bytes 1572872 | tf_op jit(solution)/shard_map/ppermute | solution.py:433
  74.8 1.0 copy-start.8
  87.7 63.7 %copy-start.13 = (bf16[16,512]{1,0:T(8,128)(2,1)S(1)}, bf16[16,512]{1,0:T(8,128)(2,1)}, u32[]{:S(2)}) copy-start(bf16[16,512]{1,0:T(8,128)(2,1)} %get-tuple-element.15) | copy-start | bytes 49156
  87.7 66.6 %copy-start.12 = (bf16[16,512]{1,0:T(8,128)(2,1)S(1)}, bf16[16,512]{1,0:T(8,128)(2,1)}, u32[]{:S(2)}) copy-start(bf16[16,512]{1,0:T(8,128)(2,1)} %get-tuple-element.16) | copy-start | bytes 49156
  87.7 70.7 %copy-start.11 = (bf16[16,512]{1,0:T(8,128)(2,1)S(1)}, bf16[16,512]{1,0:T(8,128)(2,1)}, u32[]{:S(2)}) copy-start(bf16[16,512]{1,0:T(8,128)(2,1)} %get-tuple-element.17) | copy-start | bytes 49156
  87.8 74.5 %copy-start.1 = (bf16[32,8,2048]{2,1,0:T(8,128)(2,1)S(1)}, bf16[32,8,2048]{2,1,0:T(8,128)(2,1)}, u32[]{:S(2)}) copy-start(bf16[32,8,2048]{2,1,0:T(8,128)(2,1)} %copy-done) | copy-start | bytes 3145732
  87.8 74.5 %copy-start.7 = (bf16[16,512]{1,0:T(8,128)(2,1)S(1)}, bf16[16,512]{1,0:T(8,128)(2,1)}, u32[]{:S(2)}) copy-start(bf16[16,512]{1,0:T(8,128)(2,1)} %get-tuple-element.14.c0) | copy-start | bytes 49156
  87.8 100.6 %all-to-all-start.3 = ((bf16[128,2,4096]{2,1,0:T(2,128)(2,1)}), bf16[128,2,4096]{2,1,0:T(2,128)(2,1)}, u32[]{:S(2)}, u32[]{:S(2)}) async-start(bf16[128,2,4096]{2,1,0:T(2,128)(2,1)} %get-tuple-element.18), calls=%async_computation.3 | async-start | bytes 4194304 | tf_op jit(solution)/shard_map/all_to_all | solution.py:441
  96.9 65.3 %collective-permute-start.13 = (bf16[128,2048]{1,0:T(8,128)(2,1)}, bf16[128,2048]{1,0:T(8,128)(2,1)S(1)}, u32[]{:S(2)}, u32[]{:S(2)}) collective-permute-start(bf16[128,2048]{1,0:T(8,128)(2,1)} %get-tuple-element.21), channel_id=1, source_target_pairs={{0,6},{2,0},{4,2},{6,4},{1,7},{3,1},{5,3},{7,5},{8,14},{10,8},{12,... | collective-permute-start | bytes 1572872 | tf_op jit(solution)/shard_map/ppermute | solution.py:433
  99.6 62.7 %collective-permute-start.17 = (bf16[128,2048]{1,0:T(8,128)(2,1)S(1)}, bf16[128,2048]{1,0:T(8,128)(2,1)}, u32[]{:S(2)}, u32[]{:S(2)}) collective-permute-start(bf16[128,2048]{1,0:T(8,128)(2,1)S(1)} %get-tuple-element.22), channel_id=1, source_target_pairs={{0,2},{2,4},{4,6},{6,0},{1,3},{3,5},{5,7},{7,1},{8,10},{10,12},{12... | collective-permute-start | bytes 1572872 | tf_op jit(solution)/shard_map/ppermute | solution.py:433
  99.6 62.7 %collective-permute-start.14 = (bf16[128,2048]{1,0:T(8,128)(2,1)S(1)}, bf16[128,2048]{1,0:T(8,128)(2,1)}, u32[]{:S(2)}, u32[]{:S(2)}) collective-permute-start(bf16[128,2048]{1,0:T(8,128)(2,1)S(1)} %collective-permute-done.12.refs_1_), channel_id=1, source_target_pairs={{0,6},{2,0},{4,2},{6,4},{1,7},{3,1},{5,3},{7,5},{8,14},{10,8},{12,... | collective-permute-start | bytes 1572872 | tf_op jit(solution)/shard_map/ppermute | solution.py:433
  102.3 60.0 %collective-permute-start.16 = (bf16[128,2048]{1,0:T(8,128)(2,1)S(1)}, bf16[128,2048]{1,0:T(8,128)(2,1)}, u32[]{:S(2)}, u32[]{:S(2)}) collective-permute-start(bf16[128,2048]{1,0:T(8,128)(2,1)S(1)} %collective-permute-done.15.refs_6_), channel_id=1, source_target_pairs={{0,2},{2,4},{4,6},{6,0},{1,3},{3,5},{5,7},{7,1},{8,10},{10,12},{12... | collective-permute-start | bytes 1572872 | tf_op jit(solution)/shard_map/ppermute | solution.py:433
  102.3 42.4 %collective-permute-start.10 = (s32[16,512]{1,0:T(8,128)S(1)}, s32[16,512]{1,0:T(8,128)S(1)}, u32[]{:S(2)}, u32[]{:S(2)}) collective-permute-start(s32[16,512]{1,0:T(8,128)S(1)} %get-tuple-element.24), channel_id=1, source_target_pairs={{0,4},{2,6},{4,0},{6,2},{1,5},{3,7},{5,1},{7,3},{8,12},{10,14},{12... | collective-permute-start | bytes 98312 | tf_op jit(solution)/shard_map/ppermute | solution.py:433
  144.6 4.0 %collective-permute-start.11 = (s32[16,512]{1,0:T(8,128)S(1)}, s32[16,512]{1,0:T(8,128)S(1)}, u32[]{:S(2)}, u32[]{:S(2)}) collective-permute-start(s32[16,512]{1,0:T(8,128)S(1)} %get-tuple-element.23), channel_id=1, source_target_pairs={{0,2},{2,4},{4,6},{6,0},{1,3},{3,5},{5,7},{7,1},{8,10},{10,12},{12... | collective-permute-start | bytes 98312 | tf_op jit(solution)/shard_map/ppermute | solution.py:433
  148.6 2.8 %collective-permute-start.9 = (s32[16,512]{1,0:T(8,128)S(1)}, s32[16,512]{1,0:T(8,128)S(1)}, u32[]{:S(2)}, u32[]{:S(2)}) collective-permute-start(s32[16,512]{1,0:T(8,128)S(1)} %get-tuple-element.25), channel_id=1, source_target_pairs={{0,6},{2,0},{4,2},{6,4},{1,7},{3,1},{5,3},{7,5},{8,14},{10,8},{12,... | collective-permute-start | bytes 98312 | tf_op jit(solution)/shard_map/ppermute | solution.py:433
  151.4 2.9 %collective-permute-start.6 = (bf16[16,512]{1,0:T(8,128)(2,1)S(1)}, bf16[16,512]{1,0:T(8,128)(2,1)S(1)}, u32[]{:S(2)}, u32[]{:S(2)}) collective-permute-start(bf16[16,512]{1,0:T(8,128)(2,1)S(1)} %copy-done.13), channel_id=1, source_target_pairs={{0,6},{2,0},{4,2},{6,4},{1,7},{3,1},{5,3},{7,5},{8,14},{10,8},{12,... | collective-permute-start | bytes 49160 | tf_op jit(solution)/shard_map/ppermute | solution.py:433
  154.3 4.1 %collective-permute-start.7 = (bf16[16,512]{1,0:T(8,128)(2,1)S(1)}, bf16[16,512]{1,0:T(8,128)(2,1)S(1)}, u32[]{:S(2)}, u32[]{:S(2)}) collective-permute-start(bf16[16,512]{1,0:T(8,128)(2,1)S(1)} %copy-done.12), channel_id=1, source_target_pairs={{0,4},{2,6},{4,0},{6,2},{1,5},{3,7},{5,1},{7,3},{8,12},{10,14},{12... | collective-permute-start | bytes 49160 | tf_op jit(solution)/shard_map/ppermute | solution.py:433
  158.4 3.8 %collective-permute-start.8 = (bf16[16,512]{1,0:T(8,128)(2,1)S(1)}, bf16[16,512]{1,0:T(8,128)(2,1)S(1)}, u32[]{:S(2)}, u32[]{:S(2)}) collective-permute-start(bf16[16,512]{1,0:T(8,128)(2,1)S(1)} %copy-done.11), channel_id=1, source_target_pairs={{0,2},{2,4},{4,6},{6,0},{1,3},{3,5},{5,7},{7,1},{8,10},{10,12},{12... | collective-permute-start | bytes 49160 | tf_op jit(solution)/shard_map/ppermute | solution.py:433
  162.2 3.7 %copy-start.3 = (bf16[128,2048]{1,0:T(8,128)(2,1)}, bf16[128,2048]{1,0:T(8,128)(2,1)S(1)}, u32[]{:S(2)}) copy-start(bf16[128,2048]{1,0:T(8,128)(2,1)S(1)} %collective-permute-done.13.refs_2_) | copy-start | bytes 1572868
  165.9 25.9 %collective-permute-start.18 = (bf16[256,2048]{1,0:T(8,128)(2,1)}, bf16[256,2048]{1,0:T(8,128)(2,1)}, u32[]{:S(2)}, u32[]{:S(2)}) collective-permute-start(bf16[256,2048]{1,0:T(8,128)(2,1)} %give.1), channel_id=1, source_target_pairs={{0,1},{1,0},{2,3},{3,2},{4,5},{5,4},{6,7},{7,6},{8,9},{9,8},{10,11... | collective-permute-start | bytes 3145736 | tf_op jit(solution)/shard_map/ppermute | solution.py:480
  172.9 5.0 %collective-permute-start.19 = (s32[256,128]{1,0:T(8,128)S(1)}, s32[256,128]{1,0:T(8,128)S(1)}, u32[]{:S(2)}, u32[]{:S(2)}) collective-permute-start(s32[256,128]{1,0:T(8,128)S(1)} %bitcast.41), channel_id=1, source_target_pairs={{0,6},{2,0},{4,2},{6,4},{1,7},{3,1},{5,3},{7,5},{8,14},{10,8},{12,... | collective-permute-start | bytes 393224 | tf_op jit(solution)/shard_map/ppermute | solution.py:433
  173.6 6.2 %collective-permute-start.20 = (s32[256,128]{1,0:T(8,128)S(1)}, s32[256,128]{1,0:T(8,128)S(1)}, u32[]{:S(2)}, u32[]{:S(2)}) collective-permute-start(s32[256,128]{1,0:T(8,128)S(1)} %bitcast.42), channel_id=1, source_target_pairs={{0,4},{2,6},{4,0},{6,2},{1,5},{3,7},{5,1},{7,3},{8,12},{10,14},{12... | collective-permute-start | bytes 393224 | tf_op jit(solution)/shard_map/ppermute | solution.py:433
  173.6 9.8 %collective-permute-start.21 = (s32[256,128]{1,0:T(8,128)S(1)}, s32[256,128]{1,0:T(8,128)S(1)}, u32[]{:S(2)}, u32[]{:S(2)}) collective-permute-start(s32[256,128]{1,0:T(8,128)S(1)} %bitcast.43), channel_id=1, source_target_pairs={{0,2},{2,4},{4,6},{6,0},{1,3},{3,5},{5,7},{7,1},{8,10},{10,12},{12... | collective-permute-start | bytes 393224 | tf_op jit(solution)/shard_map/ppermute | solution.py:433
  183.7 1.0 copy-start.4

commit v11 on v7

--- a/solution.py
+++ b/solution.py
@@ -168,15 +168,17 @@
     row = iota((16, block), 0)
     lines = []
     for k in range(topk):
-        want = slot[k : k + 1, :] - row
-        found = jnp.zeros((16, block), F32)
+        want = (slot[k : k + 1, :] - row).astype(jnp.int16)
+        found = jnp.zeros((16, block), BF16)
         for g in range(0, left.shape[0], 16):
-            found = jnp.where(want == g, left[g : g + 16, here].astype(F32), found)
-        lines.append(jnp.sum(found, axis=0, keepdims=True))
+            found = jnp.where(want == jnp.int16(g), left[g : g + 16, here], found)
+        lines.append(jnp.sum(found.astype(F32), axis=0, keepdims=True))
     return jnp.concatenate(lines, axis=0).astype(BF16)
 
 
-def half_kernel(first, lead_hbm, other_hbm, rows_hbm, side_hbm, *refs):
+def half_kernel(
+    first, lead_hbm, other_hbm, rows_hbm, side_hbm, *refs
+):
     places = None if first else refs[0]
     extra_hbm = refs[:1] if first else refs[1 : 1 + N_Y]
     (
@@ -207,6 +209,10 @@
         for j in range(N_Y):
             cols = pl.ds(j * step, step)
             here = dot(left[:, tokens], other[tokens, cols], NN)
+            if not first and j % 2 == 0:
+                at_chunk = c - 1 + j // 2
+                mine = pl.ds(at_chunk * block, block)
+                extra[at_chunk] = at_places(left, mine, places[:, mine])
             if not last:
                 half[:, cols] = here
                 continue
@@ -237,16 +243,15 @@
             sent.append(out)
         else:
             left[:, here] = (side[c] * found).astype(BF16)
-            extra[c] = at_places(left, here, places[:, here])
         if c == N_Y // 2 - 1:
             parts(c, False)
+    parts(N_Y - 1, True)
     if not first:
         y = lax.axis_index("y")
         for r in range(N_Y):
             out = copy(extra.at[(y + r) % N_Y], extra_hbm[r], extra_sems.at[r])
             out.start()
             sent.append(out)
-    parts(N_Y - 1, True)
     for out in sent:
         out.wait()
 
@@ -255,7 +260,7 @@
     first = places is None
     count, width = lead.shape
     slots = rows.shape[0]
-    chunks = jax.ShapeDtypeStruct((devices, slots // devices, width), BF16)
+    capacity = slots // devices
     if first:
         extra = (jax.ShapeDtypeStruct(side.shape, F32),)
         held = pltpu.VMEM(side.shape, F32)
@@ -265,7 +270,7 @@
         held = pltpu.VMEM((N_Y, topk, count // N_Y), BF16)
     return pl.pallas_call(
         functools.partial(half_kernel, first),
-        out_shape=extra + (chunks,),
+        out_shape=extra + (jax.ShapeDtypeStruct((devices, capacity, width), BF16),),
         in_specs=[ANY] * 4 + ([] if first else [VMEM]),
         out_specs=(ANY,) * (len(extra) + 1),
         scratch_shapes=[
@@ -276,7 +281,7 @@
             pltpu.VMEM((slots, count), BF16),
             held,
             pltpu.VMEM((slots, width), F32),
-            pltpu.VMEM(chunks.shape, BF16),
+            pltpu.VMEM((devices, capacity, width), BF16),
             DMA((8,)), DMA((8,)), DMA, DMA((4,)), DMA((4,)), DMA((4,)),
         ],
         compiler_params=params(56),
@@ -357,8 +362,10 @@
 
 
 def final_kernel(
-    mine, c0, c1, c2, c3, p0, p1, p2, p3, d0, d1, d2a, d2b, d3, out_hbm, coef, rows, out, d_sems, out_sems
+    mine, c0, c1, c2, c3, p0, p1, p2, p3, *refs
 ):
+    blocks = refs[:-6]
+    out_hbm, coef, rows, out, d_sems, out_sems = refs[-6:]
     core = lax.axis_index("core")
     which = core if mine else 1 - core
     half = out.shape[0]
@@ -366,7 +373,7 @@
     topk = c0.shape[0]
     loads = []
     start = 0
-    for i, d in enumerate((d0, d1, d2a, d2b, d3)):
+    for i, d in enumerate(blocks):
         loads.append(copy(d, rows.at[pl.ds(start, d.shape[0]), :], d_sems.at[i]))
         start += d.shape[0]
     for c in loads:
@@ -402,13 +409,13 @@
     return pl.pallas_call(
         functools.partial(final_kernel, mine),
         out_shape=jax.ShapeDtypeStruct((half, width), BF16),
-        in_specs=[VMEM] * 8 + [ANY] * 5,
+        in_specs=[VMEM] * 8 + [ANY] * len(rows),
         out_specs=ANY,
         scratch_shapes=[
             pltpu.VMEM((N_Y * slots, half), BF16),
             pltpu.VMEM((N_Y * slots, width), BF16),
             pltpu.VMEM((half, width), BF16),
-            DMA((5,)), DMA((4,)),
+            DMA((len(rows),)), DMA((4,)),
         ],
         compiler_params=params(16),
         cost_estimate=cost(2 * half * 1024 * 2048, 6 << 20),
@@ -447,22 +454,24 @@
     weight = build_weight(slot_of, jnp.transpose(gate_weights[0]), slots)
     down = column(gather_rows(asked, down_tables, width))
     lists = gathered([asked] * N_Y)
-    hits = hit_rows(lists, row_count)
     block = slot_of.shape[1] // N_Y
     blocks = [
         lax.dynamic_slice_in_dim(slot_of, ((y + r) & (N_Y - 1)) * block, block, 1) for r in range(N_Y)
     ]
     chip_places = gathered(blocks)
     up = column(gather_rows(asked, up_tables, width))
-    above, below = turn(down, 1), turn(down, 3)
+    head, tail = down[: slots // 2], down[slots // 2 :]
+    above_head, below_tail = turn(head, 1), turn(tail, 3)
+    above_tail, below_head = turn(tail, 1), turn(head, 3)
+    far_head, far_tail = turn(above_head, 1), turn(below_tail, 3)
+    down_all = (down, above_head, above_tail, far_head, far_tail, below_head, below_tail)
+    hits = hit_rows(lists, row_count)
     slope, part_up = half_terms(tokens, out_grad, down, weight, devices)
     got_up = exchange(part_up, ("dp", "core", "y"))
-    far = (turn(above[: slots // 2], 1), turn(below[slots // 2 :], 3))
     *small, part_down = half_terms(out_grad, tokens, up, slope, devices, slot_of)
     chip_coef = gathered(small)
     got_down = exchange(part_down, ("dp", "core", "y"))
     up_grad = sum_rows(hits, got_up)
-    down_all = (down, above, *far, below)
     give = final_product(False, chip_coef, chip_places, down_all)
     other = lax.ppermute(give, "core", [(0, 1), (1, 0)])
     keep = final_product(True, chip_coef, chip_places, down_all)

time: 163 us -> 206 us (1.26)
  the two profiles are of different devices: /device:TPU:1 before, /device:TPU:5 now
where the time goes in v11:
time: 206 us; the launch traced here: 205 us
  waiting for transfers between devices  80.6 us (39%)
  starting transfers between devices  58.3 us (28%)
  Pallas kernels  43.9 us (21%)
  blocking collectives  15.1 us (7%)
  local copies, waits for them, and re-layouts  3.39 us (2%)
  other arithmetic  2.63 us (1%)
    ppermute x21, waiting for transfers between devices, turn(): return lax.ppermute(x, 'y', [(i, (i - r) % N_Y) for i in range(N_Y)])  80.2 us
    all_to_all x4, starting transfers between devices, exchange(): return lax.all_to_all(x, axes, split_axis=0, concat_axis=0, tiled=True)  35.5 us
    pallas_call x2, Pallas kernels, half_terms(): pl.pallas_call(functools.partial(half_kernel, first), out_shape=extra + (...  22.5 us
    ppermute x21, starting transfers between devices, turn(): return lax.ppermute(x, 'y', [(i, (i - r) % N_Y) for i in range(N_Y)])  21.4 us
    all_to_all x1, blocking collectives, exchange(): return lax.all_to_all(x, axes, split_axis=0, concat_axis=0, tiled=True)  15.1 us
    pallas_call x2, Pallas kernels, final_product(): pl.pallas_call(functools.partial(final_kernel, mine), out_shape=jax.Shape...  7.29 us
    pallas_call x2, Pallas kernels, sum_rows(): pl.pallas_call(sums_kernel, out_shape=jax.ShapeDtypeStruct((rows, width),...  4.78 us
    pallas_call x2, Pallas kernels, gather_rows(): pl.pallas_call(gather_kernel, out_shape=jax.ShapeDtypeStruct((slots, widt...  4.56 us
  transfers between devices with their start and end apart: 26, of which 13 were waited for; matrix products, arithmetic and copies ran while one was open for 1% of the time, Pallas kernels for 14%

profile of v11, /device:TPU:5, one launch (start us, length us, event | category | flops | bytes accessed | tf_op | source)
XLA Modules:
  0.0 204.9 jit_solution(9208273063549322214)
XLA Ops:
  0.6 2.8 %collective-permute-start.3 = (bf16[64,2048]{1,0:T(8,128)(2,1)}, bf16[64,2048]{1,0:T(8,128)(2,1)S(1)}, u32[]{:S(2)}, u32[]{:S(2)}) collective-permute-start(bf16[64,2048]{1,0:T(8,128)(2,1)} %t0.3), channel_id=1, source_target_pairs={{0,6},{2,0},{4,2},{6,4},{1,7},{3,1},{5,3},{7,5},{8,14},{10,8},{12,... | collective-permute-start | bytes 786440 | tf_op jit(solution)/shard_map/ppermute | solution.py:427
  3.4 0.3 collective-permute-start.4
  3.8 0.7 collective-permute-start.5
  4.5 1.6 ids.1
  6.1 15.1 %all_to_all.25 = s32[32,8,128]{2,1,0:T(8,128)S(1)} all-to-all(s32[32,8,128]{2,1,0:T(8,128)} %bitcast.47), channel_id=1, replica_groups=mesh['dp'=16,'y'=4,'core'=2] {'dp','core'}, dimensions={0} | all-to-all | bytes 262144 | tf_op jit(solution)/shard_map/all_to_all | solution.py:435
  21.2 2.3 %shard_map.95 = bf16[256,2048]{1,0:T(8,128)(2,1)} custom-call(s32[256,128]{1,0:T(8,128)S(1)} %bitcast.39, bf16[64,2048]{1,0:T(8,128)(2,1)} %t0.3, bf16[64,2048]{1,0:T(8,128)(2,1)S(1)} %collective-permute-done.3.t1, bf16[64,2048]{1,0:T(8,128)(2,1)S(1)} %collective-permute-done.4.t2, bf16[64,2048]{1,0:T(8,128)(2,1)S(1)} %collective-permute-done.5.t3), custom_call_target="tpu_custom_call" | custom-call | flops 268435456 | bytes 3000000 | tf_op jit(solution)/shard_map/pallas_call | solution.py:122
  23.5 6.4 %all-to-all-start.2 = ((bf16[32,8,2048]{2,1,0:T(8,128)(2,1)}), bf16[32,8,2048]{2,1,0:T(8,128)(2,1)S(1)}, u32[]{:S(2)}, u32[]{:S(2)}) async-start(bf16[32,8,2048]{2,1,0:T(8,128)(2,1)} %bitcast.6), calls=%async_computation.2 | async-start | bytes 2097152 | tf_op jit(solution)/shard_map/all_to_all | solution.py:435
  29.9 1.8 collective-permute-start
  31.7 1.4 collective-permute-start.1
  33.1 4.3 %collective-permute-done.t1 = bf16[64,2048]{1,0:T(8,128)(2,1)S(1)} collective-permute-done((bf16[64,2048]{1,0:T(8,128)(2,1)S(1)}, bf16[64,2048]{1,0:T(8,128)(2,1)S(1)}, u32[]{:S(2)}, u32[]{:S(2)}) %collective-permute-start) | collective-permute-done | bytes 262176 | tf_op jit(solution)/shard_map/ppermute | solution.py:427
  37.5 3.0 %collective-permute-done.1.t2 = bf16[64,2048]{1,0:T(8,128)(2,1)S(1)} collective-permute-done((bf16[64,2048]{1,0:T(8,128)(2,1)S(1)}, bf16[64,2048]{1,0:T(8,128)(2,1)S(1)}, u32[]{:S(2)}, u32[]{:S(2)}) %collective-permute-start.1) | collective-permute-done | bytes 262176 | tf_op jit(solution)/shard_map/ppermute | solution.py:427
  40.5 6.6 %collective-permute-done.2.t3 = bf16[64,2048]{1,0:T(8,128)(2,1)S(1)} collective-permute-done((bf16[64,2048]{1,0:T(8,128)(2,1)S(1)}, bf16[64,2048]{1,0:T(8,128)(2,1)S(1)}, u32[]{:S(2)}, u32[]{:S(2)}) %collective-permute-start.2) | collective-permute-done | bytes 262176 | tf_op jit(solution)/shard_map/ppermute | solution.py:427
  47.1 2.2 %shard_map.94 = bf16[256,2048]{1,0:T(8,128)(2,1)} custom-call(s32[256,128]{1,0:T(8,128)S(1)} %bitcast.40, bf16[64,2048]{1,0:T(8,128)(2,1)} %t0.2, bf16[64,2048]{1,0:T(8,128)(2,1)S(1)} %collective-permute-done.t1, bf16[64,2048]{1,0:T(8,128)(2,1)S(1)} %collective-permute-done.1.t2, bf16[64,2048]{1,0:T(8,128)(2,1)S(1)} %collective-permute-done.2.t3), custom_call_target="tpu_custom_call" | custom-call | flops 268435456 | bytes 3000000 | tf_op jit(solution)/shard_map/pallas_call | solution.py:122
  49.3 7.6 %all-to-all-start.1 = ((bf16[32,8,2048]{2,1,0:T(8,128)(2,1)}), bf16[32,8,2048]{2,1,0:T(8,128)(2,1)S(1)}, u32[]{:S(2)}, u32[]{:S(2)}) async-start(bf16[32,8,2048]{2,1,0:T(8,128)(2,1)} %bitcast.4), calls=%async_computation.1 | async-start | bytes 2097152 | tf_op jit(solution)/shard_map/all_to_all | solution.py:435
  57.0 2.8 %weight.1.side_hbm = f32[4,256,512]{2,1,0:T(8,128)S(1)} custom-call(s32[16,2048]{1,0:T(8,128)S(1)} %get-tuple-element.24.places_ref.refs_0_, f32[16,2048]{1,0:T(8,128)S(1)} %bitcast.45), custom_call_target="tpu_custom_call" | custom-call | flops 25165824 | bytes 2097152 | tf_op jit(solution)/shard_map/weight/pallas_call | solution.py:154
  59.9 1.3 copy-done.2
  61.2 10.5 %first.1 = (f32[4,256,512]{2,1,0:T(8,128)}, bf16[128,2,2048]{2,1,0:T(2,128)(2,1)}) custom-call(bf16[2048,2048]{1,0:T(8,128)(2,1)} %other_hbm.3, bf16[2048,2048]{1,0:T(8,128)(2,1)} %lead_hbm.3, bf16[256,2048]{1,0:T(8,128)(2,1)} %bitcast.36, f32[4,256,512]{2,1,0:T(8,128)} %copy-done.2), custom_call_target="tpu_custom_call" | custom-call | flops 4294967296 | bytes 25165824 | tf_op jit(solution)/shard_map/first/pallas_call | solution.py:271
  71.7 0.4 all-to-all-done.1
  72.1 1.0 copy-done.6
  73.1 12.0 %second.1 = (bf16[16,512]{1,0:T(8,128)(2,1)}, bf16[16,512]{1,0:T(8,128)(2,1)}, bf16[16,512]{1,0:T(8,128)(2,1)}, bf16[16,512]{1,0:T(8,128)(2,1)}, bf16[128,2,2048]{2,1,0:T(2,128)(2,1)}) custom-call(bf16[2048,2048]{1,0:T(8,128)(2,1)} %lead_hbm.3, bf16[2048,2048]{1,0:T(8,128)(2,1)} %other_hbm.3, bf16[256,2048]{1,0:T(8,128)(2,1)} %bitcast.46, ...), custom_call_target="tpu_custom_call" | custom-call | flops 4294967296 | bytes 25165824 | tf_op jit(solution)/shard_map/second/pallas_call | solution.py:271
  85.1 8.0 %all-to-all-start.3 = ((bf16[128,2,2048]{2,1,0:T(2,128)(2,1)}), bf16[128,2,2048]{2,1,0:T(2,128)(2,1)}, u32[]{:S(2)}, u32[]{:S(2)}) async-start(bf16[128,2,2048]{2,1,0:T(2,128)(2,1)} %get-tuple-element.15), calls=%async_computation.3 | async-start | bytes 2097152 | tf_op jit(solution)/shard_map/all_to_all | solution.py:435
  93.2 1.0 slice_bitcast_fusion
  94.2 2.5 %collective-permute-start.12 = (bf16[128,2048]{1,0:T(8,128)(2,1)}, bf16[128,2048]{1,0:T(8,128)(2,1)S(1)}, u32[]{:S(2)}, u32[]{:S(2)}) collective-permute-start(bf16[128,2048]{1,0:T(8,128)(2,1)} %get-tuple-element.18), channel_id=1, source_target_pairs={{0,6},{2,0},{4,2},{6,4},{1,7},{3,1},{5,3},{7,5},{8,14},{10,8},{12,... | collective-permute-start | bytes 1572872 | tf_op jit(solution)/shard_map/ppermute | solution.py:427
  96.7 2.7 %collective-permute-start.13 = (bf16[128,2048]{1,0:T(8,128)(2,1)}, bf16[128,2048]{1,0:T(8,128)(2,1)S(1)}, u32[]{:S(2)}, u32[]{:S(2)}) collective-permute-start(bf16[128,2048]{1,0:T(8,128)(2,1)} %get-tuple-element.17), channel_id=1, source_target_pairs={{0,6},{2,0},{4,2},{6,4},{1,7},{3,1},{5,3},{7,5},{8,14},{10,8},{12,... | collective-permute-start | bytes 1572872 | tf_op jit(solution)/shard_map/ppermute | solution.py:427
  99.4 17.2 %collective-permute-done.12.refs_1_ = bf16[128,2048]{1,0:T(8,128)(2,1)S(1)} collective-permute-done((bf16[128,2048]{1,0:T(8,128)(2,1)}, bf16[128,2048]{1,0:T(8,128)(2,1)S(1)}, u32[]{:S(2)}, u32[]{:S(2)}) %collective-permute-start.12) | collective-permute-done | bytes 524320 | tf_op jit(solution)/shard_map/ppermute | solution.py:427
  116.6 1.7 collective-permute-start.14
  118.3 2.3 %collective-permute-start.10 = (s32[16,512]{1,0:T(8,128)S(1)}, s32[16,512]{1,0:T(8,128)S(1)}, u32[]{:S(2)}, u32[]{:S(2)}) collective-permute-start(s32[16,512]{1,0:T(8,128)S(1)} %get-tuple-element.20), channel_id=1, source_target_pairs={{0,4},{2,6},{4,0},{6,2},{1,5},{3,7},{5,1},{7,3},{8,12},{10,14},{12... | collective-permute-start | bytes 98312 | tf_op jit(solution)/shard_map/ppermute | solution.py:427
  120.6 20.8 %collective-permute-done.10.p2 = s32[16,512]{1,0:T(8,128)S(1)} collective-permute-done((s32[16,512]{1,0:T(8,128)S(1)}, s32[16,512]{1,0:T(8,128)S(1)}, u32[]{:S(2)}, u32[]{:S(2)}) %collective-permute-start.10) | collective-permute-done | bytes 32800 | tf_op jit(solution)/shard_map/ppermute | solution.py:427
  141.6 3.7 %collective-permute-done.11.p3 = s32[16,512]{1,0:T(8,128)S(1)} collective-permute-done((s32[16,512]{1,0:T(8,128)S(1)}, s32[16,512]{1,0:T(8,128)S(1)}, u32[]{:S(2)}, u32[]{:S(2)}) %collective-permute-start.11) | collective-permute-done | bytes 32800 | tf_op jit(solution)/shard_map/ppermute | solution.py:427
  145.4 2.8 %collective-permute-done.9.p1 = s32[16,512]{1,0:T(8,128)S(1)} collective-permute-done((s32[16,512]{1,0:T(8,128)S(1)}, s32[16,512]{1,0:T(8,128)S(1)}, u32[]{:S(2)}, u32[]{:S(2)}) %collective-permute-start.9) | collective-permute-done | bytes 32800 | tf_op jit(solution)/shard_map/ppermute | solution.py:427
  148.1 1.2 collective-permute-start.6
  149.3 1.4 collective-permute-done.6.c1
  150.7 0.9 collective-permute-start.7
  151.6 13.5 %all-to-all-start.4 = ((bf16[128,2,2048]{2,1,0:T(2,128)(2,1)}), bf16[128,2,2048]{2,1,0:T(2,128)(2,1)}, u32[]{:S(2)}, u32[]{:S(2)}) async-start(bf16[128,2,2048]{2,1,0:T(2,128)(2,1)} %get-tuple-element.16), calls=%async_computation.4 | async-start | bytes 2097152 | tf_op jit(solution)/shard_map/all_to_all | solution.py:435
  165.2 1.3 collective-permute-start.8
  166.4 11.7 %collective-permute-done.8.c3 = bf16[16,512]{1,0:T(8,128)(2,1)S(1)} collective-permute-done((bf16[16,512]{1,0:T(8,128)(2,1)S(1)}, bf16[16,512]{1,0:T(8,128)(2,1)S(1)}, u32[]{:S(2)}, u32[]{:S(2)}) %collective-permute-start.8) | collective-permute-done | bytes 16416 | tf_op jit(solution)/shard_map/ppermute | solution.py:427
  178.2 3.7 %give.1 = bf16[256,2048]{1,0:T(8,128)(2,1)} custom-call(bf16[16,512]{1,0:T(8,128)(2,1)S(1)} %copy-done.5, bf16[16,512]{1,0:T(8,128)(2,1)S(1)} %collective-permute-done.6.c1, bf16[16,512]{1,0:T(8,128)(2,1)S(1)} %collective-permute-done.7.c2, bf16[16,512]{1,0:T(8,128)(2,1)S(1)} %collective-permute-done.8.c3, s32[16,512]{1,0:T(8,128)S(1)} %get-tuple-element.22.p0, ...), custom_call_target="tpu_custom_call" | custom-call | flops 1073741824 | bytes 6291456 | tf_op jit(solution)/shard_map/give/pallas_call | solution.py:409
  181.8 1.4 collective-permute-start.18
  183.2 0.5 collective-permute-start.19
  183.8 0.4 collective-permute-start.20
  184.1 0.7 collective-permute-start.21
  184.8 3.4 %collective-permute-done.19.a1 = s32[256,128]{1,0:T(8,128)S(1)} collective-permute-done((s32[256,128]{1,0:T(8,128)S(1)}, s32[256,128]{1,0:T(8,128)S(1)}, u32[]{:S(2)}, u32[]{:S(2)}) %collective-permute-start.19) | collective-permute-done | bytes 131104 | tf_op jit(solution)/shard_map/ppermute | solution.py:427
  188.2 1.8 collective-permute-done.20.a2
  190.0 3.5 %collective-permute-done.21.a3 = s32[256,128]{1,0:T(8,128)S(1)} collective-permute-done((s32[256,128]{1,0:T(8,128)S(1)}, s32[256,128]{1,0:T(8,128)S(1)}, u32[]{:S(2)}, u32[]{:S(2)}) %collective-permute-start.21) | collective-permute-done | bytes 131104 | tf_op jit(solution)/shard_map/ppermute | solution.py:427
  193.8 2.4 %shard_map.96 = f32[64,2048]{1,0:T(8,128)} custom-call(bf16[256,64]{1,0:T(8,128)(2,1)S(1)} %hits.1.hits_ref, bf16[128,2,2048]{2,1,0:T(2,128)(2,1)} %all-to-all-done.3.got_hbm), custom_call_target="tpu_custom_call" | custom-call | flops 268435456 | bytes 2000000 | tf_op jit(solution)/shard_map/pallas_call | solution.py:348
  196.2 2.4 %shard_map.97 = f32[64,2048]{1,0:T(8,128)} custom-call(bf16[256,64]{1,0:T(8,128)(2,1)S(1)} %hits.1.hits_ref, bf16[128,2,2048]{2,1,0:T(2,128)(2,1)} %all-to-all-done.4.got_hbm), custom_call_target="tpu_custom_call" | custom-call | flops 268435456 | bytes 2000000 | tf_op jit(solution)/shard_map/pallas_call | solution.py:348
  198.6 3.6 %keep.1 = bf16[256,2048]{1,0:T(8,128)(2,1)S(1)} custom-call(bf16[16,512]{1,0:T(8,128)(2,1)S(1)} %copy-done.5, bf16[16,512]{1,0:T(8,128)(2,1)S(1)} %collective-permute-done.6.c1, bf16[16,512]{1,0:T(8,128)(2,1)S(1)} %collective-permute-done.7.c2, bf16[16,512]{1,0:T(8,128)(2,1)S(1)} %collective-permute-done.8.c3, s32[16,512]{1,0:T(8,128)S(1)} %get-tuple-element.22.p0, ...), custom_call_target="tpu_custom_call" | custom-call | flops 1073741824 | bytes 6291456 | tf_op jit(solution)/shard_map/keep/pallas_call | solution.py:409
  202.3 2.6 %add_convert_fusion = bf16[256,2048]{1,0:T(8,128)(2,1)} fusion(bf16[256,2048]{1,0:T(8,128)(2,1)} %collective-permute-done.18, bf16[256,2048]{1,0:T(8,128)(2,1)S(1)} %keep.1), kind=kLoop, calls=%fused_computation | loop fusion | flops 2097152 | bytes 3145728 | tf_op jit(solution)/shard_map/convert_element_type | solution.py:478
  (44 shorter events, 0.7 us)
Async XLA Ops:
  0.6 20.5 %collective-permute-start.3 = (bf16[64,2048]{1,0:T(8,128)(2,1)}, bf16[64,2048]{1,0:T(8,128)(2,1)S(1)}, u32[]{:S(2)}, u32[]{:S(2)}) collective-permute-start(bf16[64,2048]{1,0:T(8,128)(2,1)} %t0.3), channel_id=1, source_target_pairs={{0,6},{2,0},{4,2},{6,4},{1,7},{3,1},{5,3},{7,5},{8,14},{10,8},{12,... | collective-permute-start | bytes 786440 | tf_op jit(solution)/shard_map/ppermute | solution.py:427
  3.4 17.7 %collective-permute-start.4 = (bf16[64,2048]{1,0:T(8,128)(2,1)}, bf16[64,2048]{1,0:T(8,128)(2,1)S(1)}, u32[]{:S(2)}, u32[]{:S(2)}) collective-permute-start(bf16[64,2048]{1,0:T(8,128)(2,1)} %t0.3), channel_id=1, source_target_pairs={{0,4},{2,6},{4,0},{6,2},{1,5},{3,7},{5,1},{7,3},{8,12},{10,14},{12... | collective-permute-start | bytes 786440 | tf_op jit(solution)/shard_map/ppermute | solution.py:427
  3.8 17.4 %collective-permute-start.5 = (bf16[64,2048]{1,0:T(8,128)(2,1)}, bf16[64,2048]{1,0:T(8,128)(2,1)S(1)}, u32[]{:S(2)}, u32[]{:S(2)}) collective-permute-start(bf16[64,2048]{1,0:T(8,128)(2,1)} %t0.3), channel_id=1, source_target_pairs={{0,2},{2,4},{4,6},{6,0},{1,3},{3,5},{5,7},{7,1},{8,10},{10,12},{12... | collective-permute-start | bytes 786440 | tf_op jit(solution)/shard_map/ppermute | solution.py:427
  21.2 8.7 %copy-start.7 = (bf16[64,2048]{1,0:T(8,128)(2,1)S(1)}, bf16[64,2048]{1,0:T(8,128)(2,1)}, u32[]{:S(2)}) copy-start(bf16[64,2048]{1,0:T(8,128)(2,1)} %t0.2) | copy-start | bytes 786436
  23.5 25.8 %all-to-all-start.2 = ((bf16[32,8,2048]{2,1,0:T(8,128)(2,1)}), bf16[32,8,2048]{2,1,0:T(8,128)(2,1)S(1)}, u32[]{:S(2)}, u32[]{:S(2)}) async-start(bf16[32,8,2048]{2,1,0:T(8,128)(2,1)} %bitcast.6), calls=%async_computation.2 | async-start | bytes 2097152 | tf_op jit(solution)/shard_map/all_to_all | solution.py:435
  29.9 27.0 %copy-start.8 = (s32[1,2048,16]{1,2,0:T(8,128)S(1)}, s32[1,2048,16]{1,2,0:T(8,128)}, u32[]{:S(2)}) copy-start(s32[1,2048,16]{1,2,0:T(8,128)} %param.12) | copy-start | bytes 393220
  29.9 27.1 %copy-start.4 = (f32[1,2048,16]{1,2,0:T(8,128)S(1)}, f32[1,2048,16]{1,2,0:T(8,128)}, u32[]{:S(2)}) copy-start(f32[1,2048,16]{1,2,0:T(8,128)} %param.13) | copy-start | bytes 393220
  29.9 7.5 %collective-permute-start = (bf16[64,2048]{1,0:T(8,128)(2,1)S(1)}, bf16[64,2048]{1,0:T(8,128)(2,1)S(1)}, u32[]{:S(2)}, u32[]{:S(2)}) collective-permute-start(bf16[64,2048]{1,0:T(8,128)(2,1)S(1)} %copy-done.7), channel_id=1, source_target_pairs={{0,6},{2,0},{4,2},{6,4},{1,7},{3,1},{5,3},{7,5},{8,14},{10,8},{12,... | collective-permute-start | bytes 786440 | tf_op jit(solution)/shard_map/ppermute | solution.py:427
  31.7 8.7 %collective-permute-start.1 = (bf16[64,2048]{1,0:T(8,128)(2,1)S(1)}, bf16[64,2048]{1,0:T(8,128)(2,1)S(1)}, u32[]{:S(2)}, u32[]{:S(2)}) collective-permute-start(bf16[64,2048]{1,0:T(8,128)(2,1)S(1)} %copy-done.7), channel_id=1, source_target_pairs={{0,4},{2,6},{4,0},{6,2},{1,5},{3,7},{5,1},{7,3},{8,12},{10,14},{12... | collective-permute-start | bytes 786440 | tf_op jit(solution)/shard_map/ppermute | solution.py:427
  33.1 13.9 %collective-permute-start.2 = (bf16[64,2048]{1,0:T(8,128)(2,1)S(1)}, bf16[64,2048]{1,0:T(8,128)(2,1)S(1)}, u32[]{:S(2)}, u32[]{:S(2)}) collective-permute-start(bf16[64,2048]{1,0:T(8,128)(2,1)S(1)} %copy-done.7), channel_id=1, source_target_pairs={{0,2},{2,4},{4,6},{6,0},{1,3},{3,5},{5,7},{7,1},{8,10},{10,12},{12... | collective-permute-start | bytes 786440 | tf_op jit(solution)/shard_map/ppermute | solution.py:427
  49.3 10.5 %copy-start = (bf16[32,8,2048]{2,1,0:T(8,128)(2,1)}, bf16[32,8,2048]{2,1,0:T(8,128)(2,1)S(1)}, u32[]{:S(2)}) copy-start(bf16[32,8,2048]{2,1,0:T(8,128)(2,1)S(1)} %all-to-all-done.2) | copy-start | bytes 3145732
  49.3 22.8 %all-to-all-start.1 = ((bf16[32,8,2048]{2,1,0:T(8,128)(2,1)}), bf16[32,8,2048]{2,1,0:T(8,128)(2,1)S(1)}, u32[]{:S(2)}, u32[]{:S(2)}) async-start(bf16[32,8,2048]{2,1,0:T(8,128)(2,1)} %bitcast.4), calls=%async_computation.1 | async-start | bytes 2097152 | tf_op jit(solution)/shard_map/all_to_all | solution.py:435
  57.0 14.7 %copy-start.3 = (s32[16,2048]{1,0:T(8,128)}, s32[16,2048]{1,0:T(8,128)S(1)}, u32[]{:S(2)}) copy-start(s32[16,2048]{1,0:T(8,128)S(1)} %get-tuple-element.24.places_ref.refs_0_) | copy-start | bytes 393220
  59.9 1.3 copy-start.2
  72.1 1.0 copy-start.6
  85.1 8.1 %copy-start.1 = (bf16[32,8,2048]{2,1,0:T(8,128)(2,1)S(1)}, bf16[32,8,2048]{2,1,0:T(8,128)(2,1)}, u32[]{:S(2)}) copy-start(bf16[32,8,2048]{2,1,0:T(8,128)(2,1)} %copy-done) | copy-start | bytes 3145732
  85.1 63.0 %copy-start.11 = (bf16[16,512]{1,0:T(8,128)(2,1)S(1)}, bf16[16,512]{1,0:T(8,128)(2,1)}, u32[]{:S(2)}) copy-start(bf16[16,512]{1,0:T(8,128)(2,1)} %get-tuple-element.12) | copy-start | bytes 49156
  85.1 65.6 %copy-start.10 = (bf16[16,512]{1,0:T(8,128)(2,1)S(1)}, bf16[16,512]{1,0:T(8,128)(2,1)}, u32[]{:S(2)}) copy-start(bf16[16,512]{1,0:T(8,128)(2,1)} %get-tuple-element.13) | copy-start | bytes 49156
  85.1 66.5 %all-to-all-start.3 = ((bf16[128,2,2048]{2,1,0:T(2,128)(2,1)}), bf16[128,2,2048]{2,1,0:T(2,128)(2,1)}, u32[]{:S(2)}, u32[]{:S(2)}) async-start(bf16[128,2,2048]{2,1,0:T(2,128)(2,1)} %get-tuple-element.15), calls=%async_computation.3 | async-start | bytes 2097152 | tf_op jit(solution)/shard_map/all_to_all | solution.py:435
  93.2 72.0 %copy-start.9 = (bf16[16,512]{1,0:T(8,128)(2,1)S(1)}, bf16[16,512]{1,0:T(8,128)(2,1)}, u32[]{:S(2)}) copy-start(bf16[16,512]{1,0:T(8,128)(2,1)} %get-tuple-element.14) | copy-start | bytes 49156
  93.2 85.0 %copy-start.5 = (bf16[16,512]{1,0:T(8,128)(2,1)S(1)}, bf16[16,512]{1,0:T(8,128)(2,1)}, u32[]{:S(2)}) copy-start(bf16[16,512]{1,0:T(8,128)(2,1)} %get-tuple-element.11.c0) | copy-start | bytes 49156
  94.2 22.4 %collective-permute-start.12 = (bf16[128,2048]{1,0:T(8,128)(2,1)}, bf16[128,2048]{1,0:T(8,128)(2,1)S(1)}, u32[]{:S(2)}, u32[]{:S(2)}) collective-permute-start(bf16[128,2048]{1,0:T(8,128)(2,1)} %get-tuple-element.18), channel_id=1, source_target_pairs={{0,6},{2,0},{4,2},{6,4},{1,7},{3,1},{5,3},{7,5},{8,14},{10,8},{12,... | collective-permute-start | bytes 1572872 | tf_op jit(solution)/shard_map/ppermute | solution.py:427
  96.7 21.6 %collective-permute-start.15 = (bf16[128,2048]{1,0:T(8,128)(2,1)}, bf16[128,2048]{1,0:T(8,128)(2,1)S(1)}, u32[]{:S(2)}, u32[]{:S(2)}) collective-permute-start(bf16[128,2048]{1,0:T(8,128)(2,1)} %get-tuple-element.17), channel_id=1, source_target_pairs={{0,2},{2,4},{4,6},{6,0},{1,3},{3,5},{5,7},{7,1},{8,10},{10,12},{12... | collective-permute-start | bytes 1572872 | tf_op jit(solution)/shard_map/ppermute | solution.py:427
  96.7 81.4 %collective-permute-start.13 = (bf16[128,2048]{1,0:T(8,128)(2,1)}, bf16[128,2048]{1,0:T(8,128)(2,1)S(1)}, u32[]{:S(2)}, u32[]{:S(2)}) collective-permute-start(bf16[128,2048]{1,0:T(8,128)(2,1)} %get-tuple-element.17), channel_id=1, source_target_pairs={{0,6},{2,0},{4,2},{6,4},{1,7},{3,1},{5,3},{7,5},{8,14},{10,8},{12,... | collective-permute-start | bytes 1572872 | tf_op jit(solution)/shard_map/ppermute | solution.py:427
  99.4 78.8 %collective-permute-start.17 = (bf16[128,2048]{1,0:T(8,128)(2,1)}, bf16[128,2048]{1,0:T(8,128)(2,1)S(1)}, u32[]{:S(2)}, u32[]{:S(2)}) collective-permute-start(bf16[128,2048]{1,0:T(8,128)(2,1)} %get-tuple-element.18), channel_id=1, source_target_pairs={{0,2},{2,4},{4,6},{6,0},{1,3},{3,5},{5,7},{7,1},{8,10},{10,12},{12... | collective-permute-start | bytes 1572872 | tf_op jit(solution)/shard_map/ppermute | solution.py:427
  116.6 61.6 %collective-permute-start.14 = (bf16[128,2048]{1,0:T(8,128)(2,1)S(1)}, bf16[128,2048]{1,0:T(8,128)(2,1)}, u32[]{:S(2)}, u32[]{:S(2)}) collective-permute-start(bf16[128,2048]{1,0:T(8,128)(2,1)S(1)} %collective-permute-done.12.refs_1_), channel_id=1, source_target_pairs={{0,6},{2,0},{4,2},{6,4},{1,7},{3,1},{5,3},{7,5},{8,14},{10,8},{12,... | collective-permute-start | bytes 1572872 | tf_op jit(solution)/shard_map/ppermute | solution.py:427
  118.3 59.9 %collective-permute-start.16 = (bf16[128,2048]{1,0:T(8,128)(2,1)S(1)}, bf16[128,2048]{1,0:T(8,128)(2,1)}, u32[]{:S(2)}, u32[]{:S(2)}) collective-permute-start(bf16[128,2048]{1,0:T(8,128)(2,1)S(1)} %collective-permute-done.15.refs_6_), channel_id=1, source_target_pairs={{0,2},{2,4},{4,6},{6,0},{1,3},{3,5},{5,7},{7,1},{8,10},{10,12},{12... | collective-permute-start | bytes 1572872 | tf_op jit(solution)/shard_map/ppermute | solution.py:427
  118.3 23.1 %collective-permute-start.10 = (s32[16,512]{1,0:T(8,128)S(1)}, s32[16,512]{1,0:T(8,128)S(1)}, u32[]{:S(2)}, u32[]{:S(2)}) collective-permute-start(s32[16,512]{1,0:T(8,128)S(1)} %get-tuple-element.20), channel_id=1, source_target_pairs={{0,4},{2,6},{4,0},{6,2},{1,5},{3,7},{5,1},{7,3},{8,12},{10,14},{12... | collective-permute-start | bytes 98312 | tf_op jit(solution)/shard_map/ppermute | solution.py:427
  141.4 4.0 %collective-permute-start.11 = (s32[16,512]{1,0:T(8,128)S(1)}, s32[16,512]{1,0:T(8,128)S(1)}, u32[]{:S(2)}, u32[]{:S(2)}) collective-permute-start(s32[16,512]{1,0:T(8,128)S(1)} %get-tuple-element.19), channel_id=1, source_target_pairs={{0,2},{2,4},{4,6},{6,0},{1,3},{3,5},{5,7},{7,1},{8,10},{10,12},{12... | collective-permute-start | bytes 98312 | tf_op jit(solution)/shard_map/ppermute | solution.py:427
  145.3 2.8 %collective-permute-start.9 = (s32[16,512]{1,0:T(8,128)S(1)}, s32[16,512]{1,0:T(8,128)S(1)}, u32[]{:S(2)}, u32[]{:S(2)}) collective-permute-start(s32[16,512]{1,0:T(8,128)S(1)} %get-tuple-element.21), channel_id=1, source_target_pairs={{0,6},{2,0},{4,2},{6,4},{1,7},{3,1},{5,3},{7,5},{8,14},{10,8},{12,... | collective-permute-start | bytes 98312 | tf_op jit(solution)/shard_map/ppermute | solution.py:427
  148.1 2.6 %collective-permute-start.6 = (bf16[16,512]{1,0:T(8,128)(2,1)S(1)}, bf16[16,512]{1,0:T(8,128)(2,1)S(1)}, u32[]{:S(2)}, u32[]{:S(2)}) collective-permute-start(bf16[16,512]{1,0:T(8,128)(2,1)S(1)} %copy-done.11), channel_id=1, source_target_pairs={{0,6},{2,0},{4,2},{6,4},{1,7},{3,1},{5,3},{7,5},{8,14},{10,8},{12,... | collective-permute-start | bytes 49160 | tf_op jit(solution)/shard_map/ppermute | solution.py:427
  150.7 14.4 %collective-permute-start.7 = (bf16[16,512]{1,0:T(8,128)(2,1)S(1)}, bf16[16,512]{1,0:T(8,128)(2,1)S(1)}, u32[]{:S(2)}, u32[]{:S(2)}) collective-permute-start(bf16[16,512]{1,0:T(8,128)(2,1)S(1)} %copy-done.10), channel_id=1, source_target_pairs={{0,4},{2,6},{4,0},{6,2},{1,5},{3,7},{5,1},{7,3},{8,12},{10,14},{12... | collective-permute-start | bytes 49160 | tf_op jit(solution)/shard_map/ppermute | solution.py:427
  151.6 44.6 %all-to-all-start.4 = ((bf16[128,2,2048]{2,1,0:T(2,128)(2,1)}), bf16[128,2,2048]{2,1,0:T(2,128)(2,1)}, u32[]{:S(2)}, u32[]{:S(2)}) async-start(bf16[128,2,2048]{2,1,0:T(2,128)(2,1)} %get-tuple-element.16), calls=%async_computation.4 | async-start | bytes 2097152 | tf_op jit(solution)/shard_map/all_to_all | solution.py:435
  165.2 13.0 %collective-permute-start.8 = (bf16[16,512]{1,0:T(8,128)(2,1)S(1)}, bf16[16,512]{1,0:T(8,128)(2,1)S(1)}, u32[]{:S(2)}, u32[]{:S(2)}) collective-permute-start(bf16[16,512]{1,0:T(8,128)(2,1)S(1)} %copy-done.9), channel_id=1, source_target_pairs={{0,2},{2,4},{4,6},{6,0},{1,3},{3,5},{5,7},{7,1},{8,10},{10,12},{12... | collective-permute-start | bytes 49160 | tf_op jit(solution)/shard_map/ppermute | solution.py:427
  181.8 20.4 %collective-permute-start.18 = (bf16[256,2048]{1,0:T(8,128)(2,1)}, bf16[256,2048]{1,0:T(8,128)(2,1)}, u32[]{:S(2)}, u32[]{:S(2)}) collective-permute-start(bf16[256,2048]{1,0:T(8,128)(2,1)} %give.1), channel_id=1, source_target_pairs={{0,1},{1,0},{2,3},{3,2},{4,5},{5,4},{6,7},{7,6},{8,9},{9,8},{10,11... | collective-permute-start | bytes 3145736 | tf_op jit(solution)/shard_map/ppermute | solution.py:476
  183.2 5.0 %collective-permute-start.19 = (s32[256,128]{1,0:T(8,128)S(1)}, s32[256,128]{1,0:T(8,128)S(1)}, u32[]{:S(2)}, u32[]{:S(2)}) collective-permute-start(s32[256,128]{1,0:T(8,128)S(1)} %bitcast.41), channel_id=1, source_target_pairs={{0,6},{2,0},{4,2},{6,4},{1,7},{3,1},{5,3},{7,5},{8,14},{10,8},{12,... | collective-permute-start | bytes 393224 | tf_op jit(solution)/shard_map/ppermute | solution.py:427
  183.8 6.2 %collective-permute-start.20 = (s32[256,128]{1,0:T(8,128)S(1)}, s32[256,128]{1,0:T(8,128)S(1)}, u32[]{:S(2)}, u32[]{:S(2)}) collective-permute-start(s32[256,128]{1,0:T(8,128)S(1)} %bitcast.42), channel_id=1, source_target_pairs={{0,4},{2,6},{4,0},{6,2},{1,5},{3,7},{5,1},{7,3},{8,12},{10,14},{12... | collective-permute-start | bytes 393224 | tf_op jit(solution)/shard_map/ppermute | solution.py:427
  184.1 9.4 %collective-permute-start.21 = (s32[256,128]{1,0:T(8,128)S(1)}, s32[256,128]{1,0:T(8,128)S(1)}, u32[]{:S(2)}, u32[]{:S(2)}) collective-permute-start(s32[256,128]{1,0:T(8,128)S(1)} %bitcast.43), channel_id=1, source_target_pairs={{0,2},{2,4},{4,6},{6,0},{1,3},{3,5},{5,7},{7,1},{8,10},{10,12},{12... | collective-permute-start | bytes 393224 | tf_op jit(solution)/shard_map/ppermute | solution.py:427
